TPU v7x, 32 devices: a whole 2x2x4 slice. The times are simulated.
32 devices in a mesh: dp: 8 (over z, y), tensor: 4 (over x, core).
Axes of the slice: x: 2, y: 2, z: 4, core: 2. Of those that a mesh axis runs over, the one named last changes fastest.
Arguments:
- tokens: bfloat16 [16384, 768], P(('dp', 'tensor')), may hold values from -6 to 6
- bank: bfloat16 [16, 4096, 768], P('dp', 'tensor'), may hold values from -6 to 6
- prefix: int32 [16], P('dp'), may hold values from 102 to 512
- blocks: int32 [16, 16], P('dp'), may hold values from 0 to 63, all different within a row
- out_grad: bfloat16 [16384, 768], P(('dp', 'tensor')), may hold values from -6 to 6
- selfq_weight: float32 [768, 768], P('dp', 'tensor'), may hold values from -0.21875 to 0.21875
- selfq_bias: float32 [768], P('tensor'), may hold values from -3 to 3
- selfk_weight: float32 [768, 768], P('dp', 'tensor'), may hold values from -0.21875 to 0.21875
- selfv_weight: float32 [768, 768], P('dp', 'tensor'), may hold values from -0.21875 to 0.21875
- selfv_bias: float32 [768], P('tensor'), may hold values from -3 to 3
- selfo_weight: float32 [768, 768], P('tensor', 'dp'), may hold values from -2.5 to 2.5
- selfo_bias: float32 [768], replicated, may hold values from -3 to 3
- first_gain: float32 [768], replicated, may hold values from 0.5 to 1.5
- first_shift: float32 [768], replicated, may hold values from -2 to 2
- crossq_weight: float32 [768, 768], P('dp', 'tensor'), may hold values from -0.21875 to 0.21875
- crossq_bias: float32 [768], P('tensor'), may hold values from -3 to 3
- crossk_weight: float32 [768, 768], P('dp', 'tensor'), may hold values from -0.21875 to 0.21875
- crossv_weight: float32 [768, 768], P('dp', 'tensor'), may hold values from -0.21875 to 0.21875
- crossv_bias: float32 [768], P('tensor'), may hold values from -3 to 3
- crosso_weight: float32 [768, 768], P('tensor', 'dp'), may hold values from -2.5 to 2.5
- crosso_bias: float32 [768], replicated, may hold values from -3 to 3
- second_gain: float32 [768], replicated, may hold values from 0.5 to 1.5
- second_shift: float32 [768], replicated, may hold values from -2 to 2
- expand_weight: float32 [768, 3072], P('dp', 'tensor'), may hold values from -0.21875 to 0.21875
- expand_bias: float32 [3072], P('tensor'), may hold values from -3 to 3
- shrink_weight: float32 [3072, 768], P('tensor', 'dp'), may hold values from -0.15625 to 0.15625
- shrink_bias: float32 [768], replicated, may hold values from -3 to 3
- third_gain: float32 [768], replicated, may hold values from 0.5 to 1.5
- third_shift: float32 [768], replicated, may hold values from -2 to 2
Outputs:
- out_act: bfloat16 [16384, 768], P(('dp', 'tensor'))
- in_grad: bfloat16 [16384, 768], P(('dp', 'tensor'))
- bank_grad: float32 [16, 4096, 768], P('dp', 'tensor')
- selfq_wgrad: float32 [768, 768], P('dp', 'tensor')
- selfq_bgrad: float32 [768], P('tensor')
- selfk_wgrad: float32 [768, 768], P('dp', 'tensor')
- selfv_wgrad: float32 [768, 768], P('dp', 'tensor')
- selfv_bgrad: float32 [768], P('tensor')
- selfo_wgrad: float32 [768, 768], P('tensor', 'dp')
- selfo_bgrad: float32 [768], replicated
- first_ggrad: float32 [768], replicated
- first_sgrad: float32 [768], replicated
- crossq_wgrad: float32 [768, 768], P('dp', 'tensor')
- crossq_bgrad: float32 [768], P('tensor')
- crossk_wgrad: float32 [768, 768], P('dp', 'tensor')
- crossv_wgrad: float32 [768, 768], P('dp', 'tensor')
- crossv_bgrad: float32 [768], P('tensor')
- crosso_wgrad: float32 [768, 768], P('tensor', 'dp')
- crosso_bgrad: float32 [768], replicated
- second_ggrad: float32 [768], replicated
- second_sgrad: float32 [768], replicated
- expand_wgrad: float32 [768, 3072], P('dp', 'tensor')
- expand_bgrad: float32 [3072], P('tensor')
- shrink_wgrad: float32 [3072, 768], P('tensor', 'dp')
- shrink_bgrad: float32 [768], replicated
- third_ggrad: float32 [768], replicated
- third_sgrad: float32 [768], replicated
Inputs may be any that keep to these rules, and one draw needn't show every extreme that they name: The 16 blocks of one sequence are distinct.
All inputs are finite; a program needn't handle non-finite values.
Results may differ from a plain program's by a relative error of at most 0.025.
Values may be sent and summed in bfloat16 or wider, within the bound.
No kernel may reach another device: no remote copies, remote signals or barrier semaphores. Data moves between devices by JAX's collectives and lax.ppermute only.
A program may use at most 192 MiB of HBM per device.

v0:
```python
import functools
import math

import jax
import jax.numpy as jnp
from jax import lax
from jax.experimental import pallas as pl
from jax.experimental.pallas import tpu as pltpu
from jax.sharding import PartitionSpec as P

HD = 64
BLK = 64
NBLK = 16
EPS = 1e-05
NEGATIVE = -1e30
BF = jnp.bfloat16
F32 = jnp.float32

NT = (((1,), (1,)), ((), ()))
NN = (((1,), (0,)), ((), ()))
TN = (((0,), (0,)), ((), ()))

CORE_SWAP = ((0, 1), (1, 0), (2, 3), (3, 2))
X_SWAP = ((0, 2), (2, 0), (1, 3), (3, 1))
VMEM_LIMIT = 48 << 20


def mm(left, right, dims=NN):
    return lax.dot_general(left, right, dims, preferred_element_type=F32)


def swap_core(value):
    return lax.ppermute(value, "tensor", CORE_SWAP)


def swap_x(value):
    return lax.ppermute(value, "tensor", X_SWAP)


def swap_dp(value, bit):
    count = lax.axis_size("dp")
    return lax.ppermute(value, "dp", tuple((i, i ^ bit) for i in range(count)))


def dp_bits():
    count = lax.axis_size("dp")
    bits = []
    bit = count // 2
    while bit >= 1:
        bits.append(bit)
        bit //= 2
    return bits


def pair_backward(q, k, v, grad, lse, delta, mask):
    score = mm(k, q, NT)
    prob = jnp.exp(score - lse)
    if mask is not None:
        prob = jnp.where(mask, prob, 0.0)
    slope = prob * (mm(v, grad, NT) - delta)
    prob = prob.astype(BF)
    slope = slope.astype(BF)
    return mm(slope, k, TN), mm(slope, q, NN), mm(prob, grad, NN)


def delta_row(grad, mixed):
    return jnp.sum((grad.astype(F32) * mixed.astype(F32)).T, 0, keepdims=True)


def self_bwd_kernel(info, q_ref, k_ref, v_ref, oa_ref, ob_ref, lse_ref, ga_ref, gb_ref, *rest):
    out_ref, sums_ref, o_ref, g_ref = rest[-4:]
    dq_ref, dk_ref, dv_ref = out_ref.at[0], out_ref.at[1], out_ref.at[2]
    o_ref[0], o_ref[1] = oa_ref[...], ob_ref[...]
    g_ref[0], g_ref[1] = ga_ref[...], gb_ref[...]
    half = q_ref.shape[1]
    first = info[0]
    second = 1 - first
    prefix = info[1]
    key_pos = lax.broadcasted_iota(jnp.int32, (half, half), 0)
    query_pos = lax.broadcasted_iota(jnp.int32, (half, half), 1)
    causal = key_pos <= query_pos
    seen = causal | (key_pos < prefix)
    scale = 1.0 / math.sqrt(HD)
    for h in range(2):
        cols = slice(HD * h, HD * h + HD)

        def rows(ref, at):
            return ref[at, :, cols]

        def one(q_at, k_at, mask):
            grad = rows(g_ref, q_at)
            delta = delta_row(grad, rows(o_ref, q_at))
            lse = lse_ref[0, h, pl.ds(q_at, 1), :]
            return pair_backward(
                rows(q_ref, q_at), rows(k_ref, k_at), rows(v_ref, k_at), grad, lse, delta, mask
            )

        dq, dk_a, dv_a = one(first, first, seen)
        dq_ref[first, :, cols] = (dq.astype(BF) * scale).astype(BF)
        dq_b, dk_b, dv_b = one(second, first, None)
        dk_ref[first, :, cols] = (dk_a + dk_b).astype(BF)
        dv_ref[first, :, cols] = (dv_a + dv_b).astype(BF)
        dq_c, dk_c, dv_c = one(second, second, causal)
        dq_ref[second, :, cols] = ((dq_b + dq_c).astype(BF) * scale).astype(BF)
        dk_ref[second, :, cols] = dk_c.astype(BF)
        dv_ref[second, :, cols] = dv_c.astype(BF)
    for i in range(3):
        both = out_ref[i, 0].astype(F32) + out_ref[i, 1].astype(F32)
        sums_ref[0, i : i + 1, :] = jnp.sum(both, 0, keepdims=True)


def self_backward(info, qkv, mixed_own, mixed_oth, lse, grad_own, grad_oth, start, count, former=()):
    half, width = qkv.shape[1], qkv.shape[2] // 3
    pairs = width // 128

    def spec(which):
        return pl.BlockSpec((2, half, 128), lambda i, info: (0, 0, which * pairs + start + i))

    flat = pl.BlockSpec((half, 128), lambda i, info: (0, start + i))
    cells = 3 * half * half * count * 2
    return pl.pallas_call(
        self_bwd_kernel,
        grid_spec=pltpu.PrefetchScalarGridSpec(
            num_scalar_prefetch=1,
            grid=(count,),
            in_specs=[
                spec(0),
                spec(1),
                spec(2),
                flat,
                flat,
                pl.BlockSpec((1, 2, 2, half), lambda i, info: (start + i, 0, 0, 0)),
                flat,
                flat,
            ]
            + [pl.BlockSpec(memory_space=pl.ANY)] * len(former),
            out_specs=[
                pl.BlockSpec((3, 2, half, 128), lambda i, info: (0, 0, 0, start + i)),
                pl.BlockSpec((1, 8, 128), lambda i, info: (start + i, 0, 0)),
            ],
            scratch_shapes=[pltpu.VMEM((2, half, 128), BF)] * 2,
        ),
        out_shape=[
            jax.ShapeDtypeStruct((3, 2, half, width), BF),
            jax.ShapeDtypeStruct((pairs, 8, 128), F32),
        ],
        input_output_aliases={9 + i: i for i in range(len(former))},
        compiler_params=pltpu.CompilerParams(vmem_limit_bytes=VMEM_LIMIT),
        cost_estimate=pl.CostEstimate(
            flops=cells * HD * 10 * 4, transcendentals=cells, bytes_accessed=qkv.size * 2 * count
        ),
        name="self_bwd",
    )(info, qkv, qkv, qkv, mixed_own, mixed_oth, lse, grad_own, grad_oth, *former)


def cross_fwd_kernel(q_ref, ka_ref, kb_ref, va_ref, vb_ref, o_ref, lse_ref):
    for h in range(2):
        cols = slice(HD * h, HD * h + HD)
        q = q_ref[:, cols]
        score_a = mm(ka_ref[:, cols], q, NT)
        score_b = mm(kb_ref[:, cols], q, NT)
        top = jnp.maximum(
            jnp.max(score_a, 0, keepdims=True), jnp.max(score_b, 0, keepdims=True)
        )
        expo_a = jnp.exp(score_a - top)
        expo_b = jnp.exp(score_b - top)
        total = jnp.sum(expo_a, 0, keepdims=True) + jnp.sum(expo_b, 0, keepdims=True)
        mixed = (
            mm(va_ref[:, cols], expo_a.astype(BF), TN) + mm(vb_ref[:, cols], expo_b.astype(BF), TN)
        ) / total
        o_ref[:, cols] = mixed.T.astype(BF)
        lse_ref[0, h : h + 1, :] = top + jnp.log(total)


def cross_specs(rows, pairs):
    whole = pl.BlockSpec((rows, 128), lambda i: (0, i))
    turned = pl.BlockSpec((rows, 128), lambda i: (0, (i + pairs // 2) % pairs))
    value = pl.BlockSpec((rows, 128), lambda i: (0, pairs + i))
    value_turned = pl.BlockSpec((rows, 128), lambda i: (0, pairs + (i + pairs // 2) % pairs))
    return whole, turned, value, value_turned


def cross_forward(queries, kv_own, kv_oth):
    rows, width = queries.shape
    pairs = width // 128
    whole, turned, value, value_turned = cross_specs(rows, pairs)
    cells = 2 * rows * rows * pairs * 2
    return pl.pallas_call(
        cross_fwd_kernel,
        grid=(pairs,),
        in_specs=[whole, whole, turned, value, value_turned],
        out_specs=[whole, pl.BlockSpec((1, 2, rows), lambda i: (i, 0, 0))],
        out_shape=[
            jax.ShapeDtypeStruct((rows, width), BF),
            jax.ShapeDtypeStruct((pairs, 2, rows), F32),
        ],
        compiler_params=pltpu.CompilerParams(vmem_limit_bytes=VMEM_LIMIT),
        cost_estimate=pl.CostEstimate(
            flops=cells * HD * 4 * 4, transcendentals=cells, bytes_accessed=queries.size * 12
        ),
        name="cross_fwd",
    )(queries, kv_own, kv_oth, kv_own, kv_oth)


def cross_bwd_kernel(
    q_ref, ka_ref, kb_ref, va_ref, vb_ref, o_ref, lse_ref, g_ref,
    *rest,
):
    dq_ref, da_ref, db_ref = rest[-3:]
    scale = 1.0 / math.sqrt(HD)
    for h in range(2):
        cols = slice(HD * h, HD * h + HD)
        grad = g_ref[:, cols]
        delta = delta_row(grad, o_ref[:, cols])
        lse = lse_ref[0, h : h + 1, :]
        q = q_ref[:, cols]
        dq_a, dk, dv = pair_backward(q, ka_ref[:, cols], va_ref[:, cols], grad, lse, delta, None)
        da_ref[0, :, cols] = dk.astype(BF)
        da_ref[1, :, cols] = dv.astype(BF)
        dq_b, dk, dv = pair_backward(q, kb_ref[:, cols], vb_ref[:, cols], grad, lse, delta, None)
        db_ref[0, :, cols] = dk.astype(BF)
        db_ref[1, :, cols] = dv.astype(BF)
        dq_ref[:, cols] = ((dq_a + dq_b).astype(BF) * scale).astype(BF)


def cross_backward(queries, kv_own, kv_oth, mixed, lse, grad, start, count, former=()):
    rows, width = queries.shape
    pairs = width // 128

    def turn(i):
        return (start + i + pairs // 2) % pairs

    whole = pl.BlockSpec((rows, 128), lambda i: (0, start + i))
    turned = pl.BlockSpec((rows, 128), lambda i: (0, turn(i)))
    value = pl.BlockSpec((rows, 128), lambda i: (0, pairs + start + i))
    value_turned = pl.BlockSpec((rows, 128), lambda i: (0, pairs + turn(i)))
    cells = 2 * rows * rows * count * 2
    both = jax.ShapeDtypeStruct((2, rows, width), BF)
    return pl.pallas_call(
        cross_bwd_kernel,
        grid=(count,),
        in_specs=[
            whole, whole, turned, value, value_turned, whole,
            pl.BlockSpec((1, 2, rows), lambda i: (start + i, 0, 0)), whole,
        ]
        + [pl.BlockSpec(memory_space=pl.ANY)] * len(former),
        out_specs=[
            whole,
            pl.BlockSpec((2, rows, 128), lambda i: (0, 0, start + i)),
            pl.BlockSpec((2, rows, 128), lambda i: (0, 0, turn(i))),
        ],
        out_shape=[jax.ShapeDtypeStruct((rows, width), BF), both, both],
        input_output_aliases={8 + i: i for i in range(len(former))},
        compiler_params=pltpu.CompilerParams(vmem_limit_bytes=VMEM_LIMIT),
        cost_estimate=pl.CostEstimate(
            flops=cells * HD * 10 * 4, transcendentals=cells, bytes_accessed=rows * 128 * 24 * count
        ),
        name="cross_bwd",
    )(queries, kv_own, kv_oth, kv_own, kv_oth, mixed, lse, grad, *former)


def norm_parts(resid):
    center = resid - jnp.mean(resid, axis=-1, keepdims=True)
    rstd = lax.rsqrt(jnp.mean(center * center, axis=-1, keepdims=True) + EPS)
    return center * rstd, rstd


def norm_back(normed, rstd, grad, gain):
    scaled = grad * gain
    return rstd * (
        scaled
        - jnp.mean(scaled, axis=-1, keepdims=True)
        - normed * jnp.mean(scaled * normed, axis=-1, keepdims=True)
    )


def cross_first_kernel(
    q_ref, ka_ref, kb_ref, va_ref, vb_ref, o_ref, lse_ref, g_ref,
    q_mat, second_ref, resid_ref, vec_ref, o_mat, dq_in, former_a, former_b,
    dq_ref, da_ref, db_ref, first_ref, low_ref, keep_ref, send_ref, sums_ref, dq_part,
    *, start, count,
):
    step = pl.program_id(0)

    @pl.when(step == 0)
    def _():
        dq_ref[...] = dq_in[...]

    cross_bwd_kernel(
        q_ref, ka_ref, kb_ref, va_ref, vb_ref, o_ref, lse_ref, g_ref, dq_part, da_ref, db_ref
    )
    at = pl.multiple_of((start + step) * 128, 128)
    dq_ref[:, pl.ds(at, 128)] = dq_part[...]

    @pl.when(step == count - 1)
    def _():
        grad = second_ref[...] + mm(dq_ref[...], q_mat[...], NT)
        normed, rstd = norm_parts(resid_ref[...])
        sums_ref[0:1, :] = jnp.sum(grad, 0, keepdims=True)
        sums_ref[1:2, :] = jnp.sum(grad * normed, 0, keepdims=True)
        first_in = norm_back(normed, rstd, grad, vec_ref[0:1, :])
        first_ref[...] = first_in
        low = first_in.astype(BF)
        low_ref[...] = low
        sums_ref[2:3, :] = jnp.sum(low.astype(F32), 0, keepdims=True)
        sums_ref[3:4, :] = jnp.sum(dq_ref[...].astype(F32), 0, keepdims=True)
        sums_ref[4:8, :] = jnp.zeros((4, sums_ref.shape[1]), F32)
        mixed_grad = mm(low, o_mat[...]).astype(BF)
        cols = keep_ref.shape[1]
        keep_ref[...] = mixed_grad[:, :cols]
        send_ref[...] = mixed_grad[:, cols:]


def cross_first_backward(
    queries, kv_own, kv_oth, mixed, lse, grad, start, former, q_mat, second_in, resid, vec, o_mat
):
    rows, width = queries.shape
    pairs = width // 128
    count = pairs - start

    def turn(i):
        return (start + i + pairs // 2) % pairs

    whole = pl.BlockSpec((rows, 128), lambda i: (0, start + i))
    turned = pl.BlockSpec((rows, 128), lambda i: (0, turn(i)))
    value = pl.BlockSpec((rows, 128), lambda i: (0, pairs + start + i))
    value_turned = pl.BlockSpec((rows, 128), lambda i: (0, pairs + turn(i)))

    def fixed(shape):
        return pl.BlockSpec(shape, lambda i: (0, 0))

    both = jax.ShapeDtypeStruct((2, rows, width), BF)
    return pl.pallas_call(
        functools.partial(cross_first_kernel, start=start, count=count),
        grid=(count,),
        in_specs=[
            whole, whole, turned, value, value_turned, whole,
            pl.BlockSpec((1, 2, rows), lambda i: (start + i, 0, 0)), whole,
            fixed((width, width)), fixed((rows, width)), fixed((rows, width)),
            fixed((1, width)), fixed((width, width)), fixed((rows, width)),
            pl.BlockSpec(memory_space=pl.ANY), pl.BlockSpec(memory_space=pl.ANY),
        ],
        out_specs=[
            fixed((rows, width)),
            pl.BlockSpec((2, rows, 128), lambda i: (0, 0, start + i)),
            pl.BlockSpec((2, rows, 128), lambda i: (0, 0, turn(i))),
            fixed((rows, width)),
            fixed((rows, width)),
            fixed((rows, width // 2)),
            fixed((rows, width // 2)),
            fixed((8, width)),
        ],
        out_shape=[
            jax.ShapeDtypeStruct((rows, width), BF),
            both,
            both,
            jax.ShapeDtypeStruct((rows, width), F32),
            jax.ShapeDtypeStruct((rows, width), BF),
            jax.ShapeDtypeStruct((rows, width // 2), BF),
            jax.ShapeDtypeStruct((rows, width // 2), BF),
            jax.ShapeDtypeStruct((8, width), F32),
        ],
        scratch_shapes=[pltpu.VMEM((rows, 128), BF)],
        input_output_aliases={14: 1, 15: 2},
        compiler_params=pltpu.CompilerParams(vmem_limit_bytes=VMEM_LIMIT),
        cost_estimate=pl.CostEstimate(
            flops=2 * rows * rows * count * 2 * HD * 40, transcendentals=0,
            bytes_accessed=rows * 128 * 24 * count,
        ),
        name="cross_first",
    )(
        queries, kv_own, kv_oth, kv_own, kv_oth, mixed, lse, grad,
        q_mat, second_in, resid, vec, o_mat, *former,
    )


def gate(value, *others):
    return lax.optimization_barrier((value,) + others)[0]


def outer_count():
    return lax.axis_size("dp") // 2


def swap_both(value):
    count = lax.axis_size("dp")
    pairs = tuple(
        (d * 4 + t, (d ^ 1) * 4 + (t ^ 2)) for d in range(count) for t in range(4)
    )
    return lax.ppermute(value, ("dp", "tensor"), pairs)


def outer_exchange(value):
    groups = [[inner + 2 * o for o in range(outer_count())] for inner in range(2)]
    return lax.all_to_all(value, "dp", 0, 0, axis_index_groups=groups, tiled=True)


def plane_exchange(value):
    groups = [
        [(o * 2 + inner) * 4 + chip * 2 + core for chip in range(2) for inner in range(2)]
        for o in range(outer_count())
        for core in range(2)
    ]
    return lax.all_to_all(value, ("dp", "tensor"), 0, 0, axis_index_groups=groups, tiled=True)


def add_low(left, right):
    return (left.astype(F32) + right.astype(F32)).astype(BF)


def total_dp(value):
    for bit in dp_bits():
        value = value + swap_dp(value, bit)
    return value


ANY = pl.BlockSpec(memory_space=pl.ANY)
VM = pl.BlockSpec(memory_space=pltpu.VMEM)
SM = pl.BlockSpec(memory_space=pltpu.SMEM)


def call(kernel, out_shape, args, in_specs, out_specs, scratch=(), flops=0, moved=0, name=None):
    return pl.pallas_call(
        kernel,
        out_shape=out_shape,
        in_specs=in_specs,
        out_specs=out_specs,
        scratch_shapes=list(scratch),
        compiler_params=pltpu.CompilerParams(vmem_limit_bytes=58 << 20),
        cost_estimate=pl.CostEstimate(flops=flops, bytes_accessed=moved, transcendentals=0),
        name=name,
    )(*args)


def struct(shape, dtype):
    return jax.ShapeDtypeStruct(shape, dtype)


def pack_self_kernel(q_ref, k_ref, v_ref, out_ref):
    cols = q_ref.shape[1]
    for i, ref in enumerate((q_ref, k_ref, v_ref)):
        low = ref[...].astype(BF)
        for copy in range(out_ref.shape[0]):
            out_ref[copy, :, i * cols : (i + 1) * cols] = low


def turned(ref):
    depth = ref.shape[1]
    eye = (
        lax.broadcasted_iota(jnp.int32, (depth, depth), 0)
        == lax.broadcasted_iota(jnp.int32, (depth, depth), 1)
    )
    eye = jnp.where(eye, 1.0, 0.0).astype(BF)
    return mm(eye, ref[...].astype(BF), NT).astype(BF)


def pack_rest_kernel(ck_ref, cv_ref, cq_ref, so_ref, co_ref, ex_ref, sh_ref, attn_ref, ex_out, sh_out):
    cols = ck_ref.shape[1]
    parts = [ref[...].astype(BF) for ref in (ck_ref, cv_ref, cq_ref)]
    parts += [turned(so_ref), turned(co_ref)]
    expand = ex_ref[...].astype(BF)
    shrink = turned(sh_ref)
    for copy in range(attn_ref.shape[0]):
        for i, low in enumerate(parts):
            attn_ref[copy, :, i * cols : (i + 1) * cols] = low
        ex_out[copy] = expand
    sh_out[...] = shrink


def self_forward_kernel(
    info, own_ref, oth_ref, bias_ref, w_ref, wx_ref, wy_ref, wxy_ref,
    qkv_ref, mat_ref, oa_ref, ob_ref, lse_ref, w_own, w_x, o_ref, sems,
):
    pair = pl.program_id(0)
    width = own_ref.shape[1]
    half = own_ref.shape[0]
    wide = qkv_ref.shape[2] // 3

    @pl.when(pair == 0)
    def _():
        place = info[0]
        cols = w_own.shape[3]
        copies = [
            pltpu.make_async_copy(w_ref, w_own.at[:, place], sems.at[0]),
            pltpu.make_async_copy(wy_ref, w_own.at[:, 1 - place], sems.at[1]),
            pltpu.make_async_copy(wx_ref, w_x.at[:, place], sems.at[2]),
            pltpu.make_async_copy(wxy_ref, w_x.at[:, 1 - place], sems.at[3]),
        ]
        for copy in copies:
            copy.start()
        for copy in copies:
            copy.wait()
        piece = cols // 3
        scale = 1.0 / math.sqrt(HD)
        for x, ref in enumerate((w_own, w_x)):
            mat = ref[...].reshape(width, cols)
            for i in range(3):
                at = (2 * i + x) * piece
                mat_ref[:, at : at + piece] = mat[:, i * piece : (i + 1) * piece]
        for rel, src in enumerate((own_ref, oth_ref)):
            for i in range(3):
                at = slice(wide * i, wide * (i + 1))
                part = mm(src[...], mat_ref[:, at]) + bias_ref[i : i + 1, :]
                if i == 0:
                    part = part * scale
                qkv_ref[rel, :, at] = part.astype(BF)

    first = info[3]
    second = 1 - first
    prefix = info[4]
    key_pos = lax.broadcasted_iota(jnp.int32, (half, half), 0)
    query_pos = lax.broadcasted_iota(jnp.int32, (half, half), 1)
    causal = key_pos <= query_pos
    seen = causal | (key_pos < prefix)

    def load(which, at):
        start = pl.multiple_of(which * wide + pair * 128, 128)
        return qkv_ref[at, :, pl.ds(start, 128)]

    q_both = (load(0, first), load(0, second))
    k_both = (load(1, first), load(1, second))
    v_both = (load(2, first), load(2, second))
    for h in range(2):
        cols = slice(HD * h, HD * h + HD)
        k0, k1 = (k[:, cols] for k in k_both)
        v0, v1 = (v[:, cols] for v in v_both)
        q0, q1 = (q[:, cols] for q in q_both)
        score = jnp.where(seen, mm(k0, q0, NT), NEGATIVE)
        top = jnp.max(score, 0, keepdims=True)
        expo = jnp.exp(score - top)
        total = jnp.sum(expo, 0, keepdims=True)
        mixed = mm(v0, expo.astype(BF), TN) / total
        o_ref[first, :, cols] = mixed.T.astype(BF)
        lse_ref[0, h, pl.ds(first, 1), :] = top + jnp.log(total)

        score_a = mm(k0, q1, NT)
        score_b = jnp.where(causal, mm(k1, q1, NT), NEGATIVE)
        top = jnp.maximum(
            jnp.max(score_a, 0, keepdims=True), jnp.max(score_b, 0, keepdims=True)
        )
        expo_a = jnp.exp(score_a - top)
        expo_b = jnp.exp(score_b - top)
        total = jnp.sum(expo_a, 0, keepdims=True) + jnp.sum(expo_b, 0, keepdims=True)
        mixed = (mm(v0, expo_a.astype(BF), TN) + mm(v1, expo_b.astype(BF), TN)) / total
        o_ref[second, :, cols] = mixed.T.astype(BF)
        lse_ref[0, h, pl.ds(second, 1), :] = top + jnp.log(total)
    oa_ref[...] = o_ref[0]
    ob_ref[...] = o_ref[1]


def self_forward(info, own, oth, bias, pieces):
    half, width = own.shape
    outer, depth, cols = pieces[0].shape
    wide = 2 * cols // 3
    pairs = wide // 128
    fixed2 = pl.BlockSpec((half, width), lambda i, info: (0, 0))
    pair_cols = pl.BlockSpec((half, 128), lambda i, info: (0, i))
    return pl.pallas_call(
        self_forward_kernel,
        grid_spec=pltpu.PrefetchScalarGridSpec(
            num_scalar_prefetch=1,
            grid=(pairs,),
            in_specs=[
                fixed2,
                fixed2,
                pl.BlockSpec(bias.shape, lambda i, info: (0, 0)),
                ANY,
                ANY,
                ANY,
                ANY,
            ],
            out_specs=[
                pl.BlockSpec((2, half, 3 * wide), lambda i, info: (0, 0, 0)),
                pl.BlockSpec((width, 3 * wide), lambda i, info: (0, 0)),
                pair_cols,
                pair_cols,
                pl.BlockSpec((1, 2, 2, half), lambda i, info: (i, 0, 0, 0)),
            ],
            scratch_shapes=[
                pltpu.VMEM((outer, 2, depth, cols), BF),
                pltpu.VMEM((outer, 2, depth, cols), BF),
                pltpu.VMEM((2, half, 128), BF),
                pltpu.SemaphoreType.DMA((4,)),
            ],
        ),
        out_shape=[
            struct((2, half, 3 * wide), BF),
            struct((width, 3 * wide), BF),
            struct((half, wide), BF),
            struct((half, wide), BF),
            struct((pairs, 2, 2, half), F32),
        ],
        compiler_params=pltpu.CompilerParams(vmem_limit_bytes=VMEM_LIMIT),
        cost_estimate=pl.CostEstimate(
            flops=2 * 2 * half * width * 3 * wide, bytes_accessed=own.size * 12, transcendentals=0
        ),
        name="self_fwd",
    )(info, own, oth, bias, *pieces)


def assemble_kernel(info, *refs):
    pieces, (kv_ref, q_ref, so_ref, co_ref) = refs[:8], refs[8:]
    place = info[0]
    outer, depth, cols = pieces[0].shape
    piece = cols // 5
    for j in range(4):
        for y in range(2):
            at = place if y == 0 else 1 - place
            for o in range(outer):
                value = pieces[2 * j + y][o]
                own = slice(piece * j, piece * (j + 1))
                low = slice(4 * piece + piece * j, 4 * piece + piece * (j + 1))
                kv_ref[o, at, :, own] = value[:, :piece]
                kv_ref[o, at, :, low] = value[:, piece : 2 * piece]
                q_ref[o, at, :, own] = value[:, 2 * piece : 3 * piece]
                so_ref[o, at, :, own] = value[:, 3 * piece : 4 * piece]
                co_ref[o, at, :, own] = value[:, 4 * piece :]


def assemble(info, pieces):
    outer, depth, cols = pieces[0].shape
    wide = cols // 5 * 4
    outs = call(
        assemble_kernel,
        [struct((outer, 2, depth, 2 * wide), BF)] + [struct((outer, 2, depth, wide), BF)] * 3,
        [info] + list(pieces),
        [SM] + [VM] * 8,
        [VM] * 4,
        moved=pieces[0].size * 32,
        name="assemble",
    )
    return [out.reshape(-1, out.shape[-1]) for out in outs]


def copies_kernel(info, own_ref, x_ref, y_ref, xy_ref, out_ref):
    place = info[0]
    for copy in range(out_ref.shape[0]):
        out_ref[copy, 0, place] = own_ref[...]
        out_ref[copy, 0, 1 - place] = y_ref[...]
        out_ref[copy, 1, place] = x_ref[...]
        out_ref[copy, 1, 1 - place] = xy_ref[...]


def plane_copies(info, own, x, y, xy):
    depth, cols = own.shape
    outer = outer_count()
    return call(
        copies_kernel,
        struct((outer, 2, 2, depth, cols), BF),
        [info, own, x, y, xy],
        [SM] + [VM] * 4,
        VM,
        moved=own.size * 2 * 4 * (outer + 1),
        name="plane_copies",
    )


def first_forward_kernel(
    tok_ref, own_ref, oth_ref, o_mat, vec_ref, q_mat, qb_ref,
    resid_ref, first_ref, low_ref, q_ref, mixed_ref,
):
    cols = own_ref.shape[1]
    mixed_ref[:, :cols] = own_ref[...]
    mixed_ref[:, cols:] = oth_ref[...]
    resid = tok_ref[...].astype(F32) + mm(mixed_ref[...], o_mat[...], NT) + vec_ref[0:1, :]
    resid_ref[...] = resid
    normed, rstd = norm_parts(resid)
    first = normed * vec_ref[1:2, :] + vec_ref[2:3, :]
    first_ref[...] = first
    low_ref[...] = first.astype(BF)
    scale = 1.0 / math.sqrt(HD)
    q_ref[...] = ((mm(low_ref[...], q_mat[...]) + qb_ref[...]) * scale).astype(BF)


def first_forward(tokens, own, oth, o_mat, vecs, q_mat, q_bias):
    rows, width = tokens.shape
    return call(
        first_forward_kernel,
        [struct((rows, width), F32)] * 2 + [struct((rows, width), BF)] * 3,
        [tokens, own, oth, o_mat, vecs, q_mat, q_bias],
        [VM] * 7,
        [VM] * 5,
        flops=2 * rows * width * width * 2 * 2,
        moved=width * width * 4 + rows * width * 18,
        name="first_forward",
    )


def feed_kernel(
    info, mixed_ref, first_ref, cot_ref, vec_ref, wo_hbm,
    e0, e1, e2, e3, e4, e5, e6, e7, s0, s1,
    out_ref, second_ref, low_ref, grad_ref, sums_ref,
    keep_e, keep_s, send_e, send_s,
    wo, we, ws, hid, slo, out_a, out_b, norm2, h2low, e3low, acc, wsem, osem,
):
    first_copy = pltpu.make_async_copy(wo_hbm, wo, wsem.at[0])
    first_copy.start()
    place = info[0]
    copies = []
    for j, pair in enumerate(((e0, e1), (e2, e3), (e4, e5), (e6, e7))):
        for y, ref in enumerate(pair):
            at = place if y == 0 else 1 - place
            copies.append(pltpu.make_async_copy(ref, we.at[j, :, at], wsem.at[1 + 2 * j + y]))
    for j in range(4):
        ref = (s0, s1)[j // 2]
        copies.append(pltpu.make_async_copy(ref.at[:, j % 2], ws.at[j], wsem.at[9 + j]))
    for copy in copies:
        copy.start()

    width = first_ref.shape[1]
    hidden_cols = we.shape[-1]

    def expand_mat(j):
        return we[j].reshape(width, hidden_cols)

    def shrink_mat(j):
        return ws[j].reshape(width, hidden_cols)

    def row(i):
        return vec_ref[i : i + 1, :]

    first_copy.wait()
    resid = first_ref[...] + mm(mixed_ref[...], wo[...], NT) + row(0)
    normed, rstd2 = norm_parts(resid)
    norm2[...] = normed
    second = normed * row(1) + row(2)
    h2low[...] = second.astype(BF)
    acc[...] = second + row(7)
    for copy in copies:
        copy.wait()

    def forward(j, carry):
        inner = mm(h2low[...], expand_mat(j)) + vec_ref[pl.ds(3 + j, 1), :]
        phi = 0.5 + 0.5 * lax.erf(inner * (1.0 / math.sqrt(2.0)))
        hidden = (inner * phi).astype(BF)
        hid[j] = hidden
        bell = jnp.exp(-0.5 * inner * inner) * (1.0 / math.sqrt(2.0 * math.pi))
        slo[j] = (phi + inner * bell).astype(BF)
        acc[...] += mm(hidden, shrink_mat(j), NT)
        return carry

    lax.fori_loop(0, 4, forward, 0)
    norm3, rstd3 = norm_parts(acc[...])
    out_ref[...] = (norm3 * row(8) + row(9)).astype(BF)
    cot = cot_ref[...].astype(F32)
    sums_ref[0:1, :] = jnp.sum(cot, 0, keepdims=True)
    sums_ref[1:2, :] = jnp.sum(cot * norm3, 0, keepdims=True)
    third = norm_back(norm3, rstd3, cot, row(8))
    low = third.astype(BF)
    e3low[...] = low
    sums_ref[2:3, :] = jnp.sum(low.astype(F32), 0, keepdims=True)
    acc[...] = third

    def out_copies(to_e, to_s, at, slot):
        copies = []
        for y in range(2):
            rel = y ^ place
            copies.append(
                pltpu.make_async_copy(
                    out_a.at[slot, :, y], to_e.at[at, rel], osem.at[0, slot, y]
                )
            )
            copies.append(
                pltpu.make_async_copy(
                    out_b.at[slot, :, y], to_s.at[:, at, rel], osem.at[1, slot, y]
                )
            )
        return copies

    def backward(step, carry):
        j = (step + 2) % 4
        slot = step % 2
        slope = slo[j].astype(F32)
        inner_grad = (mm(e3low[...], shrink_mat(j)) * slope).astype(BF)
        true_block = info[1] ^ (2 * (j % 2) + j // 2)
        sums_ref[pl.ds(8 + true_block, 1), :] = jnp.sum(
            inner_grad.astype(F32), 0, keepdims=True
        )

        @pl.when(step >= 2)
        def _():
            for copy in out_copies(send_e, send_s, slot, slot):
                copy.wait()

        out_a[slot] = mm(h2low[...], inner_grad, TN).astype(BF).reshape(out_a.shape[1:])
        out_b[slot] = mm(e3low[...], hid[j], TN).astype(BF).reshape(out_b.shape[1:])

        @pl.when(step < 2)
        def _():
            for copy in out_copies(send_e, send_s, slot, slot):
                copy.start()

        @pl.when(step >= 2)
        def _():
            for copy in out_copies(keep_e, keep_s, slot, slot):
                copy.start()

        acc[...] += mm(inner_grad, expand_mat(j), NT)
        return carry

    lax.fori_loop(0, 4, backward, 0)
    grad = acc[...]
    normed = norm2[...]
    sums_ref[3:4, :] = jnp.sum(grad, 0, keepdims=True)
    sums_ref[4:5, :] = jnp.sum(grad * normed, 0, keepdims=True)
    second_in = norm_back(normed, rstd2, grad, row(1))
    second_ref[...] = second_in
    low = second_in.astype(BF)
    low_ref[...] = low
    sums_ref[5:6, :] = jnp.sum(low.astype(F32), 0, keepdims=True)
    sums_ref[6:8, :] = jnp.zeros((2, sums_ref.shape[1]), F32)
    sums_ref[12:16, :] = jnp.zeros((4, sums_ref.shape[1]), F32)
    grad_ref[...] = mm(low, wo[...]).astype(BF)
    for slot in range(2):
        for copy in out_copies(keep_e, keep_s, slot, slot):
            copy.wait()


def feed(info, mixed, first, cot, vecs, wo, expand, shrink):
    rows, width = mixed.shape
    outer, depth, hidden = expand[0].shape
    grad_e = struct((2, 2, outer, depth, hidden), BF)
    grad_s = struct((outer, 2, 2, depth, hidden), BF)
    return call(
        feed_kernel,
        [
            struct((rows, width), BF),
            struct((rows, width), F32),
            struct((rows, width), BF),
            struct((rows, width), BF),
            struct((16, width), F32),
            grad_e,
            grad_s,
            grad_e,
            grad_s,
        ],
        [info, mixed, first, cot, vecs, wo] + list(expand) + list(shrink),
        [SM, VM, VM, VM, VM] + [ANY] * 11,
        [VM] * 5 + [ANY] * 4,
        [
            pltpu.VMEM((width, width), BF),
            pltpu.VMEM((4, outer, 2, depth, hidden), BF),
            pltpu.VMEM((4, outer, 2, depth, hidden), BF),
            pltpu.VMEM((4, rows, hidden), BF),
            pltpu.VMEM((4, rows, hidden), BF),
            pltpu.VMEM((2, outer, 2, depth, hidden), BF),
            pltpu.VMEM((2, outer, 2, depth, hidden), BF),
            pltpu.VMEM((rows, width), F32),
            pltpu.VMEM((rows, width), BF),
            pltpu.VMEM((rows, width), BF),
            pltpu.VMEM((rows, width), F32),
            pltpu.SemaphoreType.DMA((13,)),
            pltpu.SemaphoreType.DMA((2, 2, 2)),
        ],
        flops=2 * rows * width * (6 * 4 * hidden + 2 * width) * 2,
        moved=width * hidden * 4 * 4 * 2,
        name="feed",
    )


def first_back_kernel(
    dq_ref, q_mat, second_ref, resid_ref, vec_ref, o_mat, first_ref, low_ref, keep_ref, send_ref, sums_ref
):
    grad = second_ref[...] + mm(dq_ref[...], q_mat[...], NT)
    normed, rstd = norm_parts(resid_ref[...])
    sums_ref[0:1, :] = jnp.sum(grad, 0, keepdims=True)
    sums_ref[1:2, :] = jnp.sum(grad * normed, 0, keepdims=True)
    first_in = norm_back(normed, rstd, grad, vec_ref[0:1, :])
    first_ref[...] = first_in
    low = first_in.astype(BF)
    low_ref[...] = low
    sums_ref[2:3, :] = jnp.sum(low.astype(F32), 0, keepdims=True)
    sums_ref[3:4, :] = jnp.sum(dq_ref[...].astype(F32), 0, keepdims=True)
    sums_ref[4:8, :] = jnp.zeros((4, sums_ref.shape[1]), F32)
    mixed_grad = mm(low, o_mat[...]).astype(BF)
    cols = keep_ref.shape[1]
    keep_ref[...] = mixed_grad[:, :cols]
    send_ref[...] = mixed_grad[:, cols:]


def first_back(dq, q_mat, second_in, resid, vec, o_mat):
    rows, width = dq.shape
    cols = width // 2
    return call(
        first_back_kernel,
        [
            struct((rows, width), F32),
            struct((rows, width), BF),
            struct((rows, cols), BF),
            struct((rows, cols), BF),
            struct((8, width), F32),
        ],
        [dq, q_mat, second_in, resid, vec, o_mat],
        [VM] * 6,
        [VM] * 5,
        flops=2 * rows * width * width * 2 * 2,
        moved=width * width * 4 + rows * width * 18,
        name="first_back",
    )


def put_rows(ref, x, full, at, place):
    outer, depth = ref.shape[2], ref.shape[3]
    for o in range(outer):
        for y in range(2):
            start = (2 * o + y) * depth
            ref[x, y ^ place, o, :, at] = full[start : start + depth]


def put_blocks(keep_ref, send_ref, full, i, place):
    piece = full.shape[1] // 4
    at = slice(i * piece, (i + 1) * piece)
    for j in range(4):
        put_rows((keep_ref, send_ref)[j // 2], j % 2, full[:, j * piece : (j + 1) * piece], at, place)


def query_grads_kernel(
    info, h1_ref, dq_ref, e1_ref, o1_ref, e2_ref, o2_ref, keep_ref, send_ref
):
    for i, (left, right) in enumerate(((h1_ref, dq_ref), (e1_ref, o1_ref), (e2_ref, o2_ref))):
        full = mm(left[...], right[...], TN).astype(BF)
        put_blocks(keep_ref, send_ref, full, i, info[0])


def key_grads_kernel(info, fet_ref, own_ref, got_ref, mat_ref, keep_ref, send_ref, grad_ref, sum_ref):
    width = fet_ref.shape[1]
    total = None
    for i in range(2):
        low = add_low(own_ref[i], got_ref[i])
        full = mm(fet_ref[...], low, TN).astype(BF)
        put_blocks(keep_ref, send_ref, full, i, info[0])
        term = mm(low, mat_ref[:, i * width : (i + 1) * width], NT)
        total = term if total is None else total + term
        if i == 1:
            sum_ref[0:1, :] = jnp.sum(low.astype(F32), 0, keepdims=True)
            sum_ref[1:8, :] = jnp.zeros((7, width), F32)
    grad_ref[...] = total.astype(BF)


def query_grads(info, args, depth):
    width = args[0].shape[1]
    out = struct((2, 2, width // depth // 2, depth, 3 * width // 4), BF)
    return call(
        query_grads_kernel,
        [out, out],
        [info] + list(args),
        [SM] + [VM] * 6,
        [VM] * 2,
        flops=2 * 512 * width * width * 3,
        moved=width * width * 10,
        name="query_grads",
    )


def key_grads(info, fetched, own, got, mat, depth):
    rows, width = fetched.shape
    out = struct((2, 2, width // depth // 2, depth, 2 * width // 4), BF)
    return call(
        key_grads_kernel,
        [out, out, struct((rows, width), BF), struct((8, width), F32)],
        [info, fetched, own, got, mat],
        [SM] + [VM] * 4,
        [VM] * 4,
        flops=2 * rows * width * width * 4,
        moved=width * width * 10,
        name="key_grads",
    )


def self_grads_kernel(info, own_ref, oth_ref, d_ref, a_ref, x_ref, y_ref, xy_ref):
    place = info[0]
    cols = d_ref.shape[3]
    piece = cols // 2
    outer, depth = a_ref.shape[0], a_ref.shape[1]
    for i in range(3):
        full = mm(own_ref[...], d_ref[i, 0], TN) + mm(oth_ref[...], d_ref[i, 1], TN)
        full = full.astype(BF)
        at = slice(i * piece, (i + 1) * piece)
        for x, (near, away) in enumerate(((a_ref, y_ref), (x_ref, xy_ref))):
            for o in range(outer):
                start = 2 * o * depth
                first = full[start : start + depth, x * piece : (x + 1) * piece]
                second = full[start + depth : start + 2 * depth, x * piece : (x + 1) * piece]
                near[o, :, at] = jnp.where(place == 0, first, second)
                away[o, :, at] = jnp.where(place == 0, second, first)


def self_grads(info, own, oth, grads, depth):
    half, width = own.shape
    cols = grads.shape[3]
    out = struct((width // depth // 2, depth, 3 * cols // 2), BF)
    return call(
        self_grads_kernel,
        [out] * 4,
        [info, own, oth, grads],
        [SM] + [VM] * 3,
        [VM] * 4,
        flops=2 * 2 * half * width * 3 * cols * 2,
        moved=half * width * 4 + half * cols * 12 + width * cols * 6,
        name="self_grads",
    )


def self_back_kernel(d_ref, mat_ref, first_ref, keep_ref, send_ref):
    cols = d_ref.shape[3]
    for rel in (1, 0):
        total = mm(d_ref[0, rel], mat_ref[:, :cols], NT)
        for i in (1, 2):
            total = total + mm(d_ref[i, rel], mat_ref[:, i * cols : (i + 1) * cols], NT)
        if rel == 1:
            send_ref[...] = total.astype(BF)
        else:
            keep_ref[...] = total + first_ref[...]


def self_back(grads, mat, first_in):
    half, width = first_in.shape
    cols = grads.shape[3]
    return call(
        self_back_kernel,
        [struct((half, width), F32), struct((half, width), BF)],
        [grads, mat, first_in],
        [VM] * 3,
        [VM] * 2,
        flops=2 * 2 * half * width * 3 * cols * 2,
        moved=half * width * 10 + half * cols * 12 + width * cols * 6,
        name="self_back",
    )


def fetch_kernel(table, bank_ref, mine_ref, send_ref, sem):
    count = table.shape[0] // 2

    def each(act):
        for group, out_ref in enumerate((mine_ref, send_ref)):

            def body(i, carry, group=group, out_ref=out_ref):
                at = table[group * count + i]
                copy = pltpu.make_async_copy(
                    bank_ref.at[jnp.maximum(at, 0)], out_ref.at[i], sem.at[group * count + i]
                )
                act(copy, at >= 0, out_ref, i)
                return carry

            lax.fori_loop(0, count, body, 0)

    def start(copy, held, out_ref, i):
        @pl.when(held)
        def _():
            copy.start()

        @pl.when(jnp.logical_not(held))
        def _():
            out_ref[i] = jnp.zeros(out_ref.shape[1:], out_ref.dtype)

    def finish(copy, held, out_ref, i):
        @pl.when(held)
        def _():
            copy.wait()

    each(start)
    each(finish)


def fetch(table, bank_blocks):
    count = table.shape[0]
    blk, width = bank_blocks.shape[1:]
    out = struct((count // 2, blk, width), BF)
    mine, send = call(
        fetch_kernel,
        [out, out],
        [table, bank_blocks],
        [SM, ANY],
        [VM, VM],
        [pltpu.SemaphoreType.DMA((count,))],
        moved=count * blk * width * 4,
        name="fetch",
    )
    return [part.reshape(2, count // 4, blk, width) for part in (mine, send)]


def scatter_kernel(table, a_ref, b_ref, c_ref, d_ref, out_ref, slots, sems):
    step = pl.program_id(0)
    per = out_ref.shape[0]

    @pl.when(step == 0)
    def _():
        copies = [
            pltpu.make_async_copy(ref, slots.at[i], sems.at[i])
            for i, ref in enumerate((a_ref, b_ref, c_ref, d_ref))
        ]
        for copy in copies:
            copy.start()
        for copy in copies:
            copy.wait()

    for i in range(per):
        at = table[step * per + i]
        group = jnp.maximum(at, 0) // slots.shape[1]
        place = jnp.maximum(at, 0) % slots.shape[1]
        value = slots[group, place].astype(F32)
        out_ref[i] = jnp.where(at >= 0, value, 0.0)


def scatter(table, parts):
    count = table.shape[0]
    slots, blk, width = parts[0].shape
    per = 4
    return pl.pallas_call(
        scatter_kernel,
        grid_spec=pltpu.PrefetchScalarGridSpec(
            num_scalar_prefetch=1,
            grid=(count // per,),
            in_specs=[ANY] * 4,
            out_specs=pl.BlockSpec((per, blk, width), lambda i, t: (i, 0, 0)),
            scratch_shapes=[
                pltpu.VMEM((4, slots, blk, width), BF),
                pltpu.SemaphoreType.DMA((4,)),
            ],
        ),
        out_shape=struct((count, blk, width), F32),
        compiler_params=pltpu.CompilerParams(vmem_limit_bytes=VMEM_LIMIT),
        cost_estimate=pl.CostEstimate(
            flops=0, bytes_accessed=count * blk * width * 6, transcendentals=0
        ),
        name="scatter",
    )(table, *parts)


def sum_all(ref):
    total = ref[0].astype(F32)
    for i in range(1, ref.shape[0]):
        total = total + ref[i].astype(F32)
    return total


def sum_query_kernel(in_ref, q_ref, so_ref, co_ref):
    total = sum_all(in_ref)
    piece = total.shape[1] // 3
    q_ref[...] = total[:, :piece]
    so_ref[...] = total[:, piece : 2 * piece].T
    co_ref[...] = total[:, 2 * piece :].T


def sum_query(value):
    count, depth, cols = value.shape
    piece = cols // 3
    return call(
        sum_query_kernel,
        [struct((depth, piece), F32)] + [struct((piece, depth), F32)] * 2,
        [value],
        [VM],
        [VM] * 3,
        moved=value.size * 2 + depth * cols * 4,
        name="sum_query",
    )


def sum_turned_kernel(in_ref, out_ref):
    out_ref[...] = sum_all(in_ref).T


def sum_turned(value):
    count, depth, cols = value.shape
    return call(
        sum_turned_kernel,
        struct((cols, depth), F32),
        [value],
        [VM],
        VM,
        moved=value.size * 2 + depth * cols * 4,
        name="sum_turned",
    )


def local(
    tokens,
    bank,
    prefix,
    blocks,
    out_grad,
    selfq_weight,
    selfq_bias,
    selfk_weight,
    selfv_weight,
    selfv_bias,
    selfo_weight,
    selfo_bias,
    first_gain,
    first_shift,
    crossq_weight,
    crossq_bias,
    crossk_weight,
    crossv_weight,
    crossv_bias,
    crosso_weight,
    crosso_bias,
    second_gain,
    second_shift,
    expand_weight,
    expand_bias,
    shrink_weight,
    shrink_bias,
    third_gain,
    third_shift,
):
    rank = lax.axis_index("tensor")
    core = rank % 2
    chip = rank // 2
    inner = lax.axis_index("dp") % 2
    outer = outer_count()
    half, width = tokens.shape
    seq_count = prefix.shape[0]
    local_blocks = bank.shape[1] // BLK
    head_cols = selfq_bias.shape[0]
    hidden_cols = expand_bias.shape[0]
    depth = selfq_weight.shape[0]
    slots = NBLK // 2
    two = 2 * head_cols
    attn_cols = 5 * head_cols
    info = jnp.stack([inner, rank, chip]).astype(jnp.int32)

    self_leaf = call(
        pack_self_kernel,
        struct((outer, depth, 3 * head_cols), BF),
        [selfq_weight, selfk_weight, selfv_weight],
        [VM] * 3,
        VM,
        name="pack_self",
    )
    self_z = outer_exchange(self_leaf)
    bias_own = jnp.concatenate(
        [selfq_bias, selfv_bias, crossq_bias, crossv_bias, expand_bias]
    ).reshape(1, -1)
    bias_two = jnp.concatenate([bias_own, swap_x(bias_own)], axis=0)
    bias_four = jnp.concatenate([bias_two, swap_core(bias_two)], axis=0)
    cq_bias = bias_four[:, two : 3 * head_cols].reshape(-1)
    cv_bias = bias_four[:, 3 * head_cols : 4 * head_cols].reshape(-1)
    ex_bias = bias_four[:, 4 * head_cols :]
    self_bias = jnp.stack(
        [
            bias_two[:, :head_cols].reshape(-1),
            jnp.zeros((two,), F32),
            bias_two[:, head_cols:two].reshape(-1),
        ]
    )
    attn_leaf, expand_leaf, shrink_leaf = call(
        pack_rest_kernel,
        [
            struct((outer, depth, attn_cols), BF),
            struct((outer, depth, hidden_cols), BF),
            struct((depth, hidden_cols), BF),
        ],
        [
            gate(crossk_weight, self_leaf), crossv_weight, crossq_weight, selfo_weight,
            crosso_weight, expand_weight, shrink_weight,
        ],
        [VM] * 7,
        [VM] * 3,
        name="pack_rest",
    )
    shrink_x, shrink_y = swap_x(shrink_leaf), swap_dp(shrink_leaf, 1)
    shrink_xy = swap_both(shrink_leaf)
    tokens_oth = swap_core(tokens)
    shrink_pack = plane_copies(info, shrink_leaf, shrink_x, shrink_y, shrink_xy)

    self_z, shrink_pack, self_bias = lax.optimization_barrier((self_z, shrink_pack, self_bias))
    self_near, self_away, self_both = swap_x(self_z), swap_dp(self_z, 1), swap_both(self_z)
    attn_z = outer_exchange(gate(attn_leaf, self_z))

    seq_order = jnp.stack([chip, 1 - chip])
    near = blocks[seq_order].reshape(2, 2, slots)
    near = jnp.stack([near[:, core], near[:, 1 - core]])
    near = near - rank * local_blocks
    held = (near >= 0) & (near < local_blocks)
    fetch_table = jnp.where(held, near + seq_order[None, :, None] * local_blocks, -1)
    fetch_table = gate(fetch_table.reshape(-1).astype(jnp.int32), self_z)
    part_mine, part_send = fetch(fetch_table, bank.reshape(seq_count * local_blocks, BLK, width))
    part_got = swap_core(part_send)
    part_keep = part_mine[0] + part_got[0]
    part_away = part_mine[1] + part_got[1]
    attn_z, tokens_in, self_near, self_away, self_both, part_away = lax.optimization_barrier(
        (attn_z, tokens, self_near, self_away, self_both, part_away)
    )
    attn_x, attn_y, attn_xy = swap_x(attn_z), swap_dp(attn_z, 1), swap_both(attn_z)
    part_back = swap_x(part_away)
    expand_z = outer_exchange(gate(expand_leaf, attn_z))

    my_prefix = lax.dynamic_index_in_dim(prefix, chip, 0, keepdims=False)
    attn_info = jnp.stack([core, my_prefix]).astype(jnp.int32)
    qkv, self_mat, self_own, self_send, self_lse = self_forward(
        jnp.concatenate([info, attn_info]),
        tokens_in,
        tokens_oth,
        self_bias,
        (self_z, self_near, self_away, self_both),
    )
    self_got = swap_core(self_send)
    part_back, attn_x, attn_y, attn_xy, expand_z = lax.optimization_barrier(
        (part_back, attn_x, attn_y, attn_xy, expand_z, self_own)
    )[:5]
    shrink_z = outer_exchange(gate(shrink_pack, expand_z))
    fetched = (part_keep + part_back).reshape(slots * BLK, width)
    expand_x, expand_y, expand_xy = swap_x(expand_z), swap_dp(expand_z, 1), swap_both(expand_z)

    attn_own = (attn_z, attn_y, attn_x, attn_xy)
    attn_oth = tuple(swap_core(piece) for piece in attn_own)
    cross_kv, cross_q, self_o, cross_o = assemble(info, attn_own + attn_oth)
    first_sum, first_out, first_low, queries, mixed_one = first_forward(
        tokens,
        self_own,
        self_got,
        self_o,
        jnp.stack([selfo_bias, first_gain, first_shift]),
        cross_q,
        cq_bias.reshape(1, -1),
    )

    kv_bias = jnp.concatenate([jnp.zeros_like(cv_bias), cv_bias])
    kv_own = (mm(fetched, cross_kv) + kv_bias).astype(BF)
    kv_oth = swap_core(kv_own)
    queries, expand_x, expand_y, expand_xy, shrink_z = lax.optimization_barrier(
        (queries, expand_x, expand_y, expand_xy, shrink_z)
    )
    mixed_two, cross_lse = cross_forward(queries, kv_own, kv_oth)

    expand_own = (expand_z, expand_y, expand_x, expand_xy)
    expand_oth = tuple(swap_core(piece) for piece in expand_own)
    vecs = jnp.concatenate(
        [
            jnp.stack([crosso_bias, second_gain, second_shift]),
            ex_bias,
            jnp.stack([shrink_bias, third_gain, third_shift]),
        ]
    )
    (
        out_act, second_in, cross_low, cross_grad, late_vec,
        expand_keep, shrink_keep, expand_send, shrink_send,
    ) = feed(
        info, mixed_two, first_out, out_grad, vecs, cross_o,
        expand_own + expand_oth, (shrink_z, swap_core(shrink_z)),
    )

    def plane_send(keep, got):
        return tuple(add_low(keep[x, y], got[x, y]) for x, y in ((1, 0), (0, 1), (1, 1)))

    def plane_swap(parts):
        return swap_x(parts[0]), swap_dp(parts[1], 1), swap_both(parts[2])

    def plane_sum(own, got):
        total = sum(part.astype(F32) for part in own)
        return total + sum(part.astype(F32) for part in got)

    def fold(value, dtype):
        return jnp.sum(value.astype(F32), axis=0).astype(dtype)

    shrink_got = swap_core(shrink_send)
    expand_got = swap_core(expand_send)
    part_one = cross_backward(queries, kv_own, kv_oth, mixed_two, cross_lse, cross_grad, 0, 2)
    shrink_places, expand_plane, part_one = lax.optimization_barrier(
        (
            add_low(gate(shrink_keep, part_one[0]), shrink_got),
            plane_send(gate(expand_keep, part_one[0]), expand_got),
            tuple(part_one),
        )
    )
    expand_parts = plane_swap(expand_plane)
    shrink_parts = outer_exchange(shrink_places)

    dq, dkv_own, dkv_send, first_in, self_low, grad_own, grad_send, early_vec = cross_first_backward(
        queries, kv_own, kv_oth, mixed_two, cross_lse, cross_grad, 2, part_one,
        cross_q, second_in, first_sum, first_gain.reshape(1, -1), self_o,
    )
    dkv_got = swap_core(dkv_send)
    grad_got = swap_core(grad_send)
    self_low, expand_parts = lax.optimization_barrier((self_low, expand_parts))
    expand_three = plane_sum((expand_keep[0, 0], expand_got[0, 0]), expand_parts).astype(BF)
    query_keep, query_send = query_grads(
        info, (first_low, dq, self_low, mixed_one, cross_low, mixed_two), depth
    )
    dkv_own, query_send = lax.optimization_barrier((dkv_own, query_send))
    query_got = swap_core(query_send)
    key_keep, key_send, fetched_grad, cv_rows = key_grads(
        info, fetched, dkv_own, dkv_got, cross_kv, depth
    )
    query_plane = plane_send(gate(query_keep, cv_rows), query_got)
    query_plane, key_send, grad_got, fetched_grad = lax.optimization_barrier(
        (query_plane, key_send, grad_got, fetched_grad)
    )
    query_parts = plane_swap(query_plane)
    key_got = swap_core(key_send)

    self_args = (attn_info, qkv, self_own, self_send, self_lse, grad_own, grad_got)
    pairs = two // 128
    half_grads = self_backward(*self_args, 0, pairs - 1)
    key_plane = plane_send(gate(key_keep, half_grads[1]), key_got)
    key_plane, half_grads, query_parts, shrink_parts, expand_three, fetched_send = (
        lax.optimization_barrier(
            (key_plane, tuple(half_grads), query_parts, shrink_parts, expand_three, fetched_grad)
        )
    )
    key_parts = plane_swap(key_plane)
    expand_last = outer_exchange(expand_three)
    shrink_three = fold(shrink_parts, BF)
    query_three = plane_sum((query_keep[0, 0], query_got[0, 0]), query_parts).astype(BF)
    grads, self_sums = self_backward(*self_args, pairs - 1, 1, half_grads)

    order = jnp.arange(4) ^ rank
    order = 2 * (order % 2) + order // 2

    def straight(vecs):
        return vecs.reshape(vecs.shape[0], 4, -1)[:, order].reshape(vecs.shape[0], -1)

    self_sums = self_sums[:, :3].transpose(1, 0, 2).reshape(3, two)
    self_sums = jnp.concatenate([self_sums, jnp.zeros_like(self_sums)], axis=1)
    turned_vecs = jnp.concatenate([early_vec[3:4], cv_rows[:1], self_sums[0:1], self_sums[2:3]])
    sums = jnp.concatenate([late_vec, early_vec[:3], straight(turned_vecs)])
    sums = sums + swap_core(sums)
    sums, grads, shrink_three = lax.optimization_barrier((sums, grads, shrink_three))
    sums_got = swap_x(sums)
    shrink_near = (
        swap_x(shrink_three[1, 0]), swap_dp(shrink_three[0, 1], 1), swap_both(shrink_three[1, 1])
    )
    self_places = self_grads(info, tokens, tokens_oth, grads, depth)
    sums, self_places, grads, key_parts = lax.optimization_barrier(
        (sums + sums_got, tuple(self_places), grads, key_parts)
    )
    bits = dp_bits()
    sums_got = swap_dp(sums, bits[-1])
    self_parts = (swap_x(self_places[1]), swap_dp(self_places[2], 1), swap_both(self_places[3]))
    key_three = plane_sum((key_keep[0, 0], key_got[0, 0]), key_parts).astype(BF)
    query_last = outer_exchange(gate(query_three, expand_last))
    back_keep, back_send = self_back(grads, self_mat, first_in)
    sums = sums + gate(sums_got, back_send)
    for bit in bits[:-1]:
        sums = sums + swap_dp(sums, bit)
    fetched_send = gate(fetched_send, back_send)
    fetched_away = swap_x(fetched_send).reshape(slots, BLK, width)
    fetched_near = fetched_send.reshape(slots, BLK, width)
    self_three = plane_sum((self_places[0],), gate(self_parts, back_send)).astype(BF)
    self_last = outer_exchange(jnp.concatenate([self_three, key_three], axis=-1))
    in_grad = (back_keep + swap_core(back_send).astype(F32)).astype(BF)
    shrink_last = jnp.stack((shrink_three[0, 0],) + shrink_near)

    cq_grad, so_grad, co_grad = sum_query(query_last)
    self_total = fold(self_last, F32)
    ck_grad = self_total[:, 3 * head_cols : 4 * head_cols]
    cv_grad = self_total[:, 4 * head_cols :]
    expand_grad = fold(expand_last, F32)
    shrink_grad = sum_turned(shrink_last)

    near_core = swap_core(fetched_near)
    away_core = swap_core(fetched_away)
    slot_ids = jnp.arange(NBLK)
    places = (
        (((slot_ids[None, :] // slots) != core) * 2 + (jnp.arange(seq_count)[:, None] != chip))
        * slots
        + slot_ids[None, :] % slots
    )
    hits = blocks[:, None, :] == (rank * local_blocks + jnp.arange(local_blocks))[None, :, None]
    scatter_table = jnp.max(jnp.where(hits, places[:, None, :], -1), axis=-1)
    bank_grad = scatter(
        scatter_table.reshape(-1).astype(jnp.int32),
        (fetched_near, fetched_away, near_core, away_core),
    ).reshape(bank.shape)

    late_vec, early_vec = sums[:16], sums[16:]

    def own_part(vec, part_len):
        return lax.dynamic_slice_in_dim(vec, rank * part_len, part_len, 0)

    def self_part(which):
        return self_total[:, which * head_cols : (which + 1) * head_cols]

    return (
        out_act,
        in_grad,
        bank_grad,
        self_part(0),
        own_part(early_vec[5], head_cols),
        self_part(1),
        self_part(2),
        own_part(early_vec[6], head_cols),
        so_grad,
        early_vec[2],
        early_vec[1],
        early_vec[0],
        cq_grad,
        own_part(early_vec[3], head_cols),
        ck_grad,
        cv_grad,
        own_part(early_vec[4], head_cols),
        co_grad,
        late_vec[5],
        late_vec[4],
        late_vec[3],
        expand_grad,
        lax.dynamic_index_in_dim(late_vec, 8 + rank, 0, keepdims=False),
        shrink_grad,
        late_vec[2],
        late_vec[1],
        late_vec[0],
    )


def solution(mesh):
    rows = P(("dp", "tensor"), None)
    wide = P("dp", "tensor")
    tall = P("tensor", "dp")
    part = P("tensor")
    full = P()
    return jax.shard_map(
        local,
        mesh=mesh,
        in_specs=(
            rows, P("dp", "tensor", None), P("dp"), P("dp", None), rows,
            wide, part, wide, wide, part, tall, full, full, full,
            wide, part, wide, wide, part, tall, full, full, full,
            wide, part, tall, full, full, full,
        ),
        out_specs=(
            rows, rows, P("dp", "tensor", None),
            wide, part, wide, wide, part, tall, full, full, full,
            wide, part, wide, wide, part, tall, full, full, full,
            wide, part, tall, full, full, full,
        ),
        check_vma=False,
    )
```

profile of v0, /device:TPU:19, one launch (start us, length us, event | category | flops | bytes accessed | tf_op | source)
XLA Modules:
  0.0 444.9 jit_solution(148697205970885956)
XLA Ops:
  0.7 1.9 pack_self.1
  2.6 1.9 copy.66.sh_ref
  4.5 2.7 pack_rest.1
  9.8 4.6 %all-to-all-start = ((bf16[4,96,576]{2,1,0:T(8,128)(2,1)}), bf16[4,96,576]{2,1,0:T(8,128)(2,1)S(1)}, u32[]{:S(2)}, u32[]{:S(2)}) async-start(bf16[4,96,576]{2,1,0:T(8,128)(2,1)} %pack_self.1), calls=%async_computation | async-start | bytes 983040 | tf_op jit(solution)/shard_map/all_to_all | solution.py:395
  19.1 2.8 plane_copies.1
  21.9 2.8 all-to-all-done.w_ref
  24.6 4.0 fetch.1
  28.7 1.8 collective-permute-start.7
  30.5 7.1 %all-to-all-start.1 = ((bf16[4,96,960]{2,1,0:T(8,128)(2,1)}), bf16[4,96,960]{2,1,0:T(8,128)(2,1)}, u32[]{:S(2)}, u32[]{:S(2)}) async-start(bf16[4,96,960]{2,1,0:T(8,128)(2,1)} %get-tuple-element.167), calls=%async_computation.1 | async-start | bytes 1572864 | tf_op jit(solution)/shard_map/all_to_all | solution.py:395
  37.7 1.4 collective-permute-start.5
  41.5 2.3 fusion.5
  43.9 6.2 %collective-permute-done.4.wx_ref = bf16[4,96,576]{2,1,0:T(8,128)(2,1)S(1)} collective-permute-done((bf16[4,96,576]{2,1,0:T(8,128)(2,1)S(1)}, bf16[4,96,576]{2,1,0:T(8,128)(2,1)S(1)}, u32[]{:S(2)}, u32[]{:S(2)}) %collective-permute-start.4) | collective-permute-done | bytes 442400 | tf_op jit(solution)/shard_map/ppermute | solution.py:37
  50.1 11.4 %collective-permute-done.6.wxy_ref = bf16[4,96,576]{2,1,0:T(8,128)(2,1)S(1)} collective-permute-done((bf16[4,96,576]{2,1,0:T(8,128)(2,1)S(1)}, bf16[4,96,576]{2,1,0:T(8,128)(2,1)S(1)}, u32[]{:S(2)}, u32[]{:S(2)}) %collective-permute-start.6) | collective-permute-done | bytes 442400 | tf_op jit(solution)/shard_map/ppermute | solution.py:390
  61.4 4.5 %all-to-all-start.2 = ((bf16[4,96,768]{2,1,0:T(8,128)(2,1)}), bf16[4,96,768]{2,1,0:T(8,128)(2,1)}, u32[]{:S(2)}, u32[]{:S(2)}) async-start(bf16[4,96,768]{2,1,0:T(8,128)(2,1)} %get-tuple-element.181), calls=%async_computation.2 | async-start | bytes 1179648 | tf_op jit(solution)/shard_map/all_to_all | solution.py:395
  70.3 12.9 %self_fwd.1 = (bf16[2,512,1152]{2,1,0:T(8,128)(2,1)}, bf16[768,1152]{1,0:T(8,128)(2,1)S(1)}, bf16[512,384]{1,0:T(8,128)(2,1)S(1)}, bf16[512,384]{1,0:T(8,128)(2,1)S(1)}, f32[3,2,2,512]{3,2,1,0:T(2,128)S(1)}) custom-call(s32[5]{0:T(128)S(1)} %concatenate.55.info, bf16[512,768]{1,0:T(8,128)(2,1)S(1)} %copy-done.3, ...), custom_call_target="tpu_custom_call" | custom-call | flops 1811939328 | bytes 4718592 | tf_op jit(solution)/shard_map/self_fwd/pallas_call | solution.py:558
  86.5 13.8 %collective-permute-done.11.refs_2_ = bf16[4,96,960]{2,1,0:T(8,128)(2,1)} collective-permute-done((bf16[4,96,960]{2,1,0:T(8,128)(2,1)}, bf16[4,96,960]{2,1,0:T(8,128)(2,1)}, u32[]{:S(2)}, u32[]{:S(2)}) %collective-permute-start.11) | collective-permute-done | bytes 737312 | tf_op jit(solution)/shard_map/ppermute | solution.py:37
  100.3 16.6 %collective-permute-done.13.refs_3_ = bf16[4,96,960]{2,1,0:T(8,128)(2,1)} collective-permute-done((bf16[4,96,960]{2,1,0:T(8,128)(2,1)}, bf16[4,96,960]{2,1,0:T(8,128)(2,1)}, u32[]{:S(2)}, u32[]{:S(2)}) %collective-permute-start.13) | collective-permute-done | bytes 737312 | tf_op jit(solution)/shard_map/ppermute | solution.py:390
  116.9 5.3 %all-to-all-start.3 = ((bf16[4,2,2,96,768]{4,3,2,1,0:T(8,128)(2,1)}), bf16[4,2,2,96,768]{4,3,2,1,0:T(8,128)(2,1)}, u32[]{:S(2)}, u32[]{:S(2)}) async-start(bf16[4,2,2,96,768]{4,3,2,1,0:T(8,128)(2,1)} %plane_copies.1), calls=%async_computation.3 | async-start | bytes 4718592 | tf_op jit(solution)/shard_map/all_to_all | solution.py:395
  122.2 3.3 collective-permute-start.14
  133.8 1.4 pad_maximum_fusion.9
  139.3 2.4 fusion.4
  141.7 7.9 %assemble.1 = (bf16[4,2,96,1536]{3,2,1,0:T(8,128)(2,1)}, bf16[4,2,96,768]{3,2,1,0:T(8,128)(2,1)}, bf16[4,2,96,768]{3,2,1,0:T(8,128)(2,1)}, bf16[4,2,96,768]{3,2,1,0:T(8,128)(2,1)}) custom-call(s32[3]{0:T(128)} %pad_add_fusion.info, bf16[4,96,960]{2,1,0:T(8,128)(2,1)} %all-to-all-done.1.refs_0_, bf16[4,96,960]{2,1,0:T(8,128)(2,1)} %collective-permute-done.12.refs_1_, ...), custom_call_target="tpu_custom_call" | custom-call | bytes 11796480 | tf_op jit(solution)/shard_map/assemble/pallas_call | solution.py:423
  149.6 5.6 %first_forward.1 = (f32[512,768]{1,0:T(8,128)}, f32[512,768]{1,0:T(8,128)}, bf16[512,768]{1,0:T(8,128)(2,1)}, bf16[512,768]{1,0:T(8,128)(2,1)}, bf16[512,768]{1,0:T(8,128)(2,1)}) custom-call(bf16[512,768]{1,0:T(8,128)(2,1)} %own_ref.2, bf16[512,384]{1,0:T(8,128)(2,1)} %copy-done.15, bf16[512,384]{1,0:T(8,128)(2,1)} %collective-permute-done.9.oth_ref, ...), custom_call_target="tpu_custom_call" | custom-call | flops 2415919104 | bytes 9437184 | tf_op jit(solution)/shard_map/first_forward/pallas_call | solution.py:423
  155.2 4.6 %collective-permute-done.21.e3 = bf16[4,96,768]{2,1,0:T(8,128)(2,1)} collective-permute-done((bf16[4,96,768]{2,1,0:T(8,128)(2,1)}, bf16[4,96,768]{2,1,0:T(8,128)(2,1)}, u32[]{:S(2)}, u32[]{:S(2)}) %collective-permute-start.21) | collective-permute-done | bytes 589856 | tf_op jit(solution)/shard_map/ppermute | solution.py:390
  159.9 12.7 %all-to-all-done.3.s0 = bf16[4,2,2,96,768]{4,3,2,1,0:T(8,128)(2,1)} async-done(((bf16[4,2,2,96,768]{4,3,2,1,0:T(8,128)(2,1)}), bf16[4,2,2,96,768]{4,3,2,1,0:T(8,128)(2,1)}, u32[]{:S(2)}, u32[]{:S(2)}) %all-to-all-start.3) | async-done | bytes 2359328 | tf_op jit(solution)/shard_map/all_to_all | solution.py:395
  172.5 1.5 collective-permute-start.27
  174.1 3.1 fusion.ka_ref.va_ref
  177.4 1.5 concatenate.60.vec_ref
  180.8 1.6 copy-done.18
  182.4 13.7 %cross_fwd.1 = (bf16[512,768]{1,0:T(8,128)(2,1)S(1)}, f32[6,2,512]{2,1,0:T(2,128)S(1)}) custom-call(bf16[512,768]{1,0:T(8,128)(2,1)S(1)} %copy-done.18, bf16[512,1536]{1,0:T(8,128)(2,1)S(1)} %fusion.ka_ref.va_ref, bf16[512,1536]{1,0:T(8,128)(2,1)S(1)} %collective-permute-done.22.kb_ref.vb_ref, bf16[512,1536]{1,0:T(8,128)(2,1)S(1)} %fusion.ka_ref.va_ref, ...), custom_call_target="tpu_custom_call" | custom-call | flops 6442450944 | bytes 4718592 | tf_op jit(solution)/shard_map/cross_fwd/pallas_call | solution.py:188
  198.3 31.4 %feed.1 = (bf16[512,768]{1,0:T(8,128)(2,1)}, f32[512,768]{1,0:T(8,128)}, bf16[512,768]{1,0:T(8,128)(2,1)}, bf16[512,768]{1,0:T(8,128)(2,1)}, f32[16,768]{1,0:T(8...) custom-call(s32[3]{0:T(128)} %pad_add_fusion.info, ...), custom_call_target="tpu_custom_call" | custom-call | flops 31406948352 | bytes 18874368 | tf_op jit(solution)/shard_map/feed/pallas_call | solution.py:423
  231.4 9.3 %cross_bwd.1 = (bf16[512,768]{1,0:T(8,128)(2,1)S(1)}, bf16[2,512,768]{2,1,0:T(8,128)(2,1)S(1)}, bf16[2,512,768]{2,1,0:T(8,128)(2,1)}) custom-call(bf16[512,768]{1,0:T(8,128)(2,1)S(1)} %copy-done.19, bf16[512,1536]{1,0:T(8,128)(2,1)} %copy-done.1, bf16[512,1536]{1,0:T(8,128)(2,1)} %copy-done.2, bf16[512,1536]{1,0:T(8,128)(2,1)} %copy-done.1, ...), custom_call_target="tpu_custom_call" | custom-call | flops 5368709120 | bytes 3145728 | tf_op jit(solution)/shard_map/cross_bwd/pallas_call | solution.py:239
  240.7 4.0 fusion.8
  244.8 2.1 add_convert_fusion
  249.6 21.9 %cross_first.1 = (bf16[512,768]{1,0:T(8,128)(2,1)S(1)}, bf16[2,512,768]{2,1,0:T(8,128)(2,1)}, bf16[2,512,768]{2,1,0:T(8,128)(2,1)}, f32[512,768]{1,0:T(8,128)}, ...) custom-call(bf16[512,768]{1,0:T(8,128)(2,1)S(1)} %copy-done.19, ...), custom_call_target="tpu_custom_call", output_to_operand_aliasing={{1}: (14, {}), {2}: (15, {})} | custom-call | flops 10737418240 | bytes 6291456 | tf_op jit(solution)/shard_map/cross_first/pallas_call | solution.py:333
  275.0 7.7 %all-to-all-start.4 = ((bf16[4,2,2,96,768]{4,3,2,1,0:T(8,128)(2,1)}), bf16[4,2,2,96,768]{4,3,2,1,0:T(8,128)(2,1)}, u32[]{:S(2)}, u32[]{:S(2)}) async-start(bf16[4,2,2,96,768]{4,3,2,1,0:T(8,128)(2,1)} %add_convert_fusion), calls=%async_computation.4 | async-start | bytes 4718592 | tf_op jit(solution)/shard_map/all_to_all | solution.py:395
  282.8 7.0 %query_grads.1 = (bf16[2,2,4,96,576]{4,3,2,1,0:T(8,128)(2,1)}, bf16[2,2,4,96,576]{4,3,2,1,0:T(8,128)(2,1)}) custom-call(s32[3]{0:T(128)} %pad_add_fusion.info, bf16[512,768]{1,0:T(8,128)(2,1)} %get-tuple-element.221.h1_ref, bf16[512,768]{1,0:T(8,128)(2,1)} %copy-done.11, bf16[512,768]{1,0:T(8,128)(2,1)} %copy-done.12, ...), custom_call_target="tpu_custom_call" | custom-call | flops 1811939328 | bytes 5898240 | tf_op jit(solution)/shard_map/query_grads/pallas_call | solution.py:423
  291.8 6.7 %key_grads.1 = (bf16[2,2,4,96,384]{4,3,2,1,0:T(8,128)(2,1)}, bf16[2,2,4,96,384]{4,3,2,1,0:T(8,128)(2,1)}, bf16[512,768]{1,0:T(8,128)(2,1)}, f32[8,768]{1,0:T(8,128)}) custom-call(s32[3]{0:T(128)} %pad_add_fusion.info, bf16[512,768]{1,0:T(8,128)(2,1)} %bitcast.92, bf16[2,512,768]{2,1,0:T(8,128)(2,1)} %get-tuple-element.231.own_ref, ...), custom_call_target="tpu_custom_call" | custom-call | flops 2415919104 | bytes 5898240 | tf_op jit(solution)/shard_map/key_grads/pallas_call | solution.py:423
  301.3 2.5 fusion.1
  307.3 13.2 %self_bwd.2 = (bf16[3,2,512,384]{3,2,1,0:T(8,128)(2,1)S(1)}, f32[3,8,128]{2,1,0:T(8,128)S(1)}) custom-call(s32[2]{0:T(128)S(1)} %pad_add_fusion.1.info, bf16[2,512,1152]{2,1,0:T(8,128)(2,1)} %get-tuple-element.234.q_ref.k_ref.v_ref, bf16[2,512,1152]{2,1,0:T(8,128)(2,1)} %get-tuple-element.234.q_ref.k_ref.v_ref, ...), custom_call_target="tpu_custom_call" | custom-call | flops 8053063680 | bytes 4718592 | tf_op jit(solution)/shard_map/self_bwd/pallas_call | solution.py:121
  323.4 5.7 %collective-permute-done.39 = bf16[4,96,576]{2,1,0:T(8,128)(2,1)} collective-permute-done((bf16[4,96,576]{2,1,0:T(8,128)(2,1)S(1)}, bf16[4,96,576]{2,1,0:T(8,128)(2,1)}, u32[]{:S(2)}, u32[]{:S(2)}) %collective-permute-start.39) | collective-permute-done | bytes 442400 | tf_op jit(solution)/shard_map/ppermute | solution.py:390
  329.1 4.6 %all-to-all-done.4 = bf16[4,2,2,96,768]{4,3,2,1,0:T(8,128)(2,1)} async-done(((bf16[4,2,2,96,768]{4,3,2,1,0:T(8,128)(2,1)}), bf16[4,2,2,96,768]{4,3,2,1,0:T(8,128)(2,1)}, u32[]{:S(2)}, u32[]{:S(2)}) %all-to-all-start.4) | async-done | bytes 2359328 | tf_op jit(solution)/shard_map/all_to_all | solution.py:395
  335.7 7.2 %self_bwd.3 = (bf16[3,2,512,384]{3,2,1,0:T(8,128)(2,1)S(1)}, f32[3,8,128]{2,1,0:T(8,128)S(1)}) custom-call(s32[2]{0:T(128)S(1)} %pad_add_fusion.1.info, bf16[2,512,1152]{2,1,0:T(8,128)(2,1)} %get-tuple-element.234.q_ref.k_ref.v_ref, bf16[2,512,1152]{2,1,0:T(8,128)(2,1)} %get-tuple-element.234.q_ref.k_ref.v_ref, ...), custom_call_target="tpu_custom_call", output_to_operand_aliasing={{0}: (9, {}), {1}: (10, {})} | custom-call | flops 4026531840 | bytes 2359296 | tf_op jit(solution)/shard_map/self_bwd/pallas_call | solution.py:121
  347.3 7.2 %all-to-all-start.6 = ((bf16[4,96,768]{2,1,0:T(8,128)(2,1)}), bf16[4,96,768]{2,1,0:T(8,128)(2,1)}, u32[]{:S(2)}, u32[]{:S(2)}) async-start(bf16[4,96,768]{2,1,0:T(8,128)(2,1)} %fusion.1), calls=%async_computation.6 | async-start | bytes 1179648 | tf_op jit(solution)/shard_map/all_to_all | solution.py:395
  354.5 2.6 fusion.2
  357.1 2.1 reduce_sum.30
  361.5 6.2 %self_grads.1 = (bf16[4,96,576]{2,1,0:T(8,128)(2,1)}, bf16[4,96,576]{2,1,0:T(8,128)(2,1)}, bf16[4,96,576]{2,1,0:T(8,128)(2,1)}, bf16[4,96,576]{2,1,0:T(8,128)(2,1)}) custom-call(s32[3]{0:T(128)} %pad_add_fusion.info, bf16[512,768]{1,0:T(8,128)(2,1)} %own_ref.2, bf16[512,768]{1,0:T(8,128)(2,1)} %copy-done.4, bf16[3,2,512,384]{3,2,1,0:T(8,128)(2,1)} %copy-done.14), custom_call_target="tpu_custom_call" | custom-call | flops 3623878656 | bytes 5701632 | tf_op jit(solution)/shard_map/self_grads/pallas_call | solution.py:423
  367.7 1.5 collective-permute-start.52
  370.3 1.5 collective-permute-start.51
  371.9 6.6 %self_back.1 = (f32[512,768]{1,0:T(8,128)}, bf16[512,768]{1,0:T(8,128)(2,1)}) custom-call(bf16[3,2,512,384]{3,2,1,0:T(8,128)(2,1)} %copy-done.14, bf16[768,1152]{1,0:T(8,128)(2,1)} %copy-done.13, f32[512,768]{1,0:T(8,128)} %get-tuple-element.273.first_ref), custom_call_target="tpu_custom_call" | custom-call | flops 3623878656 | bytes 8060928 | tf_op jit(solution)/shard_map/self_back/pallas_call | solution.py:423
  378.4 4.7 %all-to-all-start.7 = ((bf16[4,96,576]{2,1,0:T(8,128)(2,1)}), bf16[4,96,576]{2,1,0:T(8,128)(2,1)S(1)}, u32[]{:S(2)}, u32[]{:S(2)}) async-start(bf16[4,96,576]{2,1,0:T(8,128)(2,1)} %fusion.2), calls=%async_computation.7 | async-start | bytes 983040 | tf_op jit(solution)/shard_map/all_to_all | solution.py:395
  387.4 3.3 collective-permute-done.51
  391.0 1.4 add_convert_fusion.5
  393.5 1.7 collective-permute-done.53
  395.2 10.7 %collective-permute-start.45 = (bf16[512,768]{1,0:T(8,128)(2,1)}, bf16[512,768]{1,0:T(8,128)(2,1)}, u32[]{:S(2)}, u32[]{:S(2)}) collective-permute-start(bf16[512,768]{1,0:T(8,128)(2,1)} %get-tuple-element.275), channel_id=1, source_target_pairs={{0,1},{1,0},{2,3},{3,2},{4,5},{5,4},{6,7},{7,6},{8,9},{9,8},{10,11... | collective-permute-start | bytes 2359304 | tf_op jit(solution)/shard_map/ppermute | solution.py:33
  406.0 5.2 %all-to-all-start.5 = ((bf16[4,96,960]{2,1,0:T(8,128)(2,1)}), bf16[4,96,960]{2,1,0:T(8,128)(2,1)}, u32[]{:S(2)}, u32[]{:S(2)}) async-start(bf16[4,96,960]{2,1,0:T(8,128)(2,1)} %pad_maximum_fusion), calls=%async_computation.5 | async-start | bytes 1572864 | tf_op jit(solution)/shard_map/all_to_all | solution.py:395
  412.8 1.9 pad_maximum_fusion.1.in_ref
  414.7 2.0 sum_turned.1
  416.7 1.9 copy.69
  419.4 8.0 %collective-permute-done.54 = f32[23,768]{1,0:T(8,128)S(1)} collective-permute-done((f32[23,768]{1,0:T(8,128)S(1)}, f32[23,768]{1,0:T(8,128)S(1)}, u32[]{:S(2)}, u32[]{:S(2)}) %collective-permute-start.54) | collective-permute-done | bytes 70688 | tf_op jit(solution)/shard_map/ppermute | solution.py:42
  431.2 1.9 convert_reduce_fusion.1
  433.1 2.6 add_convert_fusion.1
  435.7 1.9 sum_query.1
  439.8 4.8 %scatter.1 = f32[32,64,768]{2,1,0:T(8,128)} custom-call(s32[32]{0:T(128)S(1)} %reshape.480.table, bf16[8,64,768]{2,1,0:T(8,128)(2,1)S(1)} %bitcast.87, bf16[8,64,768]{2,1,0:T(8,128)(2,1)S(1)} %bitcast.89, bf16[8,64,768]{2,1,0:T(8,128)(2,1)S(1)} %collective-permute-done.47.c_ref, bf16[8,64,768]{2,1,0:T(8,128)(2,1)S(1)} %collective-permute-done.48.d_ref), custom_call_target="tpu_custom_call" | custom-call | bytes 9437184 | tf_op jit(solution)/shard_map/scatter/pallas_call | solution.py:1109
  (329 shorter events, 76.6 us)
Async XLA Ops:
  7.2 10.5 %collective-permute-start = (bf16[96,768]{1,0:T(8,128)(2,1)}, bf16[96,768]{1,0:T(8,128)(2,1)S(1)}, u32[]{:S(2)}, u32[]{:S(2)}) collective-permute-start(bf16[96,768]{1,0:T(8,128)(2,1)} %get-tuple-element.165.own_ref), channel_id=1, source_target_pairs={{0,2},{2,0},{1,3},{3,1},{4,6},{6,4},{5,7},{7,5},{8,10},{10,8},{9,1... | collective-permute-start | bytes 442376 | tf_op jit(solution)/shard_map/ppermute | solution.py:37
  7.4 10.3 %collective-permute-start.1 = (bf16[96,768]{1,0:T(8,128)(2,1)}, bf16[96,768]{1,0:T(8,128)(2,1)S(1)}, u32[]{:S(2)}, u32[]{:S(2)}) collective-permute-start(bf16[96,768]{1,0:T(8,128)(2,1)} %get-tuple-element.165.own_ref), channel_id=1, source_target_pairs={{0,4},{4,0},{8,12},{12,8},{16,20},{20,16},{24,28},{28,24},{1,5},{5... | collective-permute-start | bytes 442376 | tf_op jit(solution)/shard_map/ppermute | solution.py:42
  8.7 9.0 %collective-permute-start.2 = (bf16[96,768]{1,0:T(8,128)(2,1)}, bf16[96,768]{1,0:T(8,128)(2,1)S(1)}, u32[]{:S(2)}, u32[]{:S(2)}) collective-permute-start(bf16[96,768]{1,0:T(8,128)(2,1)} %get-tuple-element.165.own_ref), channel_id=1, source_target_pairs={{0,6},{1,7},{2,4},{3,5},{4,2},{5,3},{6,0},{7,1},{8,14},{9,15},{10,... | collective-permute-start | bytes 442376 | tf_op jit(solution)/shard_map/ppermute | solution.py:390
  9.8 14.8 %all-to-all-start = ((bf16[4,96,576]{2,1,0:T(8,128)(2,1)}), bf16[4,96,576]{2,1,0:T(8,128)(2,1)S(1)}, u32[]{:S(2)}, u32[]{:S(2)}) async-start(bf16[4,96,576]{2,1,0:T(8,128)(2,1)} %pack_self.1), calls=%async_computation | async-start | bytes 983040 | tf_op jit(solution)/shard_map/all_to_all | solution.py:395
  28.7 12.9 %collective-permute-start.7 = (bf16[2,8,64,768]{3,2,1,0:T(8,128)(2,1)}, bf16[2,8,64,768]{3,2,1,0:T(8,128)(2,1)}, u32[]{:S(2)}, u32[]{:S(2)}) collective-permute-start(bf16[2,8,64,768]{3,2,1,0:T(8,128)(2,1)} %bitcast.104), channel_id=1, source_target_pairs={{0,1},{1,0},{2,3},{3,2},{4,5},{5,4},{6,7},{7,6},{8,9},{9,8},{10,11... | collective-permute-start | bytes 4718600 | tf_op jit(solution)/shard_map/ppermute | solution.py:33
  30.5 31.0 %all-to-all-start.1 = ((bf16[4,96,960]{2,1,0:T(8,128)(2,1)}), bf16[4,96,960]{2,1,0:T(8,128)(2,1)}, u32[]{:S(2)}, u32[]{:S(2)}) async-start(bf16[4,96,960]{2,1,0:T(8,128)(2,1)} %get-tuple-element.167), calls=%async_computation.1 | async-start | bytes 1572864 | tf_op jit(solution)/shard_map/all_to_all | solution.py:395
  37.6 12.5 %collective-permute-start.4 = (bf16[4,96,576]{2,1,0:T(8,128)(2,1)S(1)}, bf16[4,96,576]{2,1,0:T(8,128)(2,1)S(1)}, u32[]{:S(2)}, u32[]{:S(2)}) collective-permute-start(bf16[4,96,576]{2,1,0:T(8,128)(2,1)S(1)} %all-to-all-done.w_ref), channel_id=1, source_target_pairs={{0,2},{2,0},{1,3},{3,1},{4,6},{6,4},{5,7},{7,5},{8,10},{10,8},{9,1... | collective-permute-start | bytes 1327112 | tf_op jit(solution)/shard_map/ppermute | solution.py:37
  37.7 12.4 %collective-permute-start.5 = (bf16[4,96,576]{2,1,0:T(8,128)(2,1)S(1)}, bf16[4,96,576]{2,1,0:T(8,128)(2,1)S(1)}, u32[]{:S(2)}, u32[]{:S(2)}) collective-permute-start(bf16[4,96,576]{2,1,0:T(8,128)(2,1)S(1)} %all-to-all-done.w_ref), channel_id=1, source_target_pairs={{0,4},{4,0},{8,12},{12,8},{16,20},{20,16},{24,28},{28,24},{1,5},{5... | collective-permute-start | bytes 1327112 | tf_op jit(solution)/shard_map/ppermute | solution.py:42
  39.1 22.3 %collective-permute-start.6 = (bf16[4,96,576]{2,1,0:T(8,128)(2,1)S(1)}, bf16[4,96,576]{2,1,0:T(8,128)(2,1)S(1)}, u32[]{:S(2)}, u32[]{:S(2)}) collective-permute-start(bf16[4,96,576]{2,1,0:T(8,128)(2,1)S(1)} %all-to-all-done.w_ref), channel_id=1, source_target_pairs={{0,6},{1,7},{2,4},{3,5},{4,2},{5,3},{6,0},{7,1},{8,14},{9,15},{10,... | collective-permute-start | bytes 1327112 | tf_op jit(solution)/shard_map/ppermute | solution.py:390
  40.3 30.0 %collective-permute-start.8 = (bf16[512,768]{1,0:T(8,128)(2,1)S(1)}, bf16[512,768]{1,0:T(8,128)(2,1)S(1)}, u32[]{:S(2)}, u32[]{:S(2)}) collective-permute-start(bf16[512,768]{1,0:T(8,128)(2,1)S(1)} %copy-done.3), channel_id=1, source_target_pairs={{0,1},{1,0},{2,3},{3,2},{4,5},{5,4},{6,7},{7,6},{8,9},{9,8},{10,11... | collective-permute-start | bytes 2359304 | tf_op jit(solution)/shard_map/ppermute | solution.py:33
  61.4 55.5 %all-to-all-start.2 = ((bf16[4,96,768]{2,1,0:T(8,128)(2,1)}), bf16[4,96,768]{2,1,0:T(8,128)(2,1)}, u32[]{:S(2)}, u32[]{:S(2)}) async-start(bf16[4,96,768]{2,1,0:T(8,128)(2,1)} %get-tuple-element.181), calls=%async_computation.2 | async-start | bytes 1179648 | tf_op jit(solution)/shard_map/all_to_all | solution.py:395
  66.0 50.9 %collective-permute-start.10 = (bf16[8,64,768]{2,1,0:T(8,128)(2,1)}, bf16[8,64,768]{2,1,0:T(8,128)(2,1)}, u32[]{:S(2)}, u32[]{:S(2)}) collective-permute-start(bf16[8,64,768]{2,1,0:T(8,128)(2,1)} %fusion.5), channel_id=1, source_target_pairs={{0,2},{2,0},{1,3},{3,1},{4,6},{6,4},{5,7},{7,5},{8,10},{10,8},{9,1... | collective-permute-start | bytes 2359304 | tf_op jit(solution)/shard_map/ppermute | solution.py:37
  66.3 34.0 %collective-permute-start.11 = (bf16[4,96,960]{2,1,0:T(8,128)(2,1)}, bf16[4,96,960]{2,1,0:T(8,128)(2,1)}, u32[]{:S(2)}, u32[]{:S(2)}) collective-permute-start(bf16[4,96,960]{2,1,0:T(8,128)(2,1)} %all-to-all-done.1.refs_0_), channel_id=1, source_target_pairs={{0,2},{2,0},{1,3},{3,1},{4,6},{6,4},{5,7},{7,5},{8,10},{10,8},{9,1... | collective-permute-start | bytes 2211848 | tf_op jit(solution)/shard_map/ppermute | solution.py:37
  67.4 32.9 %collective-permute-start.12 = (bf16[4,96,960]{2,1,0:T(8,128)(2,1)}, bf16[4,96,960]{2,1,0:T(8,128)(2,1)}, u32[]{:S(2)}, u32[]{:S(2)}) collective-permute-start(bf16[4,96,960]{2,1,0:T(8,128)(2,1)} %all-to-all-done.1.refs_0_), channel_id=1, source_target_pairs={{0,4},{4,0},{8,12},{12,8},{16,20},{20,16},{24,28},{28,24},{1,5},{5... | collective-permute-start | bytes 2211848 | tf_op jit(solution)/shard_map/ppermute | solution.py:42
  67.7 49.2 %collective-permute-start.13 = (bf16[4,96,960]{2,1,0:T(8,128)(2,1)}, bf16[4,96,960]{2,1,0:T(8,128)(2,1)}, u32[]{:S(2)}, u32[]{:S(2)}) collective-permute-start(bf16[4,96,960]{2,1,0:T(8,128)(2,1)} %all-to-all-done.1.refs_0_), channel_id=1, source_target_pairs={{0,6},{1,7},{2,4},{3,5},{4,2},{5,3},{6,0},{7,1},{8,14},{9,15},{10,... | collective-permute-start | bytes 2211848 | tf_op jit(solution)/shard_map/ppermute | solution.py:390
  116.9 55.6 %all-to-all-start.3 = ((bf16[4,2,2,96,768]{4,3,2,1,0:T(8,128)(2,1)}), bf16[4,2,2,96,768]{4,3,2,1,0:T(8,128)(2,1)}, u32[]{:S(2)}, u32[]{:S(2)}) async-start(bf16[4,2,2,96,768]{4,3,2,1,0:T(8,128)(2,1)} %plane_copies.1), calls=%async_computation.3 | async-start | bytes 4718592 | tf_op jit(solution)/shard_map/all_to_all | solution.py:395
  122.2 9.0 %collective-permute-start.14 = (bf16[4,96,960]{2,1,0:T(8,128)(2,1)}, bf16[4,96,960]{2,1,0:T(8,128)(2,1)S(1)}, u32[]{:S(2)}, u32[]{:S(2)}) collective-permute-start(bf16[4,96,960]{2,1,0:T(8,128)(2,1)} %all-to-all-done.1.refs_0_), channel_id=1, source_target_pairs={{0,1},{1,0},{2,3},{3,2},{4,5},{5,4},{6,7},{7,6},{8,9},{9,8},{10,11... | collective-permute-start | bytes 2211848 | tf_op jit(solution)/shard_map/ppermute | solution.py:33
  125.5 6.8 %collective-permute-start.15 = (bf16[4,96,960]{2,1,0:T(8,128)(2,1)}, bf16[4,96,960]{2,1,0:T(8,128)(2,1)S(1)}, u32[]{:S(2)}, u32[]{:S(2)}) collective-permute-start(bf16[4,96,960]{2,1,0:T(8,128)(2,1)} %collective-permute-done.12.refs_1_), channel_id=1, source_target_pairs={{0,1},{1,0},{2,3},{3,2},{4,5},{5,4},{6,7},{7,6},{8,9},{9,8},{10,11... | collective-permute-start | bytes 2211848 | tf_op jit(solution)/shard_map/ppermute | solution.py:33
  125.6 7.1 %collective-permute-start.16 = (bf16[4,96,960]{2,1,0:T(8,128)(2,1)}, bf16[4,96,960]{2,1,0:T(8,128)(2,1)}, u32[]{:S(2)}, u32[]{:S(2)}) collective-permute-start(bf16[4,96,960]{2,1,0:T(8,128)(2,1)} %collective-permute-done.11.refs_2_), channel_id=1, source_target_pairs={{0,1},{1,0},{2,3},{3,2},{4,5},{5,4},{6,7},{7,6},{8,9},{9,8},{10,11... | collective-permute-start | bytes 2211848 | tf_op jit(solution)/shard_map/ppermute | solution.py:33
  128.1 13.6 %collective-permute-start.17 = (bf16[4,96,960]{2,1,0:T(8,128)(2,1)}, bf16[4,96,960]{2,1,0:T(8,128)(2,1)}, u32[]{:S(2)}, u32[]{:S(2)}) collective-permute-start(bf16[4,96,960]{2,1,0:T(8,128)(2,1)} %collective-permute-done.13.refs_3_), channel_id=1, source_target_pairs={{0,1},{1,0},{2,3},{3,2},{4,5},{5,4},{6,7},{7,6},{8,9},{9,8},{10,11... | collective-permute-start | bytes 2211848 | tf_op jit(solution)/shard_map/ppermute | solution.py:33
  130.8 18.8 %collective-permute-start.9 = (bf16[512,384]{1,0:T(8,128)(2,1)S(1)}, bf16[512,384]{1,0:T(8,128)(2,1)}, u32[]{:S(2)}, u32[]{:S(2)}) collective-permute-start(bf16[512,384]{1,0:T(8,128)(2,1)S(1)} %copy-done.6), channel_id=1, source_target_pairs={{0,1},{1,0},{2,3},{3,2},{4,5},{5,4},{6,7},{7,6},{8,9},{9,8},{10,11... | collective-permute-start | bytes 1179656 | tf_op jit(solution)/shard_map/ppermute | solution.py:33
  131.2 24.1 %collective-permute-start.19 = (bf16[4,96,768]{2,1,0:T(8,128)(2,1)}, bf16[4,96,768]{2,1,0:T(8,128)(2,1)}, u32[]{:S(2)}, u32[]{:S(2)}) collective-permute-start(bf16[4,96,768]{2,1,0:T(8,128)(2,1)} %all-to-all-done.2.e0), channel_id=1, source_target_pairs={{0,2},{2,0},{1,3},{3,1},{4,6},{6,4},{5,7},{7,5},{8,10},{10,8},{9,1... | collective-permute-start | bytes 1769480 | tf_op jit(solution)/shard_map/ppermute | solution.py:37
  132.3 22.9 %collective-permute-start.20 = (bf16[4,96,768]{2,1,0:T(8,128)(2,1)}, bf16[4,96,768]{2,1,0:T(8,128)(2,1)}, u32[]{:S(2)}, u32[]{:S(2)}) collective-permute-start(bf16[4,96,768]{2,1,0:T(8,128)(2,1)} %all-to-all-done.2.e0), channel_id=1, source_target_pairs={{0,4},{4,0},{8,12},{12,8},{16,20},{20,16},{24,28},{28,24},{1,5},{5... | collective-permute-start | bytes 1769480 | tf_op jit(solution)/shard_map/ppermute | solution.py:42
  132.7 27.1 %collective-permute-start.21 = (bf16[4,96,768]{2,1,0:T(8,128)(2,1)}, bf16[4,96,768]{2,1,0:T(8,128)(2,1)}, u32[]{:S(2)}, u32[]{:S(2)}) collective-permute-start(bf16[4,96,768]{2,1,0:T(8,128)(2,1)} %all-to-all-done.2.e0), channel_id=1, source_target_pairs={{0,6},{1,7},{2,4},{3,5},{4,2},{5,3},{6,0},{7,1},{8,14},{9,15},{10,... | collective-permute-start | bytes 1769480 | tf_op jit(solution)/shard_map/ppermute | solution.py:390
  172.5 24.5 %collective-permute-start.27 = (bf16[4,2,2,96,768]{4,3,2,1,0:T(8,128)(2,1)}, bf16[4,2,2,96,768]{4,3,2,1,0:T(8,128)(2,1)}, u32[]{:S(2)}, u32[]{:S(2)}) collective-permute-start(bf16[4,2,2,96,768]{4,3,2,1,0:T(8,128)(2,1)} %all-to-all-done.3.s0), channel_id=1, source_target_pairs={{0,1},{1,0},{2,3},{3,2},{4,5},{5,4},{6,7},{7,6},{8,9},{9,8},{10,11... | collective-permute-start | bytes 7077896 | tf_op jit(solution)/shard_map/ppermute | solution.py:33
  177.2 3.5 collective-permute-start.22
  178.9 18.0 %collective-permute-start.23 = (bf16[4,96,768]{2,1,0:T(8,128)(2,1)}, bf16[4,96,768]{2,1,0:T(8,128)(2,1)S(1)}, u32[]{:S(2)}, u32[]{:S(2)}) collective-permute-start(bf16[4,96,768]{2,1,0:T(8,128)(2,1)} %all-to-all-done.2.e0), channel_id=1, source_target_pairs={{0,1},{1,0},{2,3},{3,2},{4,5},{5,4},{6,7},{7,6},{8,9},{9,8},{10,11... | collective-permute-start | bytes 1769480 | tf_op jit(solution)/shard_map/ppermute | solution.py:33
  179.2 17.8 %collective-permute-start.24 = (bf16[4,96,768]{2,1,0:T(8,128)(2,1)}, bf16[4,96,768]{2,1,0:T(8,128)(2,1)S(1)}, u32[]{:S(2)}, u32[]{:S(2)}) collective-permute-start(bf16[4,96,768]{2,1,0:T(8,128)(2,1)} %collective-permute-done.20.e1), channel_id=1, source_target_pairs={{0,1},{1,0},{2,3},{3,2},{4,5},{5,4},{6,7},{7,6},{8,9},{9,8},{10,11... | collective-permute-start | bytes 1769480 | tf_op jit(solution)/shard_map/ppermute | solution.py:33
  179.4 17.5 %collective-permute-start.25 = (bf16[4,96,768]{2,1,0:T(8,128)(2,1)}, bf16[4,96,768]{2,1,0:T(8,128)(2,1)S(1)}, u32[]{:S(2)}, u32[]{:S(2)}) collective-permute-start(bf16[4,96,768]{2,1,0:T(8,128)(2,1)} %collective-permute-done.19.e2), channel_id=1, source_target_pairs={{0,1},{1,0},{2,3},{3,2},{4,5},{5,4},{6,7},{7,6},{8,9},{9,8},{10,11... | collective-permute-start | bytes 1769480 | tf_op jit(solution)/shard_map/ppermute | solution.py:33
  180.7 16.3 %collective-permute-start.26 = (bf16[4,96,768]{2,1,0:T(8,128)(2,1)}, bf16[4,96,768]{2,1,0:T(8,128)(2,1)S(1)}, u32[]{:S(2)}, u32[]{:S(2)}) collective-permute-start(bf16[4,96,768]{2,1,0:T(8,128)(2,1)} %collective-permute-done.21.e3), channel_id=1, source_target_pairs={{0,1},{1,0},{2,3},{3,2},{4,5},{5,4},{6,7},{7,6},{8,9},{9,8},{10,11... | collective-permute-start | bytes 1769480 | tf_op jit(solution)/shard_map/ppermute | solution.py:33
  229.7 11.0 %collective-permute-start.29 = (bf16[2,2,4,96,768]{4,3,2,1,0:T(8,128)(2,1)}, bf16[2,2,4,96,768]{4,3,2,1,0:T(8,128)(2,1)}, u32[]{:S(2)}, u32[]{:S(2)}) collective-permute-start(bf16[2,2,4,96,768]{4,3,2,1,0:T(8,128)(2,1)} %get-tuple-element.213), channel_id=1, source_target_pairs={{0,1},{1,0},{2,3},{3,2},{4,5},{5,4},{6,7},{7,6},{8,9},{9,8},{10,11... | collective-permute-start | bytes 7077896 | tf_op jit(solution)/shard_map/ppermute | solution.py:33
  229.9 14.9 %collective-permute-start.28 = (bf16[4,2,2,96,768]{4,3,2,1,0:T(8,128)(2,1)}, bf16[4,2,2,96,768]{4,3,2,1,0:T(8,128)(2,1)S(1)}, u32[]{:S(2)}, u32[]{:S(2)}) collective-permute-start(bf16[4,2,2,96,768]{4,3,2,1,0:T(8,128)(2,1)} %get-tuple-element.210), channel_id=1, source_target_pairs={{0,1},{1,0},{2,3},{3,2},{4,5},{5,4},{6,7},{7,6},{8,9},{9,8},{10,11... | collective-permute-start | bytes 7077896 | tf_op jit(solution)/shard_map/ppermute | solution.py:33
  246.9 35.8 %collective-permute-start.30 = (bf16[4,96,768]{2,1,0:T(8,128)(2,1)}, bf16[4,96,768]{2,1,0:T(8,128)(2,1)S(1)}, u32[]{:S(2)}, u32[]{:S(2)}) collective-permute-start(bf16[4,96,768]{2,1,0:T(8,128)(2,1)} %get-tuple-element.224), channel_id=1, source_target_pairs={{0,2},{2,0},{1,3},{3,1},{4,6},{6,4},{5,7},{7,5},{8,10},{10,8},{9,1... | collective-permute-start | bytes 1769480 | tf_op jit(solution)/shard_map/ppermute | solution.py:37
  248.1 34.7 %collective-permute-start.31 = (bf16[4,96,768]{2,1,0:T(8,128)(2,1)}, bf16[4,96,768]{2,1,0:T(8,128)(2,1)S(1)}, u32[]{:S(2)}, u32[]{:S(2)}) collective-permute-start(bf16[4,96,768]{2,1,0:T(8,128)(2,1)} %get-tuple-element.225), channel_id=1, source_target_pairs={{0,4},{4,0},{8,12},{12,8},{16,20},{20,16},{24,28},{28,24},{1,5},{5... | collective-permute-start | bytes 1769480 | tf_op jit(solution)/shard_map/ppermute | solution.py:42
  248.6 34.2 %collective-permute-start.32 = (bf16[4,96,768]{2,1,0:T(8,128)(2,1)}, bf16[4,96,768]{2,1,0:T(8,128)(2,1)S(1)}, u32[]{:S(2)}, u32[]{:S(2)}) collective-permute-start(bf16[4,96,768]{2,1,0:T(8,128)(2,1)} %get-tuple-element.226), channel_id=1, source_target_pairs={{0,6},{1,7},{2,4},{3,5},{4,2},{5,3},{6,0},{7,1},{8,14},{9,15},{10,... | collective-permute-start | bytes 1769480 | tf_op jit(solution)/shard_map/ppermute | solution.py:390
  274.1 17.7 %collective-permute-start.33 = (bf16[2,512,768]{2,1,0:T(8,128)(2,1)}, bf16[2,512,768]{2,1,0:T(8,128)(2,1)}, u32[]{:S(2)}, u32[]{:S(2)}) collective-permute-start(bf16[2,512,768]{2,1,0:T(8,128)(2,1)} %get-tuple-element.232), channel_id=1, source_target_pairs={{0,1},{1,0},{2,3},{3,2},{4,5},{5,4},{6,7},{7,6},{8,9},{9,8},{10,11... | collective-permute-start | bytes 4718600 | tf_op jit(solution)/shard_map/ppermute | solution.py:33
  275.0 58.7 %all-to-all-start.4 = ((bf16[4,2,2,96,768]{4,3,2,1,0:T(8,128)(2,1)}), bf16[4,2,2,96,768]{4,3,2,1,0:T(8,128)(2,1)}, u32[]{:S(2)}, u32[]{:S(2)}) async-start(bf16[4,2,2,96,768]{4,3,2,1,0:T(8,128)(2,1)} %add_convert_fusion), calls=%async_computation.4 | async-start | bytes 4718592 | tf_op jit(solution)/shard_map/all_to_all | solution.py:395
  289.8 8.7 %collective-permute-start.34 = (bf16[2,2,4,96,576]{4,3,2,1,0:T(8,128)(2,1)}, bf16[2,2,4,96,576]{4,3,2,1,0:T(8,128)(2,1)S(1)}, u32[]{:S(2)}, u32[]{:S(2)}) collective-permute-start(bf16[2,2,4,96,576]{4,3,2,1,0:T(8,128)(2,1)} %get-tuple-element.239), channel_id=1, source_target_pairs={{0,1},{1,0},{2,3},{3,2},{4,5},{5,4},{6,7},{7,6},{8,9},{9,8},{10,11... | collective-permute-start | bytes 5308424 | tf_op jit(solution)/shard_map/ppermute | solution.py:33
  291.5 8.2 %collective-permute-start.35 = (bf16[512,384]{1,0:T(8,128)(2,1)S(1)}, bf16[512,384]{1,0:T(8,128)(2,1)S(1)}, u32[]{:S(2)}, u32[]{:S(2)}) collective-permute-start(bf16[512,384]{1,0:T(8,128)(2,1)S(1)} %get-tuple-element.241), channel_id=1, source_target_pairs={{0,1},{1,0},{2,3},{3,2},{4,5},{5,4},{6,7},{7,6},{8,9},{9,8},{10,11... | collective-permute-start | bytes 1179656 | tf_op jit(solution)/shard_map/ppermute | solution.py:33
  300.4 20.0 %collective-permute-start.36 = (bf16[2,2,4,96,384]{4,3,2,1,0:T(8,128)(2,1)S(1)}, bf16[2,2,4,96,384]{4,3,2,1,0:T(8,128)(2,1)S(1)}, u32[]{:S(2)}, u32[]{:S(2)}) collective-permute-start(bf16[2,2,4,96,384]{4,3,2,1,0:T(8,128)(2,1)S(1)} %copy-done.71), channel_id=1, source_target_pairs={{0,1},{1,0},{2,3},{3,2},{4,5},{5,4},{6,7},{7,6},{8,9},{9,8},{10,11... | collective-permute-start | bytes 3538952 | tf_op jit(solution)/shard_map/ppermute | solution.py:33
  304.6 17.2 %collective-permute-start.37 = (bf16[4,96,576]{2,1,0:T(8,128)(2,1)S(1)}, bf16[4,96,576]{2,1,0:T(8,128)(2,1)S(1)}, u32[]{:S(2)}, u32[]{:S(2)}) collective-permute-start(bf16[4,96,576]{2,1,0:T(8,128)(2,1)S(1)} %get-tuple-element.249), channel_id=1, source_target_pairs={{0,2},{2,0},{1,3},{3,1},{4,6},{6,4},{5,7},{7,5},{8,10},{10,8},{9,1... | collective-permute-start | bytes 1327112 | tf_op jit(solution)/shard_map/ppermute | solution.py:37
  305.7 16.9 %collective-permute-start.38 = (bf16[4,96,576]{2,1,0:T(8,128)(2,1)S(1)}, bf16[4,96,576]{2,1,0:T(8,128)(2,1)S(1)}, u32[]{:S(2)}, u32[]{:S(2)}) collective-permute-start(bf16[4,96,576]{2,1,0:T(8,128)(2,1)S(1)} %get-tuple-element.250), channel_id=1, source_target_pairs={{0,4},{4,0},{8,12},{12,8},{16,20},{20,16},{24,28},{28,24},{1,5},{5... | collective-permute-start | bytes 1327112 | tf_op jit(solution)/shard_map/ppermute | solution.py:42
  306.3 22.8 %collective-permute-start.39 = (bf16[4,96,576]{2,1,0:T(8,128)(2,1)S(1)}, bf16[4,96,576]{2,1,0:T(8,128)(2,1)}, u32[]{:S(2)}, u32[]{:S(2)}) collective-permute-start(bf16[4,96,576]{2,1,0:T(8,128)(2,1)S(1)} %get-tuple-element.251), channel_id=1, source_target_pairs={{0,6},{1,7},{2,4},{3,5},{4,2},{5,3},{6,0},{7,1},{8,14},{9,15},{10,... | collective-permute-start | bytes 1327112 | tf_op jit(solution)/shard_map/ppermute | solution.py:390
  343.8 15.4 %collective-permute-start.40 = (f32[23,768]{1,0:T(8,128)S(1)}, f32[23,768]{1,0:T(8,128)S(1)}, u32[]{:S(2)}, u32[]{:S(2)}) collective-permute-start(f32[23,768]{1,0:T(8,128)S(1)} %pad_maximum_fusion.2), channel_id=1, source_target_pairs={{0,1},{1,0},{2,3},{3,2},{4,5},{5,4},{6,7},{7,6},{8,9},{9,8},{10,11... | collective-permute-start | bytes 211976 | tf_op jit(solution)/shard_map/ppermute | solution.py:33
  344.6 23.0 %collective-permute-start.42 = (bf16[4,96,384]{2,1,0:T(8,128)(2,1)}, bf16[4,96,384]{2,1,0:T(8,128)(2,1)S(1)}, u32[]{:S(2)}, u32[]{:S(2)}) collective-permute-start(bf16[4,96,384]{2,1,0:T(8,128)(2,1)} %get-tuple-element.268), channel_id=1, source_target_pairs={{0,2},{2,0},{1,3},{3,1},{4,6},{6,4},{5,7},{7,5},{8,10},{10,8},{9,1... | collective-permute-start | bytes 884744 | tf_op jit(solution)/shard_map/ppermute | solution.py:37
  345.7 21.9 %collective-permute-start.43 = (bf16[4,96,384]{2,1,0:T(8,128)(2,1)}, bf16[4,96,384]{2,1,0:T(8,128)(2,1)}, u32[]{:S(2)}, u32[]{:S(2)}) collective-permute-start(bf16[4,96,384]{2,1,0:T(8,128)(2,1)} %get-tuple-element.269), channel_id=1, source_target_pairs={{0,4},{4,0},{8,12},{12,8},{16,20},{20,16},{24,28},{28,24},{1,5},{5... | collective-permute-start | bytes 884744 | tf_op jit(solution)/shard_map/ppermute | solution.py:42
  346.3 21.4 %collective-permute-start.44 = (bf16[4,96,384]{2,1,0:T(8,128)(2,1)}, bf16[4,96,384]{2,1,0:T(8,128)(2,1)}, u32[]{:S(2)}, u32[]{:S(2)}) collective-permute-start(bf16[4,96,384]{2,1,0:T(8,128)(2,1)} %get-tuple-element.270), channel_id=1, source_target_pairs={{0,6},{1,7},{2,4},{3,5},{4,2},{5,3},{6,0},{7,1},{8,14},{9,15},{10,... | collective-permute-start | bytes 884744 | tf_op jit(solution)/shard_map/ppermute | solution.py:390
  347.3 31.2 %all-to-all-start.6 = ((bf16[4,96,768]{2,1,0:T(8,128)(2,1)}), bf16[4,96,768]{2,1,0:T(8,128)(2,1)}, u32[]{:S(2)}, u32[]{:S(2)}) async-start(bf16[4,96,768]{2,1,0:T(8,128)(2,1)} %fusion.1), calls=%async_computation.6 | async-start | bytes 1179648 | tf_op jit(solution)/shard_map/all_to_all | solution.py:395
  360.0 51.5 %collective-permute-start.55 = (bf16[96,768]{1,0:T(8,128)(2,1)}, bf16[96,768]{1,0:T(8,128)(2,1)}, u32[]{:S(2)}, u32[]{:S(2)}) collective-permute-start(bf16[96,768]{1,0:T(8,128)(2,1)} %get-tuple-element.401), channel_id=1, source_target_pairs={{0,2},{2,0},{1,3},{3,1},{4,6},{6,4},{5,7},{7,5},{8,10},{10,8},{9,1... | collective-permute-start | bytes 442376 | tf_op jit(solution)/shard_map/ppermute | solution.py:37
  361.1 6.5 %collective-permute-start.41 = (f32[23,768]{1,0:T(8,128)S(1)}, f32[23,768]{1,0:T(8,128)S(1)}, u32[]{:S(2)}, u32[]{:S(2)}) collective-permute-start(f32[23,768]{1,0:T(8,128)S(1)} %fusion.22), channel_id=1, source_target_pairs={{0,2},{2,0},{1,3},{3,1},{4,6},{6,4},{5,7},{7,5},{8,10},{10,8},{9,1... | collective-permute-start | bytes 211976 | tf_op jit(solution)/shard_map/ppermute | solution.py:37
  367.7 16.9 %collective-permute-start.52 = (f32[23,768]{1,0:T(8,128)S(1)}, f32[23,768]{1,0:T(8,128)S(1)}, u32[]{:S(2)}, u32[]{:S(2)}) collective-permute-start(f32[23,768]{1,0:T(8,128)S(1)} %add.315), channel_id=1, source_target_pairs={{0,4},{4,0},{8,12},{12,8},{16,20},{20,16},{24,28},{28,24},{1,5},{5... | collective-permute-start | bytes 211976 | tf_op jit(solution)/shard_map/ppermute | solution.py:42
  369.2 15.5 %collective-permute-start.49 = (bf16[4,96,576]{2,1,0:T(8,128)(2,1)}, bf16[4,96,576]{2,1,0:T(8,128)(2,1)S(1)}, u32[]{:S(2)}, u32[]{:S(2)}) collective-permute-start(bf16[4,96,576]{2,1,0:T(8,128)(2,1)} %get-tuple-element.279), channel_id=1, source_target_pairs={{0,2},{2,0},{1,3},{3,1},{4,6},{6,4},{5,7},{7,5},{8,10},{10,8},{9,1... | collective-permute-start | bytes 1327112 | tf_op jit(solution)/shard_map/ppermute | solution.py:37
  369.4 16.7 %collective-permute-start.50 = (bf16[4,96,576]{2,1,0:T(8,128)(2,1)}, bf16[4,96,576]{2,1,0:T(8,128)(2,1)}, u32[]{:S(2)}, u32[]{:S(2)}) collective-permute-start(bf16[4,96,576]{2,1,0:T(8,128)(2,1)} %get-tuple-element.280), channel_id=1, source_target_pairs={{0,4},{4,0},{8,12},{12,8},{16,20},{20,16},{24,28},{28,24},{1,5},{5... | collective-permute-start | bytes 1327112 | tf_op jit(solution)/shard_map/ppermute | solution.py:42
  370.3 20.3 %collective-permute-start.51 = (bf16[4,96,576]{2,1,0:T(8,128)(2,1)}, bf16[4,96,576]{2,1,0:T(8,128)(2,1)}, u32[]{:S(2)}, u32[]{:S(2)}) collective-permute-start(bf16[4,96,576]{2,1,0:T(8,128)(2,1)} %get-tuple-element.281), channel_id=1, source_target_pairs={{0,6},{1,7},{2,4},{3,5},{4,2},{5,3},{6,0},{7,1},{8,14},{9,15},{10,... | collective-permute-start | bytes 1327112 | tf_op jit(solution)/shard_map/ppermute | solution.py:390
  378.4 27.5 %all-to-all-start.7 = ((bf16[4,96,576]{2,1,0:T(8,128)(2,1)}), bf16[4,96,576]{2,1,0:T(8,128)(2,1)S(1)}, u32[]{:S(2)}, u32[]{:S(2)}) async-start(bf16[4,96,576]{2,1,0:T(8,128)(2,1)} %fusion.2), calls=%async_computation.7 | async-start | bytes 983040 | tf_op jit(solution)/shard_map/all_to_all | solution.py:395
  384.5 28.2 %collective-permute-start.56 = (bf16[96,768]{1,0:T(8,128)(2,1)}, bf16[96,768]{1,0:T(8,128)(2,1)S(1)}, u32[]{:S(2)}, u32[]{:S(2)}) collective-permute-start(bf16[96,768]{1,0:T(8,128)(2,1)} %get-tuple-element.400), channel_id=1, source_target_pairs={{0,4},{4,0},{8,12},{12,8},{16,20},{20,16},{24,28},{28,24},{1,5},{5... | collective-permute-start | bytes 442376 | tf_op jit(solution)/shard_map/ppermute | solution.py:42
  384.7 28.1 %collective-permute-start.57 = (bf16[96,768]{1,0:T(8,128)(2,1)}, bf16[96,768]{1,0:T(8,128)(2,1)}, u32[]{:S(2)}, u32[]{:S(2)}) collective-permute-start(bf16[96,768]{1,0:T(8,128)(2,1)} %get-tuple-element.399), channel_id=1, source_target_pairs={{0,6},{1,7},{2,4},{3,5},{4,2},{5,3},{6,0},{7,1},{8,14},{9,15},{10,... | collective-permute-start | bytes 442376 | tf_op jit(solution)/shard_map/ppermute | solution.py:390
  386.1 43.9 %collective-permute-start.46 = (bf16[512,768]{1,0:T(8,128)(2,1)S(1)}, bf16[512,768]{1,0:T(8,128)(2,1)S(1)}, u32[]{:S(2)}, u32[]{:S(2)}) collective-permute-start(bf16[512,768]{1,0:T(8,128)(2,1)S(1)} %copy-done), channel_id=1, source_target_pairs={{0,2},{2,0},{1,3},{3,1},{4,6},{6,4},{5,7},{7,5},{8,10},{10,8},{9,1... | collective-permute-start | bytes 2359304 | tf_op jit(solution)/shard_map/ppermute | solution.py:37
  390.7 4.6 %collective-permute-start.53 = (f32[23,768]{1,0:T(8,128)S(1)}, f32[23,768]{1,0:T(8,128)S(1)}, u32[]{:S(2)}, u32[]{:S(2)}) collective-permute-start(f32[23,768]{1,0:T(8,128)S(1)} %add.333), channel_id=1, source_target_pairs={{0,16},{4,20},{8,24},{12,28},{16,0},{20,4},{24,8},{28,12},{1,17},{... | collective-permute-start | bytes 211976 | tf_op jit(solution)/shard_map/ppermute | solution.py:42
  395.2 37.8 %collective-permute-start.45 = (bf16[512,768]{1,0:T(8,128)(2,1)}, bf16[512,768]{1,0:T(8,128)(2,1)}, u32[]{:S(2)}, u32[]{:S(2)}) collective-permute-start(bf16[512,768]{1,0:T(8,128)(2,1)} %get-tuple-element.275), channel_id=1, source_target_pairs={{0,1},{1,0},{2,3},{3,2},{4,5},{5,4},{6,7},{7,6},{8,9},{9,8},{10,11... | collective-permute-start | bytes 2359304 | tf_op jit(solution)/shard_map/ppermute | solution.py:33
  406.0 31.6 %all-to-all-start.5 = ((bf16[4,96,960]{2,1,0:T(8,128)(2,1)}), bf16[4,96,960]{2,1,0:T(8,128)(2,1)}, u32[]{:S(2)}, u32[]{:S(2)}) async-start(bf16[4,96,960]{2,1,0:T(8,128)(2,1)} %pad_maximum_fusion), calls=%async_computation.5 | async-start | bytes 1572864 | tf_op jit(solution)/shard_map/all_to_all | solution.py:395
  411.5 15.9 %collective-permute-start.54 = (f32[23,768]{1,0:T(8,128)S(1)}, f32[23,768]{1,0:T(8,128)S(1)}, u32[]{:S(2)}, u32[]{:S(2)}) collective-permute-start(f32[23,768]{1,0:T(8,128)S(1)} %add.334), channel_id=1, source_target_pairs={{0,8},{4,12},{8,0},{12,4},{16,24},{20,28},{24,16},{28,20},{1,9},{5... | collective-permute-start | bytes 211976 | tf_op jit(solution)/shard_map/ppermute | solution.py:42
  418.6 21.2 %collective-permute-start.47 = (bf16[8,64,768]{2,1,0:T(8,128)(2,1)S(1)}, bf16[8,64,768]{2,1,0:T(8,128)(2,1)S(1)}, u32[]{:S(2)}, u32[]{:S(2)}) collective-permute-start(bf16[8,64,768]{2,1,0:T(8,128)(2,1)S(1)} %bitcast.86), channel_id=1, source_target_pairs={{0,1},{1,0},{2,3},{3,2},{4,5},{5,4},{6,7},{7,6},{8,9},{9,8},{10,11... | collective-permute-start | bytes 2359304 | tf_op jit(solution)/shard_map/ppermute | solution.py:33
  430.0 9.7 %collective-permute-start.48 = (bf16[8,64,768]{2,1,0:T(8,128)(2,1)S(1)}, bf16[8,64,768]{2,1,0:T(8,128)(2,1)S(1)}, u32[]{:S(2)}, u32[]{:S(2)}) collective-permute-start(bf16[8,64,768]{2,1,0:T(8,128)(2,1)S(1)} %bitcast.88), channel_id=1, source_target_pairs={{0,1},{1,0},{2,3},{3,2},{4,5},{5,4},{6,7},{7,6},{8,9},{9,8},{10,11... | collective-permute-start | bytes 2359304 | tf_op jit(solution)/shard_map/ppermute | solution.py:33
  (79 other events, 591.0 us)
where the time goes:
time: 453 us; the launch traced here: 445 us
  Pallas kernels  169 us (37%)
  starting transfers between devices  102 us (23%)
  waiting for transfers between devices  93.5 us (21%)
  local copies, waits for them, and re-layouts  37.7 us (8%)
  other arithmetic  37.2 us (8%)
    pallas_call x13, Pallas kernels, call(): pl.pallas_call(kernel, out_shape=out_shape, in_specs=in_specs, out_specs=...  86.6 us
    all_to_all x8, starting transfers between devices, outer_exchange(): lax.all_to_all(value, 'dp', 0, 0, axis_index_groups=groups, tiled=True)  46.5 us
    ppermute x9, waiting for transfers between devices, swap_both(): return lax.ppermute(value, ('dp', 'tensor'), pairs)  41.5 us
    ppermute x24, starting transfers between devices, swap_core(): return lax.ppermute(value, 'tensor', CORE_SWAP)  26.2 us
    pallas_call x1, Pallas kernels, cross_first_backward(): pl.pallas_call(functools.partial(cross_first_kernel, start=start, count=c...  21.9 us
    unnamed x156, local copies, waits for them, and re-layouts  21.4 us
    pallas_call x2, Pallas kernels, self_backward(): pl.pallas_call(self_bwd_kernel, grid_spec=pltpu.PrefetchScalarGridSpec(nu...  20.4 us
    ppermute x13, waiting for transfers between devices, swap_x(): return lax.ppermute(value, 'tensor', X_SWAP)  20.3 us
  transfers between devices with their start and end apart: 66, of which 15 were waited for; matrix products, arithmetic and copies ran while one was open for 12% of the time, Pallas kernels for 26%

commit v1 on v0

--- a/solution.py
+++ b/solution.py
@@ -23,6 +23,7 @@
 CORE_SWAP = ((0, 1), (1, 0), (2, 3), (3, 2))
 X_SWAP = ((0, 2), (2, 0), (1, 3), (3, 1))
 VMEM_LIMIT = 48 << 20
+COST = pl.CostEstimate(flops=1000, bytes_accessed=1000, transcendentals=0)
 
 
 def mm(left, right, dims=NN):
@@ -146,9 +147,7 @@
         ],
         input_output_aliases={9 + i: i for i in range(len(former))},
         compiler_params=pltpu.CompilerParams(vmem_limit_bytes=VMEM_LIMIT),
-        cost_estimate=pl.CostEstimate(
-            flops=cells * HD * 10 * 4, transcendentals=cells, bytes_accessed=qkv.size * 2 * count
-        ),
+        cost_estimate=COST,
         name="self_bwd",
     )(info, qkv, qkv, qkv, mixed_own, mixed_oth, lse, grad_own, grad_oth, *former)
 
@@ -195,9 +194,7 @@
             jax.ShapeDtypeStruct((pairs, 2, rows), F32),
         ],
         compiler_params=pltpu.CompilerParams(vmem_limit_bytes=VMEM_LIMIT),
-        cost_estimate=pl.CostEstimate(
-            flops=cells * HD * 4 * 4, transcendentals=cells, bytes_accessed=queries.size * 12
-        ),
+        cost_estimate=COST,
         name="cross_fwd",
     )(queries, kv_own, kv_oth, kv_own, kv_oth)
 
@@ -252,9 +249,7 @@
         out_shape=[jax.ShapeDtypeStruct((rows, width), BF), both, both],
         input_output_aliases={8 + i: i for i in range(len(former))},
         compiler_params=pltpu.CompilerParams(vmem_limit_bytes=VMEM_LIMIT),
-        cost_estimate=pl.CostEstimate(
-            flops=cells * HD * 10 * 4, transcendentals=cells, bytes_accessed=rows * 128 * 24 * count
-        ),
+        cost_estimate=COST,
         name="cross_bwd",
     )(queries, kv_own, kv_oth, kv_own, kv_oth, mixed, lse, grad, *former)
 
@@ -363,10 +358,7 @@
         scratch_shapes=[pltpu.VMEM((rows, 128), BF)],
         input_output_aliases={14: 1, 15: 2},
         compiler_params=pltpu.CompilerParams(vmem_limit_bytes=VMEM_LIMIT),
-        cost_estimate=pl.CostEstimate(
-            flops=2 * rows * rows * count * 2 * HD * 40, transcendentals=0,
-            bytes_accessed=rows * 128 * 24 * count,
-        ),
+        cost_estimate=COST,
         name="cross_first",
     )(
         queries, kv_own, kv_oth, kv_own, kv_oth, mixed, lse, grad,
@@ -427,13 +419,31 @@
         out_specs=out_specs,
         scratch_shapes=list(scratch),
         compiler_params=pltpu.CompilerParams(vmem_limit_bytes=58 << 20),
-        cost_estimate=pl.CostEstimate(flops=flops, bytes_accessed=moved, transcendentals=0),
+        cost_estimate=COST,
         name=name,
     )(*args)
 
 
 def struct(shape, dtype):
     return jax.ShapeDtypeStruct(shape, dtype)
+
+
+def tail_start(depth):
+    return (depth + 15) // 16 * 16
+
+
+def high_low(row):
+    high = row.astype(BF).astype(F32)
+    return high, row - high
+
+
+def stack_rows(rows, count):
+    cols = rows[0].shape[1]
+    at = lax.broadcasted_iota(jnp.int32, (count, cols), 0)
+    total = jnp.zeros((count, cols), F32)
+    for i, row in enumerate(rows):
+        total = jnp.where(at == i, row, total)
+    return total.astype(BF)
 
 
 def pack_self_kernel(q_ref, k_ref, v_ref, out_ref):
@@ -459,7 +469,7 @@
     parts = [ref[...].astype(BF) for ref in (ck_ref, cv_ref, cq_ref)]
     parts += [turned(so_ref), turned(co_ref)]
     expand = ex_ref[...].astype(BF)
-    shrink = turned(sh_ref)
+    shrink = sh_ref[...].astype(BF)
     for copy in range(attn_ref.shape[0]):
         for i, low in enumerate(parts):
             attn_ref[copy, :, i * cols : (i + 1) * cols] = low
@@ -591,9 +601,7 @@
             struct((pairs, 2, 2, half), F32),
         ],
         compiler_params=pltpu.CompilerParams(vmem_limit_bytes=VMEM_LIMIT),
-        cost_estimate=pl.CostEstimate(
-            flops=2 * 2 * half * width * 3 * wide, bytes_accessed=own.size * 12, transcendentals=0
-        ),
+        cost_estimate=COST,
         name="self_fwd",
     )(info, own, oth, bias, *pieces)
 
@@ -686,12 +694,31 @@
     )
 
 
+def project_kv_kernel(keep_ref, got_ref, mat_ref, bias_ref, fet_ref, out_ref):
+    fet_ref[...] = keep_ref[...] + got_ref[...]
+    width = fet_ref.shape[1]
+    out_ref[:, :width] = mm(fet_ref[...], mat_ref[:, :width]).astype(BF)
+    out_ref[:, width:] = (mm(fet_ref[...], mat_ref[:, width:]) + bias_ref[...]).astype(BF)
+
+
+def project_kv(keep, got, mat, bias):
+    rows, width = keep.shape
+    return call(
+        project_kv_kernel,
+        [struct((rows, width), BF), struct((rows, 2 * width), BF)],
+        [keep, got, mat, bias],
+        [VM] * 4,
+        [VM] * 2,
+        name="project_kv",
+    )
+
+
 def feed_kernel(
     info, mixed_ref, first_ref, cot_ref, vec_ref, wo_hbm,
     e0, e1, e2, e3, e4, e5, e6, e7, s0, s1,
-    out_ref, second_ref, low_ref, grad_ref, sums_ref,
-    keep_e, keep_s, send_e, send_s,
-    wo, we, ws, hid, slo, out_a, out_b, norm2, h2low, e3low, acc, wsem, osem,
+    out_ref, second_ref, low_ref, grad_ref,
+    keep_ref, send_ref, sums_ref, tail,
+    wo, we, ws, hid, slo, out_a, out_b, norm2, h2low, e3low, acc, wsem, osem, tsem,
 ):
     first_copy = pltpu.make_async_copy(wo_hbm, wo, wsem.at[0])
     first_copy.start()
@@ -709,6 +736,8 @@
 
     width = first_ref.shape[1]
     hidden_cols = we.shape[-1]
+    outer, depth = we.shape[1], we.shape[3]
+    base = out_a.shape[3]
 
     def expand_mat(j):
         return we[j].reshape(width, hidden_cols)
@@ -751,20 +780,19 @@
     sums_ref[2:3, :] = jnp.sum(low.astype(F32), 0, keepdims=True)
     acc[...] = third
 
-    def out_copies(to_e, to_s, at, slot):
+    def out_copies(to, at, slot):
         copies = []
         for y in range(2):
-            rel = y ^ place
-            copies.append(
-                pltpu.make_async_copy(
-                    out_a.at[slot, :, y], to_e.at[at, rel], osem.at[0, slot, y]
+            for i, part in enumerate((out_a, out_b)):
+                copies.append(
+                    pltpu.make_async_copy(
+                        part.at[slot, :, y],
+                        to.at[
+                            at, y ^ place, :, :base, i * hidden_cols : (i + 1) * hidden_cols
+                        ],
+                        osem.at[i, slot, y],
+                    )
                 )
-            )
-            copies.append(
-                pltpu.make_async_copy(
-                    out_b.at[slot, :, y], to_s.at[:, at, rel], osem.at[1, slot, y]
-                )
-            )
         return copies
 
     def backward(step, carry):
@@ -772,27 +800,27 @@
         slot = step % 2
         slope = slo[j].astype(F32)
         inner_grad = (mm(e3low[...], shrink_mat(j)) * slope).astype(BF)
-        true_block = info[1] ^ (2 * (j % 2) + j // 2)
-        sums_ref[pl.ds(8 + true_block, 1), :] = jnp.sum(
+        sums_ref[pl.ds(8 + j, 1), :] = jnp.sum(
             inner_grad.astype(F32), 0, keepdims=True
         )
 
         @pl.when(step >= 2)
         def _():
-            for copy in out_copies(send_e, send_s, slot, slot):
+            for copy in out_copies(send_ref, slot, slot):
                 copy.wait()
 
-        out_a[slot] = mm(h2low[...], inner_grad, TN).astype(BF).reshape(out_a.shape[1:])
-        out_b[slot] = mm(e3low[...], hid[j], TN).astype(BF).reshape(out_b.shape[1:])
+        shape = (outer, 2, depth, hidden_cols)
+        out_a[slot, :, :, :depth] = mm(h2low[...], inner_grad, TN).astype(BF).reshape(shape)
+        out_b[slot, :, :, :depth] = mm(e3low[...], hid[j], TN).astype(BF).reshape(shape)
 
         @pl.when(step < 2)
         def _():
-            for copy in out_copies(send_e, send_s, slot, slot):
+            for copy in out_copies(send_ref, slot, slot):
                 copy.start()
 
         @pl.when(step >= 2)
         def _():
-            for copy in out_copies(keep_e, keep_s, slot, slot):
+            for copy in out_copies(keep_ref, slot, slot):
                 copy.start()
 
         acc[...] += mm(inner_grad, expand_mat(j), NT)
@@ -808,19 +836,34 @@
     low = second_in.astype(BF)
     low_ref[...] = low
     sums_ref[5:6, :] = jnp.sum(low.astype(F32), 0, keepdims=True)
-    sums_ref[6:8, :] = jnp.zeros((2, sums_ref.shape[1]), F32)
-    sums_ref[12:16, :] = jnp.zeros((4, sums_ref.shape[1]), F32)
+    tails = []
+    pairs = [high_low(sums_ref[i : i + 1, :]) for i in range(6)]
+    for j in range(4):
+        rows_e = list(high_low(sums_ref[8 + j : 9 + j, :])) + [r for p in pairs[:3] for r in p]
+        rows_s = [r for p in pairs[3:] for r in p]
+        for o in range(outer):
+            tail[j, o, :, :hidden_cols] = stack_rows(rows_e, 8)
+            tail[j, o, :, hidden_cols:] = stack_rows(rows_s, 8)
+        for y in range(2):
+            to = (keep_ref, send_ref)[j // 2]
+            tails.append(
+                pltpu.make_async_copy(tail.at[j], to.at[j % 2, y, :, base:, :], tsem.at[2 * j + y])
+            )
+    for copy in tails:
+        copy.start()
     grad_ref[...] = mm(low, wo[...]).astype(BF)
     for slot in range(2):
-        for copy in out_copies(keep_e, keep_s, slot, slot):
+        for copy in out_copies(keep_ref, slot, slot):
             copy.wait()
+    for copy in tails:
+        copy.wait()
 
 
 def feed(info, mixed, first, cot, vecs, wo, expand, shrink):
     rows, width = mixed.shape
     outer, depth, hidden = expand[0].shape
-    grad_e = struct((2, 2, outer, depth, hidden), BF)
-    grad_s = struct((outer, 2, 2, depth, hidden), BF)
+    base = tail_start(depth)
+    grads = struct((2, 2, outer, base + 8, 2 * hidden), BF)
     return call(
         feed_kernel,
         [
@@ -828,29 +871,29 @@
             struct((rows, width), F32),
             struct((rows, width), BF),
             struct((rows, width), BF),
-            struct((16, width), F32),
-            grad_e,
-            grad_s,
-            grad_e,
-            grad_s,
+            grads,
+            grads,
         ],
         [info, mixed, first, cot, vecs, wo] + list(expand) + list(shrink),
         [SM, VM, VM, VM, VM] + [ANY] * 11,
-        [VM] * 5 + [ANY] * 4,
+        [VM] * 4 + [ANY] * 2,
         [
+            pltpu.VMEM((16, width), F32),
+            pltpu.VMEM((4, outer, 8, 2 * hidden), BF),
             pltpu.VMEM((width, width), BF),
             pltpu.VMEM((4, outer, 2, depth, hidden), BF),
             pltpu.VMEM((4, outer, 2, depth, hidden), BF),
             pltpu.VMEM((4, rows, hidden), BF),
             pltpu.VMEM((4, rows, hidden), BF),
-            pltpu.VMEM((2, outer, 2, depth, hidden), BF),
-            pltpu.VMEM((2, outer, 2, depth, hidden), BF),
+            pltpu.VMEM((2, outer, 2, base, hidden), BF),
+            pltpu.VMEM((2, outer, 2, base, hidden), BF),
             pltpu.VMEM((rows, width), F32),
             pltpu.VMEM((rows, width), BF),
             pltpu.VMEM((rows, width), BF),
             pltpu.VMEM((rows, width), F32),
             pltpu.SemaphoreType.DMA((13,)),
             pltpu.SemaphoreType.DMA((2, 2, 2)),
+            pltpu.SemaphoreType.DMA((8,)),
         ],
         flops=2 * rows * width * (6 * 4 * hidden + 2 * width) * 2,
         moved=width * hidden * 4 * 4 * 2,
@@ -900,11 +943,12 @@
 
 
 def put_rows(ref, x, full, at, place):
-    outer, depth = ref.shape[2], ref.shape[3]
+    outer = ref.shape[2]
+    depth = full.shape[0] // outer // 2
     for o in range(outer):
         for y in range(2):
             start = (2 * o + y) * depth
-            ref[x, y ^ place, o, :, at] = full[start : start + depth]
+            ref[x, y ^ place, o, :depth, at] = full[start : start + depth]
 
 
 def put_blocks(keep_ref, send_ref, full, i, place):
@@ -915,15 +959,33 @@
 
 
 def query_grads_kernel(
-    info, h1_ref, dq_ref, e1_ref, o1_ref, e2_ref, o2_ref, keep_ref, send_ref
+    info, h1_ref, dq_ref, e1_ref, o1_ref, e2_ref, o2_ref, sums_ref, keep_ref, send_ref
 ):
+    width = dq_ref.shape[1]
+    piece = width // 4
+    outer, rows = keep_ref.shape[2], keep_ref.shape[3]
+    parts = [high_low(sums_ref[i : i + 1, :]) for i in range(4)]
+    for j in range(4):
+        own = slice(j * piece, (j + 1) * piece)
+        ref = (keep_ref, send_ref)[j // 2]
+        for i in range(3):
+            lines = [parts[i][0][:, p * piece : (p + 1) * piece] for p in range(4)]
+            lines += [parts[i][1][:, p * piece : (p + 1) * piece] for p in range(4)]
+            if i == 0:
+                lines += [parts[3][0][:, own], parts[3][1][:, own]]
+            block = stack_rows(lines, 16)
+            for o in range(outer):
+                for y in range(2):
+                    ref[j % 2, y, o, rows - 16 :, i * piece : (i + 1) * piece] = block
     for i, (left, right) in enumerate(((h1_ref, dq_ref), (e1_ref, o1_ref), (e2_ref, o2_ref))):
         full = mm(left[...], right[...], TN).astype(BF)
         put_blocks(keep_ref, send_ref, full, i, info[0])
 
 
-def key_grads_kernel(info, fet_ref, own_ref, got_ref, mat_ref, keep_ref, send_ref, grad_ref, sum_ref):
+def key_grads_kernel(info, fet_ref, own_ref, got_ref, mat_ref, keep_ref, send_ref, grad_ref):
     width = fet_ref.shape[1]
+    piece = width // 4
+    outer, rows = keep_ref.shape[2], keep_ref.shape[3]
     total = None
     for i in range(2):
         low = add_low(own_ref[i], got_ref[i])
@@ -932,19 +994,26 @@
         term = mm(low, mat_ref[:, i * width : (i + 1) * width], NT)
         total = term if total is None else total + term
         if i == 1:
-            sum_ref[0:1, :] = jnp.sum(low.astype(F32), 0, keepdims=True)
-            sum_ref[1:8, :] = jnp.zeros((7, width), F32)
+            sums = high_low(jnp.sum(low.astype(F32), 0, keepdims=True))
+            for j in range(4):
+                own = slice(j * piece, (j + 1) * piece)
+                block = stack_rows([sums[0][:, own], sums[1][:, own]], 8)
+                ref = (keep_ref, send_ref)[j // 2]
+                for o in range(outer):
+                    for y in range(2):
+                        ref[j % 2, y, o, rows - 8 :, piece:] = block
+                        ref[j % 2, y, o, rows - 8 :, :piece] = jnp.zeros_like(block)
     grad_ref[...] = total.astype(BF)
 
 
 def query_grads(info, args, depth):
     width = args[0].shape[1]
-    out = struct((2, 2, width // depth // 2, depth, 3 * width // 4), BF)
+    out = struct((2, 2, width // depth // 2, tail_start(depth) + 16, 3 * width // 4), BF)
     return call(
         query_grads_kernel,
         [out, out],
         [info] + list(args),
-        [SM] + [VM] * 6,
+        [SM] + [VM] * 7,
         [VM] * 2,
         flops=2 * 512 * width * width * 3,
         moved=width * width * 10,
@@ -954,13 +1023,13 @@
 
 def key_grads(info, fetched, own, got, mat, depth):
     rows, width = fetched.shape
-    out = struct((2, 2, width // depth // 2, depth, 2 * width // 4), BF)
+    out = struct((2, 2, width // depth // 2, tail_start(depth) + 8, 2 * width // 4), BF)
     return call(
         key_grads_kernel,
-        [out, out, struct((rows, width), BF), struct((8, width), F32)],
+        [out, out, struct((rows, width), BF)],
         [info, fetched, own, got, mat],
         [SM] + [VM] * 4,
-        [VM] * 4,
+        [VM] * 3,
         flops=2 * rows * width * width * 4,
         moved=width * width * 10,
         name="key_grads",
@@ -971,32 +1040,39 @@
     place = info[0]
     cols = d_ref.shape[3]
     piece = cols // 2
-    outer, depth = a_ref.shape[0], a_ref.shape[1]
+    outer, base = a_ref.shape[0], a_ref.shape[1] - 8
+    depth = own_ref.shape[1] // outer // 2
     for i in range(3):
         full = mm(own_ref[...], d_ref[i, 0], TN) + mm(oth_ref[...], d_ref[i, 1], TN)
         full = full.astype(BF)
         at = slice(i * piece, (i + 1) * piece)
+        both = d_ref[i, 0].astype(F32) + d_ref[i, 1].astype(F32)
+        sums = jnp.sum(both, 0, keepdims=True)
+        high = sums.astype(BF).astype(F32)
+        row = lax.broadcasted_iota(jnp.int32, (8, cols), 0)
+        tail = jnp.where(row == 0, high, jnp.where(row == 1, sums - high, 0.0)).astype(BF)
         for x, (near, away) in enumerate(((a_ref, y_ref), (x_ref, xy_ref))):
+            part = slice(x * piece, (x + 1) * piece)
             for o in range(outer):
                 start = 2 * o * depth
-                first = full[start : start + depth, x * piece : (x + 1) * piece]
-                second = full[start + depth : start + 2 * depth, x * piece : (x + 1) * piece]
-                near[o, :, at] = jnp.where(place == 0, first, second)
-                away[o, :, at] = jnp.where(place == 0, second, first)
+                first = full[start : start + depth, part]
+                second = full[start + depth : start + 2 * depth, part]
+                near[o, :depth, at] = jnp.where(place == 0, first, second)
+                away[o, :depth, at] = jnp.where(place == 0, second, first)
+                near[o, base:, at] = tail[:, part]
+                away[o, base:, at] = tail[:, part]
 
 
 def self_grads(info, own, oth, grads, depth):
     half, width = own.shape
     cols = grads.shape[3]
-    out = struct((width // depth // 2, depth, 3 * cols // 2), BF)
+    out = struct((width // depth // 2, tail_start(depth) + 8, 3 * cols // 2), BF)
     return call(
         self_grads_kernel,
         [out] * 4,
         [info, own, oth, grads],
         [SM] + [VM] * 3,
         [VM] * 4,
-        flops=2 * 2 * half * width * 3 * cols * 2,
-        moved=half * width * 4 + half * cols * 12 + width * cols * 6,
         name="self_grads",
     )
 
@@ -1120,9 +1196,7 @@
         ),
         out_shape=struct((count, blk, width), F32),
         compiler_params=pltpu.CompilerParams(vmem_limit_bytes=VMEM_LIMIT),
-        cost_estimate=pl.CostEstimate(
-            flops=0, bytes_accessed=count * blk * width * 6, transcendentals=0
-        ),
+        cost_estimate=COST,
         name="scatter",
     )(table, *parts)
 
@@ -1134,42 +1208,82 @@
     return total
 
 
-def sum_query_kernel(in_ref, q_ref, so_ref, co_ref):
+def sum_query_kernel(in_ref, q_ref, so_ref, co_ref, qb_ref, v0_ref, v1_ref, v2_ref):
     total = sum_all(in_ref)
     piece = total.shape[1] // 3
-    q_ref[...] = total[:, :piece]
-    so_ref[...] = total[:, piece : 2 * piece].T
-    co_ref[...] = total[:, 2 * piece :].T
-
-
-def sum_query(value):
-    count, depth, cols = value.shape
+    depth = q_ref.shape[0]
+    q_ref[...] = total[:depth, :piece]
+    so_ref[...] = total[:depth, piece : 2 * piece].T
+    co_ref[...] = total[:depth, 2 * piece :].T
+    tail = total[total.shape[0] - 16 :]
+    qb_ref[...] = (tail[8:9, :piece] + tail[9:10, :piece])[0]
+    for i, ref in enumerate((v0_ref, v1_ref, v2_ref)):
+        cols = slice(i * piece, (i + 1) * piece)
+        parts = [tail[p : p + 1, cols] + tail[p + 4 : p + 5, cols] for p in range(4)]
+        ref[...] = jnp.concatenate(parts, axis=1)[0]
+
+
+def sum_query(value, depth):
+    count, rows, cols = value.shape
     piece = cols // 3
+    wide, tall = struct((depth, piece), F32), struct((piece, depth), F32)
+    vec = struct((4 * piece,), F32)
     return call(
         sum_query_kernel,
-        [struct((depth, piece), F32)] + [struct((piece, depth), F32)] * 2,
+        [wide, tall, tall, struct((piece,), F32), vec, vec, vec],
         [value],
         [VM],
-        [VM] * 3,
-        moved=value.size * 2 + depth * cols * 4,
+        [VM] * 7,
         name="sum_query",
     )
 
 
-def sum_turned_kernel(in_ref, out_ref):
-    out_ref[...] = sum_all(in_ref).T
-
-
-def sum_turned(value):
-    count, depth, cols = value.shape
+def sum_cols_kernel(in_ref, *refs):
+    count = len(refs) // 2
+    total = sum_all(in_ref)
+    depth, piece = refs[0].shape
+    tail = total[total.shape[0] - 8 :]
+    for i in range(count):
+        cols = slice(i * piece, (i + 1) * piece)
+        refs[i][...] = total[:depth, cols]
+        refs[count + i][...] = (tail[0:1, cols] + tail[1:2, cols])[0]
+
+
+def sum_cols(value, depth, count):
+    piece = value.shape[2] // count
     return call(
-        sum_turned_kernel,
-        struct((cols, depth), F32),
+        sum_cols_kernel,
+        [struct((depth, piece), F32)] * count + [struct((piece,), F32)] * count,
         [value],
         [VM],
-        VM,
-        moved=value.size * 2 + depth * cols * 4,
-        name="sum_turned",
+        [VM] * (2 * count),
+        name="sum_cols",
+    )
+
+
+def sum_feed_kernel(in_ref, e_ref, s_ref, eb_ref, *vecs):
+    total = sum_all(in_ref)
+    depth, cols = e_ref.shape
+    e_ref[...] = total[:depth, :cols]
+    s_ref[...] = total[:depth, cols:]
+    tail = total[total.shape[0] - 8 :]
+    eb_ref[...] = (tail[0:1, :cols] + tail[1:2, :cols])[0]
+    for i in range(3):
+        at = 2 + 2 * i
+        vecs[i][...] = (tail[at : at + 1, :cols] + tail[at + 1 : at + 2, :cols])[0]
+        at = 2 * i
+        vecs[3 + i][...] = (tail[at : at + 1, cols:] + tail[at + 1 : at + 2, cols:])[0]
+
+
+def sum_feed(value, depth):
+    cols = value.shape[2] // 2
+    return call(
+        sum_feed_kernel,
+        [struct((depth, cols), F32)] * 2 + [struct((cols,), F32)] * 7,
+        [value],
+        [VM],
+        [VM] * 9,
+        name="sum_feed",
     )
 
 
@@ -1220,15 +1334,23 @@
     attn_cols = 5 * head_cols
     info = jnp.stack([inner, rank, chip]).astype(jnp.int32)
 
+    seq_order = jnp.stack([chip, 1 - chip])
+    near = blocks[seq_order].reshape(2, 2, slots)
+    near = jnp.stack([near[:, core], near[:, 1 - core]])
+    near = near - rank * local_blocks
+    held = (near >= 0) & (near < local_blocks)
+    fetch_table = jnp.where(held, near + seq_order[None, :, None] * local_blocks, -1)
+    fetch_table = fetch_table.reshape(-1).astype(jnp.int32)
+    part_mine, part_send = fetch(fetch_table, bank.reshape(seq_count * local_blocks, BLK, width))
+
     self_leaf = call(
         pack_self_kernel,
         struct((outer, depth, 3 * head_cols), BF),
-        [selfq_weight, selfk_weight, selfv_weight],
+        [gate(selfq_weight, part_send), selfk_weight, selfv_weight],
         [VM] * 3,
         VM,
         name="pack_self",
     )
-    self_z = outer_exchange(self_leaf)
     bias_own = jnp.concatenate(
         [selfq_bias, selfv_bias, crossq_bias, crossv_bias, expand_bias]
     ).reshape(1, -1)
@@ -1253,41 +1375,52 @@
         ],
         [
             gate(crossk_weight, self_leaf), crossv_weight, crossq_weight, selfo_weight,
-            crosso_weight, expand_weight, shrink_weight,
+            crosso_weight, expand_weight, shrink_weight.T,
         ],
         [VM] * 7,
         [VM] * 3,
         name="pack_rest",
     )
+    tokens_oth = swap_core(tokens)
+    vecs = jnp.concatenate(
+        [
+            jnp.stack([crosso_bias, second_gain, second_shift]),
+            ex_bias,
+            jnp.stack([shrink_bias, third_gain, third_shift]),
+        ]
+    )
+    first_vecs = jnp.stack([selfo_bias, first_gain, first_shift])
+    cq_bias, cv_bias = cq_bias.reshape(1, -1), cv_bias.reshape(1, -1)
+    my_prefix = lax.dynamic_index_in_dim(prefix, chip, 0, keepdims=False)
+    attn_info = jnp.stack([core, my_prefix]).astype(jnp.int32)
+
+    part_got = swap_core(part_send)
+    self_leaf, attn_leaf = lax.optimization_barrier((self_leaf, attn_leaf))
+    self_z = outer_exchange(self_leaf)
+    shrink_leaf = gate(shrink_leaf, bias_two)
     shrink_x, shrink_y = swap_x(shrink_leaf), swap_dp(shrink_leaf, 1)
     shrink_xy = swap_both(shrink_leaf)
-    tokens_oth = swap_core(tokens)
     shrink_pack = plane_copies(info, shrink_leaf, shrink_x, shrink_y, shrink_xy)
 
-    self_z, shrink_pack, self_bias = lax.optimization_barrier((self_z, shrink_pack, self_bias))
+    (
+        self_z, self_bias, vecs, first_vecs, cq_bias, cv_bias, attn_leaf, attn_info,
+        part_got, tokens_oth, shrink_pack,
+    ) = lax.optimization_barrier(
+        (
+            self_z, self_bias, vecs, first_vecs, cq_bias, cv_bias, attn_leaf, attn_info,
+            part_got, tokens_oth, shrink_pack,
+        )
+    )
     self_near, self_away, self_both = swap_x(self_z), swap_dp(self_z, 1), swap_both(self_z)
-    attn_z = outer_exchange(gate(attn_leaf, self_z))
-
-    seq_order = jnp.stack([chip, 1 - chip])
-    near = blocks[seq_order].reshape(2, 2, slots)
-    near = jnp.stack([near[:, core], near[:, 1 - core]])
-    near = near - rank * local_blocks
-    held = (near >= 0) & (near < local_blocks)
-    fetch_table = jnp.where(held, near + seq_order[None, :, None] * local_blocks, -1)
-    fetch_table = gate(fetch_table.reshape(-1).astype(jnp.int32), self_z)
-    part_mine, part_send = fetch(fetch_table, bank.reshape(seq_count * local_blocks, BLK, width))
-    part_got = swap_core(part_send)
-    part_keep = part_mine[0] + part_got[0]
-    part_away = part_mine[1] + part_got[1]
-    attn_z, tokens_in, self_near, self_away, self_both, part_away = lax.optimization_barrier(
-        (attn_z, tokens, self_near, self_away, self_both, part_away)
+    attn_z = outer_exchange(attn_leaf)
+    part_got, self_near = lax.optimization_barrier((part_got, self_near))
+    part_back = swap_x(part_mine[1] + part_got[1])
+    attn_z, tokens_in, self_near, self_away, self_both = lax.optimization_barrier(
+        (attn_z, tokens, self_near, self_away, self_both)
     )
     attn_x, attn_y, attn_xy = swap_x(attn_z), swap_dp(attn_z, 1), swap_both(attn_z)
-    part_back = swap_x(part_away)
     expand_z = outer_exchange(gate(expand_leaf, attn_z))
 
-    my_prefix = lax.dynamic_index_in_dim(prefix, chip, 0, keepdims=False)
-    attn_info = jnp.stack([core, my_prefix]).astype(jnp.int32)
     qkv, self_mat, self_own, self_send, self_lse = self_forward(
         jnp.concatenate([info, attn_info]),
         tokens_in,
@@ -1296,46 +1429,43 @@
         (self_z, self_near, self_away, self_both),
     )
     self_got = swap_core(self_send)
-    part_back, attn_x, attn_y, attn_xy, expand_z = lax.optimization_barrier(
-        (part_back, attn_x, attn_y, attn_xy, expand_z, self_own)
-    )[:5]
-    shrink_z = outer_exchange(gate(shrink_pack, expand_z))
-    fetched = (part_keep + part_back).reshape(slots * BLK, width)
+    attn_x, attn_y, shrink_pack = lax.optimization_barrier((attn_x, attn_y, shrink_pack, self_own))[:3]
+    shrink_pack, expand_z = lax.optimization_barrier((shrink_pack, expand_z))
+    shrink_z = outer_exchange(shrink_pack)
     expand_x, expand_y, expand_xy = swap_x(expand_z), swap_dp(expand_z, 1), swap_both(expand_z)
 
     attn_own = (attn_z, attn_y, attn_x, attn_xy)
     attn_oth = tuple(swap_core(piece) for piece in attn_own)
     cross_kv, cross_q, self_o, cross_o = assemble(info, attn_own + attn_oth)
+    fetched, kv_own = project_kv(
+        (part_mine[0] + part_got[0]).reshape(slots * BLK, width),
+        part_back.reshape(slots * BLK, width),
+        cross_kv,
+        cv_bias,
+    )
+    self_got, kv_own = lax.optimization_barrier((self_got, kv_own))
+    kv_oth = swap_core(kv_own)
     first_sum, first_out, first_low, queries, mixed_one = first_forward(
         tokens,
         self_own,
         self_got,
         self_o,
-        jnp.stack([selfo_bias, first_gain, first_shift]),
+        first_vecs,
         cross_q,
-        cq_bias.reshape(1, -1),
-    )
-
-    kv_bias = jnp.concatenate([jnp.zeros_like(cv_bias), cv_bias])
-    kv_own = (mm(fetched, cross_kv) + kv_bias).astype(BF)
-    kv_oth = swap_core(kv_own)
-    queries, expand_x, expand_y, expand_xy, shrink_z = lax.optimization_barrier(
-        (queries, expand_x, expand_y, expand_xy, shrink_z)
+        cq_bias,
+    )
+
+    queries, kv_oth = lax.optimization_barrier((queries, kv_oth))
+    queries, expand_x, expand_y, shrink_z = lax.optimization_barrier(
+        (queries, expand_x, expand_y, shrink_z)
     )
     mixed_two, cross_lse = cross_forward(queries, kv_own, kv_oth)
 
     expand_own = (expand_z, expand_y, expand_x, expand_xy)
     expand_oth = tuple(swap_core(piece) for piece in expand_own)
-    vecs = jnp.concatenate(
-        [
-            jnp.stack([crosso_bias, second_gain, second_shift]),
-            ex_bias,
-            jnp.stack([shrink_bias, third_gain, third_shift]),
-        ]
-    )
     (
-        out_act, second_in, cross_low, cross_grad, late_vec,
-        expand_keep, shrink_keep, expand_send, shrink_send,
+        out_act, second_in, cross_low, cross_grad,
+        feed_keep, feed_send,
     ) = feed(
         info, mixed_two, first_out, out_grad, vecs, cross_o,
         expand_own + expand_oth, (shrink_z, swap_core(shrink_z)),
@@ -1354,38 +1484,54 @@
     def fold(value, dtype):
         return jnp.sum(value.astype(F32), axis=0).astype(dtype)
 
-    shrink_got = swap_core(shrink_send)
-    expand_got = swap_core(expand_send)
+    feed_got = swap_core(feed_send)
     part_one = cross_backward(queries, kv_own, kv_oth, mixed_two, cross_lse, cross_grad, 0, 2)
-    shrink_places, expand_plane, part_one = lax.optimization_barrier(
-        (
-            add_low(gate(shrink_keep, part_one[0]), shrink_got),
-            plane_send(gate(expand_keep, part_one[0]), expand_got),
-            tuple(part_one),
-        )
-    )
-    expand_parts = plane_swap(expand_plane)
-    shrink_parts = outer_exchange(shrink_places)
+    feed_keep = gate(feed_keep, part_one[0])
+
+    def feed_sum(x, y, which, *others):
+        at = (x, y, Ellipsis, slice(which * hidden_cols, (which + 1) * hidden_cols))
+        total = feed_keep[at].astype(F32) + feed_got[at].astype(F32)
+        for other in others:
+            total = total + other.astype(F32)
+        return total.astype(BF)
+
+    expand_send = feed_sum(1, slice(None), 0)
+    shrink_send = feed_sum(slice(None), 1, 1)
+    expand_send, shrink_send, part_one = lax.optimization_barrier(
+        (expand_send, shrink_send, tuple(part_one))
+    )
+    expand_got = swap_x(expand_send)
+    shrink_got = swap_dp(shrink_send, 1)
 
     dq, dkv_own, dkv_send, first_in, self_low, grad_own, grad_send, early_vec = cross_first_backward(
         queries, kv_own, kv_oth, mixed_two, cross_lse, cross_grad, 2, part_one,
         cross_q, second_in, first_sum, first_gain.reshape(1, -1), self_o,
     )
+    expand_got, shrink_got, dkv_send, grad_send = lax.optimization_barrier(
+        (expand_got, shrink_got, dkv_send, grad_send)
+    )
     dkv_got = swap_core(dkv_send)
     grad_got = swap_core(grad_send)
-    self_low, expand_parts = lax.optimization_barrier((self_low, expand_parts))
-    expand_three = plane_sum((expand_keep[0, 0], expand_got[0, 0]), expand_parts).astype(BF)
+    expand_send = feed_sum(0, 1, 0, expand_got[1])
+    shrink_send = feed_sum(1, 0, 1, shrink_got[1])
+    self_low, dkv_got, grad_got, expand_send, shrink_send = lax.optimization_barrier(
+        (self_low, dkv_got, grad_got, expand_send, shrink_send)
+    )
+    expand_last = swap_dp(expand_send, 1)
+    shrink_last = swap_x(shrink_send)
     query_keep, query_send = query_grads(
-        info, (first_low, dq, self_low, mixed_one, cross_low, mixed_two), depth
+        info, (first_low, dq, self_low, mixed_one, cross_low, mixed_two, early_vec), depth
     )
     dkv_own, query_send = lax.optimization_barrier((dkv_own, query_send))
     query_got = swap_core(query_send)
-    key_keep, key_send, fetched_grad, cv_rows = key_grads(
+    key_keep, key_send, fetched_grad = key_grads(
         info, fetched, dkv_own, dkv_got, cross_kv, depth
     )
-    query_plane = plane_send(gate(query_keep, cv_rows), query_got)
-    query_plane, key_send, grad_got, fetched_grad = lax.optimization_barrier(
-        (query_plane, key_send, grad_got, fetched_grad)
+    query_plane = plane_send(gate(query_keep, fetched_grad), query_got)
+    query_plane, key_send, grad_got, fetched_grad, expand_last, shrink_last = (
+        lax.optimization_barrier(
+            (query_plane, key_send, grad_got, fetched_grad, expand_last, shrink_last)
+        )
     )
     query_parts = plane_swap(query_plane)
     key_got = swap_core(key_send)
@@ -1394,60 +1540,52 @@
     pairs = two // 128
     half_grads = self_backward(*self_args, 0, pairs - 1)
     key_plane = plane_send(gate(key_keep, half_grads[1]), key_got)
-    key_plane, half_grads, query_parts, shrink_parts, expand_three, fetched_send = (
-        lax.optimization_barrier(
-            (key_plane, tuple(half_grads), query_parts, shrink_parts, expand_three, fetched_grad)
-        )
+    feed_three = jnp.concatenate(
+        [
+            feed_sum(0, 0, 0, expand_got[0], gate(expand_last, half_grads[1])),
+            feed_sum(0, 0, 1, shrink_got[0], gate(shrink_last, half_grads[1])),
+        ],
+        axis=-1,
+    )
+    query_three = plane_sum((query_keep[0, 0], query_got[0, 0]), query_parts).astype(BF)
+    key_plane, half_grads, feed_three, query_three = lax.optimization_barrier(
+        (key_plane, tuple(half_grads), feed_three, query_three)
     )
     key_parts = plane_swap(key_plane)
-    expand_last = outer_exchange(expand_three)
-    shrink_three = fold(shrink_parts, BF)
-    query_three = plane_sum((query_keep[0, 0], query_got[0, 0]), query_parts).astype(BF)
-    grads, self_sums = self_backward(*self_args, pairs - 1, 1, half_grads)
-
-    order = jnp.arange(4) ^ rank
-    order = 2 * (order % 2) + order // 2
-
-    def straight(vecs):
-        return vecs.reshape(vecs.shape[0], 4, -1)[:, order].reshape(vecs.shape[0], -1)
-
-    self_sums = self_sums[:, :3].transpose(1, 0, 2).reshape(3, two)
-    self_sums = jnp.concatenate([self_sums, jnp.zeros_like(self_sums)], axis=1)
-    turned_vecs = jnp.concatenate([early_vec[3:4], cv_rows[:1], self_sums[0:1], self_sums[2:3]])
-    sums = jnp.concatenate([late_vec, early_vec[:3], straight(turned_vecs)])
-    sums = sums + swap_core(sums)
-    sums, grads, shrink_three = lax.optimization_barrier((sums, grads, shrink_three))
-    sums_got = swap_x(sums)
-    shrink_near = (
-        swap_x(shrink_three[1, 0]), swap_dp(shrink_three[0, 1], 1), swap_both(shrink_three[1, 1])
-    )
+    feed_last = outer_exchange(feed_three)
+    grads, self_rows = self_backward(*self_args, pairs - 1, 1, half_grads)
+    grads, key_parts = lax.optimization_barrier((grads, key_parts))
     self_places = self_grads(info, tokens, tokens_oth, grads, depth)
-    sums, self_places, grads, key_parts = lax.optimization_barrier(
-        (sums + sums_got, tuple(self_places), grads, key_parts)
-    )
-    bits = dp_bits()
-    sums_got = swap_dp(sums, bits[-1])
+    self_places, grads = lax.optimization_barrier((tuple(self_places), grads))
     self_parts = (swap_x(self_places[1]), swap_dp(self_places[2], 1), swap_both(self_places[3]))
+    grads, feed_last, query_three = lax.optimization_barrier((grads, feed_last, query_three))
+    query_last = outer_exchange(query_three)
+    back_keep, back_send = self_back(grads, self_mat, first_in)
+    back_send, query_last, key_parts, self_near, self_away = lax.optimization_barrier(
+        (back_send, query_last, key_parts, self_parts[0], self_parts[1])
+    )
     key_three = plane_sum((key_keep[0, 0], key_got[0, 0]), key_parts).astype(BF)
-    query_last = outer_exchange(gate(query_three, expand_last))
-    back_keep, back_send = self_back(grads, self_mat, first_in)
-    sums = sums + gate(sums_got, back_send)
-    for bit in bits[:-1]:
-        sums = sums + swap_dp(sums, bit)
-    fetched_send = gate(fetched_send, back_send)
+    back_got = swap_core(back_send)
+    self_three = plane_sum((self_places[0],), (self_near, self_away, self_parts[2])).astype(BF)
+    self_last = outer_exchange(
+        gate(jnp.concatenate([self_three, key_three], axis=-1), query_last)
+    )
+    fetched_send = gate(fetched_grad, self_three)
     fetched_away = swap_x(fetched_send).reshape(slots, BLK, width)
     fetched_near = fetched_send.reshape(slots, BLK, width)
-    self_three = plane_sum((self_places[0],), gate(self_parts, back_send)).astype(BF)
-    self_last = outer_exchange(jnp.concatenate([self_three, key_three], axis=-1))
-    in_grad = (back_keep + swap_core(back_send).astype(F32)).astype(BF)
-    shrink_last = jnp.stack((shrink_three[0, 0],) + shrink_near)
-
-    cq_grad, so_grad, co_grad = sum_query(query_last)
-    self_total = fold(self_last, F32)
-    ck_grad = self_total[:, 3 * head_cols : 4 * head_cols]
-    cv_grad = self_total[:, 4 * head_cols :]
-    expand_grad = fold(expand_last, F32)
-    shrink_grad = sum_turned(shrink_last)
+    in_grad = (back_keep + back_got.astype(F32)).astype(BF)
+
+    cq_grad, so_grad, co_grad, cq_rows, first_shift_rows, first_gain_rows, so_rows = sum_query(
+        query_last, depth
+    )
+    (
+        sq_grad, sk_grad, sv_grad, ck_grad, cv_grad, sq_rows, sk_rows, sv_rows, ck_rows, cv_rows,
+    ) = sum_cols(self_last, depth, 5)
+    (
+        expand_grad, shrink_grad, expand_rows, third_shift_rows, third_gain_rows, shrink_rows,
+        second_shift_rows, second_gain_rows, co_rows,
+    ) = sum_feed(feed_last, depth)
+    shrink_grad = shrink_grad.T
 
     near_core = swap_core(fetched_near)
     away_core = swap_core(fetched_away)
@@ -1464,42 +1602,37 @@
         (fetched_near, fetched_away, near_core, away_core),
     ).reshape(bank.shape)
 
-    late_vec, early_vec = sums[:16], sums[16:]
-
-    def own_part(vec, part_len):
-        return lax.dynamic_slice_in_dim(vec, rank * part_len, part_len, 0)
-
-    def self_part(which):
-        return self_total[:, which * head_cols : (which + 1) * head_cols]
+    def line(row):
+        return row.reshape(-1)
 
     return (
         out_act,
         in_grad,
         bank_grad,
-        self_part(0),
-        own_part(early_vec[5], head_cols),
-        self_part(1),
-        self_part(2),
-        own_part(early_vec[6], head_cols),
+        sq_grad,
+        line(sq_rows),
+        sk_grad,
+        sv_grad,
+        line(sv_rows),
         so_grad,
-        early_vec[2],
-        early_vec[1],
-        early_vec[0],
+        line(so_rows),
+        line(first_gain_rows),
+        line(first_shift_rows),
         cq_grad,
-        own_part(early_vec[3], head_cols),
+        line(cq_rows),
         ck_grad,
         cv_grad,
-        own_part(early_vec[4], head_cols),
+        line(cv_rows),
         co_grad,
-        late_vec[5],
-        late_vec[4],
-        late_vec[3],
+        line(co_rows),
+        line(second_gain_rows),
+        line(second_shift_rows),
         expand_grad,
-        lax.dynamic_index_in_dim(late_vec, 8 + rank, 0, keepdims=False),
+        line(expand_rows),
         shrink_grad,
-        late_vec[2],
-        late_vec[1],
-        late_vec[0],
+        line(shrink_rows),
+        line(third_gain_rows),
+        line(third_shift_rows),
     )
 
 

time: 453 us -> 440 us (0.971)
  the two profiles are of different devices: /device:TPU:19 before, /device:TPU:0 now
where the time goes in v1:
time: 440 us; the launch traced here: 433 us
  Pallas kernels  180 us (41%)
  waiting for transfers between devices  124 us (28%)
  starting transfers between devices  71.5 us (16%)
  other arithmetic  28.6 us (6%)
  local copies, waits for them, and re-layouts  26.2 us (6%)
    pallas_call x15, Pallas kernels, call(): pl.pallas_call(kernel, out_shape=out_shape, in_specs=in_specs, out_specs=...  96.4 us
    ppermute x7, waiting for transfers between devices, swap_both(): return lax.ppermute(value, ('dp', 'tensor'), pairs)  41.7 us
    ppermute x9, waiting for transfers between devices, swap_dp(): lax.ppermute(value, 'dp', tuple(((i, i ^ bit) for i in range(count))))  39.8 us
    all_to_all x7, starting transfers between devices, outer_exchange(): lax.all_to_all(value, 'dp', 0, 0, axis_index_groups=groups, tiled=True)  34 us
    ppermute x12, waiting for transfers between devices, swap_x(): return lax.ppermute(value, 'tensor', X_SWAP)  31.4 us
    pallas_call x1, Pallas kernels, cross_first_backward(): pl.pallas_call(functools.partial(cross_first_kernel, start=start, count=c...  22.6 us
    pallas_call x2, Pallas kernels, self_backward(): pl.pallas_call(self_bwd_kernel, grid_spec=pltpu.PrefetchScalarGridSpec(nu...  20.4 us
    unnamed x146, local copies, waits for them, and re-layouts  19.3 us
  transfers between devices with their start and end apart: 57, of which 22 were waited for; matrix products, arithmetic and copies ran while one was open for 6% of the time, Pallas kernels for 30%

profile of v1, /device:TPU:0, one launch (start us, length us, event | category | flops | bytes accessed | tf_op | source)
XLA Modules:
  0.0 432.6 jit_solution(18278044510842706321)
XLA Ops:
  2.9 4.2 fetch.1
  7.9 2.4 collective-permute-start
  10.5 1.8 pack_self.1
  12.4 2.7 pack_rest.1
  15.1 5.1 %all-to-all-start = ((bf16[4,96,576]{2,1,0:T(8,128)(2,1)}), bf16[4,96,576]{2,1,0:T(8,128)(2,1)S(1)}, u32[]{:S(2)}, u32[]{:S(2)}) async-start(bf16[4,96,576]{2,1,0:T(8,128)(2,1)} %pack_self.1), calls=%async_computation | async-start | bytes 983040 | tf_op jit(solution)/shard_map/all_to_all | solution.py:387
  25.3 1.6 collective-permute-start.4
  30.9 2.7 collective-permute-done.5.y_ref
  34.8 2.7 plane_copies.1
  37.6 5.1 %all-to-all-start.1 = ((bf16[4,96,960]{2,1,0:T(8,128)(2,1)}), bf16[4,96,960]{2,1,0:T(8,128)(2,1)}, u32[]{:S(2)}, u32[]{:S(2)}) async-start(bf16[4,96,960]{2,1,0:T(8,128)(2,1)} %get-tuple-element.208), calls=%async_computation.1 | async-start | bytes 1572864 | tf_op jit(solution)/shard_map/all_to_all | solution.py:387
  43.2 1.7 collective-permute-start.9
  46.2 10.6 %collective-permute-done.7.wx_ref = bf16[4,96,576]{2,1,0:T(8,128)(2,1)S(1)} collective-permute-done((bf16[4,96,576]{2,1,0:T(8,128)(2,1)S(1)}, bf16[4,96,576]{2,1,0:T(8,128)(2,1)S(1)}, u32[]{:S(2)}, u32[]{:S(2)}) %collective-permute-start.7) | collective-permute-done | bytes 442400 | tf_op jit(solution)/shard_map/ppermute | solution.py:38
  56.8 9.1 %collective-permute-done.9.wxy_ref = bf16[4,96,576]{2,1,0:T(8,128)(2,1)S(1)} collective-permute-done((bf16[4,96,576]{2,1,0:T(8,128)(2,1)S(1)}, bf16[4,96,576]{2,1,0:T(8,128)(2,1)S(1)}, u32[]{:S(2)}, u32[]{:S(2)}) %collective-permute-start.9) | collective-permute-done | bytes 442400 | tf_op jit(solution)/shard_map/ppermute | solution.py:382
  68.1 4.8 %all-to-all-start.2 = ((bf16[4,96,768]{2,1,0:T(8,128)(2,1)}), bf16[4,96,768]{2,1,0:T(8,128)(2,1)}, u32[]{:S(2)}, u32[]{:S(2)}) async-start(bf16[4,96,768]{2,1,0:T(8,128)(2,1)} %get-tuple-element.239), calls=%async_computation.2 | async-start | bytes 1179648 | tf_op jit(solution)/shard_map/all_to_all | solution.py:387
  72.9 1.7 collective-permute-start.13
  76.2 12.9 %self_fwd.1 = (bf16[2,512,1152]{2,1,0:T(8,128)(2,1)}, bf16[768,1152]{1,0:T(8,128)(2,1)S(1)}, bf16[512,384]{1,0:T(8,128)(2,1)S(1)}, bf16[512,384]{1,0:T(8,128)(2,1)S(1)}, f32[3,2,2,512]{3,2,1,0:T(2,128)S(1)}) custom-call(s32[5]{0:T(128)S(1)} %pad_add_fusion.2.info, bf16[512,768]{1,0:T(8,128)(2,1)S(1)} %copy-done.5, ...), custom_call_target="tpu_custom_call" | custom-call | flops 1000 | bytes 1000 | tf_op jit(solution)/shard_map/self_fwd/pallas_call | solution.py:568
  92.9 5.4 %all-to-all-start.3 = ((bf16[4,2,2,96,768]{4,3,2,1,0:T(8,128)(2,1)}), bf16[4,2,2,96,768]{4,3,2,1,0:T(8,128)(2,1)}, u32[]{:S(2)}, u32[]{:S(2)}) async-start(bf16[4,2,2,96,768]{4,3,2,1,0:T(8,128)(2,1)} %plane_copies.1), calls=%async_computation.3 | async-start | bytes 4718592 | tf_op jit(solution)/shard_map/all_to_all | solution.py:387
  99.7 2.3 bitcast_add_fusion.1
  102.0 1.8 collective-permute-start.11
  104.0 16.0 %collective-permute-done.14.refs_3_ = bf16[4,96,960]{2,1,0:T(8,128)(2,1)S(1)} collective-permute-done((bf16[4,96,960]{2,1,0:T(8,128)(2,1)}, bf16[4,96,960]{2,1,0:T(8,128)(2,1)S(1)}, u32[]{:S(2)}, u32[]{:S(2)}) %collective-permute-start.14) | collective-permute-done | bytes 737312 | tf_op jit(solution)/shard_map/ppermute | solution.py:382
  125.2 7.9 %assemble.1 = (bf16[4,2,96,1536]{3,2,1,0:T(8,128)(2,1)}, bf16[4,2,96,768]{3,2,1,0:T(8,128)(2,1)}, bf16[4,2,96,768]{3,2,1,0:T(8,128)(2,1)}, bf16[4,2,96,768]{3,2,1,0:T(8,128)(2,1)}) custom-call(s32[3]{0:T(128)} %pad_add_fusion.info, bf16[4,96,960]{2,1,0:T(8,128)(2,1)} %all-to-all-done.1.refs_0_, bf16[4,96,960]{2,1,0:T(8,128)(2,1)} %copy-done.38, ...), custom_call_target="tpu_custom_call" | custom-call | flops 1000 | bytes 1000 | tf_op jit(solution)/shard_map/assemble/pallas_call | solution.py:415
  133.1 4.7 %project_kv.1 = (bf16[512,768]{1,0:T(8,128)(2,1)}, bf16[512,1536]{1,0:T(8,128)(2,1)}) custom-call(bf16[512,768]{1,0:T(8,128)(2,1)} %bitcast_add_fusion.2.keep_ref, bf16[512,768]{1,0:T(8,128)(2,1)} %bitcast.16.got_ref, bf16[768,1536]{1,0:T(8,128)(2,1)} %bitcast.78, f32[1,768]{1,0:T(1,128)} %reshape_reshape.7.bias_ref), custom_call_target="tpu_custom_call" | custom-call | flops 1000 | bytes 1000 | tf_op jit(solution)/shard_map/project_kv/pallas_call | solution.py:415
  138.0 1.6 collective-permute-start.21
  139.9 5.7 %first_forward.1 = (f32[512,768]{1,0:T(8,128)}, f32[512,768]{1,0:T(8,128)}, bf16[512,768]{1,0:T(8,128)(2,1)}, bf16[512,768]{1,0:T(8,128)(2,1)}, bf16[512,768]{1,0:T(8,128)(2,1)}) custom-call(bf16[512,768]{1,0:T(8,128)(2,1)} %own_ref.2, bf16[512,384]{1,0:T(8,128)(2,1)} %copy-done.9, bf16[512,384]{1,0:T(8,128)(2,1)} %collective-permute-done.10.oth_ref, ...), custom_call_target="tpu_custom_call" | custom-call | flops 1000 | bytes 1000 | tf_op jit(solution)/shard_map/first_forward/pallas_call | solution.py:415
  145.6 8.3 %collective-permute-done.21.e1 = bf16[4,96,768]{2,1,0:T(8,128)(2,1)} collective-permute-done((bf16[4,96,768]{2,1,0:T(8,128)(2,1)}, bf16[4,96,768]{2,1,0:T(8,128)(2,1)}, u32[]{:S(2)}, u32[]{:S(2)}) %collective-permute-start.21) | collective-permute-done | bytes 589856 | tf_op jit(solution)/shard_map/ppermute | solution.py:43
  156.8 15.2 %collective-permute-done.22.e3 = bf16[4,96,768]{2,1,0:T(8,128)(2,1)S(1)} collective-permute-done((bf16[4,96,768]{2,1,0:T(8,128)(2,1)}, bf16[4,96,768]{2,1,0:T(8,128)(2,1)S(1)}, u32[]{:S(2)}, u32[]{:S(2)}) %collective-permute-start.22) | collective-permute-done | bytes 589856 | tf_op jit(solution)/shard_map/ppermute | solution.py:382
  173.7 13.7 %cross_fwd.1 = (bf16[512,768]{1,0:T(8,128)(2,1)S(1)}, f32[6,2,512]{2,1,0:T(2,128)S(1)}) custom-call(bf16[512,768]{1,0:T(8,128)(2,1)S(1)} %copy-done.6, bf16[512,1536]{1,0:T(8,128)(2,1)S(1)} %copy-done, bf16[512,1536]{1,0:T(8,128)(2,1)S(1)} %collective-permute-done.19.kb_ref.vb_ref, bf16[512,1536]{1,0:T(8,128)(2,1)S(1)} %copy-done, ...), custom_call_target="tpu_custom_call" | custom-call | flops 1000 | bytes 1000 | tf_op jit(solution)/shard_map/cross_fwd/pallas_call | solution.py:187
  190.4 33.0 %feed.1 = (bf16[512,768]{1,0:T(8,128)(2,1)}, f32[512,768]{1,0:T(8,128)}, bf16[512,768]{1,0:T(8,128)(2,1)}, bf16[512,768]{1,0:T(8,128)(2,1)}, bf16[2,2,4,104,1536...) custom-call(s32[3]{0:T(128)} %pad_add_fusion.info, bf16[512,768]{1,0:T(8,128)(2,1)} %copy-done.3, ...), custom_call_target="tpu_custom_call" | custom-call | flops 1000 | bytes 1000 | tf_op jit(solution)/shard_map/feed/pallas_call | solution.py:415
  225.1 9.5 %cross_bwd.1 = (bf16[512,768]{1,0:T(8,128)(2,1)S(1)}, bf16[2,512,768]{2,1,0:T(8,128)(2,1)S(1)}, bf16[2,512,768]{2,1,0:T(8,128)(2,1)}) custom-call(bf16[512,768]{1,0:T(8,128)(2,1)S(1)} %copy-done.7, bf16[512,1536]{1,0:T(8,128)(2,1)} %get-tuple-element.235.ka_ref.va_ref, bf16[512,1536]{1,0:T(8,128)(2,1)} %copy-done.1, ...), custom_call_target="tpu_custom_call" | custom-call | flops 1000 | bytes 1000 | tf_op jit(solution)/shard_map/cross_bwd/pallas_call | solution.py:236
  234.6 3.4 fusion.1
  238.0 2.7 fusion
  241.0 1.7 collective-permute-start.30
  242.7 22.6 %cross_first.1 = (bf16[512,768]{1,0:T(8,128)(2,1)S(1)}, bf16[2,512,768]{2,1,0:T(8,128)(2,1)}, bf16[2,512,768]{2,1,0:T(8,128)(2,1)}, f32[512,768]{1,0:T(8,128)}, ...) custom-call(bf16[512,768]{1,0:T(8,128)(2,1)S(1)} %copy-done.7, ...), custom_call_target="tpu_custom_call", output_to_operand_aliasing={{1}: (14, {}), {2}: (15, {})} | custom-call | flops 1000 | bytes 1000 | tf_op jit(solution)/shard_map/cross_first/pallas_call | solution.py:328
  265.3 5.6 %collective-permute-done.29 = bf16[2,4,104,768]{3,2,1,0:T(8,128)(2,1)S(1)} collective-permute-done((bf16[2,4,104,768]{3,2,1,0:T(8,128)(2,1)}, bf16[2,4,104,768]{3,2,1,0:T(8,128)(2,1)S(1)}, u32[]{:S(2)}, u32[]{:S(2)}) %collective-permute-start.29) | collective-permute-done | bytes 1277984 | tf_op jit(solution)/shard_map/ppermute | solution.py:38
  271.5 3.2 fusion.6
  275.3 7.2 %query_grads.1 = (bf16[2,2,4,112,576]{4,3,2,1,0:T(8,128)(2,1)}, bf16[2,2,4,112,576]{4,3,2,1,0:T(8,128)(2,1)}) custom-call(s32[3]{0:T(128)} %pad_add_fusion.info, bf16[512,768]{1,0:T(8,128)(2,1)} %get-tuple-element.268.h1_ref, bf16[512,768]{1,0:T(8,128)(2,1)} %copy-done.17, bf16[512,768]{1,0:T(8,128)(2,1)} %copy-done.18, ...), custom_call_target="tpu_custom_call" | custom-call | flops 1000 | bytes 1000 | tf_op jit(solution)/shard_map/query_grads/pallas_call | solution.py:415
  282.6 1.6 collective-permute-start.34
  284.8 7.4 %key_grads.1 = (bf16[2,2,4,104,384]{4,3,2,1,0:T(8,128)(2,1)}, bf16[2,2,4,104,384]{4,3,2,1,0:T(8,128)(2,1)}, bf16[512,768]{1,0:T(8,128)(2,1)}) custom-call(s32[3]{0:T(128)} %pad_add_fusion.info, bf16[512,768]{1,0:T(8,128)(2,1)} %get-tuple-element.284.fet_ref, bf16[2,512,768]{2,1,0:T(8,128)(2,1)} %get-tuple-element.287.own_ref, ...), custom_call_target="tpu_custom_call" | custom-call | flops 1000 | bytes 1000 | tf_op jit(solution)/shard_map/key_grads/pallas_call | solution.py:415
  293.6 6.0 %collective-permute-done.34 = bf16[4,104,768]{2,1,0:T(8,128)(2,1)} collective-permute-done((bf16[4,104,768]{2,1,0:T(8,128)(2,1)}, bf16[4,104,768]{2,1,0:T(8,128)(2,1)}, u32[]{:S(2)}, u32[]{:S(2)}) %collective-permute-start.34) | collective-permute-done | bytes 639008 | tf_op jit(solution)/shard_map/ppermute | solution.py:43
  301.5 1.6 collective-permute-start.38
  304.5 13.2 %self_bwd.2 = (bf16[3,2,512,384]{3,2,1,0:T(8,128)(2,1)S(1)}, f32[3,8,128]{2,1,0:T(8,128)S(1)}) custom-call(s32[2]{0:T(128)S(1)} %pad_add_fusion.1.info, bf16[2,512,1152]{2,1,0:T(8,128)(2,1)} %get-tuple-element.252.q_ref.k_ref.v_ref, bf16[2,512,1152]{2,1,0:T(8,128)(2,1)} %get-tuple-element.252.q_ref.k_ref.v_ref, ...), custom_call_target="tpu_custom_call" | custom-call | flops 1000 | bytes 1000 | tf_op jit(solution)/shard_map/self_bwd/pallas_call | solution.py:122
  317.7 2.7 fusion.5
  321.5 7.3 %collective-permute-done.38 = bf16[4,112,576]{2,1,0:T(8,128)(2,1)S(1)} collective-permute-done((bf16[4,112,576]{2,1,0:T(8,128)(2,1)S(1)}, bf16[4,112,576]{2,1,0:T(8,128)(2,1)S(1)}, u32[]{:S(2)}, u32[]{:S(2)}) %collective-permute-start.38) | collective-permute-done | bytes 516128 | tf_op jit(solution)/shard_map/ppermute | solution.py:43
  328.9 2.4 fusion.8
  332.7 5.3 %all-to-all-start.4 = ((bf16[4,104,1536]{2,1,0:T(8,128)(2,1)}), bf16[4,104,1536]{2,1,0:T(8,128)(2,1)}, u32[]{:S(2)}, u32[]{:S(2)}) async-start(bf16[4,104,1536]{2,1,0:T(8,128)(2,1)} %pad_maximum_fusion), calls=%async_computation.4 | async-start | bytes 2555904 | tf_op jit(solution)/shard_map/all_to_all | solution.py:387
  338.1 1.6 collective-permute-start.40
  340.0 1.6 collective-permute-start.42
  343.4 7.2 %self_bwd.3 = (bf16[3,2,512,384]{3,2,1,0:T(8,128)(2,1)S(1)}, f32[3,8,128]{2,1,0:T(8,128)S(1)}) custom-call(s32[2]{0:T(128)S(1)} %pad_add_fusion.1.info, bf16[2,512,1152]{2,1,0:T(8,128)(2,1)} %get-tuple-element.252.q_ref.k_ref.v_ref, bf16[2,512,1152]{2,1,0:T(8,128)(2,1)} %get-tuple-element.252.q_ref.k_ref.v_ref, ...), custom_call_target="tpu_custom_call", output_to_operand_aliasing={{0}: (9, {}), {1}: (10, {})} | custom-call | flops 1000 | bytes 1000 | tf_op jit(solution)/shard_map/self_bwd/pallas_call | solution.py:122
  352.0 3.3 collective-permute-done.41
  355.2 6.2 %self_grads.1 = (bf16[4,104,576]{2,1,0:T(8,128)(2,1)}, bf16[4,104,576]{2,1,0:T(8,128)(2,1)}, bf16[4,104,576]{2,1,0:T(8,128)(2,1)}, bf16[4,104,576]{2,1,0:T(8,128)(2,1)}) custom-call(s32[3]{0:T(128)} %pad_add_fusion.info, bf16[512,768]{1,0:T(8,128)(2,1)} %own_ref.2, bf16[512,768]{1,0:T(8,128)(2,1)} %copy-done.11, bf16[3,2,512,384]{3,2,1,0:T(8,128)(2,1)} %copy-done.2), custom_call_target="tpu_custom_call" | custom-call | flops 1000 | bytes 1000 | tf_op jit(solution)/shard_map/self_grads/pallas_call | solution.py:415
  361.4 6.9 %all-to-all-done.4.in_ref = bf16[4,104,1536]{2,1,0:T(8,128)(2,1)} async-done(((bf16[4,104,1536]{2,1,0:T(8,128)(2,1)}), bf16[4,104,1536]{2,1,0:T(8,128)(2,1)}, u32[]{:S(2)}, u32[]{:S(2)}) %all-to-all-start.4) | async-done | bytes 1277984 | tf_op jit(solution)/shard_map/all_to_all | solution.py:387
  368.3 3.5 all-to-all-start.5
  371.8 1.8 collective-permute-start.43
  375.4 6.6 %self_back.1 = (f32[512,768]{1,0:T(8,128)}, bf16[512,768]{1,0:T(8,128)(2,1)}) custom-call(bf16[3,2,512,384]{3,2,1,0:T(8,128)(2,1)} %copy-done.2, bf16[768,1152]{1,0:T(8,128)(2,1)} %copy-done.13, f32[512,768]{1,0:T(8,128)} %get-tuple-element.325.first_ref), custom_call_target="tpu_custom_call" | custom-call | flops 1000 | bytes 1000 | tf_op jit(solution)/shard_map/self_back/pallas_call | solution.py:415
  382.0 5.1 %collective-permute-done.43 = bf16[4,104,576]{2,1,0:T(8,128)(2,1)S(1)} collective-permute-done((bf16[4,104,576]{2,1,0:T(8,128)(2,1)}, bf16[4,104,576]{2,1,0:T(8,128)(2,1)S(1)}, u32[]{:S(2)}, u32[]{:S(2)}) %collective-permute-start.43) | collective-permute-done | bytes 479264 | tf_op jit(solution)/shard_map/ppermute | solution.py:38
  387.1 10.8 %collective-permute-done.44 = bf16[4,104,576]{2,1,0:T(8,128)(2,1)S(1)} collective-permute-done((bf16[4,104,576]{2,1,0:T(8,128)(2,1)}, bf16[4,104,576]{2,1,0:T(8,128)(2,1)S(1)}, u32[]{:S(2)}, u32[]{:S(2)}) %collective-permute-start.44) | collective-permute-done | bytes 479264 | tf_op jit(solution)/shard_map/ppermute | solution.py:43
  400.3 1.6 fusion.9
  403.0 4.8 %all-to-all-start.6 = ((bf16[4,104,960]{2,1,0:T(8,128)(2,1)}), bf16[4,104,960]{2,1,0:T(8,128)(2,1)}, u32[]{:S(2)}, u32[]{:S(2)}) async-start(bf16[4,104,960]{2,1,0:T(8,128)(2,1)} %pad_maximum_fusion.1), calls=%async_computation.6 | async-start | bytes 1703936 | tf_op jit(solution)/shard_map/all_to_all | solution.py:387
  408.3 7.3 %collective-permute-done.47 = bf16[512,768]{1,0:T(8,128)(2,1)S(1)} collective-permute-done((bf16[512,768]{1,0:T(8,128)(2,1)S(1)}, bf16[512,768]{1,0:T(8,128)(2,1)S(1)}, u32[]{:S(2)}, u32[]{:S(2)}) %collective-permute-start.47) | collective-permute-done | bytes 786464 | tf_op jit(solution)/shard_map/ppermute | solution.py:38
  416.0 2.3 sum_feed.1
  418.3 1.9 sum_query.1
  420.3 2.2 add_convert_fusion.2
  422.4 3.0 all-to-all-done.6.in_ref
  425.5 2.0 sum_cols.1
  427.5 4.8 %scatter.1 = f32[32,64,768]{2,1,0:T(8,128)} custom-call(s32[32]{0:T(128)S(1)} %reshape.389.table, bf16[8,64,768]{2,1,0:T(8,128)(2,1)S(1)} %bitcast.75, bf16[8,64,768]{2,1,0:T(8,128)(2,1)S(1)} %bitcast.77, bf16[8,64,768]{2,1,0:T(8,128)(2,1)S(1)} %collective-permute-done.48.c_ref, bf16[8,64,768]{2,1,0:T(8,128)(2,1)S(1)} %collective-permute-done.49.d_ref), custom_call_target="tpu_custom_call" | custom-call | flops 1000 | bytes 1000 | tf_op jit(solution)/shard_map/scatter/pallas_call | solution.py:1185
  (275 shorter events, 58.2 us)
Async XLA Ops:
  7.1 30.5 %collective-permute-start.2 = (bf16[2,8,64,768]{3,2,1,0:T(8,128)(2,1)}, bf16[2,8,64,768]{3,2,1,0:T(8,128)(2,1)}, u32[]{:S(2)}, u32[]{:S(2)}) collective-permute-start(bf16[2,8,64,768]{3,2,1,0:T(8,128)(2,1)} %bitcast.90), channel_id=1, source_target_pairs={{0,1},{1,0},{2,3},{3,2},{4,5},{5,4},{6,7},{7,6},{8,9},{9,8},{10,11... | collective-permute-start | bytes 4718600 | tf_op jit(solution)/shard_map/ppermute | solution.py:34
  7.9 15.0 %collective-permute-start = (f32[1,1536]{1,0:T(1,128)S(1)}, f32[1,1536]{1,0:T(1,128)S(1)}, u32[]{:S(2)}, u32[]{:S(2)}) collective-permute-start(f32[1,1536]{1,0:T(1,128)S(1)} %reshape.383), channel_id=1, source_target_pairs={{0,2},{2,0},{1,3},{3,1},{4,6},{6,4},{5,7},{7,5},{8,10},{10,8},{9,1... | collective-permute-start | bytes 18440 | tf_op jit(solution)/shard_map/ppermute | solution.py:38
  10.3 27.3 %collective-permute-start.3 = (bf16[512,768]{1,0:T(8,128)(2,1)S(1)}, bf16[512,768]{1,0:T(8,128)(2,1)S(1)}, u32[]{:S(2)}, u32[]{:S(2)}) collective-permute-start(bf16[512,768]{1,0:T(8,128)(2,1)S(1)} %copy-done.5), channel_id=1, source_target_pairs={{0,1},{1,0},{2,3},{3,2},{4,5},{5,4},{6,7},{7,6},{8,9},{9,8},{10,11... | collective-permute-start | bytes 2359304 | tf_op jit(solution)/shard_map/ppermute | solution.py:34
  15.1 22.5 %all-to-all-start = ((bf16[4,96,576]{2,1,0:T(8,128)(2,1)}), bf16[4,96,576]{2,1,0:T(8,128)(2,1)S(1)}, u32[]{:S(2)}, u32[]{:S(2)}) async-start(bf16[4,96,576]{2,1,0:T(8,128)(2,1)} %pack_self.1), calls=%async_computation | async-start | bytes 983040 | tf_op jit(solution)/shard_map/all_to_all | solution.py:387
  22.9 2.4 collective-permute-start.1
  23.0 7.8 %collective-permute-start.6 = (bf16[96,768]{1,0:T(8,128)(2,1)}, bf16[96,768]{1,0:T(8,128)(2,1)S(1)}, u32[]{:S(2)}, u32[]{:S(2)}) collective-permute-start(bf16[96,768]{1,0:T(8,128)(2,1)} %get-tuple-element.206.own_ref), channel_id=1, source_target_pairs={{0,6},{1,7},{2,4},{3,5},{4,2},{5,3},{6,0},{7,1},{8,14},{9,15},{10,... | collective-permute-start | bytes 442376 | tf_op jit(solution)/shard_map/ppermute | solution.py:382
  24.5 9.0 %collective-permute-start.5 = (bf16[96,768]{1,0:T(8,128)(2,1)}, bf16[96,768]{1,0:T(8,128)(2,1)S(1)}, u32[]{:S(2)}, u32[]{:S(2)}) collective-permute-start(bf16[96,768]{1,0:T(8,128)(2,1)} %get-tuple-element.206.own_ref), channel_id=1, source_target_pairs={{0,4},{4,0},{8,12},{12,8},{16,20},{20,16},{24,28},{28,24},{1,5},{5... | collective-permute-start | bytes 442376 | tf_op jit(solution)/shard_map/ppermute | solution.py:43
  25.3 8.3 %collective-permute-start.4 = (bf16[96,768]{1,0:T(8,128)(2,1)}, bf16[96,768]{1,0:T(8,128)(2,1)S(1)}, u32[]{:S(2)}, u32[]{:S(2)}) collective-permute-start(bf16[96,768]{1,0:T(8,128)(2,1)} %get-tuple-element.206.own_ref), channel_id=1, source_target_pairs={{0,2},{2,0},{1,3},{3,1},{4,6},{6,4},{5,7},{7,5},{8,10},{10,8},{9,1... | collective-permute-start | bytes 442376 | tf_op jit(solution)/shard_map/ppermute | solution.py:38
  37.6 37.6 %copy-start.11 = (bf16[512,768]{1,0:T(8,128)(2,1)}, bf16[512,768]{1,0:T(8,128)(2,1)S(1)}, u32[]{:S(2)}) copy-start(bf16[512,768]{1,0:T(8,128)(2,1)S(1)} %collective-permute-done.3.oth_ref) | copy-start | bytes 2359300
  37.6 30.5 %all-to-all-start.1 = ((bf16[4,96,960]{2,1,0:T(8,128)(2,1)}), bf16[4,96,960]{2,1,0:T(8,128)(2,1)}, u32[]{:S(2)}, u32[]{:S(2)}) async-start(bf16[4,96,960]{2,1,0:T(8,128)(2,1)} %get-tuple-element.208), calls=%async_computation.1 | async-start | bytes 1572864 | tf_op jit(solution)/shard_map/all_to_all | solution.py:387
  42.7 14.1 %collective-permute-start.7 = (bf16[4,96,576]{2,1,0:T(8,128)(2,1)S(1)}, bf16[4,96,576]{2,1,0:T(8,128)(2,1)S(1)}, u32[]{:S(2)}, u32[]{:S(2)}) collective-permute-start(bf16[4,96,576]{2,1,0:T(8,128)(2,1)S(1)} %all-to-all-done.w_ref), channel_id=1, source_target_pairs={{0,2},{2,0},{1,3},{3,1},{4,6},{6,4},{5,7},{7,5},{8,10},{10,8},{9,1... | collective-permute-start | bytes 1327112 | tf_op jit(solution)/shard_map/ppermute | solution.py:38
  43.2 22.8 %collective-permute-start.9 = (bf16[4,96,576]{2,1,0:T(8,128)(2,1)S(1)}, bf16[4,96,576]{2,1,0:T(8,128)(2,1)S(1)}, u32[]{:S(2)}, u32[]{:S(2)}) collective-permute-start(bf16[4,96,576]{2,1,0:T(8,128)(2,1)S(1)} %all-to-all-done.w_ref), channel_id=1, source_target_pairs={{0,6},{1,7},{2,4},{3,5},{4,2},{5,3},{6,0},{7,1},{8,14},{9,15},{10,... | collective-permute-start | bytes 1327112 | tf_op jit(solution)/shard_map/ppermute | solution.py:382
  44.9 22.4 %collective-permute-start.8 = (bf16[4,96,576]{2,1,0:T(8,128)(2,1)S(1)}, bf16[4,96,576]{2,1,0:T(8,128)(2,1)S(1)}, u32[]{:S(2)}, u32[]{:S(2)}) collective-permute-start(bf16[4,96,576]{2,1,0:T(8,128)(2,1)S(1)} %all-to-all-done.w_ref), channel_id=1, source_target_pairs={{0,4},{4,0},{8,12},{12,8},{16,20},{20,16},{24,28},{28,24},{1,5},{5... | collective-permute-start | bytes 1327112 | tf_op jit(solution)/shard_map/ppermute | solution.py:43
  68.1 24.8 %all-to-all-start.2 = ((bf16[4,96,768]{2,1,0:T(8,128)(2,1)}), bf16[4,96,768]{2,1,0:T(8,128)(2,1)}, u32[]{:S(2)}, u32[]{:S(2)}) async-start(bf16[4,96,768]{2,1,0:T(8,128)(2,1)} %get-tuple-element.239), calls=%async_computation.2 | async-start | bytes 1179648 | tf_op jit(solution)/shard_map/all_to_all | solution.py:387
  72.9 18.2 %collective-permute-start.13 = (bf16[4,96,960]{2,1,0:T(8,128)(2,1)}, bf16[4,96,960]{2,1,0:T(8,128)(2,1)S(1)}, u32[]{:S(2)}, u32[]{:S(2)}) collective-permute-start(bf16[4,96,960]{2,1,0:T(8,128)(2,1)} %all-to-all-done.1.refs_0_), channel_id=1, source_target_pairs={{0,4},{4,0},{8,12},{12,8},{16,20},{20,16},{24,28},{28,24},{1,5},{5... | collective-permute-start | bytes 2211848 | tf_op jit(solution)/shard_map/ppermute | solution.py:43
  74.6 16.5 %collective-permute-start.12 = (bf16[4,96,960]{2,1,0:T(8,128)(2,1)}, bf16[4,96,960]{2,1,0:T(8,128)(2,1)S(1)}, u32[]{:S(2)}, u32[]{:S(2)}) collective-permute-start(bf16[4,96,960]{2,1,0:T(8,128)(2,1)} %all-to-all-done.1.refs_0_), channel_id=1, source_target_pairs={{0,2},{2,0},{1,3},{3,1},{4,6},{6,4},{5,7},{7,5},{8,10},{10,8},{9,1... | collective-permute-start | bytes 2211848 | tf_op jit(solution)/shard_map/ppermute | solution.py:38
  92.9 62.3 %all-to-all-start.3 = ((bf16[4,2,2,96,768]{4,3,2,1,0:T(8,128)(2,1)}), bf16[4,2,2,96,768]{4,3,2,1,0:T(8,128)(2,1)}, u32[]{:S(2)}, u32[]{:S(2)}) async-start(bf16[4,2,2,96,768]{4,3,2,1,0:T(8,128)(2,1)} %plane_copies.1), calls=%async_computation.3 | async-start | bytes 4718592 | tf_op jit(solution)/shard_map/all_to_all | solution.py:387
  98.3 21.7 %collective-permute-start.14 = (bf16[4,96,960]{2,1,0:T(8,128)(2,1)}, bf16[4,96,960]{2,1,0:T(8,128)(2,1)S(1)}, u32[]{:S(2)}, u32[]{:S(2)}) collective-permute-start(bf16[4,96,960]{2,1,0:T(8,128)(2,1)} %all-to-all-done.1.refs_0_), channel_id=1, source_target_pairs={{0,6},{1,7},{2,4},{3,5},{4,2},{5,3},{6,0},{7,1},{8,14},{9,15},{10,... | collective-permute-start | bytes 2211848 | tf_op jit(solution)/shard_map/ppermute | solution.py:382
  99.7 20.8 %collective-permute-start.15 = (bf16[4,96,960]{2,1,0:T(8,128)(2,1)}, bf16[4,96,960]{2,1,0:T(8,128)(2,1)S(1)}, u32[]{:S(2)}, u32[]{:S(2)}) collective-permute-start(bf16[4,96,960]{2,1,0:T(8,128)(2,1)} %all-to-all-done.1.refs_0_), channel_id=1, source_target_pairs={{0,1},{1,0},{2,3},{3,2},{4,5},{5,4},{6,7},{7,6},{8,9},{9,8},{10,11... | collective-permute-start | bytes 2211848 | tf_op jit(solution)/shard_map/ppermute | solution.py:34
  102.0 31.1 %collective-permute-start.11 = (bf16[8,64,768]{2,1,0:T(8,128)(2,1)}, bf16[8,64,768]{2,1,0:T(8,128)(2,1)}, u32[]{:S(2)}, u32[]{:S(2)}) collective-permute-start(bf16[8,64,768]{2,1,0:T(8,128)(2,1)} %get-tuple-element.381), channel_id=1, source_target_pairs={{0,2},{2,0},{1,3},{3,1},{4,6},{6,4},{5,7},{7,5},{8,10},{10,8},{9,1... | collective-permute-start | bytes 2359304 | tf_op jit(solution)/shard_map/ppermute | solution.py:38
  103.7 19.4 %collective-permute-start.16 = (bf16[4,96,960]{2,1,0:T(8,128)(2,1)S(1)}, bf16[4,96,960]{2,1,0:T(8,128)(2,1)S(1)}, u32[]{:S(2)}, u32[]{:S(2)}) collective-permute-start(bf16[4,96,960]{2,1,0:T(8,128)(2,1)S(1)} %copy-done.39), channel_id=1, source_target_pairs={{0,1},{1,0},{2,3},{3,2},{4,5},{5,4},{6,7},{7,6},{8,9},{9,8},{10,11... | collective-permute-start | bytes 2211848 | tf_op jit(solution)/shard_map/ppermute | solution.py:34
  120.0 3.1 collective-permute-start.18
  120.0 4.0 collective-permute-start.17
  120.5 17.3 %collective-permute-start.10 = (bf16[512,384]{1,0:T(8,128)(2,1)S(1)}, bf16[512,384]{1,0:T(8,128)(2,1)}, u32[]{:S(2)}, u32[]{:S(2)}) collective-permute-start(bf16[512,384]{1,0:T(8,128)(2,1)S(1)} %get-tuple-element.219.ob_ref), channel_id=1, source_target_pairs={{0,1},{1,0},{2,3},{3,2},{4,5},{5,4},{6,7},{7,6},{8,9},{9,8},{10,11... | collective-permute-start | bytes 1179656 | tf_op jit(solution)/shard_map/ppermute | solution.py:34
  137.8 7.8 %collective-permute-start.19 = (bf16[512,1536]{1,0:T(8,128)(2,1)}, bf16[512,1536]{1,0:T(8,128)(2,1)S(1)}, u32[]{:S(2)}, u32[]{:S(2)}) collective-permute-start(bf16[512,1536]{1,0:T(8,128)(2,1)} %get-tuple-element.235.ka_ref.va_ref), channel_id=1, source_target_pairs={{0,1},{1,0},{2,3},{3,2},{4,5},{5,4},{6,7},{7,6},{8,9},{9,8},{10,11... | collective-permute-start | bytes 4718600 | tf_op jit(solution)/shard_map/ppermute | solution.py:34
  138.0 15.8 %collective-permute-start.21 = (bf16[4,96,768]{2,1,0:T(8,128)(2,1)}, bf16[4,96,768]{2,1,0:T(8,128)(2,1)}, u32[]{:S(2)}, u32[]{:S(2)}) collective-permute-start(bf16[4,96,768]{2,1,0:T(8,128)(2,1)} %all-to-all-done.2.e0), channel_id=1, source_target_pairs={{0,4},{4,0},{8,12},{12,8},{16,20},{20,16},{24,28},{28,24},{1,5},{5... | collective-permute-start | bytes 1769480 | tf_op jit(solution)/shard_map/ppermute | solution.py:43
  139.6 15.6 %collective-permute-start.20 = (bf16[4,96,768]{2,1,0:T(8,128)(2,1)}, bf16[4,96,768]{2,1,0:T(8,128)(2,1)}, u32[]{:S(2)}, u32[]{:S(2)}) collective-permute-start(bf16[4,96,768]{2,1,0:T(8,128)(2,1)} %all-to-all-done.2.e0), channel_id=1, source_target_pairs={{0,2},{2,0},{1,3},{3,1},{4,6},{6,4},{5,7},{7,5},{8,10},{10,8},{9,1... | collective-permute-start | bytes 1769480 | tf_op jit(solution)/shard_map/ppermute | solution.py:38
  139.9 32.7 %copy-start = (bf16[512,1536]{1,0:T(8,128)(2,1)S(1)}, bf16[512,1536]{1,0:T(8,128)(2,1)}, u32[]{:S(2)}) copy-start(bf16[512,1536]{1,0:T(8,128)(2,1)} %get-tuple-element.235.ka_ref.va_ref) | copy-start | bytes 4718596
  145.5 41.8 %copy-start.1 = (bf16[512,1536]{1,0:T(8,128)(2,1)}, bf16[512,1536]{1,0:T(8,128)(2,1)S(1)}, u32[]{:S(2)}) copy-start(bf16[512,1536]{1,0:T(8,128)(2,1)S(1)} %collective-permute-done.19.kb_ref.vb_ref) | copy-start | bytes 4718596
  155.2 33.2 %collective-permute-start.27 = (bf16[4,2,2,96,768]{4,3,2,1,0:T(8,128)(2,1)}, bf16[4,2,2,96,768]{4,3,2,1,0:T(8,128)(2,1)S(1)}, u32[]{:S(2)}, u32[]{:S(2)}) collective-permute-start(bf16[4,2,2,96,768]{4,3,2,1,0:T(8,128)(2,1)} %all-to-all-done.3.s0), channel_id=1, source_target_pairs={{0,1},{1,0},{2,3},{3,2},{4,5},{5,4},{6,7},{7,6},{8,9},{9,8},{10,11... | collective-permute-start | bytes 7077896 | tf_op jit(solution)/shard_map/ppermute | solution.py:34
  155.2 16.9 %collective-permute-start.22 = (bf16[4,96,768]{2,1,0:T(8,128)(2,1)}, bf16[4,96,768]{2,1,0:T(8,128)(2,1)S(1)}, u32[]{:S(2)}, u32[]{:S(2)}) collective-permute-start(bf16[4,96,768]{2,1,0:T(8,128)(2,1)} %all-to-all-done.2.e0), channel_id=1, source_target_pairs={{0,6},{1,7},{2,4},{3,5},{4,2},{5,3},{6,0},{7,1},{8,14},{9,15},{10,... | collective-permute-start | bytes 1769480 | tf_op jit(solution)/shard_map/ppermute | solution.py:382
  156.6 31.7 %collective-permute-start.23 = (bf16[4,96,768]{2,1,0:T(8,128)(2,1)}, bf16[4,96,768]{2,1,0:T(8,128)(2,1)S(1)}, u32[]{:S(2)}, u32[]{:S(2)}) collective-permute-start(bf16[4,96,768]{2,1,0:T(8,128)(2,1)} %all-to-all-done.2.e0), channel_id=1, source_target_pairs={{0,1},{1,0},{2,3},{3,2},{4,5},{5,4},{6,7},{7,6},{8,9},{9,8},{10,11... | collective-permute-start | bytes 1769480 | tf_op jit(solution)/shard_map/ppermute | solution.py:34
  172.0 16.3 %collective-permute-start.26 = (bf16[4,96,768]{2,1,0:T(8,128)(2,1)S(1)}, bf16[4,96,768]{2,1,0:T(8,128)(2,1)S(1)}, u32[]{:S(2)}, u32[]{:S(2)}) collective-permute-start(bf16[4,96,768]{2,1,0:T(8,128)(2,1)S(1)} %collective-permute-done.22.e3), channel_id=1, source_target_pairs={{0,1},{1,0},{2,3},{3,2},{4,5},{5,4},{6,7},{7,6},{8,9},{9,8},{10,11... | collective-permute-start | bytes 1769480 | tf_op jit(solution)/shard_map/ppermute | solution.py:34
  172.0 16.3 %collective-permute-start.24 = (bf16[4,96,768]{2,1,0:T(8,128)(2,1)}, bf16[4,96,768]{2,1,0:T(8,128)(2,1)S(1)}, u32[]{:S(2)}, u32[]{:S(2)}) collective-permute-start(bf16[4,96,768]{2,1,0:T(8,128)(2,1)} %collective-permute-done.21.e1), channel_id=1, source_target_pairs={{0,1},{1,0},{2,3},{3,2},{4,5},{5,4},{6,7},{7,6},{8,9},{9,8},{10,11... | collective-permute-start | bytes 1769480 | tf_op jit(solution)/shard_map/ppermute | solution.py:34
  172.5 15.8 %collective-permute-start.25 = (bf16[4,96,768]{2,1,0:T(8,128)(2,1)}, bf16[4,96,768]{2,1,0:T(8,128)(2,1)S(1)}, u32[]{:S(2)}, u32[]{:S(2)}) collective-permute-start(bf16[4,96,768]{2,1,0:T(8,128)(2,1)} %collective-permute-done.20.e2), channel_id=1, source_target_pairs={{0,1},{1,0},{2,3},{3,2},{4,5},{5,4},{6,7},{7,6},{8,9},{9,8},{10,11... | collective-permute-start | bytes 1769480 | tf_op jit(solution)/shard_map/ppermute | solution.py:34
  190.4 33.6 %copy-start.4 = (bf16[512,768]{1,0:T(8,128)(2,1)S(1)}, bf16[512,768]{1,0:T(8,128)(2,1)}, u32[]{:S(2)}) copy-start(bf16[512,768]{1,0:T(8,128)(2,1)} %copy-done.3) | copy-start | bytes 2359300
  190.4 33.6 %copy-start.7 = (bf16[512,768]{1,0:T(8,128)(2,1)S(1)}, bf16[512,768]{1,0:T(8,128)(2,1)}, u32[]{:S(2)}) copy-start(bf16[512,768]{1,0:T(8,128)(2,1)} %get-tuple-element.242.q_ref) | copy-start | bytes 2359300
  223.4 11.2 %collective-permute-start.28 = (bf16[2,2,4,104,1536]{4,3,2,1,0:T(8,128)(2,1)}, bf16[2,2,4,104,1536]{4,3,2,1,0:T(8,128)(2,1)}, u32[]{:S(2)}, u32[]{:S(2)}) collective-permute-start(bf16[2,2,4,104,1536]{4,3,2,1,0:T(8,128)(2,1)} %get-tuple-element.261), channel_id=1, source_target_pairs={{0,1},{1,0},{2,3},{3,2},{4,5},{5,4},{6,7},{7,6},{8,9},{9,8},{10,11... | collective-permute-start | bytes 15335432 | tf_op jit(solution)/shard_map/ppermute | solution.py:34
  240.7 30.2 %collective-permute-start.29 = (bf16[2,4,104,768]{3,2,1,0:T(8,128)(2,1)}, bf16[2,4,104,768]{3,2,1,0:T(8,128)(2,1)S(1)}, u32[]{:S(2)}, u32[]{:S(2)}) collective-permute-start(bf16[2,4,104,768]{3,2,1,0:T(8,128)(2,1)} %fusion), channel_id=1, source_target_pairs={{0,2},{2,0},{1,3},{3,1},{4,6},{6,4},{5,7},{7,5},{8,10},{10,8},{9,1... | collective-permute-start | bytes 3833864 | tf_op jit(solution)/shard_map/ppermute | solution.py:38
  241.0 29.9 %collective-permute-start.30 = (bf16[2,4,104,768]{3,2,1,0:T(8,128)(2,1)}, bf16[2,4,104,768]{3,2,1,0:T(8,128)(2,1)S(1)}, u32[]{:S(2)}, u32[]{:S(2)}) collective-permute-start(bf16[2,4,104,768]{3,2,1,0:T(8,128)(2,1)} %fusion.1), channel_id=1, source_target_pairs={{0,4},{4,0},{8,12},{12,8},{16,20},{20,16},{24,28},{28,24},{1,5},{5... | collective-permute-start | bytes 3833864 | tf_op jit(solution)/shard_map/ppermute | solution.py:43
  271.0 4.3 %collective-permute-start.31 = (bf16[2,512,768]{2,1,0:T(8,128)(2,1)}, bf16[2,512,768]{2,1,0:T(8,128)(2,1)}, u32[]{:S(2)}, u32[]{:S(2)}) collective-permute-start(bf16[2,512,768]{2,1,0:T(8,128)(2,1)} %get-tuple-element.275), channel_id=1, source_target_pairs={{0,1},{1,0},{2,3},{3,2},{4,5},{5,4},{6,7},{7,6},{8,9},{9,8},{10,11... | collective-permute-start | bytes 4718600 | tf_op jit(solution)/shard_map/ppermute | solution.py:34
  271.0 3.7 collective-permute-start.32
  274.7 29.8 %copy-start.14 = (bf16[512,384]{1,0:T(8,128)(2,1)}, bf16[512,384]{1,0:T(8,128)(2,1)S(1)}, u32[]{:S(2)}) copy-start(bf16[512,384]{1,0:T(8,128)(2,1)S(1)} %collective-permute-done.32.gb_ref) | copy-start | bytes 1179652
  282.5 9.7 %collective-permute-start.33 = (bf16[2,2,4,112,576]{4,3,2,1,0:T(8,128)(2,1)}, bf16[2,2,4,112,576]{4,3,2,1,0:T(8,128)(2,1)S(1)}, u32[]{:S(2)}, u32[]{:S(2)}) collective-permute-start(bf16[2,2,4,112,576]{4,3,2,1,0:T(8,128)(2,1)} %get-tuple-element.291), channel_id=1, source_target_pairs={{0,1},{1,0},{2,3},{3,2},{4,5},{5,4},{6,7},{7,6},{8,9},{9,8},{10,11... | collective-permute-start | bytes 6193160 | tf_op jit(solution)/shard_map/ppermute | solution.py:34
  282.6 17.0 %collective-permute-start.34 = (bf16[4,104,768]{2,1,0:T(8,128)(2,1)}, bf16[4,104,768]{2,1,0:T(8,128)(2,1)}, u32[]{:S(2)}, u32[]{:S(2)}) collective-permute-start(bf16[4,104,768]{2,1,0:T(8,128)(2,1)} %get-tuple-element.294), channel_id=1, source_target_pairs={{0,4},{4,0},{8,12},{12,8},{16,20},{20,16},{24,28},{28,24},{1,5},{5... | collective-permute-start | bytes 1916936 | tf_op jit(solution)/shard_map/ppermute | solution.py:43
  284.3 16.7 %collective-permute-start.35 = (bf16[4,104,768]{2,1,0:T(8,128)(2,1)}, bf16[4,104,768]{2,1,0:T(8,128)(2,1)}, u32[]{:S(2)}, u32[]{:S(2)}) collective-permute-start(bf16[4,104,768]{2,1,0:T(8,128)(2,1)} %get-tuple-element.295), channel_id=1, source_target_pairs={{0,2},{2,0},{1,3},{3,1},{4,6},{6,4},{5,7},{7,5},{8,10},{10,8},{9,1... | collective-permute-start | bytes 1916936 | tf_op jit(solution)/shard_map/ppermute | solution.py:38
  301.0 30.4 %collective-permute-start.36 = (bf16[2,2,4,104,384]{4,3,2,1,0:T(8,128)(2,1)S(1)}, bf16[2,2,4,104,384]{4,3,2,1,0:T(8,128)(2,1)S(1)}, u32[]{:S(2)}, u32[]{:S(2)}) collective-permute-start(bf16[2,2,4,104,384]{4,3,2,1,0:T(8,128)(2,1)S(1)} %copy-done.71), channel_id=1, source_target_pairs={{0,1},{1,0},{2,3},{3,2},{4,5},{5,4},{6,7},{7,6},{8,9},{9,8},{10,11... | collective-permute-start | bytes 3833864 | tf_op jit(solution)/shard_map/ppermute | solution.py:34
  301.0 20.6 %collective-permute-start.37 = (bf16[4,112,576]{2,1,0:T(8,128)(2,1)S(1)}, bf16[4,112,576]{2,1,0:T(8,128)(2,1)S(1)}, u32[]{:S(2)}, u32[]{:S(2)}) collective-permute-start(bf16[4,112,576]{2,1,0:T(8,128)(2,1)S(1)} %get-tuple-element.306), channel_id=1, source_target_pairs={{0,2},{2,0},{1,3},{3,1},{4,6},{6,4},{5,7},{7,5},{8,10},{10,8},{9,1... | collective-permute-start | bytes 1548296 | tf_op jit(solution)/shard_map/ppermute | solution.py:38
  301.5 27.4 %collective-permute-start.38 = (bf16[4,112,576]{2,1,0:T(8,128)(2,1)S(1)}, bf16[4,112,576]{2,1,0:T(8,128)(2,1)S(1)}, u32[]{:S(2)}, u32[]{:S(2)}) collective-permute-start(bf16[4,112,576]{2,1,0:T(8,128)(2,1)S(1)} %get-tuple-element.307), channel_id=1, source_target_pairs={{0,4},{4,0},{8,12},{12,8},{16,20},{20,16},{24,28},{28,24},{1,5},{5... | collective-permute-start | bytes 1548296 | tf_op jit(solution)/shard_map/ppermute | solution.py:43
  303.1 25.8 %collective-permute-start.39 = (bf16[4,112,576]{2,1,0:T(8,128)(2,1)S(1)}, bf16[4,112,576]{2,1,0:T(8,128)(2,1)S(1)}, u32[]{:S(2)}, u32[]{:S(2)}) collective-permute-start(bf16[4,112,576]{2,1,0:T(8,128)(2,1)S(1)} %get-tuple-element.308), channel_id=1, source_target_pairs={{0,6},{1,7},{2,4},{3,5},{4,2},{5,3},{6,0},{7,1},{8,14},{9,15},{10,... | collective-permute-start | bytes 1548296 | tf_op jit(solution)/shard_map/ppermute | solution.py:382
  332.7 35.6 %all-to-all-start.4 = ((bf16[4,104,1536]{2,1,0:T(8,128)(2,1)}), bf16[4,104,1536]{2,1,0:T(8,128)(2,1)}, u32[]{:S(2)}, u32[]{:S(2)}) async-start(bf16[4,104,1536]{2,1,0:T(8,128)(2,1)} %pad_maximum_fusion), calls=%async_computation.4 | async-start | bytes 2555904 | tf_op jit(solution)/shard_map/all_to_all | solution.py:387
  338.1 13.9 %collective-permute-start.40 = (bf16[4,104,384]{2,1,0:T(8,128)(2,1)}, bf16[4,104,384]{2,1,0:T(8,128)(2,1)}, u32[]{:S(2)}, u32[]{:S(2)}) collective-permute-start(bf16[4,104,384]{2,1,0:T(8,128)(2,1)} %get-tuple-element.312), channel_id=1, source_target_pairs={{0,2},{2,0},{1,3},{3,1},{4,6},{6,4},{5,7},{7,5},{8,10},{10,8},{9,1... | collective-permute-start | bytes 958472 | tf_op jit(solution)/shard_map/ppermute | solution.py:38
  339.7 15.6 %collective-permute-start.41 = (bf16[4,104,384]{2,1,0:T(8,128)(2,1)}, bf16[4,104,384]{2,1,0:T(8,128)(2,1)}, u32[]{:S(2)}, u32[]{:S(2)}) collective-permute-start(bf16[4,104,384]{2,1,0:T(8,128)(2,1)} %get-tuple-element.313), channel_id=1, source_target_pairs={{0,4},{4,0},{8,12},{12,8},{16,20},{20,16},{24,28},{28,24},{1,5},{5... | collective-permute-start | bytes 958472 | tf_op jit(solution)/shard_map/ppermute | solution.py:43
  340.0 15.2 %collective-permute-start.42 = (bf16[4,104,384]{2,1,0:T(8,128)(2,1)}, bf16[4,104,384]{2,1,0:T(8,128)(2,1)}, u32[]{:S(2)}, u32[]{:S(2)}) collective-permute-start(bf16[4,104,384]{2,1,0:T(8,128)(2,1)} %get-tuple-element.314), channel_id=1, source_target_pairs={{0,6},{1,7},{2,4},{3,5},{4,2},{5,3},{6,0},{7,1},{8,14},{9,15},{10,... | collective-permute-start | bytes 958472 | tf_op jit(solution)/shard_map/ppermute | solution.py:382
  368.3 29.6 %all-to-all-start.5 = ((bf16[4,112,576]{2,1,0:T(8,128)(2,1)}), bf16[4,112,576]{2,1,0:T(8,128)(2,1)S(1)}, u32[]{:S(2)}, u32[]{:S(2)}) async-start(bf16[4,112,576]{2,1,0:T(8,128)(2,1)} %fusion.8), calls=%async_computation.5 | async-start | bytes 1146880 | tf_op jit(solution)/shard_map/all_to_all | solution.py:387
  371.8 15.3 %collective-permute-start.43 = (bf16[4,104,576]{2,1,0:T(8,128)(2,1)}, bf16[4,104,576]{2,1,0:T(8,128)(2,1)S(1)}, u32[]{:S(2)}, u32[]{:S(2)}) collective-permute-start(bf16[4,104,576]{2,1,0:T(8,128)(2,1)} %get-tuple-element.332), channel_id=1, source_target_pairs={{0,2},{2,0},{1,3},{3,1},{4,6},{6,4},{5,7},{7,5},{8,10},{10,8},{9,1... | collective-permute-start | bytes 1437704 | tf_op jit(solution)/shard_map/ppermute | solution.py:38
  373.6 24.4 %collective-permute-start.44 = (bf16[4,104,576]{2,1,0:T(8,128)(2,1)}, bf16[4,104,576]{2,1,0:T(8,128)(2,1)S(1)}, u32[]{:S(2)}, u32[]{:S(2)}) collective-permute-start(bf16[4,104,576]{2,1,0:T(8,128)(2,1)} %get-tuple-element.333), channel_id=1, source_target_pairs={{0,4},{4,0},{8,12},{12,8},{16,20},{20,16},{24,28},{28,24},{1,5},{5... | collective-permute-start | bytes 1437704 | tf_op jit(solution)/shard_map/ppermute | solution.py:43
  374.0 24.8 %collective-permute-start.46 = (bf16[4,104,576]{2,1,0:T(8,128)(2,1)}, bf16[4,104,576]{2,1,0:T(8,128)(2,1)S(1)}, u32[]{:S(2)}, u32[]{:S(2)}) collective-permute-start(bf16[4,104,576]{2,1,0:T(8,128)(2,1)} %get-tuple-element.339), channel_id=1, source_target_pairs={{0,6},{1,7},{2,4},{3,5},{4,2},{5,3},{6,0},{7,1},{8,14},{9,15},{10,... | collective-permute-start | bytes 1437704 | tf_op jit(solution)/shard_map/ppermute | solution.py:382
  375.4 23.4 %copy-start.52 = (bf16[4,104,576]{2,1,0:T(8,128)(2,1)S(1)}, bf16[4,104,576]{2,1,0:T(8,128)(2,1)}, u32[]{:S(2)}) copy-start(bf16[4,104,576]{2,1,0:T(8,128)(2,1)} %get-tuple-element.336) | copy-start | bytes 1437700
  399.9 15.7 %collective-permute-start.47 = (bf16[512,768]{1,0:T(8,128)(2,1)S(1)}, bf16[512,768]{1,0:T(8,128)(2,1)S(1)}, u32[]{:S(2)}, u32[]{:S(2)}) collective-permute-start(bf16[512,768]{1,0:T(8,128)(2,1)S(1)} %copy-done.16), channel_id=1, source_target_pairs={{0,2},{2,0},{1,3},{3,1},{4,6},{6,4},{5,7},{7,5},{8,10},{10,8},{9,1... | collective-permute-start | bytes 2359304 | tf_op jit(solution)/shard_map/ppermute | solution.py:38
  403.0 22.5 %all-to-all-start.6 = ((bf16[4,104,960]{2,1,0:T(8,128)(2,1)}), bf16[4,104,960]{2,1,0:T(8,128)(2,1)}, u32[]{:S(2)}, u32[]{:S(2)}) async-start(bf16[4,104,960]{2,1,0:T(8,128)(2,1)} %pad_maximum_fusion.1), calls=%async_computation.6 | async-start | bytes 1703936 | tf_op jit(solution)/shard_map/all_to_all | solution.py:387
  407.8 12.4 %collective-permute-start.45 = (bf16[512,768]{1,0:T(8,128)(2,1)}, bf16[512,768]{1,0:T(8,128)(2,1)}, u32[]{:S(2)}, u32[]{:S(2)}) collective-permute-start(bf16[512,768]{1,0:T(8,128)(2,1)} %get-tuple-element.334), channel_id=1, source_target_pairs={{0,1},{1,0},{2,3},{3,2},{4,5},{5,4},{6,7},{7,6},{8,9},{9,8},{10,11... | collective-permute-start | bytes 2359304 | tf_op jit(solution)/shard_map/ppermute | solution.py:34
  407.8 19.7 %collective-permute-start.48 = (bf16[8,64,768]{2,1,0:T(8,128)(2,1)S(1)}, bf16[8,64,768]{2,1,0:T(8,128)(2,1)S(1)}, u32[]{:S(2)}, u32[]{:S(2)}) collective-permute-start(bf16[8,64,768]{2,1,0:T(8,128)(2,1)S(1)} %bitcast.74), channel_id=1, source_target_pairs={{0,1},{1,0},{2,3},{3,2},{4,5},{5,4},{6,7},{7,6},{8,9},{9,8},{10,11... | collective-permute-start | bytes 2359304 | tf_op jit(solution)/shard_map/ppermute | solution.py:34
  415.6 11.9 %collective-permute-start.49 = (bf16[8,64,768]{2,1,0:T(8,128)(2,1)S(1)}, bf16[8,64,768]{2,1,0:T(8,128)(2,1)S(1)}, u32[]{:S(2)}, u32[]{:S(2)}) collective-permute-start(bf16[8,64,768]{2,1,0:T(8,128)(2,1)S(1)} %bitcast.76), channel_id=1, source_target_pairs={{0,1},{1,0},{2,3},{3,2},{4,5},{5,4},{6,7},{7,6},{8,9},{9,8},{10,11... | collective-permute-start | bytes 2359304 | tf_op jit(solution)/shard_map/ppermute | solution.py:34
  (66 other events, 374.2 us)

commit v2 on v1

--- a/solution.py
+++ b/solution.py
@@ -464,17 +464,17 @@
     return mm(eye, ref[...].astype(BF), NT).astype(BF)
 
 
-def pack_rest_kernel(ck_ref, cv_ref, cq_ref, so_ref, co_ref, ex_ref, sh_ref, attn_ref, ex_out, sh_out):
+def pack_rest_kernel(ck_ref, cv_ref, cq_ref, so_ref, co_ref, ex_ref, sh_ref, next_ref, sh_out):
     cols = ck_ref.shape[1]
+    wide = ex_ref.shape[1]
     parts = [ref[...].astype(BF) for ref in (ck_ref, cv_ref, cq_ref)]
     parts += [turned(so_ref), turned(co_ref)]
     expand = ex_ref[...].astype(BF)
-    shrink = sh_ref[...].astype(BF)
-    for copy in range(attn_ref.shape[0]):
+    for copy in range(next_ref.shape[0]):
+        next_ref[copy, :, :wide] = expand
         for i, low in enumerate(parts):
-            attn_ref[copy, :, i * cols : (i + 1) * cols] = low
-        ex_out[copy] = expand
-    sh_out[...] = shrink
+            next_ref[copy, :, wide + i * cols : wide + (i + 1) * cols] = low
+    sh_out[...] = sh_ref[...].astype(BF)
 
 
 def self_forward_kernel(
@@ -1343,6 +1343,10 @@
     fetch_table = fetch_table.reshape(-1).astype(jnp.int32)
     part_mine, part_send = fetch(fetch_table, bank.reshape(seq_count * local_blocks, BLK, width))
 
+    part_got = swap_core(part_send)
+    part_away = part_mine[1] + part_got[1]
+    part_back = swap_x(part_away)
+
     self_leaf = call(
         pack_self_kernel,
         struct((outer, depth, 3 * head_cols), BF),
@@ -1366,19 +1370,18 @@
             bias_two[:, head_cols:two].reshape(-1),
         ]
     )
-    attn_leaf, expand_leaf, shrink_leaf = call(
+    next_leaf, shrink_leaf = call(
         pack_rest_kernel,
         [
-            struct((outer, depth, attn_cols), BF),
-            struct((outer, depth, hidden_cols), BF),
+            struct((outer, depth, hidden_cols + attn_cols), BF),
             struct((depth, hidden_cols), BF),
         ],
         [
-            gate(crossk_weight, self_leaf), crossv_weight, crossq_weight, selfo_weight,
+            gate(crossk_weight, self_leaf, part_away), crossv_weight, crossq_weight, selfo_weight,
             crosso_weight, expand_weight, shrink_weight.T,
         ],
         [VM] * 7,
-        [VM] * 3,
+        [VM] * 2,
         name="pack_rest",
     )
     tokens_oth = swap_core(tokens)
@@ -1394,32 +1397,28 @@
     my_prefix = lax.dynamic_index_in_dim(prefix, chip, 0, keepdims=False)
     attn_info = jnp.stack([core, my_prefix]).astype(jnp.int32)
 
-    part_got = swap_core(part_send)
-    self_leaf, attn_leaf = lax.optimization_barrier((self_leaf, attn_leaf))
     self_z = outer_exchange(self_leaf)
-    shrink_leaf = gate(shrink_leaf, bias_two)
+
+    self_z, self_bias, vecs, first_vecs, cq_bias, cv_bias, next_leaf, attn_info, tokens_oth, part_back = (
+        lax.optimization_barrier(
+            (self_z, self_bias, vecs, first_vecs, cq_bias, cv_bias, next_leaf, attn_info, tokens_oth, part_back)
+        )
+    )
+    self_near, self_away, self_both = swap_x(self_z), swap_dp(self_z, 1), swap_both(self_z)
+    next_z = outer_exchange(next_leaf)
+
+    shrink_leaf = gate(shrink_leaf, self_near)
     shrink_x, shrink_y = swap_x(shrink_leaf), swap_dp(shrink_leaf, 1)
     shrink_xy = swap_both(shrink_leaf)
     shrink_pack = plane_copies(info, shrink_leaf, shrink_x, shrink_y, shrink_xy)
-
     (
-        self_z, self_bias, vecs, first_vecs, cq_bias, cv_bias, attn_leaf, attn_info,
-        part_got, tokens_oth, shrink_pack,
+        next_z, tokens_in, self_near, self_away, self_both, shrink_pack, part_got,
     ) = lax.optimization_barrier(
-        (
-            self_z, self_bias, vecs, first_vecs, cq_bias, cv_bias, attn_leaf, attn_info,
-            part_got, tokens_oth, shrink_pack,
-        )
-    )
-    self_near, self_away, self_both = swap_x(self_z), swap_dp(self_z, 1), swap_both(self_z)
-    attn_z = outer_exchange(attn_leaf)
-    part_got, self_near = lax.optimization_barrier((part_got, self_near))
-    part_back = swap_x(part_mine[1] + part_got[1])
-    attn_z, tokens_in, self_near, self_away, self_both = lax.optimization_barrier(
-        (attn_z, tokens, self_near, self_away, self_both)
-    )
+        (next_z, tokens, self_near, self_away, self_both, shrink_pack, part_got)
+    )
+    expand_z, attn_z = next_z[..., :hidden_cols], next_z[..., hidden_cols:]
+    shrink_z = outer_exchange(gate(shrink_pack, next_z))
     attn_x, attn_y, attn_xy = swap_x(attn_z), swap_dp(attn_z, 1), swap_both(attn_z)
-    expand_z = outer_exchange(gate(expand_leaf, attn_z))
 
     qkv, self_mat, self_own, self_send, self_lse = self_forward(
         jnp.concatenate([info, attn_info]),
@@ -1429,14 +1428,16 @@
         (self_z, self_near, self_away, self_both),
     )
     self_got = swap_core(self_send)
-    attn_x, attn_y, shrink_pack = lax.optimization_barrier((attn_x, attn_y, shrink_pack, self_own))[:3]
-    shrink_pack, expand_z = lax.optimization_barrier((shrink_pack, expand_z))
-    shrink_z = outer_exchange(shrink_pack)
-    expand_x, expand_y, expand_xy = swap_x(expand_z), swap_dp(expand_z, 1), swap_both(expand_z)
-
+    attn_x, attn_y, attn_xy, self_got = lax.optimization_barrier(
+        (attn_x, attn_y, attn_xy, self_got, self_own)
+    )[:4]
     attn_own = (attn_z, attn_y, attn_x, attn_xy)
     attn_oth = tuple(swap_core(piece) for piece in attn_own)
+    attn_oth, expand_z = lax.optimization_barrier((attn_oth, expand_z))
+    expand_x, expand_y = swap_x(expand_z), swap_dp(expand_z, 1)
     cross_kv, cross_q, self_o, cross_o = assemble(info, attn_own + attn_oth)
+    cross_kv, expand_x, expand_y = lax.optimization_barrier((cross_kv, expand_x, expand_y))
+    expand_xy = swap_both(expand_z)
     fetched, kv_own = project_kv(
         (part_mine[0] + part_got[0]).reshape(slots * BLK, width),
         part_back.reshape(slots * BLK, width),
@@ -1456,13 +1457,13 @@
     )
 
     queries, kv_oth = lax.optimization_barrier((queries, kv_oth))
-    queries, expand_x, expand_y, shrink_z = lax.optimization_barrier(
-        (queries, expand_x, expand_y, shrink_z)
-    )
+    queries, shrink_z = lax.optimization_barrier((queries, shrink_z))
     mixed_two, cross_lse = cross_forward(queries, kv_own, kv_oth)
 
+    expand_oth = tuple(swap_core(piece) for piece in (expand_z, expand_y, expand_x))
+    expand_xy, expand_oth, mixed_two = lax.optimization_barrier((expand_xy, expand_oth, mixed_two))
     expand_own = (expand_z, expand_y, expand_x, expand_xy)
-    expand_oth = tuple(swap_core(piece) for piece in expand_own)
+    expand_oth = expand_oth + (swap_core(expand_xy),)
     (
         out_act, second_in, cross_low, cross_grad,
         feed_keep, feed_send,

time: 440 us -> 420 us (0.955)
  starting transfers between devices: 71.5 us -> 64.4 us
  waiting for transfers between devices: 124 us -> 117 us
    ppermute x7, waiting for transfers between devices: 41.7 us -> 11.4 us  [swap_both(): return lax.ppermute(value, ('dp', 'tensor'), pairs)]
    ppermute x12, waiting for transfers between devices: 31.4 us -> 40.5 us  [swap_x(): return lax.ppermute(value, 'tensor', X_SWAP)]
    ppermute x22, waiting for transfers between devices: 1.48 us -> 8.1 us  [swap_core(): return lax.ppermute(value, 'tensor', CORE_SWAP)]
    unnamed x146 -> x140, local copies, waits for them, and re-layouts: 19.3 us -> 12.8 us
    all_to_all x7 -> x6, starting transfers between devices: 34 us -> 27.5 us  [outer_exchange(): lax.all_to_all(value, 'dp', 0, 0, axis_index_groups=groups, tiled=True)]
    ppermute x9, waiting for transfers between devices: 39.8 us -> 44.3 us  [swap_dp(): lax.ppermute(value, 'dp', tuple(((i, i ^ bit) for i in range(count))))]
    all_to_all x7 -> x6, waiting for transfers between devices: 9.97 us -> 12.9 us  [outer_exchange(): lax.all_to_all(value, 'dp', 0, 0, axis_index_groups=groups, tiled=True)]
  transfers between devices with their start and end apart: 57 -> 56, of which waited for: 22 -> 28; matrix products, arithmetic and copies ran while one was open for 6% -> 6% of each run, Pallas kernels for 30% -> 32%
where the time goes in v2:
time: 420 us; the launch traced here: 416 us
  Pallas kernels  181 us (43%)
  waiting for transfers between devices  117 us (28%)
  starting transfers between devices  64.4 us (15%)
  other arithmetic  28.8 us (7%)
  local copies, waits for them, and re-layouts  22.9 us (5%)
    pallas_call x15, Pallas kernels, call(): pl.pallas_call(kernel, out_shape=out_shape, in_specs=in_specs, out_specs=...  96.6 us
    ppermute x9, waiting for transfers between devices, swap_dp(): lax.ppermute(value, 'dp', tuple(((i, i ^ bit) for i in range(count))))  44.3 us
    ppermute x12, waiting for transfers between devices, swap_x(): return lax.ppermute(value, 'tensor', X_SWAP)  40.5 us
    all_to_all x6, starting transfers between devices, outer_exchange(): lax.all_to_all(value, 'dp', 0, 0, axis_index_groups=groups, tiled=True)  27.5 us
    pallas_call x1, Pallas kernels, cross_first_backward(): pl.pallas_call(functools.partial(cross_first_kernel, start=start, count=c...  22.1 us
    pallas_call x2, Pallas kernels, self_backward(): pl.pallas_call(self_bwd_kernel, grid_spec=pltpu.PrefetchScalarGridSpec(nu...  20.4 us
    pallas_call x1, Pallas kernels, cross_forward(): pl.pallas_call(cross_fwd_kernel, grid=(pairs,), in_specs=[whole, whole, t...  13.9 us
    ppermute x12, starting transfers between devices, swap_x(): return lax.ppermute(value, 'tensor', X_SWAP)  13.7 us
  transfers between devices with their start and end apart: 56, of which 28 were waited for; matrix products, arithmetic and copies ran while one was open for 6% of the time, Pallas kernels for 32%

profile of v2, /device:TPU:0, one launch (start us, length us, event | category | flops | bytes accessed | tf_op | source)
XLA Modules:
  0.0 415.6 jit_solution(16784517382535170460)
XLA Ops:
  2.9 4.3 %fetch.1 = (bf16[16,64,768]{2,1,0:T(8,128)(2,1)}, bf16[16,64,768]{2,1,0:T(8,128)(2,1)}) custom-call(s32[32]{0:T(128)} %select_n.75.table, bf16[32,64,768]{2,1,0:T(8,128)(2,1)} %bitcast.87), custom_call_target="tpu_custom_call" | custom-call | flops 1000 | bytes 1000 | tf_op jit(solution)/shard_map/fetch/pallas_call | solution.py:415
  7.9 2.4 collective-permute-start
  10.5 1.8 pack_self.1
  12.3 5.0 %all-to-all-start = ((bf16[4,96,576]{2,1,0:T(8,128)(2,1)}), bf16[4,96,576]{2,1,0:T(8,128)(2,1)S(1)}, u32[]{:S(2)}, u32[]{:S(2)}) async-start(bf16[4,96,576]{2,1,0:T(8,128)(2,1)} %pack_self.1), calls=%async_computation | async-start | bytes 983040 | tf_op jit(solution)/shard_map/all_to_all | solution.py:387
  19.5 2.9 fusion.20
  27.2 2.6 pack_rest.1
  29.8 1.8 all-to-all-done.w_ref
  31.6 10.5 %collective-permute-done.4 = bf16[8,64,768]{2,1,0:T(8,128)(2,1)S(1)} collective-permute-done((bf16[8,64,768]{2,1,0:T(8,128)(2,1)}, bf16[8,64,768]{2,1,0:T(8,128)(2,1)S(1)}, u32[]{:S(2)}, u32[]{:S(2)}) %collective-permute-start.4) | collective-permute-done | bytes 786464 | tf_op jit(solution)/shard_map/ppermute | solution.py:38
  43.0 4.8 %all-to-all-start.1 = ((bf16[4,96,1728]{2,1,0:T(8,128)(2,1)}), bf16[4,96,1728]{2,1,0:T(8,128)(2,1)}, u32[]{:S(2)}, u32[]{:S(2)}) async-start(bf16[4,96,1728]{2,1,0:T(8,128)(2,1)} %get-tuple-element.210), calls=%async_computation.1 | async-start | bytes 2752512 | tf_op jit(solution)/shard_map/all_to_all | solution.py:387
  48.4 2.5 collective-permute-start.7
  51.3 10.7 %collective-permute-done.5.wx_ref = bf16[4,96,576]{2,1,0:T(8,128)(2,1)S(1)} collective-permute-done((bf16[4,96,576]{2,1,0:T(8,128)(2,1)S(1)}, bf16[4,96,576]{2,1,0:T(8,128)(2,1)S(1)}, u32[]{:S(2)}, u32[]{:S(2)}) %collective-permute-start.5) | collective-permute-done | bytes 442400 | tf_op jit(solution)/shard_map/ppermute | solution.py:38
  61.9 1.6 collective-permute-start.10
  64.0 1.4 collective-permute-start.8
  66.0 10.2 %collective-permute-done.10.xy_ref = bf16[96,768]{1,0:T(8,128)(2,1)} collective-permute-done((bf16[96,768]{1,0:T(8,128)(2,1)}, bf16[96,768]{1,0:T(8,128)(2,1)}, u32[]{:S(2)}, u32[]{:S(2)}) %collective-permute-start.10) | collective-permute-done | bytes 147488 | tf_op jit(solution)/shard_map/ppermute | solution.py:382
  76.2 2.9 collective-permute-done.9.y_ref
  79.2 2.7 plane_copies.1
  81.9 2.2 slice.138.refs_0_
  84.6 1.5 collective-permute-start.13
  86.2 1.5 collective-permute-start.12
  87.7 4.9 %all-to-all-start.2 = ((bf16[4,2,2,96,768]{4,3,2,1,0:T(8,128)(2,1)}), bf16[4,2,2,96,768]{4,3,2,1,0:T(8,128)(2,1)}, u32[]{:S(2)}, u32[]{:S(2)}) async-start(bf16[4,2,2,96,768]{4,3,2,1,0:T(8,128)(2,1)} %plane_copies.1), calls=%async_computation.2 | async-start | bytes 4718592 | tf_op jit(solution)/shard_map/all_to_all | solution.py:387
  93.7 12.9 %self_fwd.1 = (bf16[2,512,1152]{2,1,0:T(8,128)(2,1)}, bf16[768,1152]{1,0:T(8,128)(2,1)S(1)}, bf16[512,384]{1,0:T(8,128)(2,1)S(1)}, bf16[512,384]{1,0:T(8,128)(2,1)S(1)}, f32[3,2,2,512]{3,2,1,0:T(2,128)S(1)}) custom-call(s32[5]{0:T(128)S(1)} %pad_add_fusion.2.info, bf16[512,768]{1,0:T(8,128)(2,1)S(1)} %copy-done.5, ...), custom_call_target="tpu_custom_call" | custom-call | flops 1000 | bytes 1000 | tf_op jit(solution)/shard_map/self_fwd/pallas_call | solution.py:568
  108.4 11.1 %collective-permute-done.13.refs_1_ = bf16[4,96,960]{2,1,0:T(8,128)(2,1)} collective-permute-done((bf16[4,96,960]{2,1,0:T(8,128)(2,1)}, bf16[4,96,960]{2,1,0:T(8,128)(2,1)}, u32[]{:S(2)}, u32[]{:S(2)}) %collective-permute-start.13) | collective-permute-done | bytes 737312 | tf_op jit(solution)/shard_map/ppermute | solution.py:43
  128.5 7.9 %assemble.1 = (bf16[4,2,96,1536]{3,2,1,0:T(8,128)(2,1)}, bf16[4,2,96,768]{3,2,1,0:T(8,128)(2,1)}, bf16[4,2,96,768]{3,2,1,0:T(8,128)(2,1)}, bf16[4,2,96,768]{3,2,1,0:T(8,128)(2,1)}) custom-call(s32[3]{0:T(128)} %pad_add_fusion.info, bf16[4,96,960]{2,1,0:T(8,128)(2,1)} %slice.138.refs_0_, bf16[4,96,960]{2,1,0:T(8,128)(2,1)} %collective-permute-done.13.refs_1_, ...), custom_call_target="tpu_custom_call" | custom-call | flops 1000 | bytes 1000 | tf_op jit(solution)/shard_map/assemble/pallas_call | solution.py:415
  136.4 3.4 collective-permute-done.22.e1
  140.2 4.9 %project_kv.1 = (bf16[512,768]{1,0:T(8,128)(2,1)}, bf16[512,1536]{1,0:T(8,128)(2,1)}) custom-call(bf16[512,768]{1,0:T(8,128)(2,1)} %bitcast_add_fusion.1.keep_ref, bf16[512,768]{1,0:T(8,128)(2,1)} %bitcast.89, bf16[768,1536]{1,0:T(8,128)(2,1)} %bitcast.80, f32[1,768]{1,0:T(1,128)} %reshape_reshape.7.bias_ref), custom_call_target="tpu_custom_call" | custom-call | flops 1000 | bytes 1000 | tf_op jit(solution)/shard_map/project_kv/pallas_call | solution.py:415
  145.2 5.7 %first_forward.1 = (f32[512,768]{1,0:T(8,128)}, f32[512,768]{1,0:T(8,128)}, bf16[512,768]{1,0:T(8,128)(2,1)}, bf16[512,768]{1,0:T(8,128)(2,1)}, bf16[512,768]{1,0:T(8,128)(2,1)}) custom-call(bf16[512,768]{1,0:T(8,128)(2,1)} %own_ref.2, bf16[512,384]{1,0:T(8,128)(2,1)} %copy-done.9, bf16[512,384]{1,0:T(8,128)(2,1)} %copy-done.52, bf16[768,768]{1,0:T(8,128)(2,1)} %bitcast.85, ...), custom_call_target="tpu_custom_call" | custom-call | flops 1000 | bytes 1000 | tf_op jit(solution)/shard_map/first_forward/pallas_call | solution.py:415
  151.6 1.7 collective-permute-start.19
  154.9 13.9 %cross_fwd.1 = (bf16[512,768]{1,0:T(8,128)(2,1)S(1)}, f32[6,2,512]{2,1,0:T(2,128)S(1)}) custom-call(bf16[512,768]{1,0:T(8,128)(2,1)S(1)} %copy-done.6, bf16[512,1536]{1,0:T(8,128)(2,1)S(1)} %copy-done, bf16[512,1536]{1,0:T(8,128)(2,1)S(1)} %collective-permute-done.25.kb_ref.vb_ref, bf16[512,1536]{1,0:T(8,128)(2,1)S(1)} %copy-done, ...), custom_call_target="tpu_custom_call" | custom-call | flops 1000 | bytes 1000 | tf_op jit(solution)/shard_map/cross_fwd/pallas_call | solution.py:187
  170.0 1.8 collective-permute-done.26.e7
  171.9 1.4 copy-done.27
  173.5 32.8 %feed.1 = (bf16[512,768]{1,0:T(8,128)(2,1)}, f32[512,768]{1,0:T(8,128)}, bf16[512,768]{1,0:T(8,128)(2,1)}, bf16[512,768]{1,0:T(8,128)(2,1)}, bf16[2,2,4,104,1536...) custom-call(s32[3]{0:T(128)} %pad_add_fusion.info, bf16[512,768]{1,0:T(8,128)(2,1)} %copy-done.3, ...), custom_call_target="tpu_custom_call" | custom-call | flops 1000 | bytes 1000 | tf_op jit(solution)/shard_map/feed/pallas_call | solution.py:415
  207.6 10.0 %cross_bwd.1 = (bf16[512,768]{1,0:T(8,128)(2,1)S(1)}, bf16[2,512,768]{2,1,0:T(8,128)(2,1)S(1)}, bf16[2,512,768]{2,1,0:T(8,128)(2,1)}) custom-call(bf16[512,768]{1,0:T(8,128)(2,1)S(1)} %copy-done.7, bf16[512,1536]{1,0:T(8,128)(2,1)} %get-tuple-element.247.ka_ref.va_ref, bf16[512,1536]{1,0:T(8,128)(2,1)} %copy-done.1, ...), custom_call_target="tpu_custom_call" | custom-call | flops 1000 | bytes 1000 | tf_op jit(solution)/shard_map/cross_bwd/pallas_call | solution.py:236
  217.6 3.4 fusion.1
  221.0 2.7 fusion
  225.5 22.1 %cross_first.1 = (bf16[512,768]{1,0:T(8,128)(2,1)S(1)}, bf16[2,512,768]{2,1,0:T(8,128)(2,1)}, bf16[2,512,768]{2,1,0:T(8,128)(2,1)}, f32[512,768]{1,0:T(8,128)}, ...) custom-call(bf16[512,768]{1,0:T(8,128)(2,1)S(1)} %copy-done.7, ...), custom_call_target="tpu_custom_call", output_to_operand_aliasing={{1}: (14, {}), {2}: (15, {})} | custom-call | flops 1000 | bytes 1000 | tf_op jit(solution)/shard_map/cross_first/pallas_call | solution.py:328
  247.6 6.6 %collective-permute-done.29 = bf16[2,4,104,768]{3,2,1,0:T(8,128)(2,1)S(1)} collective-permute-done((bf16[2,4,104,768]{3,2,1,0:T(8,128)(2,1)}, bf16[2,4,104,768]{3,2,1,0:T(8,128)(2,1)S(1)}, u32[]{:S(2)}, u32[]{:S(2)}) %collective-permute-start.29) | collective-permute-done | bytes 1277984 | tf_op jit(solution)/shard_map/ppermute | solution.py:38
  255.5 2.9 fusion.6
  259.3 7.2 %query_grads.1 = (bf16[2,2,4,112,576]{4,3,2,1,0:T(8,128)(2,1)}, bf16[2,2,4,112,576]{4,3,2,1,0:T(8,128)(2,1)}) custom-call(s32[3]{0:T(128)} %pad_add_fusion.info, bf16[512,768]{1,0:T(8,128)(2,1)} %get-tuple-element.280.h1_ref, bf16[512,768]{1,0:T(8,128)(2,1)} %copy-done.17, bf16[512,768]{1,0:T(8,128)(2,1)} %copy-done.18, ...), custom_call_target="tpu_custom_call" | custom-call | flops 1000 | bytes 1000 | tf_op jit(solution)/shard_map/query_grads/pallas_call | solution.py:415
  268.5 7.5 %key_grads.1 = (bf16[2,2,4,104,384]{4,3,2,1,0:T(8,128)(2,1)}, bf16[2,2,4,104,384]{4,3,2,1,0:T(8,128)(2,1)}, bf16[512,768]{1,0:T(8,128)(2,1)}) custom-call(s32[3]{0:T(128)} %pad_add_fusion.info, bf16[512,768]{1,0:T(8,128)(2,1)} %get-tuple-element.296.fet_ref, bf16[2,512,768]{2,1,0:T(8,128)(2,1)} %get-tuple-element.299.own_ref, ...), custom_call_target="tpu_custom_call" | custom-call | flops 1000 | bytes 1000 | tf_op jit(solution)/shard_map/key_grads/pallas_call | solution.py:415
  277.4 6.2 %collective-permute-done.34 = bf16[4,104,768]{2,1,0:T(8,128)(2,1)} collective-permute-done((bf16[4,104,768]{2,1,0:T(8,128)(2,1)}, bf16[4,104,768]{2,1,0:T(8,128)(2,1)}, u32[]{:S(2)}, u32[]{:S(2)}) %collective-permute-start.34) | collective-permute-done | bytes 639008 | tf_op jit(solution)/shard_map/ppermute | solution.py:43
  287.6 13.1 %self_bwd.2 = (bf16[3,2,512,384]{3,2,1,0:T(8,128)(2,1)S(1)}, f32[3,8,128]{2,1,0:T(8,128)S(1)}) custom-call(s32[2]{0:T(128)S(1)} %pad_add_fusion.1.info, bf16[2,512,1152]{2,1,0:T(8,128)(2,1)} %get-tuple-element.264.q_ref.k_ref.v_ref, bf16[2,512,1152]{2,1,0:T(8,128)(2,1)} %get-tuple-element.264.q_ref.k_ref.v_ref, ...), custom_call_target="tpu_custom_call" | custom-call | flops 1000 | bytes 1000 | tf_op jit(solution)/shard_map/self_bwd/pallas_call | solution.py:122
  300.8 2.7 fusion.5
  304.7 6.6 %collective-permute-done.38 = bf16[4,112,576]{2,1,0:T(8,128)(2,1)S(1)} collective-permute-done((bf16[4,112,576]{2,1,0:T(8,128)(2,1)S(1)}, bf16[4,112,576]{2,1,0:T(8,128)(2,1)S(1)}, u32[]{:S(2)}, u32[]{:S(2)}) %collective-permute-start.38) | collective-permute-done | bytes 516128 | tf_op jit(solution)/shard_map/ppermute | solution.py:43
  312.5 2.4 fusion.8
  316.4 4.5 %all-to-all-start.3 = ((bf16[4,104,1536]{2,1,0:T(8,128)(2,1)}), bf16[4,104,1536]{2,1,0:T(8,128)(2,1)}, u32[]{:S(2)}, u32[]{:S(2)}) async-start(bf16[4,104,1536]{2,1,0:T(8,128)(2,1)} %pad_maximum_fusion), calls=%async_computation.3 | async-start | bytes 2555904 | tf_op jit(solution)/shard_map/all_to_all | solution.py:387
  326.2 7.2 %self_bwd.3 = (bf16[3,2,512,384]{3,2,1,0:T(8,128)(2,1)S(1)}, f32[3,8,128]{2,1,0:T(8,128)S(1)}) custom-call(s32[2]{0:T(128)S(1)} %pad_add_fusion.1.info, bf16[2,512,1152]{2,1,0:T(8,128)(2,1)} %get-tuple-element.264.q_ref.k_ref.v_ref, bf16[2,512,1152]{2,1,0:T(8,128)(2,1)} %get-tuple-element.264.q_ref.k_ref.v_ref, ...), custom_call_target="tpu_custom_call", output_to_operand_aliasing={{0}: (9, {}), {1}: (10, {})} | custom-call | flops 1000 | bytes 1000 | tf_op jit(solution)/shard_map/self_bwd/pallas_call | solution.py:122
  333.5 1.4 copy-done.2
  334.9 3.1 collective-permute-done.41
  338.0 6.2 %self_grads.1 = (bf16[4,104,576]{2,1,0:T(8,128)(2,1)}, bf16[4,104,576]{2,1,0:T(8,128)(2,1)}, bf16[4,104,576]{2,1,0:T(8,128)(2,1)}, bf16[4,104,576]{2,1,0:T(8,128)(2,1)}) custom-call(s32[3]{0:T(128)} %pad_add_fusion.info, bf16[512,768]{1,0:T(8,128)(2,1)} %own_ref.2, bf16[512,768]{1,0:T(8,128)(2,1)} %copy-done.11, bf16[3,2,512,384]{3,2,1,0:T(8,128)(2,1)} %copy-done.2), custom_call_target="tpu_custom_call" | custom-call | flops 1000 | bytes 1000 | tf_op jit(solution)/shard_map/self_grads/pallas_call | solution.py:415
  344.2 7.5 %all-to-all-done.3.in_ref = bf16[4,104,1536]{2,1,0:T(8,128)(2,1)} async-done(((bf16[4,104,1536]{2,1,0:T(8,128)(2,1)}), bf16[4,104,1536]{2,1,0:T(8,128)(2,1)}, u32[]{:S(2)}, u32[]{:S(2)}) %all-to-all-start.3) | async-done | bytes 1277984 | tf_op jit(solution)/shard_map/all_to_all | solution.py:387
  351.7 3.5 all-to-all-start.4
  357.1 1.6 collective-permute-start.46
  358.8 6.6 %self_back.1 = (f32[512,768]{1,0:T(8,128)}, bf16[512,768]{1,0:T(8,128)(2,1)}) custom-call(bf16[3,2,512,384]{3,2,1,0:T(8,128)(2,1)} %copy-done.2, bf16[768,1152]{1,0:T(8,128)(2,1)} %copy-done.13, f32[512,768]{1,0:T(8,128)} %get-tuple-element.337.first_ref), custom_call_target="tpu_custom_call" | custom-call | flops 1000 | bytes 1000 | tf_op jit(solution)/shard_map/self_back/pallas_call | solution.py:415
  365.4 5.1 %collective-permute-done.43 = bf16[4,104,576]{2,1,0:T(8,128)(2,1)S(1)} collective-permute-done((bf16[4,104,576]{2,1,0:T(8,128)(2,1)}, bf16[4,104,576]{2,1,0:T(8,128)(2,1)S(1)}, u32[]{:S(2)}, u32[]{:S(2)}) %collective-permute-start.43) | collective-permute-done | bytes 479264 | tf_op jit(solution)/shard_map/ppermute | solution.py:38
  370.5 10.2 %collective-permute-done.44 = bf16[4,104,576]{2,1,0:T(8,128)(2,1)S(1)} collective-permute-done((bf16[4,104,576]{2,1,0:T(8,128)(2,1)}, bf16[4,104,576]{2,1,0:T(8,128)(2,1)S(1)}, u32[]{:S(2)}, u32[]{:S(2)}) %collective-permute-start.44) | collective-permute-done | bytes 479264 | tf_op jit(solution)/shard_map/ppermute | solution.py:43
  383.7 1.6 fusion.10
  386.4 4.8 %all-to-all-start.5 = ((bf16[4,104,960]{2,1,0:T(8,128)(2,1)}), bf16[4,104,960]{2,1,0:T(8,128)(2,1)}, u32[]{:S(2)}, u32[]{:S(2)}) async-start(bf16[4,104,960]{2,1,0:T(8,128)(2,1)} %pad_maximum_fusion.1), calls=%async_computation.5 | async-start | bytes 1703936 | tf_op jit(solution)/shard_map/all_to_all | solution.py:387
  391.7 6.5 %collective-permute-done.47 = bf16[512,768]{1,0:T(8,128)(2,1)S(1)} collective-permute-done((bf16[512,768]{1,0:T(8,128)(2,1)S(1)}, bf16[512,768]{1,0:T(8,128)(2,1)S(1)}, u32[]{:S(2)}, u32[]{:S(2)}) %collective-permute-start.47) | collective-permute-done | bytes 786464 | tf_op jit(solution)/shard_map/ppermute | solution.py:38
  398.6 2.3 sum_feed.1
  400.9 1.9 sum_query.1
  402.8 2.2 add_convert_fusion.2
  405.0 3.5 all-to-all-done.5.in_ref
  408.5 2.0 sum_cols.1
  410.6 4.8 %scatter.1 = f32[32,64,768]{2,1,0:T(8,128)} custom-call(s32[32]{0:T(128)S(1)} %reshape.389.table, bf16[8,64,768]{2,1,0:T(8,128)(2,1)S(1)} %bitcast.77, bf16[8,64,768]{2,1,0:T(8,128)(2,1)S(1)} %bitcast.79, bf16[8,64,768]{2,1,0:T(8,128)(2,1)S(1)} %collective-permute-done.48.c_ref, bf16[8,64,768]{2,1,0:T(8,128)(2,1)S(1)} %collective-permute-done.49.d_ref), custom_call_target="tpu_custom_call" | custom-call | flops 1000 | bytes 1000 | tf_op jit(solution)/shard_map/scatter/pallas_call | solution.py:1185
  (269 shorter events, 57.9 us)
Async XLA Ops:
  7.3 12.2 %collective-permute-start.2 = (bf16[2,8,64,768]{3,2,1,0:T(8,128)(2,1)}, bf16[2,8,64,768]{3,2,1,0:T(8,128)(2,1)}, u32[]{:S(2)}, u32[]{:S(2)}) collective-permute-start(bf16[2,8,64,768]{3,2,1,0:T(8,128)(2,1)} %bitcast.93), channel_id=1, source_target_pairs={{0,1},{1,0},{2,3},{3,2},{4,5},{5,4},{6,7},{7,6},{8,9},{9,8},{10,11... | collective-permute-start | bytes 4718600 | tf_op jit(solution)/shard_map/ppermute | solution.py:34
  7.9 15.1 %collective-permute-start = (f32[1,1536]{1,0:T(1,128)S(1)}, f32[1,1536]{1,0:T(1,128)S(1)}, u32[]{:S(2)}, u32[]{:S(2)}) collective-permute-start(f32[1,1536]{1,0:T(1,128)S(1)} %reshape.383), channel_id=1, source_target_pairs={{0,2},{2,0},{1,3},{3,1},{4,6},{6,4},{5,7},{7,5},{8,10},{10,8},{9,1... | collective-permute-start | bytes 18440 | tf_op jit(solution)/shard_map/ppermute | solution.py:38
  10.3 21.3 %collective-permute-start.3 = (bf16[512,768]{1,0:T(8,128)(2,1)S(1)}, bf16[512,768]{1,0:T(8,128)(2,1)S(1)}, u32[]{:S(2)}, u32[]{:S(2)}) collective-permute-start(bf16[512,768]{1,0:T(8,128)(2,1)S(1)} %copy-done.5), channel_id=1, source_target_pairs={{0,1},{1,0},{2,3},{3,2},{4,5},{5,4},{6,7},{7,6},{8,9},{9,8},{10,11... | collective-permute-start | bytes 2359304 | tf_op jit(solution)/shard_map/ppermute | solution.py:34
  12.3 19.3 %all-to-all-start = ((bf16[4,96,576]{2,1,0:T(8,128)(2,1)}), bf16[4,96,576]{2,1,0:T(8,128)(2,1)S(1)}, u32[]{:S(2)}, u32[]{:S(2)}) async-start(bf16[4,96,576]{2,1,0:T(8,128)(2,1)} %pack_self.1), calls=%async_computation | async-start | bytes 983040 | tf_op jit(solution)/shard_map/all_to_all | solution.py:387
  22.4 19.7 %collective-permute-start.4 = (bf16[8,64,768]{2,1,0:T(8,128)(2,1)}, bf16[8,64,768]{2,1,0:T(8,128)(2,1)S(1)}, u32[]{:S(2)}, u32[]{:S(2)}) collective-permute-start(bf16[8,64,768]{2,1,0:T(8,128)(2,1)} %get-tuple-element.394), channel_id=1, source_target_pairs={{0,2},{2,0},{1,3},{3,1},{4,6},{6,4},{5,7},{7,5},{8,10},{10,8},{9,1... | collective-permute-start | bytes 2359304 | tf_op jit(solution)/shard_map/ppermute | solution.py:38
  23.3 1.2 collective-permute-start.1
  31.6 61.1 %copy-start.11 = (bf16[512,768]{1,0:T(8,128)(2,1)}, bf16[512,768]{1,0:T(8,128)(2,1)S(1)}, u32[]{:S(2)}) copy-start(bf16[512,768]{1,0:T(8,128)(2,1)S(1)} %collective-permute-done.3.oth_ref) | copy-start | bytes 2359300
  43.0 39.0 %all-to-all-start.1 = ((bf16[4,96,1728]{2,1,0:T(8,128)(2,1)}), bf16[4,96,1728]{2,1,0:T(8,128)(2,1)}, u32[]{:S(2)}, u32[]{:S(2)}) async-start(bf16[4,96,1728]{2,1,0:T(8,128)(2,1)} %get-tuple-element.210), calls=%async_computation.1 | async-start | bytes 2752512 | tf_op jit(solution)/shard_map/all_to_all | solution.py:387
  47.8 14.2 %collective-permute-start.5 = (bf16[4,96,576]{2,1,0:T(8,128)(2,1)S(1)}, bf16[4,96,576]{2,1,0:T(8,128)(2,1)S(1)}, u32[]{:S(2)}, u32[]{:S(2)}) collective-permute-start(bf16[4,96,576]{2,1,0:T(8,128)(2,1)S(1)} %all-to-all-done.w_ref), channel_id=1, source_target_pairs={{0,2},{2,0},{1,3},{3,1},{4,6},{6,4},{5,7},{7,5},{8,10},{10,8},{9,1... | collective-permute-start | bytes 1327112 | tf_op jit(solution)/shard_map/ppermute | solution.py:38
  48.4 33.5 %collective-permute-start.7 = (bf16[4,96,576]{2,1,0:T(8,128)(2,1)S(1)}, bf16[4,96,576]{2,1,0:T(8,128)(2,1)S(1)}, u32[]{:S(2)}, u32[]{:S(2)}) collective-permute-start(bf16[4,96,576]{2,1,0:T(8,128)(2,1)S(1)} %all-to-all-done.w_ref), channel_id=1, source_target_pairs={{0,6},{1,7},{2,4},{3,5},{4,2},{5,3},{6,0},{7,1},{8,14},{9,15},{10,... | collective-permute-start | bytes 1327112 | tf_op jit(solution)/shard_map/ppermute | solution.py:382
  50.9 31.1 %collective-permute-start.6 = (bf16[4,96,576]{2,1,0:T(8,128)(2,1)S(1)}, bf16[4,96,576]{2,1,0:T(8,128)(2,1)S(1)}, u32[]{:S(2)}, u32[]{:S(2)}) collective-permute-start(bf16[4,96,576]{2,1,0:T(8,128)(2,1)S(1)} %all-to-all-done.w_ref), channel_id=1, source_target_pairs={{0,4},{4,0},{8,12},{12,8},{16,20},{20,16},{24,28},{28,24},{1,5},{5... | collective-permute-start | bytes 1327112 | tf_op jit(solution)/shard_map/ppermute | solution.py:43
  61.9 14.3 %collective-permute-start.10 = (bf16[96,768]{1,0:T(8,128)(2,1)}, bf16[96,768]{1,0:T(8,128)(2,1)}, u32[]{:S(2)}, u32[]{:S(2)}) collective-permute-start(bf16[96,768]{1,0:T(8,128)(2,1)} %get-tuple-element.213.own_ref), channel_id=1, source_target_pairs={{0,6},{1,7},{2,4},{3,5},{4,2},{5,3},{6,0},{7,1},{8,14},{9,15},{10,... | collective-permute-start | bytes 442376 | tf_op jit(solution)/shard_map/ppermute | solution.py:382
  63.5 15.7 %collective-permute-start.9 = (bf16[96,768]{1,0:T(8,128)(2,1)}, bf16[96,768]{1,0:T(8,128)(2,1)}, u32[]{:S(2)}, u32[]{:S(2)}) collective-permute-start(bf16[96,768]{1,0:T(8,128)(2,1)} %get-tuple-element.213.own_ref), channel_id=1, source_target_pairs={{0,4},{4,0},{8,12},{12,8},{16,20},{20,16},{24,28},{28,24},{1,5},{5... | collective-permute-start | bytes 442376 | tf_op jit(solution)/shard_map/ppermute | solution.py:43
  64.0 15.1 %collective-permute-start.8 = (bf16[96,768]{1,0:T(8,128)(2,1)}, bf16[96,768]{1,0:T(8,128)(2,1)}, u32[]{:S(2)}, u32[]{:S(2)}) collective-permute-start(bf16[96,768]{1,0:T(8,128)(2,1)} %get-tuple-element.213.own_ref), channel_id=1, source_target_pairs={{0,2},{2,0},{1,3},{3,1},{4,6},{6,4},{5,7},{7,5},{8,10},{10,8},{9,1... | collective-permute-start | bytes 442376 | tf_op jit(solution)/shard_map/ppermute | solution.py:38
  84.2 24.2 %collective-permute-start.14 = (bf16[4,96,960]{2,1,0:T(8,128)(2,1)}, bf16[4,96,960]{2,1,0:T(8,128)(2,1)}, u32[]{:S(2)}, u32[]{:S(2)}) collective-permute-start(bf16[4,96,960]{2,1,0:T(8,128)(2,1)} %slice.138.refs_0_), channel_id=1, source_target_pairs={{0,6},{1,7},{2,4},{3,5},{4,2},{5,3},{6,0},{7,1},{8,14},{9,15},{10,... | collective-permute-start | bytes 2211848 | tf_op jit(solution)/shard_map/ppermute | solution.py:382
  84.6 34.9 %collective-permute-start.13 = (bf16[4,96,960]{2,1,0:T(8,128)(2,1)}, bf16[4,96,960]{2,1,0:T(8,128)(2,1)}, u32[]{:S(2)}, u32[]{:S(2)}) collective-permute-start(bf16[4,96,960]{2,1,0:T(8,128)(2,1)} %slice.138.refs_0_), channel_id=1, source_target_pairs={{0,4},{4,0},{8,12},{12,8},{16,20},{20,16},{24,28},{28,24},{1,5},{5... | collective-permute-start | bytes 2211848 | tf_op jit(solution)/shard_map/ppermute | solution.py:43
  86.2 33.3 %collective-permute-start.12 = (bf16[4,96,960]{2,1,0:T(8,128)(2,1)}, bf16[4,96,960]{2,1,0:T(8,128)(2,1)}, u32[]{:S(2)}, u32[]{:S(2)}) collective-permute-start(bf16[4,96,960]{2,1,0:T(8,128)(2,1)} %slice.138.refs_0_), channel_id=1, source_target_pairs={{0,2},{2,0},{1,3},{3,1},{4,6},{6,4},{5,7},{7,5},{8,10},{10,8},{9,1... | collective-permute-start | bytes 2211848 | tf_op jit(solution)/shard_map/ppermute | solution.py:38
  87.7 63.2 %all-to-all-start.2 = ((bf16[4,2,2,96,768]{4,3,2,1,0:T(8,128)(2,1)}), bf16[4,2,2,96,768]{4,3,2,1,0:T(8,128)(2,1)}, u32[]{:S(2)}, u32[]{:S(2)}) async-start(bf16[4,2,2,96,768]{4,3,2,1,0:T(8,128)(2,1)} %plane_copies.1), calls=%async_computation.2 | async-start | bytes 4718592 | tf_op jit(solution)/shard_map/all_to_all | solution.py:387
  106.6 20.8 %copy-start.9 = (bf16[512,384]{1,0:T(8,128)(2,1)}, bf16[512,384]{1,0:T(8,128)(2,1)S(1)}, u32[]{:S(2)}) copy-start(bf16[512,384]{1,0:T(8,128)(2,1)S(1)} %get-tuple-element.223.own_ref.oa_ref) | copy-start | bytes 1179652
  106.6 20.8 %copy-start.13 = (bf16[768,1152]{1,0:T(8,128)(2,1)}, bf16[768,1152]{1,0:T(8,128)(2,1)S(1)}, u32[]{:S(2)}) copy-start(bf16[768,1152]{1,0:T(8,128)(2,1)S(1)} %get-tuple-element.336.mat_ref) | copy-start | bytes 5308420
  106.6 20.8 %copy-start.21 = (f32[3,2,2,512]{3,2,1,0:T(2,128)}, f32[3,2,2,512]{3,2,1,0:T(2,128)S(1)}, u32[]{:S(2)}) copy-start(f32[3,2,2,512]{3,2,1,0:T(2,128)S(1)} %get-tuple-element.265.lse_ref) | copy-start | bytes 73732
  106.6 1.8 collective-permute-start.15
  106.7 14.6 %collective-permute-start.11 = (bf16[4,96,960]{2,1,0:T(8,128)(2,1)}, bf16[4,96,960]{2,1,0:T(8,128)(2,1)S(1)}, u32[]{:S(2)}, u32[]{:S(2)}) collective-permute-start(bf16[4,96,960]{2,1,0:T(8,128)(2,1)} %slice.138.refs_0_), channel_id=1, source_target_pairs={{0,1},{1,0},{2,3},{3,2},{4,5},{5,4},{6,7},{7,6},{8,9},{9,8},{10,11... | collective-permute-start | bytes 2211848 | tf_op jit(solution)/shard_map/ppermute | solution.py:34
  119.5 2.6 collective-permute-start.16
  119.6 3.6 collective-permute-start.17
  120.1 4.2 %collective-permute-start.18 = (bf16[4,96,960]{2,1,0:T(8,128)(2,1)}, bf16[4,96,960]{2,1,0:T(8,128)(2,1)S(1)}, u32[]{:S(2)}, u32[]{:S(2)}) collective-permute-start(bf16[4,96,960]{2,1,0:T(8,128)(2,1)} %collective-permute-done.14.refs_3_), channel_id=1, source_target_pairs={{0,1},{1,0},{2,3},{3,2},{4,5},{5,4},{6,7},{7,6},{8,9},{9,8},{10,11... | collective-permute-start | bytes 2211848 | tf_op jit(solution)/shard_map/ppermute | solution.py:34
  124.3 15.4 %collective-permute-start.22 = (bf16[4,96,768]{2,1,0:T(8,128)(2,1)S(1)}, bf16[4,96,768]{2,1,0:T(8,128)(2,1)S(1)}, u32[]{:S(2)}, u32[]{:S(2)}) collective-permute-start(bf16[4,96,768]{2,1,0:T(8,128)(2,1)S(1)} %slice.139.e0), channel_id=1, source_target_pairs={{0,4},{4,0},{8,12},{12,8},{16,20},{20,16},{24,28},{28,24},{1,5},{5... | collective-permute-start | bytes 1769480 | tf_op jit(solution)/shard_map/ppermute | solution.py:43
  125.2 15.1 %collective-permute-start.21 = (bf16[4,96,768]{2,1,0:T(8,128)(2,1)S(1)}, bf16[4,96,768]{2,1,0:T(8,128)(2,1)S(1)}, u32[]{:S(2)}, u32[]{:S(2)}) collective-permute-start(bf16[4,96,768]{2,1,0:T(8,128)(2,1)S(1)} %slice.139.e0), channel_id=1, source_target_pairs={{0,2},{2,0},{1,3},{3,1},{4,6},{6,4},{5,7},{7,5},{8,10},{10,8},{9,1... | collective-permute-start | bytes 1769480 | tf_op jit(solution)/shard_map/ppermute | solution.py:38
  145.2 5.7 %collective-permute-start.25 = (bf16[512,1536]{1,0:T(8,128)(2,1)}, bf16[512,1536]{1,0:T(8,128)(2,1)S(1)}, u32[]{:S(2)}, u32[]{:S(2)}) collective-permute-start(bf16[512,1536]{1,0:T(8,128)(2,1)} %get-tuple-element.247.ka_ref.va_ref), channel_id=1, source_target_pairs={{0,1},{1,0},{2,3},{3,2},{4,5},{5,4},{6,7},{7,6},{8,9},{9,8},{10,11... | collective-permute-start | bytes 4718600 | tf_op jit(solution)/shard_map/ppermute | solution.py:34
  150.9 20.9 %collective-permute-start.27 = (bf16[4,2,2,96,768]{4,3,2,1,0:T(8,128)(2,1)}, bf16[4,2,2,96,768]{4,3,2,1,0:T(8,128)(2,1)S(1)}, u32[]{:S(2)}, u32[]{:S(2)}) collective-permute-start(bf16[4,2,2,96,768]{4,3,2,1,0:T(8,128)(2,1)} %all-to-all-done.2.s0), channel_id=1, source_target_pairs={{0,1},{1,0},{2,3},{3,2},{4,5},{5,4},{6,7},{7,6},{8,9},{9,8},{10,11... | collective-permute-start | bytes 7077896 | tf_op jit(solution)/shard_map/ppermute | solution.py:34
  151.5 18.2 %collective-permute-start.20 = (bf16[4,96,768]{2,1,0:T(8,128)(2,1)}, bf16[4,96,768]{2,1,0:T(8,128)(2,1)S(1)}, u32[]{:S(2)}, u32[]{:S(2)}) collective-permute-start(bf16[4,96,768]{2,1,0:T(8,128)(2,1)} %copy-done.28), channel_id=1, source_target_pairs={{0,1},{1,0},{2,3},{3,2},{4,5},{5,4},{6,7},{7,6},{8,9},{9,8},{10,11... | collective-permute-start | bytes 1769480 | tf_op jit(solution)/shard_map/ppermute | solution.py:34
  151.6 18.1 %collective-permute-start.19 = (bf16[4,96,768]{2,1,0:T(8,128)(2,1)}, bf16[4,96,768]{2,1,0:T(8,128)(2,1)S(1)}, u32[]{:S(2)}, u32[]{:S(2)}) collective-permute-start(bf16[4,96,768]{2,1,0:T(8,128)(2,1)} %copy-done.28), channel_id=1, source_target_pairs={{0,6},{1,7},{2,4},{3,5},{4,2},{5,3},{6,0},{7,1},{8,14},{9,15},{10,... | collective-permute-start | bytes 1769480 | tf_op jit(solution)/shard_map/ppermute | solution.py:382
  153.2 16.5 %collective-permute-start.23 = (bf16[4,96,768]{2,1,0:T(8,128)(2,1)}, bf16[4,96,768]{2,1,0:T(8,128)(2,1)S(1)}, u32[]{:S(2)}, u32[]{:S(2)}) collective-permute-start(bf16[4,96,768]{2,1,0:T(8,128)(2,1)} %copy-done.44), channel_id=1, source_target_pairs={{0,1},{1,0},{2,3},{3,2},{4,5},{5,4},{6,7},{7,6},{8,9},{9,8},{10,11... | collective-permute-start | bytes 1769480 | tf_op jit(solution)/shard_map/ppermute | solution.py:34
  153.4 16.3 %collective-permute-start.24 = (bf16[4,96,768]{2,1,0:T(8,128)(2,1)}, bf16[4,96,768]{2,1,0:T(8,128)(2,1)S(1)}, u32[]{:S(2)}, u32[]{:S(2)}) collective-permute-start(bf16[4,96,768]{2,1,0:T(8,128)(2,1)} %copy-done.45), channel_id=1, source_target_pairs={{0,1},{1,0},{2,3},{3,2},{4,5},{5,4},{6,7},{7,6},{8,9},{9,8},{10,11... | collective-permute-start | bytes 1769480 | tf_op jit(solution)/shard_map/ppermute | solution.py:34
  169.8 2.1 collective-permute-start.26
  173.5 33.1 %copy-start.4 = (bf16[512,768]{1,0:T(8,128)(2,1)S(1)}, bf16[512,768]{1,0:T(8,128)(2,1)}, u32[]{:S(2)}) copy-start(bf16[512,768]{1,0:T(8,128)(2,1)} %copy-done.3) | copy-start | bytes 2359300
  173.5 33.1 %copy-start.7 = (bf16[512,768]{1,0:T(8,128)(2,1)S(1)}, bf16[512,768]{1,0:T(8,128)(2,1)}, u32[]{:S(2)}) copy-start(bf16[512,768]{1,0:T(8,128)(2,1)} %get-tuple-element.251.q_ref) | copy-start | bytes 2359300
  206.3 11.4 %collective-permute-start.28 = (bf16[2,2,4,104,1536]{4,3,2,1,0:T(8,128)(2,1)}, bf16[2,2,4,104,1536]{4,3,2,1,0:T(8,128)(2,1)}, u32[]{:S(2)}, u32[]{:S(2)}) collective-permute-start(bf16[2,2,4,104,1536]{4,3,2,1,0:T(8,128)(2,1)} %get-tuple-element.273), channel_id=1, source_target_pairs={{0,1},{1,0},{2,3},{3,2},{4,5},{5,4},{6,7},{7,6},{8,9},{9,8},{10,11... | collective-permute-start | bytes 15335432 | tf_op jit(solution)/shard_map/ppermute | solution.py:34
  223.7 30.5 %collective-permute-start.29 = (bf16[2,4,104,768]{3,2,1,0:T(8,128)(2,1)}, bf16[2,4,104,768]{3,2,1,0:T(8,128)(2,1)S(1)}, u32[]{:S(2)}, u32[]{:S(2)}) collective-permute-start(bf16[2,4,104,768]{3,2,1,0:T(8,128)(2,1)} %fusion), channel_id=1, source_target_pairs={{0,2},{2,0},{1,3},{3,1},{4,6},{6,4},{5,7},{7,5},{8,10},{10,8},{9,1... | collective-permute-start | bytes 3833864 | tf_op jit(solution)/shard_map/ppermute | solution.py:38
  224.7 30.3 %collective-permute-start.30 = (bf16[2,4,104,768]{3,2,1,0:T(8,128)(2,1)}, bf16[2,4,104,768]{3,2,1,0:T(8,128)(2,1)S(1)}, u32[]{:S(2)}, u32[]{:S(2)}) collective-permute-start(bf16[2,4,104,768]{3,2,1,0:T(8,128)(2,1)} %fusion.1), channel_id=1, source_target_pairs={{0,4},{4,0},{8,12},{12,8},{16,20},{20,16},{24,28},{28,24},{1,5},{5... | collective-permute-start | bytes 3833864 | tf_op jit(solution)/shard_map/ppermute | solution.py:43
  255.0 4.3 %collective-permute-start.31 = (bf16[2,512,768]{2,1,0:T(8,128)(2,1)}, bf16[2,512,768]{2,1,0:T(8,128)(2,1)}, u32[]{:S(2)}, u32[]{:S(2)}) collective-permute-start(bf16[2,512,768]{2,1,0:T(8,128)(2,1)} %get-tuple-element.287), channel_id=1, source_target_pairs={{0,1},{1,0},{2,3},{3,2},{4,5},{5,4},{6,7},{7,6},{8,9},{9,8},{10,11... | collective-permute-start | bytes 4718600 | tf_op jit(solution)/shard_map/ppermute | solution.py:34
  255.0 3.6 collective-permute-start.32
  258.6 29.0 %copy-start.14 = (bf16[512,384]{1,0:T(8,128)(2,1)}, bf16[512,384]{1,0:T(8,128)(2,1)S(1)}, u32[]{:S(2)}) copy-start(bf16[512,384]{1,0:T(8,128)(2,1)S(1)} %collective-permute-done.32.gb_ref) | copy-start | bytes 1179652
  266.5 9.5 %collective-permute-start.33 = (bf16[2,2,4,112,576]{4,3,2,1,0:T(8,128)(2,1)}, bf16[2,2,4,112,576]{4,3,2,1,0:T(8,128)(2,1)S(1)}, u32[]{:S(2)}, u32[]{:S(2)}) collective-permute-start(bf16[2,2,4,112,576]{4,3,2,1,0:T(8,128)(2,1)} %get-tuple-element.303), channel_id=1, source_target_pairs={{0,1},{1,0},{2,3},{3,2},{4,5},{5,4},{6,7},{7,6},{8,9},{9,8},{10,11... | collective-permute-start | bytes 6193160 | tf_op jit(solution)/shard_map/ppermute | solution.py:34
  266.6 17.0 %collective-permute-start.34 = (bf16[4,104,768]{2,1,0:T(8,128)(2,1)}, bf16[4,104,768]{2,1,0:T(8,128)(2,1)}, u32[]{:S(2)}, u32[]{:S(2)}) collective-permute-start(bf16[4,104,768]{2,1,0:T(8,128)(2,1)} %get-tuple-element.306), channel_id=1, source_target_pairs={{0,4},{4,0},{8,12},{12,8},{16,20},{20,16},{24,28},{28,24},{1,5},{5... | collective-permute-start | bytes 1916936 | tf_op jit(solution)/shard_map/ppermute | solution.py:43
  267.4 16.7 %collective-permute-start.35 = (bf16[4,104,768]{2,1,0:T(8,128)(2,1)}, bf16[4,104,768]{2,1,0:T(8,128)(2,1)}, u32[]{:S(2)}, u32[]{:S(2)}) collective-permute-start(bf16[4,104,768]{2,1,0:T(8,128)(2,1)} %get-tuple-element.307), channel_id=1, source_target_pairs={{0,2},{2,0},{1,3},{3,1},{4,6},{6,4},{5,7},{7,5},{8,10},{10,8},{9,1... | collective-permute-start | bytes 1916936 | tf_op jit(solution)/shard_map/ppermute | solution.py:38
  284.1 30.8 %collective-permute-start.36 = (bf16[2,2,4,104,384]{4,3,2,1,0:T(8,128)(2,1)S(1)}, bf16[2,2,4,104,384]{4,3,2,1,0:T(8,128)(2,1)S(1)}, u32[]{:S(2)}, u32[]{:S(2)}) collective-permute-start(bf16[2,2,4,104,384]{4,3,2,1,0:T(8,128)(2,1)S(1)} %copy-done.68), channel_id=1, source_target_pairs={{0,1},{1,0},{2,3},{3,2},{4,5},{5,4},{6,7},{7,6},{8,9},{9,8},{10,11... | collective-permute-start | bytes 3833864 | tf_op jit(solution)/shard_map/ppermute | solution.py:34
  284.1 20.5 %collective-permute-start.37 = (bf16[4,112,576]{2,1,0:T(8,128)(2,1)S(1)}, bf16[4,112,576]{2,1,0:T(8,128)(2,1)S(1)}, u32[]{:S(2)}, u32[]{:S(2)}) collective-permute-start(bf16[4,112,576]{2,1,0:T(8,128)(2,1)S(1)} %get-tuple-element.318), channel_id=1, source_target_pairs={{0,2},{2,0},{1,3},{3,1},{4,6},{6,4},{5,7},{7,5},{8,10},{10,8},{9,1... | collective-permute-start | bytes 1548296 | tf_op jit(solution)/shard_map/ppermute | solution.py:38
  285.1 26.2 %collective-permute-start.38 = (bf16[4,112,576]{2,1,0:T(8,128)(2,1)S(1)}, bf16[4,112,576]{2,1,0:T(8,128)(2,1)S(1)}, u32[]{:S(2)}, u32[]{:S(2)}) collective-permute-start(bf16[4,112,576]{2,1,0:T(8,128)(2,1)S(1)} %get-tuple-element.319), channel_id=1, source_target_pairs={{0,4},{4,0},{8,12},{12,8},{16,20},{20,16},{24,28},{28,24},{1,5},{5... | collective-permute-start | bytes 1548296 | tf_op jit(solution)/shard_map/ppermute | solution.py:43
  286.4 26.2 %collective-permute-start.39 = (bf16[4,112,576]{2,1,0:T(8,128)(2,1)S(1)}, bf16[4,112,576]{2,1,0:T(8,128)(2,1)S(1)}, u32[]{:S(2)}, u32[]{:S(2)}) collective-permute-start(bf16[4,112,576]{2,1,0:T(8,128)(2,1)S(1)} %get-tuple-element.320), channel_id=1, source_target_pairs={{0,6},{1,7},{2,4},{3,5},{4,2},{5,3},{6,0},{7,1},{8,14},{9,15},{10,... | collective-permute-start | bytes 1548296 | tf_op jit(solution)/shard_map/ppermute | solution.py:382
  316.4 35.3 %all-to-all-start.3 = ((bf16[4,104,1536]{2,1,0:T(8,128)(2,1)}), bf16[4,104,1536]{2,1,0:T(8,128)(2,1)}, u32[]{:S(2)}, u32[]{:S(2)}) async-start(bf16[4,104,1536]{2,1,0:T(8,128)(2,1)} %pad_maximum_fusion), calls=%async_computation.3 | async-start | bytes 2555904 | tf_op jit(solution)/shard_map/all_to_all | solution.py:387
  320.9 13.9 %collective-permute-start.40 = (bf16[4,104,384]{2,1,0:T(8,128)(2,1)}, bf16[4,104,384]{2,1,0:T(8,128)(2,1)}, u32[]{:S(2)}, u32[]{:S(2)}) collective-permute-start(bf16[4,104,384]{2,1,0:T(8,128)(2,1)} %get-tuple-element.324), channel_id=1, source_target_pairs={{0,2},{2,0},{1,3},{3,1},{4,6},{6,4},{5,7},{7,5},{8,10},{10,8},{9,1... | collective-permute-start | bytes 958472 | tf_op jit(solution)/shard_map/ppermute | solution.py:38
  322.0 16.0 %collective-permute-start.41 = (bf16[4,104,384]{2,1,0:T(8,128)(2,1)}, bf16[4,104,384]{2,1,0:T(8,128)(2,1)}, u32[]{:S(2)}, u32[]{:S(2)}) collective-permute-start(bf16[4,104,384]{2,1,0:T(8,128)(2,1)} %get-tuple-element.325), channel_id=1, source_target_pairs={{0,4},{4,0},{8,12},{12,8},{16,20},{20,16},{24,28},{28,24},{1,5},{5... | collective-permute-start | bytes 958472 | tf_op jit(solution)/shard_map/ppermute | solution.py:43
  323.3 14.7 %collective-permute-start.42 = (bf16[4,104,384]{2,1,0:T(8,128)(2,1)}, bf16[4,104,384]{2,1,0:T(8,128)(2,1)}, u32[]{:S(2)}, u32[]{:S(2)}) collective-permute-start(bf16[4,104,384]{2,1,0:T(8,128)(2,1)} %get-tuple-element.326), channel_id=1, source_target_pairs={{0,6},{1,7},{2,4},{3,5},{4,2},{5,3},{6,0},{7,1},{8,14},{9,15},{10,... | collective-permute-start | bytes 958472 | tf_op jit(solution)/shard_map/ppermute | solution.py:382
  351.7 29.0 %all-to-all-start.4 = ((bf16[4,112,576]{2,1,0:T(8,128)(2,1)}), bf16[4,112,576]{2,1,0:T(8,128)(2,1)S(1)}, u32[]{:S(2)}, u32[]{:S(2)}) async-start(bf16[4,112,576]{2,1,0:T(8,128)(2,1)} %fusion.8), calls=%async_computation.4 | async-start | bytes 1146880 | tf_op jit(solution)/shard_map/all_to_all | solution.py:387
  355.2 15.3 %collective-permute-start.43 = (bf16[4,104,576]{2,1,0:T(8,128)(2,1)}, bf16[4,104,576]{2,1,0:T(8,128)(2,1)S(1)}, u32[]{:S(2)}, u32[]{:S(2)}) collective-permute-start(bf16[4,104,576]{2,1,0:T(8,128)(2,1)} %get-tuple-element.344), channel_id=1, source_target_pairs={{0,2},{2,0},{1,3},{3,1},{4,6},{6,4},{5,7},{7,5},{8,10},{10,8},{9,1... | collective-permute-start | bytes 1437704 | tf_op jit(solution)/shard_map/ppermute | solution.py:38
  356.3 24.4 %collective-permute-start.44 = (bf16[4,104,576]{2,1,0:T(8,128)(2,1)}, bf16[4,104,576]{2,1,0:T(8,128)(2,1)S(1)}, u32[]{:S(2)}, u32[]{:S(2)}) collective-permute-start(bf16[4,104,576]{2,1,0:T(8,128)(2,1)} %get-tuple-element.345), channel_id=1, source_target_pairs={{0,4},{4,0},{8,12},{12,8},{16,20},{20,16},{24,28},{28,24},{1,5},{5... | collective-permute-start | bytes 1437704 | tf_op jit(solution)/shard_map/ppermute | solution.py:43
  357.1 24.4 %collective-permute-start.46 = (bf16[4,104,576]{2,1,0:T(8,128)(2,1)}, bf16[4,104,576]{2,1,0:T(8,128)(2,1)S(1)}, u32[]{:S(2)}, u32[]{:S(2)}) collective-permute-start(bf16[4,104,576]{2,1,0:T(8,128)(2,1)} %get-tuple-element.351), channel_id=1, source_target_pairs={{0,6},{1,7},{2,4},{3,5},{4,2},{5,3},{6,0},{7,1},{8,14},{9,15},{10,... | collective-permute-start | bytes 1437704 | tf_op jit(solution)/shard_map/ppermute | solution.py:382
  358.8 22.8 %copy-start.51 = (bf16[4,104,576]{2,1,0:T(8,128)(2,1)S(1)}, bf16[4,104,576]{2,1,0:T(8,128)(2,1)}, u32[]{:S(2)}) copy-start(bf16[4,104,576]{2,1,0:T(8,128)(2,1)} %get-tuple-element.348) | copy-start | bytes 1437700
  382.7 15.5 %collective-permute-start.47 = (bf16[512,768]{1,0:T(8,128)(2,1)S(1)}, bf16[512,768]{1,0:T(8,128)(2,1)S(1)}, u32[]{:S(2)}, u32[]{:S(2)}) collective-permute-start(bf16[512,768]{1,0:T(8,128)(2,1)S(1)} %copy-done.16), channel_id=1, source_target_pairs={{0,2},{2,0},{1,3},{3,1},{4,6},{6,4},{5,7},{7,5},{8,10},{10,8},{9,1... | collective-permute-start | bytes 2359304 | tf_op jit(solution)/shard_map/ppermute | solution.py:38
  386.4 22.2 %all-to-all-start.5 = ((bf16[4,104,960]{2,1,0:T(8,128)(2,1)}), bf16[4,104,960]{2,1,0:T(8,128)(2,1)}, u32[]{:S(2)}, u32[]{:S(2)}) async-start(bf16[4,104,960]{2,1,0:T(8,128)(2,1)} %pad_maximum_fusion.1), calls=%async_computation.5 | async-start | bytes 1703936 | tf_op jit(solution)/shard_map/all_to_all | solution.py:387
  391.2 11.6 %collective-permute-start.45 = (bf16[512,768]{1,0:T(8,128)(2,1)}, bf16[512,768]{1,0:T(8,128)(2,1)}, u32[]{:S(2)}, u32[]{:S(2)}) collective-permute-start(bf16[512,768]{1,0:T(8,128)(2,1)} %get-tuple-element.346), channel_id=1, source_target_pairs={{0,1},{1,0},{2,3},{3,2},{4,5},{5,4},{6,7},{7,6},{8,9},{9,8},{10,11... | collective-permute-start | bytes 2359304 | tf_op jit(solution)/shard_map/ppermute | solution.py:34
  391.2 19.4 %collective-permute-start.48 = (bf16[8,64,768]{2,1,0:T(8,128)(2,1)S(1)}, bf16[8,64,768]{2,1,0:T(8,128)(2,1)S(1)}, u32[]{:S(2)}, u32[]{:S(2)}) collective-permute-start(bf16[8,64,768]{2,1,0:T(8,128)(2,1)S(1)} %bitcast.76), channel_id=1, source_target_pairs={{0,1},{1,0},{2,3},{3,2},{4,5},{5,4},{6,7},{7,6},{8,9},{9,8},{10,11... | collective-permute-start | bytes 2359304 | tf_op jit(solution)/shard_map/ppermute | solution.py:34
  398.2 12.4 %collective-permute-start.49 = (bf16[8,64,768]{2,1,0:T(8,128)(2,1)S(1)}, bf16[8,64,768]{2,1,0:T(8,128)(2,1)S(1)}, u32[]{:S(2)}, u32[]{:S(2)}) collective-permute-start(bf16[8,64,768]{2,1,0:T(8,128)(2,1)S(1)} %bitcast.78), channel_id=1, source_target_pairs={{0,1},{1,0},{2,3},{3,2},{4,5},{5,4},{6,7},{7,6},{8,9},{9,8},{10,11... | collective-permute-start | bytes 2359304 | tf_op jit(solution)/shard_map/ppermute | solution.py:34
  (62 other events, 404.7 us)

commit v3 on v2

--- a/solution.py
+++ b/solution.py
@@ -61,7 +61,7 @@
     slope = prob * (mm(v, grad, NT) - delta)
     prob = prob.astype(BF)
     slope = slope.astype(BF)
-    return mm(slope, k, TN), mm(slope, q, NN), mm(prob, grad, NN)
+    return mm(k, slope, TN), mm(slope, q, NN), mm(prob, grad, NN)
 
 
 def delta_row(grad, mixed):
@@ -69,7 +69,7 @@
 
 
 def self_bwd_kernel(info, q_ref, k_ref, v_ref, oa_ref, ob_ref, lse_ref, ga_ref, gb_ref, *rest):
-    out_ref, sums_ref, o_ref, g_ref = rest[-4:]
+    out_ref, o_ref, g_ref = rest[-3:]
     dq_ref, dk_ref, dv_ref = out_ref.at[0], out_ref.at[1], out_ref.at[2]
     o_ref[0], o_ref[1] = oa_ref[...], ob_ref[...]
     g_ref[0], g_ref[1] = ga_ref[...], gb_ref[...]
@@ -77,10 +77,14 @@
     first = info[0]
     second = 1 - first
     prefix = info[1]
-    key_pos = lax.broadcasted_iota(jnp.int32, (half, half), 0)
-    query_pos = lax.broadcasted_iota(jnp.int32, (half, half), 1)
-    causal = key_pos <= query_pos
-    seen = causal | (key_pos < prefix)
+    def positions(rows):
+        shape = (rows, half)
+        return lax.broadcasted_iota(jnp.int32, shape, 0), lax.broadcasted_iota(jnp.int32, shape, 1)
+
+    key_pos, query_pos = positions(half)
+    seen = (key_pos <= query_pos) | (key_pos < prefix)
+    key_pos, query_pos = positions(2 * half)
+    seen_late = key_pos <= query_pos + half
     scale = 1.0 / math.sqrt(HD)
     for h in range(2):
         cols = slice(HD * h, HD * h + HD)
@@ -88,26 +92,23 @@
         def rows(ref, at):
             return ref[at, :, cols]
 
-        def one(q_at, k_at, mask):
-            grad = rows(g_ref, q_at)
-            delta = delta_row(grad, rows(o_ref, q_at))
-            lse = lse_ref[0, h, pl.ds(q_at, 1), :]
-            return pair_backward(
-                rows(q_ref, q_at), rows(k_ref, k_at), rows(v_ref, k_at), grad, lse, delta, mask
-            )
-
-        dq, dk_a, dv_a = one(first, first, seen)
-        dq_ref[first, :, cols] = (dq.astype(BF) * scale).astype(BF)
-        dq_b, dk_b, dv_b = one(second, first, None)
-        dk_ref[first, :, cols] = (dk_a + dk_b).astype(BF)
-        dv_ref[first, :, cols] = (dv_a + dv_b).astype(BF)
-        dq_c, dk_c, dv_c = one(second, second, causal)
-        dq_ref[second, :, cols] = ((dq_b + dq_c).astype(BF) * scale).astype(BF)
-        dk_ref[second, :, cols] = dk_c.astype(BF)
-        dv_ref[second, :, cols] = dv_c.astype(BF)
-    for i in range(3):
-        both = out_ref[i, 0].astype(F32) + out_ref[i, 1].astype(F32)
-        sums_ref[0, i : i + 1, :] = jnp.sum(both, 0, keepdims=True)
+        def both(ref):
+            return jnp.concatenate([rows(ref, first), rows(ref, second)], axis=0)
+
+        def one(at, key, value, mask):
+            grad = rows(g_ref, at)
+            delta = delta_row(grad, rows(o_ref, at))
+            lse = lse_ref[0, h, pl.ds(at, 1), :]
+            dq, dk, dv = pair_backward(rows(q_ref, at), key, value, grad, lse, delta, mask)
+            dq_ref[at, :, cols] = (dq.T.astype(BF) * scale).astype(BF)
+            return dk, dv
+
+        dk_a, dv_a = one(first, rows(k_ref, first), rows(v_ref, first), seen)
+        dk_b, dv_b = one(second, both(k_ref), both(v_ref), seen_late)
+        dk_ref[first, :, cols] = (dk_a + dk_b[:half]).astype(BF)
+        dv_ref[first, :, cols] = (dv_a + dv_b[:half]).astype(BF)
+        dk_ref[second, :, cols] = dk_b[half:].astype(BF)
+        dv_ref[second, :, cols] = dv_b[half:].astype(BF)
 
 
 def self_backward(info, qkv, mixed_own, mixed_oth, lse, grad_own, grad_oth, start, count, former=()):
@@ -135,16 +136,10 @@
                 flat,
             ]
             + [pl.BlockSpec(memory_space=pl.ANY)] * len(former),
-            out_specs=[
-                pl.BlockSpec((3, 2, half, 128), lambda i, info: (0, 0, 0, start + i)),
-                pl.BlockSpec((1, 8, 128), lambda i, info: (start + i, 0, 0)),
-            ],
+            out_specs=pl.BlockSpec((3, 2, half, 128), lambda i, info: (0, 0, 0, start + i)),
             scratch_shapes=[pltpu.VMEM((2, half, 128), BF)] * 2,
         ),
-        out_shape=[
-            jax.ShapeDtypeStruct((3, 2, half, width), BF),
-            jax.ShapeDtypeStruct((pairs, 8, 128), F32),
-        ],
+        out_shape=jax.ShapeDtypeStruct((3, 2, half, width), BF),
         input_output_aliases={9 + i: i for i in range(len(former))},
         compiler_params=pltpu.CompilerParams(vmem_limit_bytes=VMEM_LIMIT),
         cost_estimate=COST,
@@ -211,13 +206,15 @@
         delta = delta_row(grad, o_ref[:, cols])
         lse = lse_ref[0, h : h + 1, :]
         q = q_ref[:, cols]
-        dq_a, dk, dv = pair_backward(q, ka_ref[:, cols], va_ref[:, cols], grad, lse, delta, None)
-        da_ref[0, :, cols] = dk.astype(BF)
-        da_ref[1, :, cols] = dv.astype(BF)
-        dq_b, dk, dv = pair_backward(q, kb_ref[:, cols], vb_ref[:, cols], grad, lse, delta, None)
-        db_ref[0, :, cols] = dk.astype(BF)
-        db_ref[1, :, cols] = dv.astype(BF)
-        dq_ref[:, cols] = ((dq_a + dq_b).astype(BF) * scale).astype(BF)
+        rows = q.shape[0]
+        key = jnp.concatenate([ka_ref[:, cols], kb_ref[:, cols]], axis=0)
+        value = jnp.concatenate([va_ref[:, cols], vb_ref[:, cols]], axis=0)
+        dq, dk, dv = pair_backward(q, key, value, grad, lse, delta, None)
+        da_ref[0, :, cols] = dk[:rows].astype(BF)
+        da_ref[1, :, cols] = dv[:rows].astype(BF)
+        db_ref[0, :, cols] = dk[rows:].astype(BF)
+        db_ref[1, :, cols] = dv[rows:].astype(BF)
+        dq_ref[:, cols] = (dq.T.astype(BF) * scale).astype(BF)
 
 
 def cross_backward(queries, kv_own, kv_oth, mixed, lse, grad, start, count, former=()):
@@ -958,81 +955,56 @@
         put_rows((keep_ref, send_ref)[j // 2], j % 2, full[:, j * piece : (j + 1) * piece], at, place)
 
 
-def query_grads_kernel(
-    info, h1_ref, dq_ref, e1_ref, o1_ref, e2_ref, o2_ref, sums_ref, keep_ref, send_ref
+def attn_grads_kernel(
+    info, h1_ref, dq_ref, e1_ref, o1_ref, e2_ref, o2_ref, sums_ref,
+    fet_ref, own_ref, got_ref, mat_ref, keep_ref, send_ref, grad_ref,
 ):
+    place = info[0]
     width = dq_ref.shape[1]
     piece = width // 4
     outer, rows = keep_ref.shape[2], keep_ref.shape[3]
+    for i, (left, right) in enumerate(((h1_ref, dq_ref), (e1_ref, o1_ref), (e2_ref, o2_ref))):
+        full = mm(left[...], right[...], TN).astype(BF)
+        put_blocks(keep_ref, send_ref, full, i, place)
+    total = None
+    for i in range(2):
+        low = add_low(own_ref[i], got_ref[i])
+        full = mm(fet_ref[...], low, TN).astype(BF)
+        put_blocks(keep_ref, send_ref, full, 3 + i, place)
+        term = mm(low, mat_ref[:, i * width : (i + 1) * width], NT)
+        total = term if total is None else total + term
+    grad_ref[...] = total.astype(BF)
     parts = [high_low(sums_ref[i : i + 1, :]) for i in range(4)]
+    value_sums = high_low(jnp.sum(low.astype(F32), 0, keepdims=True))
+    empty = jnp.zeros((1, piece), F32)
     for j in range(4):
         own = slice(j * piece, (j + 1) * piece)
         ref = (keep_ref, send_ref)[j // 2]
-        for i in range(3):
-            lines = [parts[i][0][:, p * piece : (p + 1) * piece] for p in range(4)]
-            lines += [parts[i][1][:, p * piece : (p + 1) * piece] for p in range(4)]
+        for i in range(5):
+            lines = [empty] * 8
+            if i < 3:
+                lines = [parts[i][0][:, p * piece : (p + 1) * piece] for p in range(4)]
+                lines += [parts[i][1][:, p * piece : (p + 1) * piece] for p in range(4)]
             if i == 0:
                 lines += [parts[3][0][:, own], parts[3][1][:, own]]
+            if i == 4:
+                lines += [value_sums[0][:, own], value_sums[1][:, own]]
             block = stack_rows(lines, 16)
             for o in range(outer):
                 for y in range(2):
                     ref[j % 2, y, o, rows - 16 :, i * piece : (i + 1) * piece] = block
-    for i, (left, right) in enumerate(((h1_ref, dq_ref), (e1_ref, o1_ref), (e2_ref, o2_ref))):
-        full = mm(left[...], right[...], TN).astype(BF)
-        put_blocks(keep_ref, send_ref, full, i, info[0])
-
-
-def key_grads_kernel(info, fet_ref, own_ref, got_ref, mat_ref, keep_ref, send_ref, grad_ref):
-    width = fet_ref.shape[1]
-    piece = width // 4
-    outer, rows = keep_ref.shape[2], keep_ref.shape[3]
-    total = None
-    for i in range(2):
-        low = add_low(own_ref[i], got_ref[i])
-        full = mm(fet_ref[...], low, TN).astype(BF)
-        put_blocks(keep_ref, send_ref, full, i, info[0])
-        term = mm(low, mat_ref[:, i * width : (i + 1) * width], NT)
-        total = term if total is None else total + term
-        if i == 1:
-            sums = high_low(jnp.sum(low.astype(F32), 0, keepdims=True))
-            for j in range(4):
-                own = slice(j * piece, (j + 1) * piece)
-                block = stack_rows([sums[0][:, own], sums[1][:, own]], 8)
-                ref = (keep_ref, send_ref)[j // 2]
-                for o in range(outer):
-                    for y in range(2):
-                        ref[j % 2, y, o, rows - 8 :, piece:] = block
-                        ref[j % 2, y, o, rows - 8 :, :piece] = jnp.zeros_like(block)
-    grad_ref[...] = total.astype(BF)
-
-
-def query_grads(info, args, depth):
-    width = args[0].shape[1]
-    out = struct((2, 2, width // depth // 2, tail_start(depth) + 16, 3 * width // 4), BF)
+
+
+def attn_grads(info, args, depth):
+    rows, width = args[0].shape
+    out = struct((2, 2, width // depth // 2, tail_start(depth) + 16, 5 * width // 4), BF)
     return call(
-        query_grads_kernel,
-        [out, out],
+        attn_grads_kernel,
+        [out, out, struct((rows, width), BF)],
         [info] + list(args),
-        [SM] + [VM] * 7,
-        [VM] * 2,
-        flops=2 * 512 * width * width * 3,
-        moved=width * width * 10,
-        name="query_grads",
-    )
-
-
-def key_grads(info, fetched, own, got, mat, depth):
-    rows, width = fetched.shape
-    out = struct((2, 2, width // depth // 2, tail_start(depth) + 8, 2 * width // 4), BF)
-    return call(
-        key_grads_kernel,
-        [out, out, struct((rows, width), BF)],
-        [info, fetched, own, got, mat],
-        [SM] + [VM] * 4,
+        [SM] + [VM] * 11,
         [VM] * 3,
-        flops=2 * rows * width * width * 4,
-        moved=width * width * 10,
-        name="key_grads",
+        name="attn_grads",
     )
 
 
@@ -1208,33 +1180,38 @@
     return total
 
 
-def sum_query_kernel(in_ref, q_ref, so_ref, co_ref, qb_ref, v0_ref, v1_ref, v2_ref):
+def sum_attn_kernel(
+    in_ref, q_ref, so_ref, co_ref, k_ref, v_ref, qb_ref, vb_ref, v0_ref, v1_ref, v2_ref
+):
     total = sum_all(in_ref)
-    piece = total.shape[1] // 3
+    piece = total.shape[1] // 5
     depth = q_ref.shape[0]
     q_ref[...] = total[:depth, :piece]
     so_ref[...] = total[:depth, piece : 2 * piece].T
-    co_ref[...] = total[:depth, 2 * piece :].T
+    co_ref[...] = total[:depth, 2 * piece : 3 * piece].T
+    k_ref[...] = total[:depth, 3 * piece : 4 * piece]
+    v_ref[...] = total[:depth, 4 * piece :]
     tail = total[total.shape[0] - 16 :]
     qb_ref[...] = (tail[8:9, :piece] + tail[9:10, :piece])[0]
+    vb_ref[...] = (tail[8:9, 4 * piece :] + tail[9:10, 4 * piece :])[0]
     for i, ref in enumerate((v0_ref, v1_ref, v2_ref)):
         cols = slice(i * piece, (i + 1) * piece)
         parts = [tail[p : p + 1, cols] + tail[p + 4 : p + 5, cols] for p in range(4)]
         ref[...] = jnp.concatenate(parts, axis=1)[0]
 
 
-def sum_query(value, depth):
+def sum_attn(value, depth):
     count, rows, cols = value.shape
-    piece = cols // 3
+    piece = cols // 5
     wide, tall = struct((depth, piece), F32), struct((piece, depth), F32)
-    vec = struct((4 * piece,), F32)
+    row, vec = struct((piece,), F32), struct((4 * piece,), F32)
     return call(
-        sum_query_kernel,
-        [wide, tall, tall, struct((piece,), F32), vec, vec, vec],
+        sum_attn_kernel,
+        [wide, tall, tall, wide, wide, row, row, vec, vec, vec],
         [value],
         [VM],
-        [VM] * 7,
-        name="sum_query",
+        [VM] * 10,
+        name="sum_attn",
     )
 
 
@@ -1520,76 +1497,65 @@
     )
     expand_last = swap_dp(expand_send, 1)
     shrink_last = swap_x(shrink_send)
-    query_keep, query_send = query_grads(
-        info, (first_low, dq, self_low, mixed_one, cross_low, mixed_two, early_vec), depth
-    )
-    dkv_own, query_send = lax.optimization_barrier((dkv_own, query_send))
-    query_got = swap_core(query_send)
-    key_keep, key_send, fetched_grad = key_grads(
-        info, fetched, dkv_own, dkv_got, cross_kv, depth
-    )
-    query_plane = plane_send(gate(query_keep, fetched_grad), query_got)
-    query_plane, key_send, grad_got, fetched_grad, expand_last, shrink_last = (
-        lax.optimization_barrier(
-            (query_plane, key_send, grad_got, fetched_grad, expand_last, shrink_last)
-        )
-    )
-    query_parts = plane_swap(query_plane)
-    key_got = swap_core(key_send)
+    attn_keep, attn_send, fetched_grad = attn_grads(
+        info,
+        (
+            first_low, dq, self_low, mixed_one, cross_low, mixed_two, early_vec,
+            fetched, dkv_own, dkv_got, cross_kv,
+        ),
+        depth,
+    )
+    attn_send, grad_got, expand_last, shrink_last = lax.optimization_barrier(
+        (attn_send, grad_got, expand_last, shrink_last)
+    )
+    attn_got = swap_core(attn_send)
+    feed_three = jnp.concatenate(
+        [
+            feed_sum(0, 0, 0, expand_got[0], expand_last),
+            feed_sum(0, 0, 1, shrink_got[0], shrink_last),
+        ],
+        axis=-1,
+    )
+    feed_three, grad_got = lax.optimization_barrier((feed_three, grad_got))
+    feed_last = outer_exchange(feed_three)
 
     self_args = (attn_info, qkv, self_own, self_send, self_lse, grad_own, grad_got)
     pairs = two // 128
     half_grads = self_backward(*self_args, 0, pairs - 1)
-    key_plane = plane_send(gate(key_keep, half_grads[1]), key_got)
-    feed_three = jnp.concatenate(
-        [
-            feed_sum(0, 0, 0, expand_got[0], gate(expand_last, half_grads[1])),
-            feed_sum(0, 0, 1, shrink_got[0], gate(shrink_last, half_grads[1])),
-        ],
-        axis=-1,
-    )
-    query_three = plane_sum((query_keep[0, 0], query_got[0, 0]), query_parts).astype(BF)
-    key_plane, half_grads, feed_three, query_three = lax.optimization_barrier(
-        (key_plane, tuple(half_grads), feed_three, query_three)
-    )
-    key_parts = plane_swap(key_plane)
-    feed_last = outer_exchange(feed_three)
-    grads, self_rows = self_backward(*self_args, pairs - 1, 1, half_grads)
-    grads, key_parts = lax.optimization_barrier((grads, key_parts))
+    attn_plane, half_grads, fetched_away = lax.optimization_barrier(
+        (plane_send(gate(attn_keep, half_grads), attn_got), half_grads, swap_x(fetched_grad))
+    )
+    fetched_away = fetched_away.reshape(slots, BLK, width)
+    fetched_near = fetched_grad.reshape(slots, BLK, width)
+    attn_parts = plane_swap(attn_plane)
+    grads = self_backward(*self_args, pairs - 1, 1, (half_grads,))
     self_places = self_grads(info, tokens, tokens_oth, grads, depth)
     self_places, grads = lax.optimization_barrier((tuple(self_places), grads))
     self_parts = (swap_x(self_places[1]), swap_dp(self_places[2], 1), swap_both(self_places[3]))
-    grads, feed_last, query_three = lax.optimization_barrier((grads, feed_last, query_three))
-    query_last = outer_exchange(query_three)
     back_keep, back_send = self_back(grads, self_mat, first_in)
-    back_send, query_last, key_parts, self_near, self_away = lax.optimization_barrier(
-        (back_send, query_last, key_parts, self_parts[0], self_parts[1])
-    )
-    key_three = plane_sum((key_keep[0, 0], key_got[0, 0]), key_parts).astype(BF)
-    back_got = swap_core(back_send)
-    self_three = plane_sum((self_places[0],), (self_near, self_away, self_parts[2])).astype(BF)
+    back_send, feed_last, attn_parts = lax.optimization_barrier((back_send, feed_last, attn_parts))
+    attn_three = plane_sum((attn_keep[0, 0], attn_got[0, 0]), attn_parts).astype(BF)
+    attn_last = outer_exchange(attn_three)
+    self_three = plane_sum((self_places[0],), self_parts).astype(BF)
     self_last = outer_exchange(
-        gate(jnp.concatenate([self_three, key_three], axis=-1), query_last)
-    )
-    fetched_send = gate(fetched_grad, self_three)
-    fetched_away = swap_x(fetched_send).reshape(slots, BLK, width)
-    fetched_near = fetched_send.reshape(slots, BLK, width)
+        gate(self_three, attn_last)
+    )
+    back_got = swap_core(gate(back_send, self_three))
     in_grad = (back_keep + back_got.astype(F32)).astype(BF)
 
-    cq_grad, so_grad, co_grad, cq_rows, first_shift_rows, first_gain_rows, so_rows = sum_query(
-        query_last, depth
-    )
     (
-        sq_grad, sk_grad, sv_grad, ck_grad, cv_grad, sq_rows, sk_rows, sv_rows, ck_rows, cv_rows,
-    ) = sum_cols(self_last, depth, 5)
+        cq_grad, so_grad, co_grad, ck_grad, cv_grad, cq_rows, cv_rows,
+        first_shift_rows, first_gain_rows, so_rows,
+    ) = sum_attn(attn_last, depth)
+    sq_grad, sk_grad, sv_grad, sq_rows, sk_rows, sv_rows = sum_cols(self_last, depth, 3)
     (
         expand_grad, shrink_grad, expand_rows, third_shift_rows, third_gain_rows, shrink_rows,
         second_shift_rows, second_gain_rows, co_rows,
     ) = sum_feed(feed_last, depth)
     shrink_grad = shrink_grad.T
 
-    near_core = swap_core(fetched_near)
-    away_core = swap_core(fetched_away)
+    near_core = swap_core(gate(fetched_near, self_three))
+    away_core = swap_core(gate(fetched_away, near_core))
     slot_ids = jnp.arange(NBLK)
     places = (
         (((slot_ids[None, :] // slots) != core) * 2 + (jnp.arange(seq_count)[:, None] != chip))

time: 420 us -> 402 us (0.957)
  Pallas kernels: 181 us -> 172 us
  waiting for transfers between devices: 117 us -> 109 us
    all_to_all x6, waiting for transfers between devices: 12.9 us -> 5.83 us  [outer_exchange(): lax.all_to_all(value, 'dp', 0, 0, axis_index_groups=groups, tiled=True)]
    ppermute x9 -> x8, waiting for transfers between devices: 44.3 us -> 40.5 us  [swap_dp(): lax.ppermute(value, 'dp', tuple(((i, i ^ bit) for i in range(count))))]
    ppermute x22 -> x21, waiting for transfers between devices: 8.1 us -> 11.3 us  [swap_core(): return lax.ppermute(value, 'tensor', CORE_SWAP)]
    pallas_call x15 -> x14, Pallas kernels: 96.6 us -> 94.1 us  [call(): pl.pallas_call(kernel, out_shape=out_shape, in_specs=in_specs, out_specs=...]
    unnamed x140 -> x124, local copies, waits for them, and re-layouts: 12.8 us -> 11.1 us
    ppermute x7 -> x6, starting transfers between devices: 10.3 us -> 9.03 us  [swap_both(): return lax.ppermute(value, ('dp', 'tensor'), pairs)]
    ppermute x12 -> x11, starting transfers between devices: 13.7 us -> 12.6 us  [swap_x(): return lax.ppermute(value, 'tensor', X_SWAP)]
    ppermute x12 -> x11, waiting for transfers between devices: 40.5 us -> 39.6 us  [swap_x(): return lax.ppermute(value, 'tensor', X_SWAP)]
  transfers between devices with their start and end apart: 56 -> 52, of which waited for: 28 -> 29; matrix products, arithmetic and copies ran while one was open for 6% -> 8% of each run, Pallas kernels for 32% -> 33%
where the time goes in v3:
time: 402 us; the launch traced here: 397 us
  Pallas kernels  172 us (43%)
  waiting for transfers between devices  109 us (27%)
  starting transfers between devices  61.8 us (15%)
  other arithmetic  32.7 us (8%)
  local copies, waits for them, and re-layouts  21.1 us (5%)
    pallas_call x14, Pallas kernels, call(): pl.pallas_call(kernel, out_shape=out_shape, in_specs=in_specs, out_specs=...  94.1 us
    ppermute x8, waiting for transfers between devices, swap_dp(): lax.ppermute(value, 'dp', tuple(((i, i ^ bit) for i in range(count))))  40.5 us
    ppermute x11, waiting for transfers between devices, swap_x(): return lax.ppermute(value, 'tensor', X_SWAP)  39.6 us
    all_to_all x6, starting transfers between devices, outer_exchange(): lax.all_to_all(value, 'dp', 0, 0, axis_index_groups=groups, tiled=True)  28.1 us
    pallas_call x1, Pallas kernels, cross_first_backward(): pl.pallas_call(functools.partial(cross_first_kernel, start=start, count=c...  19.2 us
    pallas_call x2, Pallas kernels, self_backward(): pl.pallas_call(self_bwd_kernel, grid_spec=pltpu.PrefetchScalarGridSpec(nu...  18.2 us
    pallas_call x1, Pallas kernels, cross_forward(): pl.pallas_call(cross_fwd_kernel, grid=(pairs,), in_specs=[whole, whole, t...  13.9 us
    pallas_call x1, Pallas kernels, self_forward(): pl.pallas_call(self_forward_kernel, grid_spec=pltpu.PrefetchScalarGridSpe...  12.9 us
  transfers between devices with their start and end apart: 52, of which 29 were waited for; matrix products, arithmetic and copies ran while one was open for 8% of the time, Pallas kernels for 33%

profile of v3, /device:TPU:0, one launch (start us, length us, event | category | flops | bytes accessed | tf_op | source)
XLA Modules:
  0.0 397.5 jit_solution(16955312264389167527)
XLA Ops:
  2.9 4.3 %fetch.1 = (bf16[16,64,768]{2,1,0:T(8,128)(2,1)}, bf16[16,64,768]{2,1,0:T(8,128)(2,1)}) custom-call(s32[32]{0:T(128)} %select_n.75.table, bf16[32,64,768]{2,1,0:T(8,128)(2,1)} %bitcast.77), custom_call_target="tpu_custom_call" | custom-call | flops 1000 | bytes 1000 | tf_op jit(solution)/shard_map/fetch/pallas_call | solution.py:412
  8.0 2.5 collective-permute-start
  10.6 1.8 pack_self.1
  12.5 5.0 %all-to-all-start = ((bf16[4,96,576]{2,1,0:T(8,128)(2,1)}), bf16[4,96,576]{2,1,0:T(8,128)(2,1)S(1)}, u32[]{:S(2)}, u32[]{:S(2)}) async-start(bf16[4,96,576]{2,1,0:T(8,128)(2,1)} %pack_self.1), calls=%async_computation | async-start | bytes 983040 | tf_op jit(solution)/shard_map/all_to_all | solution.py:384
  19.7 2.9 fusion.16
  27.2 2.6 pack_rest.1
  29.9 1.9 all-to-all-done.w_ref
  31.8 10.5 %collective-permute-done.4 = bf16[8,64,768]{2,1,0:T(8,128)(2,1)S(1)} collective-permute-done((bf16[8,64,768]{2,1,0:T(8,128)(2,1)}, bf16[8,64,768]{2,1,0:T(8,128)(2,1)S(1)}, u32[]{:S(2)}, u32[]{:S(2)}) %collective-permute-start.4) | collective-permute-done | bytes 786464 | tf_op jit(solution)/shard_map/ppermute | solution.py:38
  43.1 4.8 %all-to-all-start.1 = ((bf16[4,96,1728]{2,1,0:T(8,128)(2,1)}), bf16[4,96,1728]{2,1,0:T(8,128)(2,1)}, u32[]{:S(2)}, u32[]{:S(2)}) async-start(bf16[4,96,1728]{2,1,0:T(8,128)(2,1)} %get-tuple-element.189), calls=%async_computation.1 | async-start | bytes 2752512 | tf_op jit(solution)/shard_map/all_to_all | solution.py:384
  48.5 2.4 collective-permute-start.7
  51.4 10.7 %collective-permute-done.5.wx_ref = bf16[4,96,576]{2,1,0:T(8,128)(2,1)S(1)} collective-permute-done((bf16[4,96,576]{2,1,0:T(8,128)(2,1)S(1)}, bf16[4,96,576]{2,1,0:T(8,128)(2,1)S(1)}, u32[]{:S(2)}, u32[]{:S(2)}) %collective-permute-start.5) | collective-permute-done | bytes 442400 | tf_op jit(solution)/shard_map/ppermute | solution.py:38
  62.1 1.5 collective-permute-start.10
  64.1 1.5 collective-permute-start.8
  66.2 10.0 %collective-permute-done.10.xy_ref = bf16[96,768]{1,0:T(8,128)(2,1)} collective-permute-done((bf16[96,768]{1,0:T(8,128)(2,1)}, bf16[96,768]{1,0:T(8,128)(2,1)}, u32[]{:S(2)}, u32[]{:S(2)}) %collective-permute-start.10) | collective-permute-done | bytes 147488 | tf_op jit(solution)/shard_map/ppermute | solution.py:379
  76.2 2.9 collective-permute-done.9.y_ref
  79.2 2.7 plane_copies.1
  81.9 2.2 slice.114.refs_0_
  84.7 1.5 collective-permute-start.13
  86.2 1.4 collective-permute-start.12
  87.7 4.9 %all-to-all-start.2 = ((bf16[4,2,2,96,768]{4,3,2,1,0:T(8,128)(2,1)}), bf16[4,2,2,96,768]{4,3,2,1,0:T(8,128)(2,1)}, u32[]{:S(2)}, u32[]{:S(2)}) async-start(bf16[4,2,2,96,768]{4,3,2,1,0:T(8,128)(2,1)} %plane_copies.1), calls=%async_computation.2 | async-start | bytes 4718592 | tf_op jit(solution)/shard_map/all_to_all | solution.py:384
  93.7 12.9 %self_fwd.1 = (bf16[2,512,1152]{2,1,0:T(8,128)(2,1)}, bf16[768,1152]{1,0:T(8,128)(2,1)S(1)}, bf16[512,384]{1,0:T(8,128)(2,1)S(1)}, bf16[512,384]{1,0:T(8,128)(2,1)S(1)}, f32[3,2,2,512]{3,2,1,0:T(2,128)S(1)}) custom-call(s32[5]{0:T(128)S(1)} %pad_add_fusion.2.info, bf16[512,768]{1,0:T(8,128)(2,1)S(1)} %copy-done.5, ...), custom_call_target="tpu_custom_call" | custom-call | flops 1000 | bytes 1000 | tf_op jit(solution)/shard_map/self_fwd/pallas_call | solution.py:565
  109.0 1.7 collective-permute-done.15.oth_ref
  110.7 8.8 %collective-permute-done.13.refs_1_ = bf16[4,96,960]{2,1,0:T(8,128)(2,1)} collective-permute-done((bf16[4,96,960]{2,1,0:T(8,128)(2,1)}, bf16[4,96,960]{2,1,0:T(8,128)(2,1)}, u32[]{:S(2)}, u32[]{:S(2)}) %collective-permute-start.13) | collective-permute-done | bytes 737312 | tf_op jit(solution)/shard_map/ppermute | solution.py:43
  128.5 7.9 %assemble.1 = (bf16[4,2,96,1536]{3,2,1,0:T(8,128)(2,1)}, bf16[4,2,96,768]{3,2,1,0:T(8,128)(2,1)}, bf16[4,2,96,768]{3,2,1,0:T(8,128)(2,1)}, bf16[4,2,96,768]{3,2,1,0:T(8,128)(2,1)}) custom-call(s32[3]{0:T(128)} %pad_add_fusion.info, bf16[4,96,960]{2,1,0:T(8,128)(2,1)} %slice.114.refs_0_, bf16[4,96,960]{2,1,0:T(8,128)(2,1)} %collective-permute-done.13.refs_1_, ...), custom_call_target="tpu_custom_call" | custom-call | flops 1000 | bytes 1000 | tf_op jit(solution)/shard_map/assemble/pallas_call | solution.py:412
  136.4 3.3 collective-permute-done.22.e1
  140.2 4.9 %project_kv.1 = (bf16[512,768]{1,0:T(8,128)(2,1)}, bf16[512,1536]{1,0:T(8,128)(2,1)}) custom-call(bf16[512,768]{1,0:T(8,128)(2,1)} %bitcast_add_fusion.1.keep_ref, bf16[512,768]{1,0:T(8,128)(2,1)} %bitcast.79, bf16[768,1536]{1,0:T(8,128)(2,1)} %bitcast.70, f32[1,768]{1,0:T(1,128)} %reshape_reshape.7.bias_ref), custom_call_target="tpu_custom_call" | custom-call | flops 1000 | bytes 1000 | tf_op jit(solution)/shard_map/project_kv/pallas_call | solution.py:412
  145.2 5.7 %first_forward.1 = (f32[512,768]{1,0:T(8,128)}, f32[512,768]{1,0:T(8,128)}, bf16[512,768]{1,0:T(8,128)(2,1)}, bf16[512,768]{1,0:T(8,128)(2,1)}, bf16[512,768]{1,0:T(8,128)(2,1)}) custom-call(bf16[512,768]{1,0:T(8,128)(2,1)} %own_ref.2, bf16[512,384]{1,0:T(8,128)(2,1)} %copy-done.9, bf16[512,384]{1,0:T(8,128)(2,1)} %copy-done.45, bf16[768,768]{1,0:T(8,128)(2,1)} %bitcast.75, ...), custom_call_target="tpu_custom_call" | custom-call | flops 1000 | bytes 1000 | tf_op jit(solution)/shard_map/first_forward/pallas_call | solution.py:412
  151.5 1.7 collective-permute-start.19
  154.9 13.9 %cross_fwd.1 = (bf16[512,768]{1,0:T(8,128)(2,1)S(1)}, f32[6,2,512]{2,1,0:T(2,128)S(1)}) custom-call(bf16[512,768]{1,0:T(8,128)(2,1)S(1)} %copy-done.6, bf16[512,1536]{1,0:T(8,128)(2,1)S(1)} %copy-done, bf16[512,1536]{1,0:T(8,128)(2,1)S(1)} %collective-permute-done.25.kb_ref.vb_ref, bf16[512,1536]{1,0:T(8,128)(2,1)S(1)} %copy-done, ...), custom_call_target="tpu_custom_call" | custom-call | flops 1000 | bytes 1000 | tf_op jit(solution)/shard_map/cross_fwd/pallas_call | solution.py:182
  169.9 1.8 collective-permute-done.26.e7
  171.8 1.5 copy-done.25
  173.4 32.8 %feed.1 = (bf16[512,768]{1,0:T(8,128)(2,1)}, f32[512,768]{1,0:T(8,128)}, bf16[512,768]{1,0:T(8,128)(2,1)}, bf16[512,768]{1,0:T(8,128)(2,1)}, bf16[2,2,4,104,1536...) custom-call(s32[3]{0:T(128)} %pad_add_fusion.info, bf16[512,768]{1,0:T(8,128)(2,1)} %copy-done.3, ...), custom_call_target="tpu_custom_call" | custom-call | flops 1000 | bytes 1000 | tf_op jit(solution)/shard_map/feed/pallas_call | solution.py:412
  207.5 8.5 %cross_bwd.1 = (bf16[512,768]{1,0:T(8,128)(2,1)S(1)}, bf16[2,512,768]{2,1,0:T(8,128)(2,1)S(1)}, bf16[2,512,768]{2,1,0:T(8,128)(2,1)}) custom-call(bf16[512,768]{1,0:T(8,128)(2,1)S(1)} %copy-done.7, bf16[512,1536]{1,0:T(8,128)(2,1)} %get-tuple-element.226.ka_ref.va_ref, bf16[512,1536]{1,0:T(8,128)(2,1)} %copy-done.1, ...), custom_call_target="tpu_custom_call" | custom-call | flops 1000 | bytes 1000 | tf_op jit(solution)/shard_map/cross_bwd/pallas_call | solution.py:233
  216.1 3.3 fusion.2
  219.4 2.8 fusion.1
  224.0 19.2 %cross_first.1 = (bf16[512,768]{1,0:T(8,128)(2,1)S(1)}, bf16[2,512,768]{2,1,0:T(8,128)(2,1)}, bf16[2,512,768]{2,1,0:T(8,128)(2,1)}, f32[512,768]{1,0:T(8,128)}, ...) custom-call(bf16[512,768]{1,0:T(8,128)(2,1)S(1)} %copy-done.7, ...), custom_call_target="tpu_custom_call", output_to_operand_aliasing={{1}: (14, {}), {2}: (15, {})} | custom-call | flops 1000 | bytes 1000 | tf_op jit(solution)/shard_map/cross_first/pallas_call | solution.py:325
  243.2 9.5 %collective-permute-done.29 = bf16[2,4,104,768]{3,2,1,0:T(8,128)(2,1)S(1)} collective-permute-done((bf16[2,4,104,768]{3,2,1,0:T(8,128)(2,1)}, bf16[2,4,104,768]{3,2,1,0:T(8,128)(2,1)S(1)}, u32[]{:S(2)}, u32[]{:S(2)}) %collective-permute-start.29) | collective-permute-done | bytes 1277984 | tf_op jit(solution)/shard_map/ppermute | solution.py:38
  254.0 2.9 fusion.5
  259.4 12.4 %attn_grads.1 = (bf16[2,2,4,112,960]{4,3,2,1,0:T(8,128)(2,1)}, bf16[2,2,4,112,960]{4,3,2,1,0:T(8,128)(2,1)}, bf16[512,768]{1,0:T(8,128)(2,1)}) custom-call(s32[3]{0:T(128)} %pad_add_fusion.info, bf16[512,768]{1,0:T(8,128)(2,1)} %get-tuple-element.264.h1_ref, bf16[512,768]{1,0:T(8,128)(2,1)} %copy-done.15, bf16[512,768]{1,0:T(8,128)(2,1)} %copy-done.16, ...), custom_call_target="tpu_custom_call" | custom-call | flops 1000 | bytes 1000 | tf_op jit(solution)/shard_map/attn_grads/pallas_call | solution.py:412
  271.9 2.4 collective-permute-done.33
  275.6 2.7 fusion.8
  279.4 4.4 %all-to-all-start.3 = ((bf16[4,104,1536]{2,1,0:T(8,128)(2,1)}), bf16[4,104,1536]{2,1,0:T(8,128)(2,1)}, u32[]{:S(2)}, u32[]{:S(2)}) async-start(bf16[4,104,1536]{2,1,0:T(8,128)(2,1)} %pad_maximum_fusion), calls=%async_computation.3 | async-start | bytes 2555904 | tf_op jit(solution)/shard_map/all_to_all | solution.py:384
  284.9 11.8 %self_bwd.2.rest_0_ = bf16[3,2,512,384]{3,2,1,0:T(8,128)(2,1)S(1)} custom-call(s32[2]{0:T(128)S(1)} %pad_add_fusion.1.info, bf16[2,512,1152]{2,1,0:T(8,128)(2,1)} %get-tuple-element.243.q_ref.k_ref.v_ref, bf16[2,512,1152]{2,1,0:T(8,128)(2,1)} %get-tuple-element.243.q_ref.k_ref.v_ref, bf16[2,512,1152]{2,1,0:T(8,128)(2,1)} %get-tuple-element.243.q_ref.k_ref.v_ref, ...), custom_call_target="tpu_custom_call" | custom-call | flops 1000 | bytes 1000 | tf_op jit(solution)/shard_map/self_bwd/pallas_call | solution.py:123
  296.8 4.2 %fusion.11 = (bf16[4,112,960]{2,1,0:T(8,128)(2,1)}, bf16[4,112,960]{2,1,0:T(8,128)(2,1)}, bf16[4,112,960]{2,1,0:T(8,128)(2,1)}) fusion(bf16[2,2,4,112,960]{4,3,2,1,0:T(8,128)(2,1)} %collective-permute-done.35, bf16[2,2,4,112,960]{4,3,2,1,0:T(8,128)(2,1)S(1)} %copy-done.23), kind=kLoop, calls=%fused_computation.25 | loop fusion | flops 5160960 | bytes 7741440 | tf_op jit(solution)/shard_map/convert_element_type | solution.py:397
  301.0 2.9 collective-permute-done.36
  307.4 6.4 %self_bwd.3.d_ref = bf16[3,2,512,384]{3,2,1,0:T(8,128)(2,1)S(1)} custom-call(s32[2]{0:T(128)S(1)} %pad_add_fusion.1.info, bf16[2,512,1152]{2,1,0:T(8,128)(2,1)} %get-tuple-element.243.q_ref.k_ref.v_ref, bf16[2,512,1152]{2,1,0:T(8,128)(2,1)} %get-tuple-element.243.q_ref.k_ref.v_ref, ...), custom_call_target="tpu_custom_call", output_to_operand_aliasing={{}: (9, {})} | custom-call | flops 1000 | bytes 1000 | tf_op jit(solution)/shard_map/self_bwd/pallas_call | solution.py:123
  315.2 6.1 %self_grads.1 = (bf16[4,104,576]{2,1,0:T(8,128)(2,1)}, bf16[4,104,576]{2,1,0:T(8,128)(2,1)}, bf16[4,104,576]{2,1,0:T(8,128)(2,1)}, bf16[4,104,576]{2,1,0:T(8,128)(2,1)}) custom-call(s32[3]{0:T(128)} %pad_add_fusion.info, bf16[512,768]{1,0:T(8,128)(2,1)} %own_ref.2, bf16[512,768]{1,0:T(8,128)(2,1)} %copy-done.11, bf16[3,2,512,384]{3,2,1,0:T(8,128)(2,1)} %copy-done.2), custom_call_target="tpu_custom_call" | custom-call | flops 1000 | bytes 1000 | tf_op jit(solution)/shard_map/self_grads/pallas_call | solution.py:412
  323.6 3.9 collective-permute-done.37
  327.4 1.7 collective-permute-start.42
  329.1 6.6 %self_back.1 = (f32[512,768]{1,0:T(8,128)}, bf16[512,768]{1,0:T(8,128)(2,1)}) custom-call(bf16[3,2,512,384]{3,2,1,0:T(8,128)(2,1)} %copy-done.2, bf16[768,1152]{1,0:T(8,128)(2,1)} %copy-done.13, f32[512,768]{1,0:T(8,128)} %get-tuple-element.296.first_ref), custom_call_target="tpu_custom_call" | custom-call | flops 1000 | bytes 1000 | tf_op jit(solution)/shard_map/self_back/pallas_call | solution.py:412
  335.7 12.4 %collective-permute-done.38 = bf16[4,112,960]{2,1,0:T(8,128)(2,1)} collective-permute-done((bf16[4,112,960]{2,1,0:T(8,128)(2,1)}, bf16[4,112,960]{2,1,0:T(8,128)(2,1)}, u32[]{:S(2)}, u32[]{:S(2)}) %collective-permute-start.38) | collective-permute-done | bytes 860192 | tf_op jit(solution)/shard_map/ppermute | solution.py:43
  348.2 4.2 %fusion = bf16[4,112,960]{2,1,0:T(8,128)(2,1)} fusion(bf16[4,112,960]{2,1,0:T(8,128)(2,1)} %collective-permute-done.39, bf16[4,112,960]{2,1,0:T(8,128)(2,1)} %collective-permute-done.38, bf16[4,112,960]{2,1,0:T(8,128)(2,1)} %collective-permute-done.37, bf16[2,2,4,112,960]{4,3,2,1,0:T(8,128)(2,1)} %collective-permute-done.35, ...), kind=kLoop, calls=%fused_computation.4 | loop fusion | flops 4300800 | bytes 5160960 | tf_op jit(solution)/shard_map/convert_element_type | solution.py:1537
  352.4 4.8 %all-to-all-start.4 = ((bf16[4,112,960]{2,1,0:T(8,128)(2,1)}), bf16[4,112,960]{2,1,0:T(8,128)(2,1)}, u32[]{:S(2)}, u32[]{:S(2)}) async-start(bf16[4,112,960]{2,1,0:T(8,128)(2,1)} %fusion), calls=%async_computation.4 | async-start | bytes 1835008 | tf_op jit(solution)/shard_map/all_to_all | solution.py:384
  358.4 9.8 %collective-permute-done.41 = bf16[4,104,576]{2,1,0:T(8,128)(2,1)S(1)} collective-permute-done((bf16[4,104,576]{2,1,0:T(8,128)(2,1)}, bf16[4,104,576]{2,1,0:T(8,128)(2,1)S(1)}, u32[]{:S(2)}, u32[]{:S(2)}) %collective-permute-start.41) | collective-permute-done | bytes 479264 | tf_op jit(solution)/shard_map/ppermute | solution.py:43
  369.5 2.1 add_convert_fusion.6
  372.1 2.9 collective-permute-done.44.c_ref
  375.2 2.5 all-to-all-done.4.in_ref
  377.6 4.1 %all-to-all-start.5 = ((bf16[4,104,576]{2,1,0:T(8,128)(2,1)}), bf16[4,104,576]{2,1,0:T(8,128)(2,1)}, u32[]{:S(2)}, u32[]{:S(2)}) async-start(bf16[4,104,576]{2,1,0:T(8,128)(2,1)} %add_convert_fusion.6), calls=%async_computation.5 | async-start | bytes 1064960 | tf_op jit(solution)/shard_map/all_to_all | solution.py:384
  382.1 2.2 sum_feed.1
  384.4 2.6 add_convert_fusion.5
  387.0 4.8 %scatter.1 = f32[32,64,768]{2,1,0:T(8,128)} custom-call(s32[32]{0:T(128)S(1)} %reshape.374.table, bf16[8,64,768]{2,1,0:T(8,128)(2,1)S(1)} %bitcast.67, bf16[8,64,768]{2,1,0:T(8,128)(2,1)S(1)} %bitcast.69, bf16[8,64,768]{2,1,0:T(8,128)(2,1)S(1)} %collective-permute-done.44.c_ref, bf16[8,64,768]{2,1,0:T(8,128)(2,1)S(1)} %collective-permute-done.45.d_ref), custom_call_target="tpu_custom_call" | custom-call | flops 1000 | bytes 1000 | tf_op jit(solution)/shard_map/scatter/pallas_call | solution.py:1157
  391.8 2.1 sum_attn.1
  394.0 1.5 all-to-all-done.5.in_ref
  395.4 1.8 sum_cols.1
  (241 shorter events, 51.1 us)
Async XLA Ops:
  7.3 12.4 %collective-permute-start.2 = (bf16[2,8,64,768]{3,2,1,0:T(8,128)(2,1)}, bf16[2,8,64,768]{3,2,1,0:T(8,128)(2,1)}, u32[]{:S(2)}, u32[]{:S(2)}) collective-permute-start(bf16[2,8,64,768]{3,2,1,0:T(8,128)(2,1)} %bitcast.83), channel_id=1, source_target_pairs={{0,1},{1,0},{2,3},{3,2},{4,5},{5,4},{6,7},{7,6},{8,9},{9,8},{10,11... | collective-permute-start | bytes 4718600 | tf_op jit(solution)/shard_map/ppermute | solution.py:34
  8.0 15.1 %collective-permute-start = (f32[1,1536]{1,0:T(1,128)S(1)}, f32[1,1536]{1,0:T(1,128)S(1)}, u32[]{:S(2)}, u32[]{:S(2)}) collective-permute-start(f32[1,1536]{1,0:T(1,128)S(1)} %reshape.368), channel_id=1, source_target_pairs={{0,2},{2,0},{1,3},{3,1},{4,6},{6,4},{5,7},{7,5},{8,10},{10,8},{9,1... | collective-permute-start | bytes 18440 | tf_op jit(solution)/shard_map/ppermute | solution.py:38
  10.4 21.3 %collective-permute-start.3 = (bf16[512,768]{1,0:T(8,128)(2,1)S(1)}, bf16[512,768]{1,0:T(8,128)(2,1)S(1)}, u32[]{:S(2)}, u32[]{:S(2)}) collective-permute-start(bf16[512,768]{1,0:T(8,128)(2,1)S(1)} %copy-done.5), channel_id=1, source_target_pairs={{0,1},{1,0},{2,3},{3,2},{4,5},{5,4},{6,7},{7,6},{8,9},{9,8},{10,11... | collective-permute-start | bytes 2359304 | tf_op jit(solution)/shard_map/ppermute | solution.py:34
  12.5 19.3 %all-to-all-start = ((bf16[4,96,576]{2,1,0:T(8,128)(2,1)}), bf16[4,96,576]{2,1,0:T(8,128)(2,1)S(1)}, u32[]{:S(2)}, u32[]{:S(2)}) async-start(bf16[4,96,576]{2,1,0:T(8,128)(2,1)} %pack_self.1), calls=%async_computation | async-start | bytes 983040 | tf_op jit(solution)/shard_map/all_to_all | solution.py:384
  22.5 19.7 %collective-permute-start.4 = (bf16[8,64,768]{2,1,0:T(8,128)(2,1)}, bf16[8,64,768]{2,1,0:T(8,128)(2,1)S(1)}, u32[]{:S(2)}, u32[]{:S(2)}) collective-permute-start(bf16[8,64,768]{2,1,0:T(8,128)(2,1)} %get-tuple-element.349), channel_id=1, source_target_pairs={{0,2},{2,0},{1,3},{3,1},{4,6},{6,4},{5,7},{7,5},{8,10},{10,8},{9,1... | collective-permute-start | bytes 2359304 | tf_op jit(solution)/shard_map/ppermute | solution.py:38
  23.3 1.2 collective-permute-start.1
  31.8 60.9 %copy-start.11 = (bf16[512,768]{1,0:T(8,128)(2,1)}, bf16[512,768]{1,0:T(8,128)(2,1)S(1)}, u32[]{:S(2)}) copy-start(bf16[512,768]{1,0:T(8,128)(2,1)S(1)} %collective-permute-done.3.oth_ref) | copy-start | bytes 2359300
  43.1 38.8 %all-to-all-start.1 = ((bf16[4,96,1728]{2,1,0:T(8,128)(2,1)}), bf16[4,96,1728]{2,1,0:T(8,128)(2,1)}, u32[]{:S(2)}, u32[]{:S(2)}) async-start(bf16[4,96,1728]{2,1,0:T(8,128)(2,1)} %get-tuple-element.189), calls=%async_computation.1 | async-start | bytes 2752512 | tf_op jit(solution)/shard_map/all_to_all | solution.py:384
  47.9 14.2 %collective-permute-start.5 = (bf16[4,96,576]{2,1,0:T(8,128)(2,1)S(1)}, bf16[4,96,576]{2,1,0:T(8,128)(2,1)S(1)}, u32[]{:S(2)}, u32[]{:S(2)}) collective-permute-start(bf16[4,96,576]{2,1,0:T(8,128)(2,1)S(1)} %all-to-all-done.w_ref), channel_id=1, source_target_pairs={{0,2},{2,0},{1,3},{3,1},{4,6},{6,4},{5,7},{7,5},{8,10},{10,8},{9,1... | collective-permute-start | bytes 1327112 | tf_op jit(solution)/shard_map/ppermute | solution.py:38
  48.5 33.4 %collective-permute-start.7 = (bf16[4,96,576]{2,1,0:T(8,128)(2,1)S(1)}, bf16[4,96,576]{2,1,0:T(8,128)(2,1)S(1)}, u32[]{:S(2)}, u32[]{:S(2)}) collective-permute-start(bf16[4,96,576]{2,1,0:T(8,128)(2,1)S(1)} %all-to-all-done.w_ref), channel_id=1, source_target_pairs={{0,6},{1,7},{2,4},{3,5},{4,2},{5,3},{6,0},{7,1},{8,14},{9,15},{10,... | collective-permute-start | bytes 1327112 | tf_op jit(solution)/shard_map/ppermute | solution.py:379
  50.9 31.0 %collective-permute-start.6 = (bf16[4,96,576]{2,1,0:T(8,128)(2,1)S(1)}, bf16[4,96,576]{2,1,0:T(8,128)(2,1)S(1)}, u32[]{:S(2)}, u32[]{:S(2)}) collective-permute-start(bf16[4,96,576]{2,1,0:T(8,128)(2,1)S(1)} %all-to-all-done.w_ref), channel_id=1, source_target_pairs={{0,4},{4,0},{8,12},{12,8},{16,20},{20,16},{24,28},{28,24},{1,5},{5... | collective-permute-start | bytes 1327112 | tf_op jit(solution)/shard_map/ppermute | solution.py:43
  62.1 14.1 %collective-permute-start.10 = (bf16[96,768]{1,0:T(8,128)(2,1)}, bf16[96,768]{1,0:T(8,128)(2,1)}, u32[]{:S(2)}, u32[]{:S(2)}) collective-permute-start(bf16[96,768]{1,0:T(8,128)(2,1)} %get-tuple-element.192.own_ref), channel_id=1, source_target_pairs={{0,6},{1,7},{2,4},{3,5},{4,2},{5,3},{6,0},{7,1},{8,14},{9,15},{10,... | collective-permute-start | bytes 442376 | tf_op jit(solution)/shard_map/ppermute | solution.py:379
  63.6 15.6 %collective-permute-start.9 = (bf16[96,768]{1,0:T(8,128)(2,1)}, bf16[96,768]{1,0:T(8,128)(2,1)}, u32[]{:S(2)}, u32[]{:S(2)}) collective-permute-start(bf16[96,768]{1,0:T(8,128)(2,1)} %get-tuple-element.192.own_ref), channel_id=1, source_target_pairs={{0,4},{4,0},{8,12},{12,8},{16,20},{20,16},{24,28},{28,24},{1,5},{5... | collective-permute-start | bytes 442376 | tf_op jit(solution)/shard_map/ppermute | solution.py:43
  64.1 15.1 %collective-permute-start.8 = (bf16[96,768]{1,0:T(8,128)(2,1)}, bf16[96,768]{1,0:T(8,128)(2,1)}, u32[]{:S(2)}, u32[]{:S(2)}) collective-permute-start(bf16[96,768]{1,0:T(8,128)(2,1)} %get-tuple-element.192.own_ref), channel_id=1, source_target_pairs={{0,2},{2,0},{1,3},{3,1},{4,6},{6,4},{5,7},{7,5},{8,10},{10,8},{9,1... | collective-permute-start | bytes 442376 | tf_op jit(solution)/shard_map/ppermute | solution.py:38
  84.2 26.6 %collective-permute-start.14 = (bf16[4,96,960]{2,1,0:T(8,128)(2,1)}, bf16[4,96,960]{2,1,0:T(8,128)(2,1)}, u32[]{:S(2)}, u32[]{:S(2)}) collective-permute-start(bf16[4,96,960]{2,1,0:T(8,128)(2,1)} %slice.114.refs_0_), channel_id=1, source_target_pairs={{0,6},{1,7},{2,4},{3,5},{4,2},{5,3},{6,0},{7,1},{8,14},{9,15},{10,... | collective-permute-start | bytes 2211848 | tf_op jit(solution)/shard_map/ppermute | solution.py:379
  84.7 34.9 %collective-permute-start.13 = (bf16[4,96,960]{2,1,0:T(8,128)(2,1)}, bf16[4,96,960]{2,1,0:T(8,128)(2,1)}, u32[]{:S(2)}, u32[]{:S(2)}) collective-permute-start(bf16[4,96,960]{2,1,0:T(8,128)(2,1)} %slice.114.refs_0_), channel_id=1, source_target_pairs={{0,4},{4,0},{8,12},{12,8},{16,20},{20,16},{24,28},{28,24},{1,5},{5... | collective-permute-start | bytes 2211848 | tf_op jit(solution)/shard_map/ppermute | solution.py:43
  86.2 33.4 %collective-permute-start.12 = (bf16[4,96,960]{2,1,0:T(8,128)(2,1)}, bf16[4,96,960]{2,1,0:T(8,128)(2,1)}, u32[]{:S(2)}, u32[]{:S(2)}) collective-permute-start(bf16[4,96,960]{2,1,0:T(8,128)(2,1)} %slice.114.refs_0_), channel_id=1, source_target_pairs={{0,2},{2,0},{1,3},{3,1},{4,6},{6,4},{5,7},{7,5},{8,10},{10,8},{9,1... | collective-permute-start | bytes 2211848 | tf_op jit(solution)/shard_map/ppermute | solution.py:38
  87.7 63.2 %all-to-all-start.2 = ((bf16[4,2,2,96,768]{4,3,2,1,0:T(8,128)(2,1)}), bf16[4,2,2,96,768]{4,3,2,1,0:T(8,128)(2,1)}, u32[]{:S(2)}, u32[]{:S(2)}) async-start(bf16[4,2,2,96,768]{4,3,2,1,0:T(8,128)(2,1)} %plane_copies.1), calls=%async_computation.2 | async-start | bytes 4718592 | tf_op jit(solution)/shard_map/all_to_all | solution.py:384
  108.5 20.0 %copy-start.19 = (f32[3,2,2,512]{3,2,1,0:T(2,128)}, f32[3,2,2,512]{3,2,1,0:T(2,128)S(1)}, u32[]{:S(2)}) copy-start(f32[3,2,2,512]{3,2,1,0:T(2,128)S(1)} %get-tuple-element.244.lse_ref) | copy-start | bytes 73732
  108.5 18.9 %copy-start.24 = (bf16[8,64,768]{2,1,0:T(8,128)(2,1)S(1)}, bf16[8,64,768]{2,1,0:T(8,128)(2,1)}, u32[]{:S(2)}) copy-start(bf16[8,64,768]{2,1,0:T(8,128)(2,1)} %get-tuple-element.348) | copy-start | bytes 2359300
  108.5 2.3 collective-permute-start.15
  108.5 12.8 %collective-permute-start.11 = (bf16[4,96,960]{2,1,0:T(8,128)(2,1)}, bf16[4,96,960]{2,1,0:T(8,128)(2,1)S(1)}, u32[]{:S(2)}, u32[]{:S(2)}) collective-permute-start(bf16[4,96,960]{2,1,0:T(8,128)(2,1)} %slice.114.refs_0_), channel_id=1, source_target_pairs={{0,1},{1,0},{2,3},{3,2},{4,5},{5,4},{6,7},{7,6},{8,9},{9,8},{10,11... | collective-permute-start | bytes 2211848 | tf_op jit(solution)/shard_map/ppermute | solution.py:34
  119.6 2.5 collective-permute-start.16
  119.6 3.6 collective-permute-start.17
  120.1 4.2 %collective-permute-start.18 = (bf16[4,96,960]{2,1,0:T(8,128)(2,1)}, bf16[4,96,960]{2,1,0:T(8,128)(2,1)S(1)}, u32[]{:S(2)}, u32[]{:S(2)}) collective-permute-start(bf16[4,96,960]{2,1,0:T(8,128)(2,1)} %collective-permute-done.14.refs_3_), channel_id=1, source_target_pairs={{0,1},{1,0},{2,3},{3,2},{4,5},{5,4},{6,7},{7,6},{8,9},{9,8},{10,11... | collective-permute-start | bytes 2211848 | tf_op jit(solution)/shard_map/ppermute | solution.py:34
  124.3 15.4 %collective-permute-start.22 = (bf16[4,96,768]{2,1,0:T(8,128)(2,1)S(1)}, bf16[4,96,768]{2,1,0:T(8,128)(2,1)S(1)}, u32[]{:S(2)}, u32[]{:S(2)}) collective-permute-start(bf16[4,96,768]{2,1,0:T(8,128)(2,1)S(1)} %slice.115.e0), channel_id=1, source_target_pairs={{0,4},{4,0},{8,12},{12,8},{16,20},{20,16},{24,28},{28,24},{1,5},{5... | collective-permute-start | bytes 1769480 | tf_op jit(solution)/shard_map/ppermute | solution.py:43
  125.1 15.1 %collective-permute-start.21 = (bf16[4,96,768]{2,1,0:T(8,128)(2,1)S(1)}, bf16[4,96,768]{2,1,0:T(8,128)(2,1)S(1)}, u32[]{:S(2)}, u32[]{:S(2)}) collective-permute-start(bf16[4,96,768]{2,1,0:T(8,128)(2,1)S(1)} %slice.115.e0), channel_id=1, source_target_pairs={{0,2},{2,0},{1,3},{3,1},{4,6},{6,4},{5,7},{7,5},{8,10},{10,8},{9,1... | collective-permute-start | bytes 1769480 | tf_op jit(solution)/shard_map/ppermute | solution.py:38
  145.2 5.7 %collective-permute-start.25 = (bf16[512,1536]{1,0:T(8,128)(2,1)}, bf16[512,1536]{1,0:T(8,128)(2,1)S(1)}, u32[]{:S(2)}, u32[]{:S(2)}) collective-permute-start(bf16[512,1536]{1,0:T(8,128)(2,1)} %get-tuple-element.226.ka_ref.va_ref), channel_id=1, source_target_pairs={{0,1},{1,0},{2,3},{3,2},{4,5},{5,4},{6,7},{7,6},{8,9},{9,8},{10,11... | collective-permute-start | bytes 4718600 | tf_op jit(solution)/shard_map/ppermute | solution.py:34
  150.9 17.9 %copy-start.1 = (bf16[512,1536]{1,0:T(8,128)(2,1)}, bf16[512,1536]{1,0:T(8,128)(2,1)S(1)}, u32[]{:S(2)}) copy-start(bf16[512,1536]{1,0:T(8,128)(2,1)S(1)} %collective-permute-done.25.kb_ref.vb_ref) | copy-start | bytes 4718596
  150.9 20.9 %collective-permute-start.27 = (bf16[4,2,2,96,768]{4,3,2,1,0:T(8,128)(2,1)}, bf16[4,2,2,96,768]{4,3,2,1,0:T(8,128)(2,1)S(1)}, u32[]{:S(2)}, u32[]{:S(2)}) collective-permute-start(bf16[4,2,2,96,768]{4,3,2,1,0:T(8,128)(2,1)} %all-to-all-done.2.s0), channel_id=1, source_target_pairs={{0,1},{1,0},{2,3},{3,2},{4,5},{5,4},{6,7},{7,6},{8,9},{9,8},{10,11... | collective-permute-start | bytes 7077896 | tf_op jit(solution)/shard_map/ppermute | solution.py:34
  151.5 18.2 %collective-permute-start.20 = (bf16[4,96,768]{2,1,0:T(8,128)(2,1)}, bf16[4,96,768]{2,1,0:T(8,128)(2,1)S(1)}, u32[]{:S(2)}, u32[]{:S(2)}) collective-permute-start(bf16[4,96,768]{2,1,0:T(8,128)(2,1)} %copy-done.26), channel_id=1, source_target_pairs={{0,1},{1,0},{2,3},{3,2},{4,5},{5,4},{6,7},{7,6},{8,9},{9,8},{10,11... | collective-permute-start | bytes 1769480 | tf_op jit(solution)/shard_map/ppermute | solution.py:34
  151.5 18.1 %collective-permute-start.19 = (bf16[4,96,768]{2,1,0:T(8,128)(2,1)}, bf16[4,96,768]{2,1,0:T(8,128)(2,1)S(1)}, u32[]{:S(2)}, u32[]{:S(2)}) collective-permute-start(bf16[4,96,768]{2,1,0:T(8,128)(2,1)} %copy-done.26), channel_id=1, source_target_pairs={{0,6},{1,7},{2,4},{3,5},{4,2},{5,3},{6,0},{7,1},{8,14},{9,15},{10,... | collective-permute-start | bytes 1769480 | tf_op jit(solution)/shard_map/ppermute | solution.py:379
  153.2 16.4 %collective-permute-start.23 = (bf16[4,96,768]{2,1,0:T(8,128)(2,1)}, bf16[4,96,768]{2,1,0:T(8,128)(2,1)S(1)}, u32[]{:S(2)}, u32[]{:S(2)}) collective-permute-start(bf16[4,96,768]{2,1,0:T(8,128)(2,1)} %copy-done.37), channel_id=1, source_target_pairs={{0,1},{1,0},{2,3},{3,2},{4,5},{5,4},{6,7},{7,6},{8,9},{9,8},{10,11... | collective-permute-start | bytes 1769480 | tf_op jit(solution)/shard_map/ppermute | solution.py:34
  153.4 16.3 %collective-permute-start.24 = (bf16[4,96,768]{2,1,0:T(8,128)(2,1)}, bf16[4,96,768]{2,1,0:T(8,128)(2,1)S(1)}, u32[]{:S(2)}, u32[]{:S(2)}) collective-permute-start(bf16[4,96,768]{2,1,0:T(8,128)(2,1)} %copy-done.38), channel_id=1, source_target_pairs={{0,1},{1,0},{2,3},{3,2},{4,5},{5,4},{6,7},{7,6},{8,9},{9,8},{10,11... | collective-permute-start | bytes 1769480 | tf_op jit(solution)/shard_map/ppermute | solution.py:34
  169.7 2.1 collective-permute-start.26
  173.4 33.0 %copy-start.4 = (bf16[512,768]{1,0:T(8,128)(2,1)S(1)}, bf16[512,768]{1,0:T(8,128)(2,1)}, u32[]{:S(2)}) copy-start(bf16[512,768]{1,0:T(8,128)(2,1)} %copy-done.3) | copy-start | bytes 2359300
  173.4 33.0 %copy-start.7 = (bf16[512,768]{1,0:T(8,128)(2,1)S(1)}, bf16[512,768]{1,0:T(8,128)(2,1)}, u32[]{:S(2)}) copy-start(bf16[512,768]{1,0:T(8,128)(2,1)} %get-tuple-element.230.q_ref) | copy-start | bytes 2359300
  206.2 9.9 %collective-permute-start.28 = (bf16[2,2,4,104,1536]{4,3,2,1,0:T(8,128)(2,1)}, bf16[2,2,4,104,1536]{4,3,2,1,0:T(8,128)(2,1)}, u32[]{:S(2)}, u32[]{:S(2)}) collective-permute-start(bf16[2,2,4,104,1536]{4,3,2,1,0:T(8,128)(2,1)} %get-tuple-element.252), channel_id=1, source_target_pairs={{0,1},{1,0},{2,3},{3,2},{4,5},{5,4},{6,7},{7,6},{8,9},{9,8},{10,11... | collective-permute-start | bytes 15335432 | tf_op jit(solution)/shard_map/ppermute | solution.py:34
  222.2 30.5 %collective-permute-start.29 = (bf16[2,4,104,768]{3,2,1,0:T(8,128)(2,1)}, bf16[2,4,104,768]{3,2,1,0:T(8,128)(2,1)S(1)}, u32[]{:S(2)}, u32[]{:S(2)}) collective-permute-start(bf16[2,4,104,768]{3,2,1,0:T(8,128)(2,1)} %fusion.1), channel_id=1, source_target_pairs={{0,2},{2,0},{1,3},{3,1},{4,6},{6,4},{5,7},{7,5},{8,10},{10,8},{9,1... | collective-permute-start | bytes 3833864 | tf_op jit(solution)/shard_map/ppermute | solution.py:38
  223.2 30.3 %collective-permute-start.30 = (bf16[2,4,104,768]{3,2,1,0:T(8,128)(2,1)}, bf16[2,4,104,768]{3,2,1,0:T(8,128)(2,1)S(1)}, u32[]{:S(2)}, u32[]{:S(2)}) collective-permute-start(bf16[2,4,104,768]{3,2,1,0:T(8,128)(2,1)} %fusion.2), channel_id=1, source_target_pairs={{0,4},{4,0},{8,12},{12,8},{16,20},{20,16},{24,28},{28,24},{1,5},{5... | collective-permute-start | bytes 3833864 | tf_op jit(solution)/shard_map/ppermute | solution.py:43
  243.2 13.6 %copy-start.15 = (bf16[512,768]{1,0:T(8,128)(2,1)}, bf16[512,768]{1,0:T(8,128)(2,1)S(1)}, u32[]{:S(2)}) copy-start(bf16[512,768]{1,0:T(8,128)(2,1)S(1)} %get-tuple-element.265.dq_ref) | copy-start | bytes 2359300
  243.2 13.6 %copy-start.16 = (bf16[512,768]{1,0:T(8,128)(2,1)}, bf16[512,768]{1,0:T(8,128)(2,1)S(1)}, u32[]{:S(2)}) copy-start(bf16[512,768]{1,0:T(8,128)(2,1)S(1)} %get-tuple-element.270.e1_ref) | copy-start | bytes 2359300
  243.2 13.6 %copy-start.21 = (f32[8,768]{1,0:T(8,128)}, f32[8,768]{1,0:T(8,128)S(1)}, u32[]{:S(2)}) copy-start(f32[8,768]{1,0:T(8,128)S(1)} %get-tuple-element.273.sums_ref) | copy-start | bytes 73732
  253.4 4.2 %collective-permute-start.31 = (bf16[2,512,768]{2,1,0:T(8,128)(2,1)}, bf16[2,512,768]{2,1,0:T(8,128)(2,1)S(1)}, u32[]{:S(2)}, u32[]{:S(2)}) collective-permute-start(bf16[2,512,768]{2,1,0:T(8,128)(2,1)} %get-tuple-element.267), channel_id=1, source_target_pairs={{0,1},{1,0},{2,3},{3,2},{4,5},{5,4},{6,7},{7,6},{8,9},{9,8},{10,11... | collective-permute-start | bytes 4718600 | tf_op jit(solution)/shard_map/ppermute | solution.py:34
  253.4 3.6 collective-permute-start.32
  257.6 16.6 %collective-permute-start.33 = (bf16[4,104,768]{2,1,0:T(8,128)(2,1)}, bf16[4,104,768]{2,1,0:T(8,128)(2,1)S(1)}, u32[]{:S(2)}, u32[]{:S(2)}) collective-permute-start(bf16[4,104,768]{2,1,0:T(8,128)(2,1)} %get-tuple-element.279), channel_id=1, source_target_pairs={{0,4},{4,0},{8,12},{12,8},{16,20},{20,16},{24,28},{28,24},{1,5},{5... | collective-permute-start | bytes 1916936 | tf_op jit(solution)/shard_map/ppermute | solution.py:43
  258.4 16.4 %collective-permute-start.34 = (bf16[4,104,768]{2,1,0:T(8,128)(2,1)}, bf16[4,104,768]{2,1,0:T(8,128)(2,1)S(1)}, u32[]{:S(2)}, u32[]{:S(2)}) collective-permute-start(bf16[4,104,768]{2,1,0:T(8,128)(2,1)} %get-tuple-element.280), channel_id=1, source_target_pairs={{0,2},{2,0},{1,3},{3,1},{4,6},{6,4},{5,7},{7,5},{8,10},{10,8},{9,1... | collective-permute-start | bytes 1916936 | tf_op jit(solution)/shard_map/ppermute | solution.py:38
  259.4 16.2 %copy-start.29 = (bf16[2,4,104,768]{3,2,1,0:T(8,128)(2,1)S(1)}, bf16[2,4,104,768]{3,2,1,0:T(8,128)(2,1)}, u32[]{:S(2)}) copy-start(bf16[2,4,104,768]{3,2,1,0:T(8,128)(2,1)} %copy-done.28) | copy-start | bytes 3833860
  275.6 21.2 %collective-permute-start.35 = (bf16[2,2,4,112,960]{4,3,2,1,0:T(8,128)(2,1)}, bf16[2,2,4,112,960]{4,3,2,1,0:T(8,128)(2,1)}, u32[]{:S(2)}, u32[]{:S(2)}) collective-permute-start(bf16[2,2,4,112,960]{4,3,2,1,0:T(8,128)(2,1)} %get-tuple-element.287), channel_id=1, source_target_pairs={{0,1},{1,0},{2,3},{3,2},{4,5},{5,4},{6,7},{7,6},{8,9},{9,8},{10,11... | collective-permute-start | bytes 10321928 | tf_op jit(solution)/shard_map/ppermute | solution.py:34
  279.4 56.3 %all-to-all-start.3 = ((bf16[4,104,1536]{2,1,0:T(8,128)(2,1)}), bf16[4,104,1536]{2,1,0:T(8,128)(2,1)}, u32[]{:S(2)}, u32[]{:S(2)}) async-start(bf16[4,104,1536]{2,1,0:T(8,128)(2,1)} %pad_maximum_fusion), calls=%async_computation.3 | async-start | bytes 2555904 | tf_op jit(solution)/shard_map/all_to_all | solution.py:384
  283.9 20.0 %collective-permute-start.36 = (bf16[512,768]{1,0:T(8,128)(2,1)S(1)}, bf16[512,768]{1,0:T(8,128)(2,1)S(1)}, u32[]{:S(2)}, u32[]{:S(2)}) collective-permute-start(bf16[512,768]{1,0:T(8,128)(2,1)S(1)} %copy-done.14), channel_id=1, source_target_pairs={{0,2},{2,0},{1,3},{3,1},{4,6},{6,4},{5,7},{7,5},{8,10},{10,8},{9,1... | collective-permute-start | bytes 2359304 | tf_op jit(solution)/shard_map/ppermute | solution.py:38
  303.9 23.6 %collective-permute-start.37 = (bf16[4,112,960]{2,1,0:T(8,128)(2,1)}, bf16[4,112,960]{2,1,0:T(8,128)(2,1)}, u32[]{:S(2)}, u32[]{:S(2)}) collective-permute-start(bf16[4,112,960]{2,1,0:T(8,128)(2,1)} %get-tuple-element.300), channel_id=1, source_target_pairs={{0,2},{2,0},{1,3},{3,1},{4,6},{6,4},{5,7},{7,5},{8,10},{10,8},{9,1... | collective-permute-start | bytes 2580488 | tf_op jit(solution)/shard_map/ppermute | solution.py:38
  304.9 43.3 %collective-permute-start.38 = (bf16[4,112,960]{2,1,0:T(8,128)(2,1)}, bf16[4,112,960]{2,1,0:T(8,128)(2,1)}, u32[]{:S(2)}, u32[]{:S(2)}) collective-permute-start(bf16[4,112,960]{2,1,0:T(8,128)(2,1)} %get-tuple-element.301), channel_id=1, source_target_pairs={{0,4},{4,0},{8,12},{12,8},{16,20},{20,16},{24,28},{28,24},{1,5},{5... | collective-permute-start | bytes 2580488 | tf_op jit(solution)/shard_map/ppermute | solution.py:43
  306.1 42.0 %collective-permute-start.39 = (bf16[4,112,960]{2,1,0:T(8,128)(2,1)}, bf16[4,112,960]{2,1,0:T(8,128)(2,1)}, u32[]{:S(2)}, u32[]{:S(2)}) collective-permute-start(bf16[4,112,960]{2,1,0:T(8,128)(2,1)} %get-tuple-element.302), channel_id=1, source_target_pairs={{0,6},{1,7},{2,4},{3,5},{4,2},{5,3},{6,0},{7,1},{8,14},{9,15},{10,... | collective-permute-start | bytes 2580488 | tf_op jit(solution)/shard_map/ppermute | solution.py:379
  321.3 37.1 %collective-permute-start.40 = (bf16[4,104,576]{2,1,0:T(8,128)(2,1)}, bf16[4,104,576]{2,1,0:T(8,128)(2,1)S(1)}, u32[]{:S(2)}, u32[]{:S(2)}) collective-permute-start(bf16[4,104,576]{2,1,0:T(8,128)(2,1)} %get-tuple-element.305), channel_id=1, source_target_pairs={{0,2},{2,0},{1,3},{3,1},{4,6},{6,4},{5,7},{7,5},{8,10},{10,8},{9,1... | collective-permute-start | bytes 1437704 | tf_op jit(solution)/shard_map/ppermute | solution.py:38
  322.4 45.9 %collective-permute-start.41 = (bf16[4,104,576]{2,1,0:T(8,128)(2,1)}, bf16[4,104,576]{2,1,0:T(8,128)(2,1)S(1)}, u32[]{:S(2)}, u32[]{:S(2)}) collective-permute-start(bf16[4,104,576]{2,1,0:T(8,128)(2,1)} %get-tuple-element.306), channel_id=1, source_target_pairs={{0,4},{4,0},{8,12},{12,8},{16,20},{20,16},{24,28},{28,24},{1,5},{5... | collective-permute-start | bytes 1437704 | tf_op jit(solution)/shard_map/ppermute | solution.py:43
  327.4 42.1 %collective-permute-start.42 = (bf16[4,104,576]{2,1,0:T(8,128)(2,1)}, bf16[4,104,576]{2,1,0:T(8,128)(2,1)}, u32[]{:S(2)}, u32[]{:S(2)}) collective-permute-start(bf16[4,104,576]{2,1,0:T(8,128)(2,1)} %get-tuple-element.307), channel_id=1, source_target_pairs={{0,6},{1,7},{2,4},{3,5},{4,2},{5,3},{6,0},{7,1},{8,14},{9,15},{10,... | collective-permute-start | bytes 1437704 | tf_op jit(solution)/shard_map/ppermute | solution.py:379
  352.4 17.1 %copy-start.44 = (bf16[4,104,576]{2,1,0:T(8,128)(2,1)S(1)}, bf16[4,104,576]{2,1,0:T(8,128)(2,1)}, u32[]{:S(2)}) copy-start(bf16[4,104,576]{2,1,0:T(8,128)(2,1)} %get-tuple-element.304) | copy-start | bytes 1437700
  352.4 25.2 %all-to-all-start.4 = ((bf16[4,112,960]{2,1,0:T(8,128)(2,1)}), bf16[4,112,960]{2,1,0:T(8,128)(2,1)}, u32[]{:S(2)}, u32[]{:S(2)}) async-start(bf16[4,112,960]{2,1,0:T(8,128)(2,1)} %fusion), calls=%async_computation.4 | async-start | bytes 1835008 | tf_op jit(solution)/shard_map/all_to_all | solution.py:384
  357.2 24.6 %copy-start.46 = (s32[2,16]{1,0:T(2,128)S(1)}, s32[2,16]{1,0:T(2,128)}, u32[]{:S(2)}) copy-start(s32[2,16]{1,0:T(2,128)} %param.32) | copy-start | bytes 388
  371.6 3.4 collective-permute-start.44
  371.6 12.7 %collective-permute-start.43 = (bf16[512,768]{1,0:T(8,128)(2,1)}, bf16[512,768]{1,0:T(8,128)(2,1)}, u32[]{:S(2)}, u32[]{:S(2)}) collective-permute-start(bf16[512,768]{1,0:T(8,128)(2,1)} %get-tuple-element.308), channel_id=1, source_target_pairs={{0,1},{1,0},{2,3},{3,2},{4,5},{5,4},{6,7},{7,6},{8,9},{9,8},{10,11... | collective-permute-start | bytes 2359304 | tf_op jit(solution)/shard_map/ppermute | solution.py:34
  375.0 12.0 %collective-permute-start.45 = (bf16[8,64,768]{2,1,0:T(8,128)(2,1)S(1)}, bf16[8,64,768]{2,1,0:T(8,128)(2,1)S(1)}, u32[]{:S(2)}, u32[]{:S(2)}) collective-permute-start(bf16[8,64,768]{2,1,0:T(8,128)(2,1)S(1)} %bitcast.68), channel_id=1, source_target_pairs={{0,1},{1,0},{2,3},{3,2},{4,5},{5,4},{6,7},{7,6},{8,9},{9,8},{10,11... | collective-permute-start | bytes 2359304 | tf_op jit(solution)/shard_map/ppermute | solution.py:34
  377.6 17.8 %all-to-all-start.5 = ((bf16[4,104,576]{2,1,0:T(8,128)(2,1)}), bf16[4,104,576]{2,1,0:T(8,128)(2,1)}, u32[]{:S(2)}, u32[]{:S(2)}) async-start(bf16[4,104,576]{2,1,0:T(8,128)(2,1)} %add_convert_fusion.6), calls=%async_computation.5 | async-start | bytes 1064960 | tf_op jit(solution)/shard_map/all_to_all | solution.py:384
  (50 other events, 270.3 us)

commit v4 on v3

--- a/solution.py
+++ b/solution.py
@@ -1327,7 +1327,7 @@
     self_leaf = call(
         pack_self_kernel,
         struct((outer, depth, 3 * head_cols), BF),
-        [gate(selfq_weight, part_send), selfk_weight, selfv_weight],
+        [gate(selfq_weight, part_away), selfk_weight, selfv_weight],
         [VM] * 3,
         VM,
         name="pack_self",

time: 402 us -> 398 us (0.990)
    ppermute x11, waiting for transfers between devices: 39.6 us -> 29.1 us  [swap_x(): return lax.ppermute(value, 'tensor', X_SWAP)]
    all_to_all x6, waiting for transfers between devices: 5.83 us -> 10.9 us  [outer_exchange(): lax.all_to_all(value, 'dp', 0, 0, axis_index_groups=groups, tiled=True)]
    unnamed x124 -> x126, local copies, waits for them, and re-layouts: 11.1 us -> 11.1 us
  transfers between devices with their start and end apart: 52 -> 52, of which waited for: 29 -> 28; matrix products, arithmetic and copies ran while one was open for 8% -> 8% of each run, Pallas kernels for 33% -> 34%
where the time goes in v4:
time: 398 us; the launch traced here: 393 us
  Pallas kernels  171 us (43%)
  waiting for transfers between devices  105 us (26%)
  starting transfers between devices  61.9 us (16%)
  other arithmetic  33.1 us (8%)
  local copies, waits for them, and re-layouts  20 us (5%)
    pallas_call x14, Pallas kernels, call(): pl.pallas_call(kernel, out_shape=out_shape, in_specs=in_specs, out_specs=...  94 us
    ppermute x8, waiting for transfers between devices, swap_dp(): lax.ppermute(value, 'dp', tuple(((i, i ^ bit) for i in range(count))))  43 us
    ppermute x11, waiting for transfers between devices, swap_x(): return lax.ppermute(value, 'tensor', X_SWAP)  29.1 us
    all_to_all x6, starting transfers between devices, outer_exchange(): lax.all_to_all(value, 'dp', 0, 0, axis_index_groups=groups, tiled=True)  27.6 us
    pallas_call x1, Pallas kernels, cross_first_backward(): pl.pallas_call(functools.partial(cross_first_kernel, start=start, count=c...  19.2 us
    pallas_call x2, Pallas kernels, self_backward(): pl.pallas_call(self_bwd_kernel, grid_spec=pltpu.PrefetchScalarGridSpec(nu...  18.2 us
    pallas_call x1, Pallas kernels, cross_forward(): pl.pallas_call(cross_fwd_kernel, grid=(pairs,), in_specs=[whole, whole, t...  13.9 us
    pallas_call x1, Pallas kernels, self_forward(): pl.pallas_call(self_forward_kernel, grid_spec=pltpu.PrefetchScalarGridSpe...  12.9 us
  transfers between devices with their start and end apart: 52, of which 28 were waited for; matrix products, arithmetic and copies ran while one was open for 8% of the time, Pallas kernels for 34%

profile of v4, /device:TPU:0, one launch (start us, length us, event | category | flops | bytes accessed | tf_op | source)
XLA Modules:
  0.0 393.4 jit_solution(11762946721837183348)
XLA Ops:
  3.0 4.2 %fetch.1 = (bf16[16,64,768]{2,1,0:T(8,128)(2,1)}, bf16[16,64,768]{2,1,0:T(8,128)(2,1)}) custom-call(s32[32]{0:T(128)} %select_n.75.table, bf16[32,64,768]{2,1,0:T(8,128)(2,1)} %bitcast.77), custom_call_target="tpu_custom_call" | custom-call | flops 1000 | bytes 1000 | tf_op jit(solution)/shard_map/fetch/pallas_call | solution.py:412
  7.9 2.6 collective-permute-start.1
  12.9 3.2 fusion.16
  17.1 1.9 pack_self.1
  19.0 4.9 %all-to-all-start = ((bf16[4,96,576]{2,1,0:T(8,128)(2,1)}), bf16[4,96,576]{2,1,0:T(8,128)(2,1)S(1)}, u32[]{:S(2)}, u32[]{:S(2)}) async-start(bf16[4,96,576]{2,1,0:T(8,128)(2,1)} %pack_self.1), calls=%async_computation | async-start | bytes 983040 | tf_op jit(solution)/shard_map/all_to_all | solution.py:384
  26.8 1.3 concatenate.46.vec_ref
  28.0 2.6 pack_rest.1
  30.7 7.0 %all-to-all-done.w_ref = bf16[4,96,576]{2,1,0:T(8,128)(2,1)S(1)} async-done(((bf16[4,96,576]{2,1,0:T(8,128)(2,1)}), bf16[4,96,576]{2,1,0:T(8,128)(2,1)S(1)}, u32[]{:S(2)}, u32[]{:S(2)}) %all-to-all-start) | async-done | bytes 442400 | tf_op jit(solution)/shard_map/all_to_all | solution.py:384
  38.6 4.3 %all-to-all-start.1 = ((bf16[4,96,1728]{2,1,0:T(8,128)(2,1)}), bf16[4,96,1728]{2,1,0:T(8,128)(2,1)}, u32[]{:S(2)}, u32[]{:S(2)}) async-start(bf16[4,96,1728]{2,1,0:T(8,128)(2,1)} %get-tuple-element.189), calls=%async_computation.1 | async-start | bytes 2752512 | tf_op jit(solution)/shard_map/all_to_all | solution.py:384
  44.2 1.7 collective-permute-start.7
  46.5 10.7 %collective-permute-done.5.wx_ref = bf16[4,96,576]{2,1,0:T(8,128)(2,1)S(1)} collective-permute-done((bf16[4,96,576]{2,1,0:T(8,128)(2,1)S(1)}, bf16[4,96,576]{2,1,0:T(8,128)(2,1)S(1)}, u32[]{:S(2)}, u32[]{:S(2)}) %collective-permute-start.5) | collective-permute-done | bytes 442400 | tf_op jit(solution)/shard_map/ppermute | solution.py:38
  57.2 2.1 collective-permute-start.10
  61.3 10.3 %collective-permute-done.10.xy_ref = bf16[96,768]{1,0:T(8,128)(2,1)} collective-permute-done((bf16[96,768]{1,0:T(8,128)(2,1)}, bf16[96,768]{1,0:T(8,128)(2,1)}, u32[]{:S(2)}, u32[]{:S(2)}) %collective-permute-start.10) | collective-permute-done | bytes 147488 | tf_op jit(solution)/shard_map/ppermute | solution.py:379
  71.5 3.0 collective-permute-done.9.y_ref
  74.5 2.7 plane_copies.1
  77.3 2.2 slice.114.refs_0_
  80.8 1.4 collective-permute-start.13
  83.0 4.9 %all-to-all-start.2 = ((bf16[4,2,2,96,768]{4,3,2,1,0:T(8,128)(2,1)}), bf16[4,2,2,96,768]{4,3,2,1,0:T(8,128)(2,1)}, u32[]{:S(2)}, u32[]{:S(2)}) async-start(bf16[4,2,2,96,768]{4,3,2,1,0:T(8,128)(2,1)} %plane_copies.1), calls=%async_computation.2 | async-start | bytes 4718592 | tf_op jit(solution)/shard_map/all_to_all | solution.py:384
  89.0 12.9 %self_fwd.1 = (bf16[2,512,1152]{2,1,0:T(8,128)(2,1)}, bf16[768,1152]{1,0:T(8,128)(2,1)S(1)}, bf16[512,384]{1,0:T(8,128)(2,1)S(1)}, bf16[512,384]{1,0:T(8,128)(2,1)S(1)}, f32[3,2,2,512]{3,2,1,0:T(2,128)S(1)}) custom-call(s32[5]{0:T(128)S(1)} %pad_add_fusion.2.info, bf16[512,768]{1,0:T(8,128)(2,1)S(1)} %copy-done.5, ...), custom_call_target="tpu_custom_call" | custom-call | flops 1000 | bytes 1000 | tf_op jit(solution)/shard_map/self_fwd/pallas_call | solution.py:565
  105.6 10.1 %collective-permute-done.13.refs_1_ = bf16[4,96,960]{2,1,0:T(8,128)(2,1)} collective-permute-done((bf16[4,96,960]{2,1,0:T(8,128)(2,1)}, bf16[4,96,960]{2,1,0:T(8,128)(2,1)}, u32[]{:S(2)}, u32[]{:S(2)}) %collective-permute-start.13) | collective-permute-done | bytes 737312 | tf_op jit(solution)/shard_map/ppermute | solution.py:43
  123.3 7.9 %assemble.1 = (bf16[4,2,96,1536]{3,2,1,0:T(8,128)(2,1)}, bf16[4,2,96,768]{3,2,1,0:T(8,128)(2,1)}, bf16[4,2,96,768]{3,2,1,0:T(8,128)(2,1)}, bf16[4,2,96,768]{3,2,1,0:T(8,128)(2,1)}) custom-call(s32[3]{0:T(128)} %pad_add_fusion.info, bf16[4,96,960]{2,1,0:T(8,128)(2,1)} %slice.114.refs_0_, bf16[4,96,960]{2,1,0:T(8,128)(2,1)} %collective-permute-done.13.refs_1_, ...), custom_call_target="tpu_custom_call" | custom-call | flops 1000 | bytes 1000 | tf_op jit(solution)/shard_map/assemble/pallas_call | solution.py:412
  131.2 4.6 %collective-permute-done.22.e1 = bf16[4,96,768]{2,1,0:T(8,128)(2,1)S(1)} collective-permute-done((bf16[4,96,768]{2,1,0:T(8,128)(2,1)S(1)}, bf16[4,96,768]{2,1,0:T(8,128)(2,1)S(1)}, u32[]{:S(2)}, u32[]{:S(2)}) %collective-permute-start.22) | collective-permute-done | bytes 589856 | tf_op jit(solution)/shard_map/ppermute | solution.py:43
  136.2 4.9 %project_kv.1 = (bf16[512,768]{1,0:T(8,128)(2,1)}, bf16[512,1536]{1,0:T(8,128)(2,1)}) custom-call(bf16[512,768]{1,0:T(8,128)(2,1)} %bitcast_add_fusion.1.keep_ref, bf16[512,768]{1,0:T(8,128)(2,1)} %bitcast.79, bf16[768,1536]{1,0:T(8,128)(2,1)} %bitcast.70, f32[1,768]{1,0:T(1,128)} %reshape_reshape.7.bias_ref), custom_call_target="tpu_custom_call" | custom-call | flops 1000 | bytes 1000 | tf_op jit(solution)/shard_map/project_kv/pallas_call | solution.py:412
  141.2 5.7 %first_forward.1 = (f32[512,768]{1,0:T(8,128)}, f32[512,768]{1,0:T(8,128)}, bf16[512,768]{1,0:T(8,128)(2,1)}, bf16[512,768]{1,0:T(8,128)(2,1)}, bf16[512,768]{1,0:T(8,128)(2,1)}) custom-call(bf16[512,768]{1,0:T(8,128)(2,1)} %own_ref.2, bf16[512,384]{1,0:T(8,128)(2,1)} %copy-done.9, bf16[512,384]{1,0:T(8,128)(2,1)} %copy-done.46, bf16[768,768]{1,0:T(8,128)(2,1)} %bitcast.75, ...), custom_call_target="tpu_custom_call" | custom-call | flops 1000 | bytes 1000 | tf_op jit(solution)/shard_map/first_forward/pallas_call | solution.py:412
  147.5 1.7 collective-permute-start.19
  150.9 13.9 %cross_fwd.1 = (bf16[512,768]{1,0:T(8,128)(2,1)S(1)}, f32[6,2,512]{2,1,0:T(2,128)S(1)}) custom-call(bf16[512,768]{1,0:T(8,128)(2,1)S(1)} %copy-done.6, bf16[512,1536]{1,0:T(8,128)(2,1)S(1)} %copy-done, bf16[512,1536]{1,0:T(8,128)(2,1)S(1)} %collective-permute-done.25.kb_ref.vb_ref, bf16[512,1536]{1,0:T(8,128)(2,1)S(1)} %copy-done, ...), custom_call_target="tpu_custom_call" | custom-call | flops 1000 | bytes 1000 | tf_op jit(solution)/shard_map/cross_fwd/pallas_call | solution.py:182
  166.0 1.8 collective-permute-done.26.e7
  167.9 1.4 copy-done.26
  169.5 32.8 %feed.1 = (bf16[512,768]{1,0:T(8,128)(2,1)}, f32[512,768]{1,0:T(8,128)}, bf16[512,768]{1,0:T(8,128)(2,1)}, bf16[512,768]{1,0:T(8,128)(2,1)}, bf16[2,2,4,104,1536...) custom-call(s32[3]{0:T(128)} %pad_add_fusion.info, bf16[512,768]{1,0:T(8,128)(2,1)} %copy-done.3, ...), custom_call_target="tpu_custom_call" | custom-call | flops 1000 | bytes 1000 | tf_op jit(solution)/shard_map/feed/pallas_call | solution.py:412
  203.6 8.5 %cross_bwd.1 = (bf16[512,768]{1,0:T(8,128)(2,1)S(1)}, bf16[2,512,768]{2,1,0:T(8,128)(2,1)S(1)}, bf16[2,512,768]{2,1,0:T(8,128)(2,1)}) custom-call(bf16[512,768]{1,0:T(8,128)(2,1)S(1)} %copy-done.7, bf16[512,1536]{1,0:T(8,128)(2,1)} %get-tuple-element.226.ka_ref.va_ref, bf16[512,1536]{1,0:T(8,128)(2,1)} %copy-done.1, ...), custom_call_target="tpu_custom_call" | custom-call | flops 1000 | bytes 1000 | tf_op jit(solution)/shard_map/cross_bwd/pallas_call | solution.py:233
  212.1 3.3 fusion.2
  215.5 2.8 fusion.1
  220.0 19.2 %cross_first.1 = (bf16[512,768]{1,0:T(8,128)(2,1)S(1)}, bf16[2,512,768]{2,1,0:T(8,128)(2,1)}, bf16[2,512,768]{2,1,0:T(8,128)(2,1)}, f32[512,768]{1,0:T(8,128)}, ...) custom-call(bf16[512,768]{1,0:T(8,128)(2,1)S(1)} %copy-done.7, ...), custom_call_target="tpu_custom_call", output_to_operand_aliasing={{1}: (14, {}), {2}: (15, {})} | custom-call | flops 1000 | bytes 1000 | tf_op jit(solution)/shard_map/cross_first/pallas_call | solution.py:325
  239.3 9.5 %collective-permute-done.29 = bf16[2,4,104,768]{3,2,1,0:T(8,128)(2,1)S(1)} collective-permute-done((bf16[2,4,104,768]{3,2,1,0:T(8,128)(2,1)}, bf16[2,4,104,768]{3,2,1,0:T(8,128)(2,1)S(1)}, u32[]{:S(2)}, u32[]{:S(2)}) %collective-permute-start.29) | collective-permute-done | bytes 1277984 | tf_op jit(solution)/shard_map/ppermute | solution.py:38
  250.0 2.9 fusion.5
  255.4 12.4 %attn_grads.1 = (bf16[2,2,4,112,960]{4,3,2,1,0:T(8,128)(2,1)}, bf16[2,2,4,112,960]{4,3,2,1,0:T(8,128)(2,1)}, bf16[512,768]{1,0:T(8,128)(2,1)}) custom-call(s32[3]{0:T(128)} %pad_add_fusion.info, bf16[512,768]{1,0:T(8,128)(2,1)} %get-tuple-element.264.h1_ref, bf16[512,768]{1,0:T(8,128)(2,1)} %copy-done.15, bf16[512,768]{1,0:T(8,128)(2,1)} %copy-done.16, ...), custom_call_target="tpu_custom_call" | custom-call | flops 1000 | bytes 1000 | tf_op jit(solution)/shard_map/attn_grads/pallas_call | solution.py:412
  267.8 2.5 collective-permute-done.33
  271.6 2.7 fusion.8
  275.4 4.6 %all-to-all-start.3 = ((bf16[4,104,1536]{2,1,0:T(8,128)(2,1)}), bf16[4,104,1536]{2,1,0:T(8,128)(2,1)}, u32[]{:S(2)}, u32[]{:S(2)}) async-start(bf16[4,104,1536]{2,1,0:T(8,128)(2,1)} %pad_maximum_fusion), calls=%async_computation.3 | async-start | bytes 2555904 | tf_op jit(solution)/shard_map/all_to_all | solution.py:384
  281.0 11.8 %self_bwd.2.rest_0_ = bf16[3,2,512,384]{3,2,1,0:T(8,128)(2,1)S(1)} custom-call(s32[2]{0:T(128)S(1)} %pad_add_fusion.1.info, bf16[2,512,1152]{2,1,0:T(8,128)(2,1)} %get-tuple-element.243.q_ref.k_ref.v_ref, bf16[2,512,1152]{2,1,0:T(8,128)(2,1)} %get-tuple-element.243.q_ref.k_ref.v_ref, bf16[2,512,1152]{2,1,0:T(8,128)(2,1)} %get-tuple-element.243.q_ref.k_ref.v_ref, ...), custom_call_target="tpu_custom_call" | custom-call | flops 1000 | bytes 1000 | tf_op jit(solution)/shard_map/self_bwd/pallas_call | solution.py:123
  292.8 4.2 %fusion.11 = (bf16[4,112,960]{2,1,0:T(8,128)(2,1)}, bf16[4,112,960]{2,1,0:T(8,128)(2,1)}, bf16[4,112,960]{2,1,0:T(8,128)(2,1)}) fusion(bf16[2,2,4,112,960]{4,3,2,1,0:T(8,128)(2,1)} %collective-permute-done.35, bf16[2,2,4,112,960]{4,3,2,1,0:T(8,128)(2,1)S(1)} %copy-done.23), kind=kLoop, calls=%fused_computation.25 | loop fusion | flops 5160960 | bytes 7741440 | tf_op jit(solution)/shard_map/convert_element_type | solution.py:397
  297.0 2.9 collective-permute-done.36
  300.9 1.3 collective-permute-start.38
  303.4 6.4 %self_bwd.3.d_ref = bf16[3,2,512,384]{3,2,1,0:T(8,128)(2,1)S(1)} custom-call(s32[2]{0:T(128)S(1)} %pad_add_fusion.1.info, bf16[2,512,1152]{2,1,0:T(8,128)(2,1)} %get-tuple-element.243.q_ref.k_ref.v_ref, bf16[2,512,1152]{2,1,0:T(8,128)(2,1)} %get-tuple-element.243.q_ref.k_ref.v_ref, ...), custom_call_target="tpu_custom_call", output_to_operand_aliasing={{}: (9, {})} | custom-call | flops 1000 | bytes 1000 | tf_op jit(solution)/shard_map/self_bwd/pallas_call | solution.py:123
  309.8 1.4 copy-done.2
  311.2 6.1 %self_grads.1 = (bf16[4,104,576]{2,1,0:T(8,128)(2,1)}, bf16[4,104,576]{2,1,0:T(8,128)(2,1)}, bf16[4,104,576]{2,1,0:T(8,128)(2,1)}, bf16[4,104,576]{2,1,0:T(8,128)(2,1)}) custom-call(s32[3]{0:T(128)} %pad_add_fusion.info, bf16[512,768]{1,0:T(8,128)(2,1)} %own_ref.2, bf16[512,768]{1,0:T(8,128)(2,1)} %copy-done.11, bf16[3,2,512,384]{3,2,1,0:T(8,128)(2,1)} %copy-done.2), custom_call_target="tpu_custom_call" | custom-call | flops 1000 | bytes 1000 | tf_op jit(solution)/shard_map/self_grads/pallas_call | solution.py:412
  318.4 1.3 collective-permute-start.41
  319.7 3.8 collective-permute-done.37
  323.5 1.7 collective-permute-start.42
  325.2 6.6 %self_back.1 = (f32[512,768]{1,0:T(8,128)}, bf16[512,768]{1,0:T(8,128)(2,1)}) custom-call(bf16[3,2,512,384]{3,2,1,0:T(8,128)(2,1)} %copy-done.2, bf16[768,1152]{1,0:T(8,128)(2,1)} %copy-done.13, f32[512,768]{1,0:T(8,128)} %get-tuple-element.296.first_ref), custom_call_target="tpu_custom_call" | custom-call | flops 1000 | bytes 1000 | tf_op jit(solution)/shard_map/self_back/pallas_call | solution.py:412
  331.8 12.4 %collective-permute-done.38 = bf16[4,112,960]{2,1,0:T(8,128)(2,1)} collective-permute-done((bf16[4,112,960]{2,1,0:T(8,128)(2,1)}, bf16[4,112,960]{2,1,0:T(8,128)(2,1)}, u32[]{:S(2)}, u32[]{:S(2)}) %collective-permute-start.38) | collective-permute-done | bytes 860192 | tf_op jit(solution)/shard_map/ppermute | solution.py:43
  344.2 4.2 %fusion = bf16[4,112,960]{2,1,0:T(8,128)(2,1)} fusion(bf16[4,112,960]{2,1,0:T(8,128)(2,1)} %collective-permute-done.39, bf16[4,112,960]{2,1,0:T(8,128)(2,1)} %collective-permute-done.38, bf16[4,112,960]{2,1,0:T(8,128)(2,1)} %collective-permute-done.37, bf16[2,2,4,112,960]{4,3,2,1,0:T(8,128)(2,1)} %collective-permute-done.35, ...), kind=kLoop, calls=%fused_computation.4 | loop fusion | flops 4300800 | bytes 5160960 | tf_op jit(solution)/shard_map/convert_element_type | solution.py:1537
  348.4 4.8 %all-to-all-start.4 = ((bf16[4,112,960]{2,1,0:T(8,128)(2,1)}), bf16[4,112,960]{2,1,0:T(8,128)(2,1)}, u32[]{:S(2)}, u32[]{:S(2)}) async-start(bf16[4,112,960]{2,1,0:T(8,128)(2,1)} %fusion), calls=%async_computation.4 | async-start | bytes 1835008 | tf_op jit(solution)/shard_map/all_to_all | solution.py:384
  354.5 9.8 %collective-permute-done.41 = bf16[4,104,576]{2,1,0:T(8,128)(2,1)S(1)} collective-permute-done((bf16[4,104,576]{2,1,0:T(8,128)(2,1)}, bf16[4,104,576]{2,1,0:T(8,128)(2,1)S(1)}, u32[]{:S(2)}, u32[]{:S(2)}) %collective-permute-start.41) | collective-permute-done | bytes 479264 | tf_op jit(solution)/shard_map/ppermute | solution.py:43
  365.5 2.1 add_convert_fusion.6
  368.1 2.9 collective-permute-done.44.c_ref
  371.1 2.4 all-to-all-done.4.in_ref
  373.6 4.2 %all-to-all-start.5 = ((bf16[4,104,576]{2,1,0:T(8,128)(2,1)}), bf16[4,104,576]{2,1,0:T(8,128)(2,1)}, u32[]{:S(2)}, u32[]{:S(2)}) async-start(bf16[4,104,576]{2,1,0:T(8,128)(2,1)} %add_convert_fusion.6), calls=%async_computation.5 | async-start | bytes 1064960 | tf_op jit(solution)/shard_map/all_to_all | solution.py:384
  378.1 2.2 sum_feed.1
  380.3 2.6 add_convert_fusion.5
  383.0 4.8 %scatter.1 = f32[32,64,768]{2,1,0:T(8,128)} custom-call(s32[32]{0:T(128)S(1)} %reshape.374.table, bf16[8,64,768]{2,1,0:T(8,128)(2,1)S(1)} %bitcast.67, bf16[8,64,768]{2,1,0:T(8,128)(2,1)S(1)} %bitcast.69, bf16[8,64,768]{2,1,0:T(8,128)(2,1)S(1)} %collective-permute-done.44.c_ref, bf16[8,64,768]{2,1,0:T(8,128)(2,1)S(1)} %collective-permute-done.45.d_ref), custom_call_target="tpu_custom_call" | custom-call | flops 1000 | bytes 1000 | tf_op jit(solution)/shard_map/scatter/pallas_call | solution.py:1157
  387.8 2.1 sum_attn.1
  389.9 1.4 all-to-all-done.5.in_ref
  391.3 1.8 sum_cols.1
  (244 shorter events, 49.4 us)
Async XLA Ops:
  7.2 5.7 %collective-permute-start = (bf16[2,8,64,768]{3,2,1,0:T(8,128)(2,1)}, bf16[2,8,64,768]{3,2,1,0:T(8,128)(2,1)S(1)}, u32[]{:S(2)}, u32[]{:S(2)}) collective-permute-start(bf16[2,8,64,768]{3,2,1,0:T(8,128)(2,1)} %bitcast.83), channel_id=1, source_target_pairs={{0,1},{1,0},{2,3},{3,2},{4,5},{5,4},{6,7},{7,6},{8,9},{9,8},{10,11... | collective-permute-start | bytes 4718600 | tf_op jit(solution)/shard_map/ppermute | solution.py:34
  7.9 9.2 %collective-permute-start.1 = (f32[1,1536]{1,0:T(1,128)S(1)}, f32[1,1536]{1,0:T(1,128)S(1)}, u32[]{:S(2)}, u32[]{:S(2)}) collective-permute-start(f32[1,1536]{1,0:T(1,128)S(1)} %reshape.368), channel_id=1, source_target_pairs={{0,2},{2,0},{1,3},{3,1},{4,6},{6,4},{5,7},{7,5},{8,10},{10,8},{9,1... | collective-permute-start | bytes 18440 | tf_op jit(solution)/shard_map/ppermute | solution.py:38
  10.5 20.1 %collective-permute-start.3 = (bf16[512,768]{1,0:T(8,128)(2,1)S(1)}, bf16[512,768]{1,0:T(8,128)(2,1)S(1)}, u32[]{:S(2)}, u32[]{:S(2)}) collective-permute-start(bf16[512,768]{1,0:T(8,128)(2,1)S(1)} %copy-done.5), channel_id=1, source_target_pairs={{0,1},{1,0},{2,3},{3,2},{4,5},{5,4},{6,7},{7,6},{8,9},{9,8},{10,11... | collective-permute-start | bytes 2359304 | tf_op jit(solution)/shard_map/ppermute | solution.py:34
  16.1 21.6 %collective-permute-start.4 = (bf16[8,64,768]{2,1,0:T(8,128)(2,1)}, bf16[8,64,768]{2,1,0:T(8,128)(2,1)S(1)}, u32[]{:S(2)}, u32[]{:S(2)}) collective-permute-start(bf16[8,64,768]{2,1,0:T(8,128)(2,1)} %get-tuple-element.349), channel_id=1, source_target_pairs={{0,2},{2,0},{1,3},{3,1},{4,6},{6,4},{5,7},{7,5},{8,10},{10,8},{9,1... | collective-permute-start | bytes 2359304 | tf_op jit(solution)/shard_map/ppermute | solution.py:38
  19.0 18.7 %all-to-all-start = ((bf16[4,96,576]{2,1,0:T(8,128)(2,1)}), bf16[4,96,576]{2,1,0:T(8,128)(2,1)S(1)}, u32[]{:S(2)}, u32[]{:S(2)}) async-start(bf16[4,96,576]{2,1,0:T(8,128)(2,1)} %pack_self.1), calls=%async_computation | async-start | bytes 983040 | tf_op jit(solution)/shard_map/all_to_all | solution.py:384
  24.1 1.2 collective-permute-start.2
  30.7 57.3 %copy-start.11 = (bf16[512,768]{1,0:T(8,128)(2,1)}, bf16[512,768]{1,0:T(8,128)(2,1)S(1)}, u32[]{:S(2)}) copy-start(bf16[512,768]{1,0:T(8,128)(2,1)S(1)} %collective-permute-done.3.oth_ref) | copy-start | bytes 2359300
  38.6 38.6 %all-to-all-start.1 = ((bf16[4,96,1728]{2,1,0:T(8,128)(2,1)}), bf16[4,96,1728]{2,1,0:T(8,128)(2,1)}, u32[]{:S(2)}, u32[]{:S(2)}) async-start(bf16[4,96,1728]{2,1,0:T(8,128)(2,1)} %get-tuple-element.189), calls=%async_computation.1 | async-start | bytes 2752512 | tf_op jit(solution)/shard_map/all_to_all | solution.py:384
  43.0 14.2 %collective-permute-start.5 = (bf16[4,96,576]{2,1,0:T(8,128)(2,1)S(1)}, bf16[4,96,576]{2,1,0:T(8,128)(2,1)S(1)}, u32[]{:S(2)}, u32[]{:S(2)}) collective-permute-start(bf16[4,96,576]{2,1,0:T(8,128)(2,1)S(1)} %all-to-all-done.w_ref), channel_id=1, source_target_pairs={{0,2},{2,0},{1,3},{3,1},{4,6},{6,4},{5,7},{7,5},{8,10},{10,8},{9,1... | collective-permute-start | bytes 1327112 | tf_op jit(solution)/shard_map/ppermute | solution.py:38
  44.2 33.0 %collective-permute-start.7 = (bf16[4,96,576]{2,1,0:T(8,128)(2,1)S(1)}, bf16[4,96,576]{2,1,0:T(8,128)(2,1)S(1)}, u32[]{:S(2)}, u32[]{:S(2)}) collective-permute-start(bf16[4,96,576]{2,1,0:T(8,128)(2,1)S(1)} %all-to-all-done.w_ref), channel_id=1, source_target_pairs={{0,6},{1,7},{2,4},{3,5},{4,2},{5,3},{6,0},{7,1},{8,14},{9,15},{10,... | collective-permute-start | bytes 1327112 | tf_op jit(solution)/shard_map/ppermute | solution.py:379
  45.9 31.3 %collective-permute-start.6 = (bf16[4,96,576]{2,1,0:T(8,128)(2,1)S(1)}, bf16[4,96,576]{2,1,0:T(8,128)(2,1)S(1)}, u32[]{:S(2)}, u32[]{:S(2)}) collective-permute-start(bf16[4,96,576]{2,1,0:T(8,128)(2,1)S(1)} %all-to-all-done.w_ref), channel_id=1, source_target_pairs={{0,4},{4,0},{8,12},{12,8},{16,20},{20,16},{24,28},{28,24},{1,5},{5... | collective-permute-start | bytes 1327112 | tf_op jit(solution)/shard_map/ppermute | solution.py:43
  57.2 14.4 %collective-permute-start.10 = (bf16[96,768]{1,0:T(8,128)(2,1)}, bf16[96,768]{1,0:T(8,128)(2,1)}, u32[]{:S(2)}, u32[]{:S(2)}) collective-permute-start(bf16[96,768]{1,0:T(8,128)(2,1)} %get-tuple-element.192.own_ref), channel_id=1, source_target_pairs={{0,6},{1,7},{2,4},{3,5},{4,2},{5,3},{6,0},{7,1},{8,14},{9,15},{10,... | collective-permute-start | bytes 442376 | tf_op jit(solution)/shard_map/ppermute | solution.py:379
  59.2 15.3 %collective-permute-start.9 = (bf16[96,768]{1,0:T(8,128)(2,1)}, bf16[96,768]{1,0:T(8,128)(2,1)}, u32[]{:S(2)}, u32[]{:S(2)}) collective-permute-start(bf16[96,768]{1,0:T(8,128)(2,1)} %get-tuple-element.192.own_ref), channel_id=1, source_target_pairs={{0,4},{4,0},{8,12},{12,8},{16,20},{20,16},{24,28},{28,24},{1,5},{5... | collective-permute-start | bytes 442376 | tf_op jit(solution)/shard_map/ppermute | solution.py:43
  59.8 14.7 %collective-permute-start.8 = (bf16[96,768]{1,0:T(8,128)(2,1)}, bf16[96,768]{1,0:T(8,128)(2,1)}, u32[]{:S(2)}, u32[]{:S(2)}) collective-permute-start(bf16[96,768]{1,0:T(8,128)(2,1)} %get-tuple-element.192.own_ref), channel_id=1, source_target_pairs={{0,2},{2,0},{1,3},{3,1},{4,6},{6,4},{5,7},{7,5},{8,10},{10,8},{9,1... | collective-permute-start | bytes 442376 | tf_op jit(solution)/shard_map/ppermute | solution.py:38
  79.5 26.0 %collective-permute-start.14 = (bf16[4,96,960]{2,1,0:T(8,128)(2,1)}, bf16[4,96,960]{2,1,0:T(8,128)(2,1)}, u32[]{:S(2)}, u32[]{:S(2)}) collective-permute-start(bf16[4,96,960]{2,1,0:T(8,128)(2,1)} %slice.114.refs_0_), channel_id=1, source_target_pairs={{0,6},{1,7},{2,4},{3,5},{4,2},{5,3},{6,0},{7,1},{8,14},{9,15},{10,... | collective-permute-start | bytes 2211848 | tf_op jit(solution)/shard_map/ppermute | solution.py:379
  80.8 34.9 %collective-permute-start.13 = (bf16[4,96,960]{2,1,0:T(8,128)(2,1)}, bf16[4,96,960]{2,1,0:T(8,128)(2,1)}, u32[]{:S(2)}, u32[]{:S(2)}) collective-permute-start(bf16[4,96,960]{2,1,0:T(8,128)(2,1)} %slice.114.refs_0_), channel_id=1, source_target_pairs={{0,4},{4,0},{8,12},{12,8},{16,20},{20,16},{24,28},{28,24},{1,5},{5... | collective-permute-start | bytes 2211848 | tf_op jit(solution)/shard_map/ppermute | solution.py:43
  82.2 33.4 %collective-permute-start.12 = (bf16[4,96,960]{2,1,0:T(8,128)(2,1)}, bf16[4,96,960]{2,1,0:T(8,128)(2,1)}, u32[]{:S(2)}, u32[]{:S(2)}) collective-permute-start(bf16[4,96,960]{2,1,0:T(8,128)(2,1)} %slice.114.refs_0_), channel_id=1, source_target_pairs={{0,2},{2,0},{1,3},{3,1},{4,6},{6,4},{5,7},{7,5},{8,10},{10,8},{9,1... | collective-permute-start | bytes 2211848 | tf_op jit(solution)/shard_map/ppermute | solution.py:38
  83.0 63.9 %all-to-all-start.2 = ((bf16[4,2,2,96,768]{4,3,2,1,0:T(8,128)(2,1)}), bf16[4,2,2,96,768]{4,3,2,1,0:T(8,128)(2,1)}, u32[]{:S(2)}, u32[]{:S(2)}) async-start(bf16[4,2,2,96,768]{4,3,2,1,0:T(8,128)(2,1)} %plane_copies.1), calls=%async_computation.2 | async-start | bytes 4718592 | tf_op jit(solution)/shard_map/all_to_all | solution.py:384
  103.8 19.4 %copy-start.19 = (f32[3,2,2,512]{3,2,1,0:T(2,128)}, f32[3,2,2,512]{3,2,1,0:T(2,128)S(1)}, u32[]{:S(2)}) copy-start(f32[3,2,2,512]{3,2,1,0:T(2,128)S(1)} %get-tuple-element.244.lse_ref) | copy-start | bytes 73732
  103.8 18.3 %slice-start = ((bf16[2,8,64,768]{3,2,1,0:T(8,128)(2,1)}), bf16[1,8,64,768]{3,2,1,0:T(8,128)(2,1)S(1)}, s32[]{:S(2)}) async-start(bf16[2,8,64,768]{3,2,1,0:T(8,128)(2,1)} %copy-done.24), calls=%async_computation.6 | async-start | bytes 1572864 | tf_op jit(solution)/shard_map/slice | solution.py:1419
  103.8 18.3 %copy-start.25 = (bf16[8,64,768]{2,1,0:T(8,128)(2,1)S(1)}, bf16[8,64,768]{2,1,0:T(8,128)(2,1)}, u32[]{:S(2)}) copy-start(bf16[8,64,768]{2,1,0:T(8,128)(2,1)} %get-tuple-element.348) | copy-start | bytes 2359300
  103.8 1.7 collective-permute-start.15
  103.9 13.5 %collective-permute-start.11 = (bf16[4,96,960]{2,1,0:T(8,128)(2,1)}, bf16[4,96,960]{2,1,0:T(8,128)(2,1)S(1)}, u32[]{:S(2)}, u32[]{:S(2)}) collective-permute-start(bf16[4,96,960]{2,1,0:T(8,128)(2,1)} %slice.114.refs_0_), channel_id=1, source_target_pairs={{0,1},{1,0},{2,3},{3,2},{4,5},{5,4},{6,7},{7,6},{8,9},{9,8},{10,11... | collective-permute-start | bytes 2211848 | tf_op jit(solution)/shard_map/ppermute | solution.py:34
  115.6 2.5 collective-permute-start.16
  115.6 3.6 collective-permute-start.17
  116.1 4.2 %collective-permute-start.18 = (bf16[4,96,960]{2,1,0:T(8,128)(2,1)}, bf16[4,96,960]{2,1,0:T(8,128)(2,1)S(1)}, u32[]{:S(2)}, u32[]{:S(2)}) collective-permute-start(bf16[4,96,960]{2,1,0:T(8,128)(2,1)} %collective-permute-done.14.refs_3_), channel_id=1, source_target_pairs={{0,1},{1,0},{2,3},{3,2},{4,5},{5,4},{6,7},{7,6},{8,9},{9,8},{10,11... | collective-permute-start | bytes 2211848 | tf_op jit(solution)/shard_map/ppermute | solution.py:34
  120.4 15.4 %collective-permute-start.22 = (bf16[4,96,768]{2,1,0:T(8,128)(2,1)S(1)}, bf16[4,96,768]{2,1,0:T(8,128)(2,1)S(1)}, u32[]{:S(2)}, u32[]{:S(2)}) collective-permute-start(bf16[4,96,768]{2,1,0:T(8,128)(2,1)S(1)} %slice.115.e0), channel_id=1, source_target_pairs={{0,4},{4,0},{8,12},{12,8},{16,20},{20,16},{24,28},{28,24},{1,5},{5... | collective-permute-start | bytes 1769480 | tf_op jit(solution)/shard_map/ppermute | solution.py:43
  121.1 15.1 %collective-permute-start.21 = (bf16[4,96,768]{2,1,0:T(8,128)(2,1)S(1)}, bf16[4,96,768]{2,1,0:T(8,128)(2,1)S(1)}, u32[]{:S(2)}, u32[]{:S(2)}) collective-permute-start(bf16[4,96,768]{2,1,0:T(8,128)(2,1)S(1)} %slice.115.e0), channel_id=1, source_target_pairs={{0,2},{2,0},{1,3},{3,1},{4,6},{6,4},{5,7},{7,5},{8,10},{10,8},{9,1... | collective-permute-start | bytes 1769480 | tf_op jit(solution)/shard_map/ppermute | solution.py:38
  141.2 5.7 %collective-permute-start.25 = (bf16[512,1536]{1,0:T(8,128)(2,1)}, bf16[512,1536]{1,0:T(8,128)(2,1)S(1)}, u32[]{:S(2)}, u32[]{:S(2)}) collective-permute-start(bf16[512,1536]{1,0:T(8,128)(2,1)} %get-tuple-element.226.ka_ref.va_ref), channel_id=1, source_target_pairs={{0,1},{1,0},{2,3},{3,2},{4,5},{5,4},{6,7},{7,6},{8,9},{9,8},{10,11... | collective-permute-start | bytes 4718600 | tf_op jit(solution)/shard_map/ppermute | solution.py:34
  146.9 17.9 %copy-start.1 = (bf16[512,1536]{1,0:T(8,128)(2,1)}, bf16[512,1536]{1,0:T(8,128)(2,1)S(1)}, u32[]{:S(2)}) copy-start(bf16[512,1536]{1,0:T(8,128)(2,1)S(1)} %collective-permute-done.25.kb_ref.vb_ref) | copy-start | bytes 4718596
  146.9 20.9 %collective-permute-start.27 = (bf16[4,2,2,96,768]{4,3,2,1,0:T(8,128)(2,1)}, bf16[4,2,2,96,768]{4,3,2,1,0:T(8,128)(2,1)S(1)}, u32[]{:S(2)}, u32[]{:S(2)}) collective-permute-start(bf16[4,2,2,96,768]{4,3,2,1,0:T(8,128)(2,1)} %all-to-all-done.2.s0), channel_id=1, source_target_pairs={{0,1},{1,0},{2,3},{3,2},{4,5},{5,4},{6,7},{7,6},{8,9},{9,8},{10,11... | collective-permute-start | bytes 7077896 | tf_op jit(solution)/shard_map/ppermute | solution.py:34
  147.5 18.2 %collective-permute-start.20 = (bf16[4,96,768]{2,1,0:T(8,128)(2,1)}, bf16[4,96,768]{2,1,0:T(8,128)(2,1)S(1)}, u32[]{:S(2)}, u32[]{:S(2)}) collective-permute-start(bf16[4,96,768]{2,1,0:T(8,128)(2,1)} %copy-done.27), channel_id=1, source_target_pairs={{0,1},{1,0},{2,3},{3,2},{4,5},{5,4},{6,7},{7,6},{8,9},{9,8},{10,11... | collective-permute-start | bytes 1769480 | tf_op jit(solution)/shard_map/ppermute | solution.py:34
  147.5 18.2 %collective-permute-start.19 = (bf16[4,96,768]{2,1,0:T(8,128)(2,1)}, bf16[4,96,768]{2,1,0:T(8,128)(2,1)S(1)}, u32[]{:S(2)}, u32[]{:S(2)}) collective-permute-start(bf16[4,96,768]{2,1,0:T(8,128)(2,1)} %copy-done.27), channel_id=1, source_target_pairs={{0,6},{1,7},{2,4},{3,5},{4,2},{5,3},{6,0},{7,1},{8,14},{9,15},{10,... | collective-permute-start | bytes 1769480 | tf_op jit(solution)/shard_map/ppermute | solution.py:379
  149.3 16.4 %collective-permute-start.23 = (bf16[4,96,768]{2,1,0:T(8,128)(2,1)}, bf16[4,96,768]{2,1,0:T(8,128)(2,1)S(1)}, u32[]{:S(2)}, u32[]{:S(2)}) collective-permute-start(bf16[4,96,768]{2,1,0:T(8,128)(2,1)} %copy-done.38), channel_id=1, source_target_pairs={{0,1},{1,0},{2,3},{3,2},{4,5},{5,4},{6,7},{7,6},{8,9},{9,8},{10,11... | collective-permute-start | bytes 1769480 | tf_op jit(solution)/shard_map/ppermute | solution.py:34
  149.4 16.3 %collective-permute-start.24 = (bf16[4,96,768]{2,1,0:T(8,128)(2,1)}, bf16[4,96,768]{2,1,0:T(8,128)(2,1)S(1)}, u32[]{:S(2)}, u32[]{:S(2)}) collective-permute-start(bf16[4,96,768]{2,1,0:T(8,128)(2,1)} %copy-done.39), channel_id=1, source_target_pairs={{0,1},{1,0},{2,3},{3,2},{4,5},{5,4},{6,7},{7,6},{8,9},{9,8},{10,11... | collective-permute-start | bytes 1769480 | tf_op jit(solution)/shard_map/ppermute | solution.py:34
  165.8 2.1 collective-permute-start.26
  169.5 33.0 %copy-start.4 = (bf16[512,768]{1,0:T(8,128)(2,1)S(1)}, bf16[512,768]{1,0:T(8,128)(2,1)}, u32[]{:S(2)}) copy-start(bf16[512,768]{1,0:T(8,128)(2,1)} %copy-done.3) | copy-start | bytes 2359300
  169.5 33.0 %copy-start.7 = (bf16[512,768]{1,0:T(8,128)(2,1)S(1)}, bf16[512,768]{1,0:T(8,128)(2,1)}, u32[]{:S(2)}) copy-start(bf16[512,768]{1,0:T(8,128)(2,1)} %get-tuple-element.230.q_ref) | copy-start | bytes 2359300
  202.2 9.9 %collective-permute-start.28 = (bf16[2,2,4,104,1536]{4,3,2,1,0:T(8,128)(2,1)}, bf16[2,2,4,104,1536]{4,3,2,1,0:T(8,128)(2,1)}, u32[]{:S(2)}, u32[]{:S(2)}) collective-permute-start(bf16[2,2,4,104,1536]{4,3,2,1,0:T(8,128)(2,1)} %get-tuple-element.252), channel_id=1, source_target_pairs={{0,1},{1,0},{2,3},{3,2},{4,5},{5,4},{6,7},{7,6},{8,9},{9,8},{10,11... | collective-permute-start | bytes 15335432 | tf_op jit(solution)/shard_map/ppermute | solution.py:34
  218.2 30.5 %collective-permute-start.29 = (bf16[2,4,104,768]{3,2,1,0:T(8,128)(2,1)}, bf16[2,4,104,768]{3,2,1,0:T(8,128)(2,1)S(1)}, u32[]{:S(2)}, u32[]{:S(2)}) collective-permute-start(bf16[2,4,104,768]{3,2,1,0:T(8,128)(2,1)} %fusion.1), channel_id=1, source_target_pairs={{0,2},{2,0},{1,3},{3,1},{4,6},{6,4},{5,7},{7,5},{8,10},{10,8},{9,1... | collective-permute-start | bytes 3833864 | tf_op jit(solution)/shard_map/ppermute | solution.py:38
  219.2 30.3 %collective-permute-start.30 = (bf16[2,4,104,768]{3,2,1,0:T(8,128)(2,1)}, bf16[2,4,104,768]{3,2,1,0:T(8,128)(2,1)S(1)}, u32[]{:S(2)}, u32[]{:S(2)}) collective-permute-start(bf16[2,4,104,768]{3,2,1,0:T(8,128)(2,1)} %fusion.2), channel_id=1, source_target_pairs={{0,4},{4,0},{8,12},{12,8},{16,20},{20,16},{24,28},{28,24},{1,5},{5... | collective-permute-start | bytes 3833864 | tf_op jit(solution)/shard_map/ppermute | solution.py:43
  239.2 13.7 %copy-start.15 = (bf16[512,768]{1,0:T(8,128)(2,1)}, bf16[512,768]{1,0:T(8,128)(2,1)S(1)}, u32[]{:S(2)}) copy-start(bf16[512,768]{1,0:T(8,128)(2,1)S(1)} %get-tuple-element.265.dq_ref) | copy-start | bytes 2359300
  239.2 13.7 %copy-start.16 = (bf16[512,768]{1,0:T(8,128)(2,1)}, bf16[512,768]{1,0:T(8,128)(2,1)S(1)}, u32[]{:S(2)}) copy-start(bf16[512,768]{1,0:T(8,128)(2,1)S(1)} %get-tuple-element.270.e1_ref) | copy-start | bytes 2359300
  249.5 4.2 %collective-permute-start.31 = (bf16[2,512,768]{2,1,0:T(8,128)(2,1)}, bf16[2,512,768]{2,1,0:T(8,128)(2,1)S(1)}, u32[]{:S(2)}, u32[]{:S(2)}) collective-permute-start(bf16[2,512,768]{2,1,0:T(8,128)(2,1)} %get-tuple-element.267), channel_id=1, source_target_pairs={{0,1},{1,0},{2,3},{3,2},{4,5},{5,4},{6,7},{7,6},{8,9},{9,8},{10,11... | collective-permute-start | bytes 4718600 | tf_op jit(solution)/shard_map/ppermute | solution.py:34
  249.5 3.6 collective-permute-start.32
  253.7 16.6 %collective-permute-start.33 = (bf16[4,104,768]{2,1,0:T(8,128)(2,1)}, bf16[4,104,768]{2,1,0:T(8,128)(2,1)S(1)}, u32[]{:S(2)}, u32[]{:S(2)}) collective-permute-start(bf16[4,104,768]{2,1,0:T(8,128)(2,1)} %get-tuple-element.279), channel_id=1, source_target_pairs={{0,4},{4,0},{8,12},{12,8},{16,20},{20,16},{24,28},{28,24},{1,5},{5... | collective-permute-start | bytes 1916936 | tf_op jit(solution)/shard_map/ppermute | solution.py:43
  254.4 16.4 %collective-permute-start.34 = (bf16[4,104,768]{2,1,0:T(8,128)(2,1)}, bf16[4,104,768]{2,1,0:T(8,128)(2,1)S(1)}, u32[]{:S(2)}, u32[]{:S(2)}) collective-permute-start(bf16[4,104,768]{2,1,0:T(8,128)(2,1)} %get-tuple-element.280), channel_id=1, source_target_pairs={{0,2},{2,0},{1,3},{3,1},{4,6},{6,4},{5,7},{7,5},{8,10},{10,8},{9,1... | collective-permute-start | bytes 1916936 | tf_op jit(solution)/shard_map/ppermute | solution.py:38
  255.4 16.2 %copy-start.30 = (bf16[2,4,104,768]{3,2,1,0:T(8,128)(2,1)S(1)}, bf16[2,4,104,768]{3,2,1,0:T(8,128)(2,1)}, u32[]{:S(2)}) copy-start(bf16[2,4,104,768]{3,2,1,0:T(8,128)(2,1)} %copy-done.29) | copy-start | bytes 3833860
  271.6 21.2 %collective-permute-start.35 = (bf16[2,2,4,112,960]{4,3,2,1,0:T(8,128)(2,1)}, bf16[2,2,4,112,960]{4,3,2,1,0:T(8,128)(2,1)}, u32[]{:S(2)}, u32[]{:S(2)}) collective-permute-start(bf16[2,2,4,112,960]{4,3,2,1,0:T(8,128)(2,1)} %get-tuple-element.287), channel_id=1, source_target_pairs={{0,1},{1,0},{2,3},{3,2},{4,5},{5,4},{6,7},{7,6},{8,9},{9,8},{10,11... | collective-permute-start | bytes 10321928 | tf_op jit(solution)/shard_map/ppermute | solution.py:34
  275.4 56.3 %all-to-all-start.3 = ((bf16[4,104,1536]{2,1,0:T(8,128)(2,1)}), bf16[4,104,1536]{2,1,0:T(8,128)(2,1)}, u32[]{:S(2)}, u32[]{:S(2)}) async-start(bf16[4,104,1536]{2,1,0:T(8,128)(2,1)} %pad_maximum_fusion), calls=%async_computation.3 | async-start | bytes 2555904 | tf_op jit(solution)/shard_map/all_to_all | solution.py:384
  280.0 19.9 %collective-permute-start.36 = (bf16[512,768]{1,0:T(8,128)(2,1)S(1)}, bf16[512,768]{1,0:T(8,128)(2,1)S(1)}, u32[]{:S(2)}, u32[]{:S(2)}) collective-permute-start(bf16[512,768]{1,0:T(8,128)(2,1)S(1)} %copy-done.14), channel_id=1, source_target_pairs={{0,2},{2,0},{1,3},{3,1},{4,6},{6,4},{5,7},{7,5},{8,10},{10,8},{9,1... | collective-permute-start | bytes 2359304 | tf_op jit(solution)/shard_map/ppermute | solution.py:38
  299.9 23.6 %collective-permute-start.37 = (bf16[4,112,960]{2,1,0:T(8,128)(2,1)}, bf16[4,112,960]{2,1,0:T(8,128)(2,1)}, u32[]{:S(2)}, u32[]{:S(2)}) collective-permute-start(bf16[4,112,960]{2,1,0:T(8,128)(2,1)} %get-tuple-element.300), channel_id=1, source_target_pairs={{0,2},{2,0},{1,3},{3,1},{4,6},{6,4},{5,7},{7,5},{8,10},{10,8},{9,1... | collective-permute-start | bytes 2580488 | tf_op jit(solution)/shard_map/ppermute | solution.py:38
  300.9 43.3 %collective-permute-start.38 = (bf16[4,112,960]{2,1,0:T(8,128)(2,1)}, bf16[4,112,960]{2,1,0:T(8,128)(2,1)}, u32[]{:S(2)}, u32[]{:S(2)}) collective-permute-start(bf16[4,112,960]{2,1,0:T(8,128)(2,1)} %get-tuple-element.301), channel_id=1, source_target_pairs={{0,4},{4,0},{8,12},{12,8},{16,20},{20,16},{24,28},{28,24},{1,5},{5... | collective-permute-start | bytes 2580488 | tf_op jit(solution)/shard_map/ppermute | solution.py:43
  302.2 42.0 %collective-permute-start.39 = (bf16[4,112,960]{2,1,0:T(8,128)(2,1)}, bf16[4,112,960]{2,1,0:T(8,128)(2,1)}, u32[]{:S(2)}, u32[]{:S(2)}) collective-permute-start(bf16[4,112,960]{2,1,0:T(8,128)(2,1)} %get-tuple-element.302), channel_id=1, source_target_pairs={{0,6},{1,7},{2,4},{3,5},{4,2},{5,3},{6,0},{7,1},{8,14},{9,15},{10,... | collective-permute-start | bytes 2580488 | tf_op jit(solution)/shard_map/ppermute | solution.py:379
  317.4 37.1 %collective-permute-start.40 = (bf16[4,104,576]{2,1,0:T(8,128)(2,1)}, bf16[4,104,576]{2,1,0:T(8,128)(2,1)S(1)}, u32[]{:S(2)}, u32[]{:S(2)}) collective-permute-start(bf16[4,104,576]{2,1,0:T(8,128)(2,1)} %get-tuple-element.305), channel_id=1, source_target_pairs={{0,2},{2,0},{1,3},{3,1},{4,6},{6,4},{5,7},{7,5},{8,10},{10,8},{9,1... | collective-permute-start | bytes 1437704 | tf_op jit(solution)/shard_map/ppermute | solution.py:38
  318.4 45.9 %collective-permute-start.41 = (bf16[4,104,576]{2,1,0:T(8,128)(2,1)}, bf16[4,104,576]{2,1,0:T(8,128)(2,1)S(1)}, u32[]{:S(2)}, u32[]{:S(2)}) collective-permute-start(bf16[4,104,576]{2,1,0:T(8,128)(2,1)} %get-tuple-element.306), channel_id=1, source_target_pairs={{0,4},{4,0},{8,12},{12,8},{16,20},{20,16},{24,28},{28,24},{1,5},{5... | collective-permute-start | bytes 1437704 | tf_op jit(solution)/shard_map/ppermute | solution.py:43
  323.5 42.0 %collective-permute-start.42 = (bf16[4,104,576]{2,1,0:T(8,128)(2,1)}, bf16[4,104,576]{2,1,0:T(8,128)(2,1)}, u32[]{:S(2)}, u32[]{:S(2)}) collective-permute-start(bf16[4,104,576]{2,1,0:T(8,128)(2,1)} %get-tuple-element.307), channel_id=1, source_target_pairs={{0,6},{1,7},{2,4},{3,5},{4,2},{5,3},{6,0},{7,1},{8,14},{9,15},{10,... | collective-permute-start | bytes 1437704 | tf_op jit(solution)/shard_map/ppermute | solution.py:379
  348.4 17.1 %copy-start.45 = (bf16[4,104,576]{2,1,0:T(8,128)(2,1)S(1)}, bf16[4,104,576]{2,1,0:T(8,128)(2,1)}, u32[]{:S(2)}) copy-start(bf16[4,104,576]{2,1,0:T(8,128)(2,1)} %get-tuple-element.304) | copy-start | bytes 1437700
  348.4 25.2 %all-to-all-start.4 = ((bf16[4,112,960]{2,1,0:T(8,128)(2,1)}), bf16[4,112,960]{2,1,0:T(8,128)(2,1)}, u32[]{:S(2)}, u32[]{:S(2)}) async-start(bf16[4,112,960]{2,1,0:T(8,128)(2,1)} %fusion), calls=%async_computation.4 | async-start | bytes 1835008 | tf_op jit(solution)/shard_map/all_to_all | solution.py:384
  353.2 24.6 %copy-start.47 = (s32[2,16]{1,0:T(2,128)S(1)}, s32[2,16]{1,0:T(2,128)}, u32[]{:S(2)}) copy-start(s32[2,16]{1,0:T(2,128)} %param.32) | copy-start | bytes 388
  367.6 3.4 collective-permute-start.44
  367.6 12.7 %collective-permute-start.43 = (bf16[512,768]{1,0:T(8,128)(2,1)}, bf16[512,768]{1,0:T(8,128)(2,1)}, u32[]{:S(2)}, u32[]{:S(2)}) collective-permute-start(bf16[512,768]{1,0:T(8,128)(2,1)} %get-tuple-element.308), channel_id=1, source_target_pairs={{0,1},{1,0},{2,3},{3,2},{4,5},{5,4},{6,7},{7,6},{8,9},{9,8},{10,11... | collective-permute-start | bytes 2359304 | tf_op jit(solution)/shard_map/ppermute | solution.py:34
  371.0 12.0 %collective-permute-start.45 = (bf16[8,64,768]{2,1,0:T(8,128)(2,1)S(1)}, bf16[8,64,768]{2,1,0:T(8,128)(2,1)S(1)}, u32[]{:S(2)}, u32[]{:S(2)}) collective-permute-start(bf16[8,64,768]{2,1,0:T(8,128)(2,1)S(1)} %bitcast.68), channel_id=1, source_target_pairs={{0,1},{1,0},{2,3},{3,2},{4,5},{5,4},{6,7},{7,6},{8,9},{9,8},{10,11... | collective-permute-start | bytes 2359304 | tf_op jit(solution)/shard_map/ppermute | solution.py:34
  373.6 17.7 %all-to-all-start.5 = ((bf16[4,104,576]{2,1,0:T(8,128)(2,1)}), bf16[4,104,576]{2,1,0:T(8,128)(2,1)}, u32[]{:S(2)}, u32[]{:S(2)}) async-start(bf16[4,104,576]{2,1,0:T(8,128)(2,1)} %add_convert_fusion.6), calls=%async_computation.5 | async-start | bytes 1064960 | tf_op jit(solution)/shard_map/all_to_all | solution.py:384
  (52 other events, 257.4 us)

commit v5 on v4

--- a/solution.py
+++ b/solution.py
@@ -1076,18 +1076,27 @@
     )
 
 
-def fetch_kernel(table, bank_ref, mine_ref, send_ref, sem):
-    count = table.shape[0] // 2
+def fetch_kernel(blocks_ref, bank_ref, mine_ref, send_ref, sem):
+    rank = lax.axis_index("tensor")
+    core, chip = rank % 2, rank // 2
+    count = mine_ref.shape[0]
+    slots = count // 2
+    here = bank_ref.shape[0] // blocks_ref.shape[0]
 
     def each(act):
         for group, out_ref in enumerate((mine_ref, send_ref)):
 
             def body(i, carry, group=group, out_ref=out_ref):
-                at = table[group * count + i]
+                seq = (i // slots + chip) % 2
+                half = (group + core) % 2
+                at = blocks_ref[seq, half * slots + i % slots] - rank * here
+                held = (at >= 0) & (at < here)
                 copy = pltpu.make_async_copy(
-                    bank_ref.at[jnp.maximum(at, 0)], out_ref.at[i], sem.at[group * count + i]
+                    bank_ref.at[jnp.where(held, at + seq * here, 0)],
+                    out_ref.at[i],
+                    sem.at[group * count + i],
                 )
-                act(copy, at >= 0, out_ref, i)
+                act(copy, held, out_ref, i)
                 return carry
 
             lax.fori_loop(0, count, body, 0)
@@ -1110,18 +1119,17 @@
     each(finish)
 
 
-def fetch(table, bank_blocks):
-    count = table.shape[0]
+def fetch(blocks, bank_blocks):
+    count = 2 * blocks.shape[1]
     blk, width = bank_blocks.shape[1:]
     out = struct((count // 2, blk, width), BF)
     mine, send = call(
         fetch_kernel,
         [out, out],
-        [table, bank_blocks],
+        [blocks, bank_blocks],
         [SM, ANY],
         [VM, VM],
         [pltpu.SemaphoreType.DMA((count,))],
-        moved=count * blk * width * 4,
         name="fetch",
     )
     return [part.reshape(2, count // 4, blk, width) for part in (mine, send)]
@@ -1311,14 +1319,7 @@
     attn_cols = 5 * head_cols
     info = jnp.stack([inner, rank, chip]).astype(jnp.int32)
 
-    seq_order = jnp.stack([chip, 1 - chip])
-    near = blocks[seq_order].reshape(2, 2, slots)
-    near = jnp.stack([near[:, core], near[:, 1 - core]])
-    near = near - rank * local_blocks
-    held = (near >= 0) & (near < local_blocks)
-    fetch_table = jnp.where(held, near + seq_order[None, :, None] * local_blocks, -1)
-    fetch_table = fetch_table.reshape(-1).astype(jnp.int32)
-    part_mine, part_send = fetch(fetch_table, bank.reshape(seq_count * local_blocks, BLK, width))
+    part_mine, part_send = fetch(blocks, bank.reshape(seq_count * local_blocks, BLK, width))
 
     part_got = swap_core(part_send)
     part_away = part_mine[1] + part_got[1]

time: 398 us -> 396 us (level)
  no operation moved by 1% of the time
where the time goes in v5:
time: 396 us; the launch traced here: 392 us
  Pallas kernels  172 us (43%)
  waiting for transfers between devices  105 us (27%)
  starting transfers between devices  62 us (16%)
  other arithmetic  32.9 us (8%)
  local copies, waits for them, and re-layouts  18 us (5%)
    pallas_call x14, Pallas kernels, call(): pl.pallas_call(kernel, out_shape=out_shape, in_specs=in_specs, out_specs=...  94.4 us
    ppermute x8, waiting for transfers between devices, swap_dp(): lax.ppermute(value, 'dp', tuple(((i, i ^ bit) for i in range(count))))  43 us
    ppermute x11, waiting for transfers between devices, swap_x(): return lax.ppermute(value, 'tensor', X_SWAP)  29 us
    all_to_all x6, starting transfers between devices, outer_exchange(): lax.all_to_all(value, 'dp', 0, 0, axis_index_groups=groups, tiled=True)  27.5 us
    pallas_call x1, Pallas kernels, cross_first_backward(): pl.pallas_call(functools.partial(cross_first_kernel, start=start, count=c...  19.2 us
    pallas_call x2, Pallas kernels, self_backward(): pl.pallas_call(self_bwd_kernel, grid_spec=pltpu.PrefetchScalarGridSpec(nu...  18.2 us
    pallas_call x1, Pallas kernels, cross_forward(): pl.pallas_call(cross_fwd_kernel, grid=(pairs,), in_specs=[whole, whole, t...  13.9 us
    pallas_call x1, Pallas kernels, self_forward(): pl.pallas_call(self_forward_kernel, grid_spec=pltpu.PrefetchScalarGridSpe...  12.9 us
  transfers between devices with their start and end apart: 52, of which 28 were waited for; matrix products, arithmetic and copies ran while one was open for 8% of the time, Pallas kernels for 34%

profile of v5, /device:TPU:0, one launch (start us, length us, event | category | flops | bytes accessed | tf_op | source)
XLA Modules:
  0.0 391.5 jit_solution(10923052979512259169)
XLA Ops:
  0.8 4.6 %fetch.1 = (bf16[16,64,768]{2,1,0:T(8,128)(2,1)}, bf16[16,64,768]{2,1,0:T(8,128)(2,1)}) custom-call(s32[2,16]{1,0:T(2,128)} %blocks_ref.1, bf16[32,64,768]{2,1,0:T(8,128)(2,1)} %bitcast.70), custom_call_target="tpu_custom_call" | custom-call | flops 1000 | bytes 1000 | tf_op jit(solution)/shard_map/fetch/pallas_call | solution.py:412
  6.2 2.6 collective-permute-start.1
  11.2 3.2 fusion.15
  15.5 1.9 pack_self.1
  17.3 4.8 %all-to-all-start = ((bf16[4,96,576]{2,1,0:T(8,128)(2,1)}), bf16[4,96,576]{2,1,0:T(8,128)(2,1)S(1)}, u32[]{:S(2)}, u32[]{:S(2)}) async-start(bf16[4,96,576]{2,1,0:T(8,128)(2,1)} %pack_self.1), calls=%async_computation | async-start | bytes 983040 | tf_op jit(solution)/shard_map/all_to_all | solution.py:384
  25.0 1.3 concatenate.23.vec_ref
  26.3 2.6 pack_rest.1
  28.9 7.0 %all-to-all-done.w_ref = bf16[4,96,576]{2,1,0:T(8,128)(2,1)S(1)} async-done(((bf16[4,96,576]{2,1,0:T(8,128)(2,1)}), bf16[4,96,576]{2,1,0:T(8,128)(2,1)S(1)}, u32[]{:S(2)}, u32[]{:S(2)}) %all-to-all-start) | async-done | bytes 442400 | tf_op jit(solution)/shard_map/all_to_all | solution.py:384
  36.9 4.3 %all-to-all-start.1 = ((bf16[4,96,1728]{2,1,0:T(8,128)(2,1)}), bf16[4,96,1728]{2,1,0:T(8,128)(2,1)}, u32[]{:S(2)}, u32[]{:S(2)}) async-start(bf16[4,96,1728]{2,1,0:T(8,128)(2,1)} %get-tuple-element.189), calls=%async_computation.1 | async-start | bytes 2752512 | tf_op jit(solution)/shard_map/all_to_all | solution.py:384
  42.5 1.7 collective-permute-start.7
  44.8 10.7 %collective-permute-done.5.wx_ref = bf16[4,96,576]{2,1,0:T(8,128)(2,1)S(1)} collective-permute-done((bf16[4,96,576]{2,1,0:T(8,128)(2,1)S(1)}, bf16[4,96,576]{2,1,0:T(8,128)(2,1)S(1)}, u32[]{:S(2)}, u32[]{:S(2)}) %collective-permute-start.5) | collective-permute-done | bytes 442400 | tf_op jit(solution)/shard_map/ppermute | solution.py:38
  55.4 2.1 collective-permute-start.10
  59.5 10.3 %collective-permute-done.10.xy_ref = bf16[96,768]{1,0:T(8,128)(2,1)} collective-permute-done((bf16[96,768]{1,0:T(8,128)(2,1)}, bf16[96,768]{1,0:T(8,128)(2,1)}, u32[]{:S(2)}, u32[]{:S(2)}) %collective-permute-start.10) | collective-permute-done | bytes 147488 | tf_op jit(solution)/shard_map/ppermute | solution.py:379
  69.8 3.0 collective-permute-done.9.y_ref
  72.8 2.7 plane_copies.1
  75.5 2.2 slice.114.refs_0_
  79.0 1.4 collective-permute-start.13
  81.3 4.9 %all-to-all-start.2 = ((bf16[4,2,2,96,768]{4,3,2,1,0:T(8,128)(2,1)}), bf16[4,2,2,96,768]{4,3,2,1,0:T(8,128)(2,1)}, u32[]{:S(2)}, u32[]{:S(2)}) async-start(bf16[4,2,2,96,768]{4,3,2,1,0:T(8,128)(2,1)} %plane_copies.1), calls=%async_computation.2 | async-start | bytes 4718592 | tf_op jit(solution)/shard_map/all_to_all | solution.py:384
  87.3 12.9 %self_fwd.1 = (bf16[2,512,1152]{2,1,0:T(8,128)(2,1)}, bf16[768,1152]{1,0:T(8,128)(2,1)S(1)}, bf16[512,384]{1,0:T(8,128)(2,1)S(1)}, bf16[512,384]{1,0:T(8,128)(2,1)S(1)}, f32[3,2,2,512]{3,2,1,0:T(2,128)S(1)}) custom-call(s32[5]{0:T(128)S(1)} %pad_add_fusion.2.info, bf16[512,768]{1,0:T(8,128)(2,1)S(1)} %copy-done.5, ...), custom_call_target="tpu_custom_call" | custom-call | flops 1000 | bytes 1000 | tf_op jit(solution)/shard_map/self_fwd/pallas_call | solution.py:565
  103.8 10.1 %collective-permute-done.13.refs_1_ = bf16[4,96,960]{2,1,0:T(8,128)(2,1)} collective-permute-done((bf16[4,96,960]{2,1,0:T(8,128)(2,1)}, bf16[4,96,960]{2,1,0:T(8,128)(2,1)}, u32[]{:S(2)}, u32[]{:S(2)}) %collective-permute-start.13) | collective-permute-done | bytes 737312 | tf_op jit(solution)/shard_map/ppermute | solution.py:43
  121.6 7.8 %assemble.1 = (bf16[4,2,96,1536]{3,2,1,0:T(8,128)(2,1)}, bf16[4,2,96,768]{3,2,1,0:T(8,128)(2,1)}, bf16[4,2,96,768]{3,2,1,0:T(8,128)(2,1)}, bf16[4,2,96,768]{3,2,1,0:T(8,128)(2,1)}) custom-call(s32[3]{0:T(128)} %pad_add_fusion.info, bf16[4,96,960]{2,1,0:T(8,128)(2,1)} %slice.114.refs_0_, bf16[4,96,960]{2,1,0:T(8,128)(2,1)} %collective-permute-done.13.refs_1_, ...), custom_call_target="tpu_custom_call" | custom-call | flops 1000 | bytes 1000 | tf_op jit(solution)/shard_map/assemble/pallas_call | solution.py:412
  129.4 4.6 %collective-permute-done.22.e1 = bf16[4,96,768]{2,1,0:T(8,128)(2,1)S(1)} collective-permute-done((bf16[4,96,768]{2,1,0:T(8,128)(2,1)S(1)}, bf16[4,96,768]{2,1,0:T(8,128)(2,1)S(1)}, u32[]{:S(2)}, u32[]{:S(2)}) %collective-permute-start.22) | collective-permute-done | bytes 589856 | tf_op jit(solution)/shard_map/ppermute | solution.py:43
  134.5 4.9 %project_kv.1 = (bf16[512,768]{1,0:T(8,128)(2,1)}, bf16[512,1536]{1,0:T(8,128)(2,1)}) custom-call(bf16[512,768]{1,0:T(8,128)(2,1)} %bitcast_add_fusion.1.keep_ref, bf16[512,768]{1,0:T(8,128)(2,1)} %bitcast.72, bf16[768,1536]{1,0:T(8,128)(2,1)} %bitcast.63, f32[1,768]{1,0:T(1,128)} %reshape_reshape.7.bias_ref), custom_call_target="tpu_custom_call" | custom-call | flops 1000 | bytes 1000 | tf_op jit(solution)/shard_map/project_kv/pallas_call | solution.py:412
  139.5 5.7 %first_forward.1 = (f32[512,768]{1,0:T(8,128)}, f32[512,768]{1,0:T(8,128)}, bf16[512,768]{1,0:T(8,128)(2,1)}, bf16[512,768]{1,0:T(8,128)(2,1)}, bf16[512,768]{1,0:T(8,128)(2,1)}) custom-call(bf16[512,768]{1,0:T(8,128)(2,1)} %own_ref.2, bf16[512,384]{1,0:T(8,128)(2,1)} %copy-done.9, bf16[512,384]{1,0:T(8,128)(2,1)} %copy-done.46, bf16[768,768]{1,0:T(8,128)(2,1)} %bitcast.68, ...), custom_call_target="tpu_custom_call" | custom-call | flops 1000 | bytes 1000 | tf_op jit(solution)/shard_map/first_forward/pallas_call | solution.py:412
  145.8 1.7 collective-permute-start.19
  149.2 13.9 %cross_fwd.1 = (bf16[512,768]{1,0:T(8,128)(2,1)S(1)}, f32[6,2,512]{2,1,0:T(2,128)S(1)}) custom-call(bf16[512,768]{1,0:T(8,128)(2,1)S(1)} %copy-done.6, bf16[512,1536]{1,0:T(8,128)(2,1)S(1)} %copy-done, bf16[512,1536]{1,0:T(8,128)(2,1)S(1)} %collective-permute-done.25.kb_ref.vb_ref, bf16[512,1536]{1,0:T(8,128)(2,1)S(1)} %copy-done, ...), custom_call_target="tpu_custom_call" | custom-call | flops 1000 | bytes 1000 | tf_op jit(solution)/shard_map/cross_fwd/pallas_call | solution.py:182
  164.2 1.8 collective-permute-done.26.e7
  166.1 1.4 copy-done.26
  167.7 32.8 %feed.1 = (bf16[512,768]{1,0:T(8,128)(2,1)}, f32[512,768]{1,0:T(8,128)}, bf16[512,768]{1,0:T(8,128)(2,1)}, bf16[512,768]{1,0:T(8,128)(2,1)}, bf16[2,2,4,104,1536...) custom-call(s32[3]{0:T(128)} %pad_add_fusion.info, bf16[512,768]{1,0:T(8,128)(2,1)} %copy-done.3, ...), custom_call_target="tpu_custom_call" | custom-call | flops 1000 | bytes 1000 | tf_op jit(solution)/shard_map/feed/pallas_call | solution.py:412
  201.9 8.5 %cross_bwd.1 = (bf16[512,768]{1,0:T(8,128)(2,1)S(1)}, bf16[2,512,768]{2,1,0:T(8,128)(2,1)S(1)}, bf16[2,512,768]{2,1,0:T(8,128)(2,1)}) custom-call(bf16[512,768]{1,0:T(8,128)(2,1)S(1)} %copy-done.7, bf16[512,1536]{1,0:T(8,128)(2,1)} %get-tuple-element.226.ka_ref.va_ref, bf16[512,1536]{1,0:T(8,128)(2,1)} %copy-done.1, ...), custom_call_target="tpu_custom_call" | custom-call | flops 1000 | bytes 1000 | tf_op jit(solution)/shard_map/cross_bwd/pallas_call | solution.py:233
  210.4 3.3 fusion.2
  213.7 2.8 fusion.1
  218.3 19.2 %cross_first.1 = (bf16[512,768]{1,0:T(8,128)(2,1)S(1)}, bf16[2,512,768]{2,1,0:T(8,128)(2,1)}, bf16[2,512,768]{2,1,0:T(8,128)(2,1)}, f32[512,768]{1,0:T(8,128)}, ...) custom-call(bf16[512,768]{1,0:T(8,128)(2,1)S(1)} %copy-done.7, ...), custom_call_target="tpu_custom_call", output_to_operand_aliasing={{1}: (14, {}), {2}: (15, {})} | custom-call | flops 1000 | bytes 1000 | tf_op jit(solution)/shard_map/cross_first/pallas_call | solution.py:325
  237.5 9.5 %collective-permute-done.29 = bf16[2,4,104,768]{3,2,1,0:T(8,128)(2,1)S(1)} collective-permute-done((bf16[2,4,104,768]{3,2,1,0:T(8,128)(2,1)}, bf16[2,4,104,768]{3,2,1,0:T(8,128)(2,1)S(1)}, u32[]{:S(2)}, u32[]{:S(2)}) %collective-permute-start.29) | collective-permute-done | bytes 1277984 | tf_op jit(solution)/shard_map/ppermute | solution.py:38
  248.3 2.9 fusion.5
  253.7 12.4 %attn_grads.1 = (bf16[2,2,4,112,960]{4,3,2,1,0:T(8,128)(2,1)}, bf16[2,2,4,112,960]{4,3,2,1,0:T(8,128)(2,1)}, bf16[512,768]{1,0:T(8,128)(2,1)}) custom-call(s32[3]{0:T(128)} %pad_add_fusion.info, bf16[512,768]{1,0:T(8,128)(2,1)} %get-tuple-element.264.h1_ref, bf16[512,768]{1,0:T(8,128)(2,1)} %copy-done.15, bf16[512,768]{1,0:T(8,128)(2,1)} %copy-done.16, ...), custom_call_target="tpu_custom_call" | custom-call | flops 1000 | bytes 1000 | tf_op jit(solution)/shard_map/attn_grads/pallas_call | solution.py:412
  266.1 2.5 collective-permute-done.33
  269.9 2.7 fusion.8
  273.7 4.5 %all-to-all-start.3 = ((bf16[4,104,1536]{2,1,0:T(8,128)(2,1)}), bf16[4,104,1536]{2,1,0:T(8,128)(2,1)}, u32[]{:S(2)}, u32[]{:S(2)}) async-start(bf16[4,104,1536]{2,1,0:T(8,128)(2,1)} %pad_maximum_fusion), calls=%async_computation.3 | async-start | bytes 2555904 | tf_op jit(solution)/shard_map/all_to_all | solution.py:384
  279.3 11.8 %self_bwd.2.rest_0_ = bf16[3,2,512,384]{3,2,1,0:T(8,128)(2,1)S(1)} custom-call(s32[2]{0:T(128)S(1)} %pad_add_fusion.1.info, bf16[2,512,1152]{2,1,0:T(8,128)(2,1)} %get-tuple-element.243.q_ref.k_ref.v_ref, bf16[2,512,1152]{2,1,0:T(8,128)(2,1)} %get-tuple-element.243.q_ref.k_ref.v_ref, bf16[2,512,1152]{2,1,0:T(8,128)(2,1)} %get-tuple-element.243.q_ref.k_ref.v_ref, ...), custom_call_target="tpu_custom_call" | custom-call | flops 1000 | bytes 1000 | tf_op jit(solution)/shard_map/self_bwd/pallas_call | solution.py:123
  291.1 4.2 %fusion.11 = (bf16[4,112,960]{2,1,0:T(8,128)(2,1)}, bf16[4,112,960]{2,1,0:T(8,128)(2,1)}, bf16[4,112,960]{2,1,0:T(8,128)(2,1)}) fusion(bf16[2,2,4,112,960]{4,3,2,1,0:T(8,128)(2,1)} %collective-permute-done.35, bf16[2,2,4,112,960]{4,3,2,1,0:T(8,128)(2,1)S(1)} %copy-done.23), kind=kLoop, calls=%fused_computation.24 | loop fusion | flops 5160960 | bytes 7741440 | tf_op jit(solution)/shard_map/convert_element_type | solution.py:397
  295.3 2.9 collective-permute-done.36
  299.2 1.3 collective-permute-start.38
  301.7 6.4 %self_bwd.3.d_ref = bf16[3,2,512,384]{3,2,1,0:T(8,128)(2,1)S(1)} custom-call(s32[2]{0:T(128)S(1)} %pad_add_fusion.1.info, bf16[2,512,1152]{2,1,0:T(8,128)(2,1)} %get-tuple-element.243.q_ref.k_ref.v_ref, bf16[2,512,1152]{2,1,0:T(8,128)(2,1)} %get-tuple-element.243.q_ref.k_ref.v_ref, ...), custom_call_target="tpu_custom_call", output_to_operand_aliasing={{}: (9, {})} | custom-call | flops 1000 | bytes 1000 | tf_op jit(solution)/shard_map/self_bwd/pallas_call | solution.py:123
  308.1 1.4 copy-done.2
  309.5 6.1 %self_grads.1 = (bf16[4,104,576]{2,1,0:T(8,128)(2,1)}, bf16[4,104,576]{2,1,0:T(8,128)(2,1)}, bf16[4,104,576]{2,1,0:T(8,128)(2,1)}, bf16[4,104,576]{2,1,0:T(8,128)(2,1)}) custom-call(s32[3]{0:T(128)} %pad_add_fusion.info, bf16[512,768]{1,0:T(8,128)(2,1)} %own_ref.2, bf16[512,768]{1,0:T(8,128)(2,1)} %copy-done.11, bf16[3,2,512,384]{3,2,1,0:T(8,128)(2,1)} %copy-done.2), custom_call_target="tpu_custom_call" | custom-call | flops 1000 | bytes 1000 | tf_op jit(solution)/shard_map/self_grads/pallas_call | solution.py:412
  316.6 1.3 collective-permute-start.41
  317.9 3.8 collective-permute-done.37
  321.7 1.7 collective-permute-start.42
  323.5 6.6 %self_back.1 = (f32[512,768]{1,0:T(8,128)}, bf16[512,768]{1,0:T(8,128)(2,1)}) custom-call(bf16[3,2,512,384]{3,2,1,0:T(8,128)(2,1)} %copy-done.2, bf16[768,1152]{1,0:T(8,128)(2,1)} %copy-done.13, f32[512,768]{1,0:T(8,128)} %get-tuple-element.296.first_ref), custom_call_target="tpu_custom_call" | custom-call | flops 1000 | bytes 1000 | tf_op jit(solution)/shard_map/self_back/pallas_call | solution.py:412
  330.0 12.4 %collective-permute-done.38 = bf16[4,112,960]{2,1,0:T(8,128)(2,1)} collective-permute-done((bf16[4,112,960]{2,1,0:T(8,128)(2,1)}, bf16[4,112,960]{2,1,0:T(8,128)(2,1)}, u32[]{:S(2)}, u32[]{:S(2)}) %collective-permute-start.38) | collective-permute-done | bytes 860192 | tf_op jit(solution)/shard_map/ppermute | solution.py:43
  342.4 4.2 %fusion = bf16[4,112,960]{2,1,0:T(8,128)(2,1)} fusion(bf16[4,112,960]{2,1,0:T(8,128)(2,1)} %collective-permute-done.39, bf16[4,112,960]{2,1,0:T(8,128)(2,1)} %collective-permute-done.38, bf16[4,112,960]{2,1,0:T(8,128)(2,1)} %collective-permute-done.37, bf16[2,2,4,112,960]{4,3,2,1,0:T(8,128)(2,1)} %collective-permute-done.35, ...), kind=kLoop, calls=%fused_computation.3 | loop fusion | flops 4300800 | bytes 5160960 | tf_op jit(solution)/shard_map/convert_element_type | solution.py:1538
  346.7 4.8 %all-to-all-start.4 = ((bf16[4,112,960]{2,1,0:T(8,128)(2,1)}), bf16[4,112,960]{2,1,0:T(8,128)(2,1)}, u32[]{:S(2)}, u32[]{:S(2)}) async-start(bf16[4,112,960]{2,1,0:T(8,128)(2,1)} %fusion), calls=%async_computation.4 | async-start | bytes 1835008 | tf_op jit(solution)/shard_map/all_to_all | solution.py:384
  352.7 9.8 %collective-permute-done.41 = bf16[4,104,576]{2,1,0:T(8,128)(2,1)S(1)} collective-permute-done((bf16[4,104,576]{2,1,0:T(8,128)(2,1)}, bf16[4,104,576]{2,1,0:T(8,128)(2,1)S(1)}, u32[]{:S(2)}, u32[]{:S(2)}) %collective-permute-start.41) | collective-permute-done | bytes 479264 | tf_op jit(solution)/shard_map/ppermute | solution.py:43
  363.7 2.1 add_convert_fusion.6
  366.4 2.9 collective-permute-done.44.c_ref
  369.4 2.4 all-to-all-done.4.in_ref
  371.8 4.1 %all-to-all-start.5 = ((bf16[4,104,576]{2,1,0:T(8,128)(2,1)}), bf16[4,104,576]{2,1,0:T(8,128)(2,1)}, u32[]{:S(2)}, u32[]{:S(2)}) async-start(bf16[4,104,576]{2,1,0:T(8,128)(2,1)} %add_convert_fusion.6), calls=%async_computation.5 | async-start | bytes 1064960 | tf_op jit(solution)/shard_map/all_to_all | solution.py:384
  376.3 2.2 sum_feed.1
  378.5 2.6 add_convert_fusion.5
  381.2 4.8 %scatter.1 = f32[32,64,768]{2,1,0:T(8,128)} custom-call(s32[32]{0:T(128)S(1)} %reshape.254.table, bf16[8,64,768]{2,1,0:T(8,128)(2,1)S(1)} %bitcast.60, bf16[8,64,768]{2,1,0:T(8,128)(2,1)S(1)} %bitcast.62, bf16[8,64,768]{2,1,0:T(8,128)(2,1)S(1)} %collective-permute-done.44.c_ref, bf16[8,64,768]{2,1,0:T(8,128)(2,1)S(1)} %collective-permute-done.45.d_ref), custom_call_target="tpu_custom_call" | custom-call | flops 1000 | bytes 1000 | tf_op jit(solution)/shard_map/scatter/pallas_call | solution.py:1165
  386.0 2.1 sum_attn.1
  388.1 1.3 all-to-all-done.5.in_ref
  389.4 1.8 sum_cols.1
  (236 shorter events, 47.3 us)
Async XLA Ops:
  5.4 5.8 %collective-permute-start = (bf16[2,8,64,768]{3,2,1,0:T(8,128)(2,1)}, bf16[2,8,64,768]{3,2,1,0:T(8,128)(2,1)S(1)}, u32[]{:S(2)}, u32[]{:S(2)}) collective-permute-start(bf16[2,8,64,768]{3,2,1,0:T(8,128)(2,1)} %bitcast.74), channel_id=1, source_target_pairs={{0,1},{1,0},{2,3},{3,2},{4,5},{5,4},{6,7},{7,6},{8,9},{9,8},{10,11... | collective-permute-start | bytes 4718600 | tf_op jit(solution)/shard_map/ppermute | solution.py:34
  6.2 9.3 %collective-permute-start.1 = (f32[1,1536]{1,0:T(1,128)S(1)}, f32[1,1536]{1,0:T(1,128)S(1)}, u32[]{:S(2)}, u32[]{:S(2)}) collective-permute-start(f32[1,1536]{1,0:T(1,128)S(1)} %reshape.248), channel_id=1, source_target_pairs={{0,2},{2,0},{1,3},{3,1},{4,6},{6,4},{5,7},{7,5},{8,10},{10,8},{9,1... | collective-permute-start | bytes 18440 | tf_op jit(solution)/shard_map/ppermute | solution.py:38
  8.8 20.1 %collective-permute-start.3 = (bf16[512,768]{1,0:T(8,128)(2,1)S(1)}, bf16[512,768]{1,0:T(8,128)(2,1)S(1)}, u32[]{:S(2)}, u32[]{:S(2)}) collective-permute-start(bf16[512,768]{1,0:T(8,128)(2,1)S(1)} %copy-done.5), channel_id=1, source_target_pairs={{0,1},{1,0},{2,3},{3,2},{4,5},{5,4},{6,7},{7,6},{8,9},{9,8},{10,11... | collective-permute-start | bytes 2359304 | tf_op jit(solution)/shard_map/ppermute | solution.py:34
  14.4 21.5 %collective-permute-start.4 = (bf16[8,64,768]{2,1,0:T(8,128)(2,1)}, bf16[8,64,768]{2,1,0:T(8,128)(2,1)S(1)}, u32[]{:S(2)}, u32[]{:S(2)}) collective-permute-start(bf16[8,64,768]{2,1,0:T(8,128)(2,1)} %get-tuple-element.349), channel_id=1, source_target_pairs={{0,2},{2,0},{1,3},{3,1},{4,6},{6,4},{5,7},{7,5},{8,10},{10,8},{9,1... | collective-permute-start | bytes 2359304 | tf_op jit(solution)/shard_map/ppermute | solution.py:38
  17.3 18.6 %all-to-all-start = ((bf16[4,96,576]{2,1,0:T(8,128)(2,1)}), bf16[4,96,576]{2,1,0:T(8,128)(2,1)S(1)}, u32[]{:S(2)}, u32[]{:S(2)}) async-start(bf16[4,96,576]{2,1,0:T(8,128)(2,1)} %pack_self.1), calls=%async_computation | async-start | bytes 983040 | tf_op jit(solution)/shard_map/all_to_all | solution.py:384
  22.4 1.2 collective-permute-start.2
  28.9 57.3 %copy-start.11 = (bf16[512,768]{1,0:T(8,128)(2,1)}, bf16[512,768]{1,0:T(8,128)(2,1)S(1)}, u32[]{:S(2)}) copy-start(bf16[512,768]{1,0:T(8,128)(2,1)S(1)} %collective-permute-done.3.oth_ref) | copy-start | bytes 2359300
  36.9 38.6 %all-to-all-start.1 = ((bf16[4,96,1728]{2,1,0:T(8,128)(2,1)}), bf16[4,96,1728]{2,1,0:T(8,128)(2,1)}, u32[]{:S(2)}, u32[]{:S(2)}) async-start(bf16[4,96,1728]{2,1,0:T(8,128)(2,1)} %get-tuple-element.189), calls=%async_computation.1 | async-start | bytes 2752512 | tf_op jit(solution)/shard_map/all_to_all | solution.py:384
  41.2 14.2 %collective-permute-start.5 = (bf16[4,96,576]{2,1,0:T(8,128)(2,1)S(1)}, bf16[4,96,576]{2,1,0:T(8,128)(2,1)S(1)}, u32[]{:S(2)}, u32[]{:S(2)}) collective-permute-start(bf16[4,96,576]{2,1,0:T(8,128)(2,1)S(1)} %all-to-all-done.w_ref), channel_id=1, source_target_pairs={{0,2},{2,0},{1,3},{3,1},{4,6},{6,4},{5,7},{7,5},{8,10},{10,8},{9,1... | collective-permute-start | bytes 1327112 | tf_op jit(solution)/shard_map/ppermute | solution.py:38
  42.5 33.0 %collective-permute-start.7 = (bf16[4,96,576]{2,1,0:T(8,128)(2,1)S(1)}, bf16[4,96,576]{2,1,0:T(8,128)(2,1)S(1)}, u32[]{:S(2)}, u32[]{:S(2)}) collective-permute-start(bf16[4,96,576]{2,1,0:T(8,128)(2,1)S(1)} %all-to-all-done.w_ref), channel_id=1, source_target_pairs={{0,6},{1,7},{2,4},{3,5},{4,2},{5,3},{6,0},{7,1},{8,14},{9,15},{10,... | collective-permute-start | bytes 1327112 | tf_op jit(solution)/shard_map/ppermute | solution.py:379
  44.2 31.3 %collective-permute-start.6 = (bf16[4,96,576]{2,1,0:T(8,128)(2,1)S(1)}, bf16[4,96,576]{2,1,0:T(8,128)(2,1)S(1)}, u32[]{:S(2)}, u32[]{:S(2)}) collective-permute-start(bf16[4,96,576]{2,1,0:T(8,128)(2,1)S(1)} %all-to-all-done.w_ref), channel_id=1, source_target_pairs={{0,4},{4,0},{8,12},{12,8},{16,20},{20,16},{24,28},{28,24},{1,5},{5... | collective-permute-start | bytes 1327112 | tf_op jit(solution)/shard_map/ppermute | solution.py:43
  55.4 14.4 %collective-permute-start.10 = (bf16[96,768]{1,0:T(8,128)(2,1)}, bf16[96,768]{1,0:T(8,128)(2,1)}, u32[]{:S(2)}, u32[]{:S(2)}) collective-permute-start(bf16[96,768]{1,0:T(8,128)(2,1)} %get-tuple-element.192.own_ref), channel_id=1, source_target_pairs={{0,6},{1,7},{2,4},{3,5},{4,2},{5,3},{6,0},{7,1},{8,14},{9,15},{10,... | collective-permute-start | bytes 442376 | tf_op jit(solution)/shard_map/ppermute | solution.py:379
  57.5 15.3 %collective-permute-start.9 = (bf16[96,768]{1,0:T(8,128)(2,1)}, bf16[96,768]{1,0:T(8,128)(2,1)}, u32[]{:S(2)}, u32[]{:S(2)}) collective-permute-start(bf16[96,768]{1,0:T(8,128)(2,1)} %get-tuple-element.192.own_ref), channel_id=1, source_target_pairs={{0,4},{4,0},{8,12},{12,8},{16,20},{20,16},{24,28},{28,24},{1,5},{5... | collective-permute-start | bytes 442376 | tf_op jit(solution)/shard_map/ppermute | solution.py:43
  58.1 14.7 %collective-permute-start.8 = (bf16[96,768]{1,0:T(8,128)(2,1)}, bf16[96,768]{1,0:T(8,128)(2,1)}, u32[]{:S(2)}, u32[]{:S(2)}) collective-permute-start(bf16[96,768]{1,0:T(8,128)(2,1)} %get-tuple-element.192.own_ref), channel_id=1, source_target_pairs={{0,2},{2,0},{1,3},{3,1},{4,6},{6,4},{5,7},{7,5},{8,10},{10,8},{9,1... | collective-permute-start | bytes 442376 | tf_op jit(solution)/shard_map/ppermute | solution.py:38
  77.8 26.1 %collective-permute-start.14 = (bf16[4,96,960]{2,1,0:T(8,128)(2,1)}, bf16[4,96,960]{2,1,0:T(8,128)(2,1)}, u32[]{:S(2)}, u32[]{:S(2)}) collective-permute-start(bf16[4,96,960]{2,1,0:T(8,128)(2,1)} %slice.114.refs_0_), channel_id=1, source_target_pairs={{0,6},{1,7},{2,4},{3,5},{4,2},{5,3},{6,0},{7,1},{8,14},{9,15},{10,... | collective-permute-start | bytes 2211848 | tf_op jit(solution)/shard_map/ppermute | solution.py:379
  79.0 34.9 %collective-permute-start.13 = (bf16[4,96,960]{2,1,0:T(8,128)(2,1)}, bf16[4,96,960]{2,1,0:T(8,128)(2,1)}, u32[]{:S(2)}, u32[]{:S(2)}) collective-permute-start(bf16[4,96,960]{2,1,0:T(8,128)(2,1)} %slice.114.refs_0_), channel_id=1, source_target_pairs={{0,4},{4,0},{8,12},{12,8},{16,20},{20,16},{24,28},{28,24},{1,5},{5... | collective-permute-start | bytes 2211848 | tf_op jit(solution)/shard_map/ppermute | solution.py:43
  80.5 33.4 %collective-permute-start.12 = (bf16[4,96,960]{2,1,0:T(8,128)(2,1)}, bf16[4,96,960]{2,1,0:T(8,128)(2,1)}, u32[]{:S(2)}, u32[]{:S(2)}) collective-permute-start(bf16[4,96,960]{2,1,0:T(8,128)(2,1)} %slice.114.refs_0_), channel_id=1, source_target_pairs={{0,2},{2,0},{1,3},{3,1},{4,6},{6,4},{5,7},{7,5},{8,10},{10,8},{9,1... | collective-permute-start | bytes 2211848 | tf_op jit(solution)/shard_map/ppermute | solution.py:38
  81.3 63.9 %all-to-all-start.2 = ((bf16[4,2,2,96,768]{4,3,2,1,0:T(8,128)(2,1)}), bf16[4,2,2,96,768]{4,3,2,1,0:T(8,128)(2,1)}, u32[]{:S(2)}, u32[]{:S(2)}) async-start(bf16[4,2,2,96,768]{4,3,2,1,0:T(8,128)(2,1)} %plane_copies.1), calls=%async_computation.2 | async-start | bytes 4718592 | tf_op jit(solution)/shard_map/all_to_all | solution.py:384
  102.1 19.4 %copy-start.19 = (f32[3,2,2,512]{3,2,1,0:T(2,128)}, f32[3,2,2,512]{3,2,1,0:T(2,128)S(1)}, u32[]{:S(2)}) copy-start(f32[3,2,2,512]{3,2,1,0:T(2,128)S(1)} %get-tuple-element.244.lse_ref) | copy-start | bytes 73732
  102.1 18.3 %slice-start = ((bf16[2,8,64,768]{3,2,1,0:T(8,128)(2,1)}), bf16[1,8,64,768]{3,2,1,0:T(8,128)(2,1)S(1)}, s32[]{:S(2)}) async-start(bf16[2,8,64,768]{3,2,1,0:T(8,128)(2,1)} %copy-done.24), calls=%async_computation.6 | async-start | bytes 1572864 | tf_op jit(solution)/shard_map/slice | solution.py:1420
  102.1 18.3 %copy-start.25 = (bf16[8,64,768]{2,1,0:T(8,128)(2,1)S(1)}, bf16[8,64,768]{2,1,0:T(8,128)(2,1)}, u32[]{:S(2)}) copy-start(bf16[8,64,768]{2,1,0:T(8,128)(2,1)} %get-tuple-element.348) | copy-start | bytes 2359300
  102.1 1.7 collective-permute-start.15
  102.1 13.5 %collective-permute-start.11 = (bf16[4,96,960]{2,1,0:T(8,128)(2,1)}, bf16[4,96,960]{2,1,0:T(8,128)(2,1)S(1)}, u32[]{:S(2)}, u32[]{:S(2)}) collective-permute-start(bf16[4,96,960]{2,1,0:T(8,128)(2,1)} %slice.114.refs_0_), channel_id=1, source_target_pairs={{0,1},{1,0},{2,3},{3,2},{4,5},{5,4},{6,7},{7,6},{8,9},{9,8},{10,11... | collective-permute-start | bytes 2211848 | tf_op jit(solution)/shard_map/ppermute | solution.py:34
  113.9 2.5 collective-permute-start.16
  113.9 3.6 collective-permute-start.17
  114.4 4.2 %collective-permute-start.18 = (bf16[4,96,960]{2,1,0:T(8,128)(2,1)}, bf16[4,96,960]{2,1,0:T(8,128)(2,1)S(1)}, u32[]{:S(2)}, u32[]{:S(2)}) collective-permute-start(bf16[4,96,960]{2,1,0:T(8,128)(2,1)} %collective-permute-done.14.refs_3_), channel_id=1, source_target_pairs={{0,1},{1,0},{2,3},{3,2},{4,5},{5,4},{6,7},{7,6},{8,9},{9,8},{10,11... | collective-permute-start | bytes 2211848 | tf_op jit(solution)/shard_map/ppermute | solution.py:34
  118.6 15.4 %collective-permute-start.22 = (bf16[4,96,768]{2,1,0:T(8,128)(2,1)S(1)}, bf16[4,96,768]{2,1,0:T(8,128)(2,1)S(1)}, u32[]{:S(2)}, u32[]{:S(2)}) collective-permute-start(bf16[4,96,768]{2,1,0:T(8,128)(2,1)S(1)} %slice.115.e0), channel_id=1, source_target_pairs={{0,4},{4,0},{8,12},{12,8},{16,20},{20,16},{24,28},{28,24},{1,5},{5... | collective-permute-start | bytes 1769480 | tf_op jit(solution)/shard_map/ppermute | solution.py:43
  119.4 15.1 %collective-permute-start.21 = (bf16[4,96,768]{2,1,0:T(8,128)(2,1)S(1)}, bf16[4,96,768]{2,1,0:T(8,128)(2,1)S(1)}, u32[]{:S(2)}, u32[]{:S(2)}) collective-permute-start(bf16[4,96,768]{2,1,0:T(8,128)(2,1)S(1)} %slice.115.e0), channel_id=1, source_target_pairs={{0,2},{2,0},{1,3},{3,1},{4,6},{6,4},{5,7},{7,5},{8,10},{10,8},{9,1... | collective-permute-start | bytes 1769480 | tf_op jit(solution)/shard_map/ppermute | solution.py:38
  139.4 5.7 %collective-permute-start.25 = (bf16[512,1536]{1,0:T(8,128)(2,1)}, bf16[512,1536]{1,0:T(8,128)(2,1)S(1)}, u32[]{:S(2)}, u32[]{:S(2)}) collective-permute-start(bf16[512,1536]{1,0:T(8,128)(2,1)} %get-tuple-element.226.ka_ref.va_ref), channel_id=1, source_target_pairs={{0,1},{1,0},{2,3},{3,2},{4,5},{5,4},{6,7},{7,6},{8,9},{9,8},{10,11... | collective-permute-start | bytes 4718600 | tf_op jit(solution)/shard_map/ppermute | solution.py:34
  145.1 17.9 %copy-start.1 = (bf16[512,1536]{1,0:T(8,128)(2,1)}, bf16[512,1536]{1,0:T(8,128)(2,1)S(1)}, u32[]{:S(2)}) copy-start(bf16[512,1536]{1,0:T(8,128)(2,1)S(1)} %collective-permute-done.25.kb_ref.vb_ref) | copy-start | bytes 4718596
  145.2 20.9 %collective-permute-start.27 = (bf16[4,2,2,96,768]{4,3,2,1,0:T(8,128)(2,1)}, bf16[4,2,2,96,768]{4,3,2,1,0:T(8,128)(2,1)S(1)}, u32[]{:S(2)}, u32[]{:S(2)}) collective-permute-start(bf16[4,2,2,96,768]{4,3,2,1,0:T(8,128)(2,1)} %all-to-all-done.2.s0), channel_id=1, source_target_pairs={{0,1},{1,0},{2,3},{3,2},{4,5},{5,4},{6,7},{7,6},{8,9},{9,8},{10,11... | collective-permute-start | bytes 7077896 | tf_op jit(solution)/shard_map/ppermute | solution.py:34
  145.7 18.2 %collective-permute-start.20 = (bf16[4,96,768]{2,1,0:T(8,128)(2,1)}, bf16[4,96,768]{2,1,0:T(8,128)(2,1)S(1)}, u32[]{:S(2)}, u32[]{:S(2)}) collective-permute-start(bf16[4,96,768]{2,1,0:T(8,128)(2,1)} %copy-done.27), channel_id=1, source_target_pairs={{0,1},{1,0},{2,3},{3,2},{4,5},{5,4},{6,7},{7,6},{8,9},{9,8},{10,11... | collective-permute-start | bytes 1769480 | tf_op jit(solution)/shard_map/ppermute | solution.py:34
  145.8 18.1 %collective-permute-start.19 = (bf16[4,96,768]{2,1,0:T(8,128)(2,1)}, bf16[4,96,768]{2,1,0:T(8,128)(2,1)S(1)}, u32[]{:S(2)}, u32[]{:S(2)}) collective-permute-start(bf16[4,96,768]{2,1,0:T(8,128)(2,1)} %copy-done.27), channel_id=1, source_target_pairs={{0,6},{1,7},{2,4},{3,5},{4,2},{5,3},{6,0},{7,1},{8,14},{9,15},{10,... | collective-permute-start | bytes 1769480 | tf_op jit(solution)/shard_map/ppermute | solution.py:379
  147.5 16.4 %collective-permute-start.23 = (bf16[4,96,768]{2,1,0:T(8,128)(2,1)}, bf16[4,96,768]{2,1,0:T(8,128)(2,1)S(1)}, u32[]{:S(2)}, u32[]{:S(2)}) collective-permute-start(bf16[4,96,768]{2,1,0:T(8,128)(2,1)} %copy-done.38), channel_id=1, source_target_pairs={{0,1},{1,0},{2,3},{3,2},{4,5},{5,4},{6,7},{7,6},{8,9},{9,8},{10,11... | collective-permute-start | bytes 1769480 | tf_op jit(solution)/shard_map/ppermute | solution.py:34
  147.7 16.3 %collective-permute-start.24 = (bf16[4,96,768]{2,1,0:T(8,128)(2,1)}, bf16[4,96,768]{2,1,0:T(8,128)(2,1)S(1)}, u32[]{:S(2)}, u32[]{:S(2)}) collective-permute-start(bf16[4,96,768]{2,1,0:T(8,128)(2,1)} %copy-done.39), channel_id=1, source_target_pairs={{0,1},{1,0},{2,3},{3,2},{4,5},{5,4},{6,7},{7,6},{8,9},{9,8},{10,11... | collective-permute-start | bytes 1769480 | tf_op jit(solution)/shard_map/ppermute | solution.py:34
  164.0 2.1 collective-permute-start.26
  167.7 33.0 %copy-start.4 = (bf16[512,768]{1,0:T(8,128)(2,1)S(1)}, bf16[512,768]{1,0:T(8,128)(2,1)}, u32[]{:S(2)}) copy-start(bf16[512,768]{1,0:T(8,128)(2,1)} %copy-done.3) | copy-start | bytes 2359300
  167.7 33.0 %copy-start.7 = (bf16[512,768]{1,0:T(8,128)(2,1)S(1)}, bf16[512,768]{1,0:T(8,128)(2,1)}, u32[]{:S(2)}) copy-start(bf16[512,768]{1,0:T(8,128)(2,1)} %get-tuple-element.230.q_ref) | copy-start | bytes 2359300
  200.5 9.9 %collective-permute-start.28 = (bf16[2,2,4,104,1536]{4,3,2,1,0:T(8,128)(2,1)}, bf16[2,2,4,104,1536]{4,3,2,1,0:T(8,128)(2,1)}, u32[]{:S(2)}, u32[]{:S(2)}) collective-permute-start(bf16[2,2,4,104,1536]{4,3,2,1,0:T(8,128)(2,1)} %get-tuple-element.252), channel_id=1, source_target_pairs={{0,1},{1,0},{2,3},{3,2},{4,5},{5,4},{6,7},{7,6},{8,9},{9,8},{10,11... | collective-permute-start | bytes 15335432 | tf_op jit(solution)/shard_map/ppermute | solution.py:34
  216.5 30.5 %collective-permute-start.29 = (bf16[2,4,104,768]{3,2,1,0:T(8,128)(2,1)}, bf16[2,4,104,768]{3,2,1,0:T(8,128)(2,1)S(1)}, u32[]{:S(2)}, u32[]{:S(2)}) collective-permute-start(bf16[2,4,104,768]{3,2,1,0:T(8,128)(2,1)} %fusion.1), channel_id=1, source_target_pairs={{0,2},{2,0},{1,3},{3,1},{4,6},{6,4},{5,7},{7,5},{8,10},{10,8},{9,1... | collective-permute-start | bytes 3833864 | tf_op jit(solution)/shard_map/ppermute | solution.py:38
  217.5 30.3 %collective-permute-start.30 = (bf16[2,4,104,768]{3,2,1,0:T(8,128)(2,1)}, bf16[2,4,104,768]{3,2,1,0:T(8,128)(2,1)S(1)}, u32[]{:S(2)}, u32[]{:S(2)}) collective-permute-start(bf16[2,4,104,768]{3,2,1,0:T(8,128)(2,1)} %fusion.2), channel_id=1, source_target_pairs={{0,4},{4,0},{8,12},{12,8},{16,20},{20,16},{24,28},{28,24},{1,5},{5... | collective-permute-start | bytes 3833864 | tf_op jit(solution)/shard_map/ppermute | solution.py:43
  237.5 13.7 %copy-start.15 = (bf16[512,768]{1,0:T(8,128)(2,1)}, bf16[512,768]{1,0:T(8,128)(2,1)S(1)}, u32[]{:S(2)}) copy-start(bf16[512,768]{1,0:T(8,128)(2,1)S(1)} %get-tuple-element.265.dq_ref) | copy-start | bytes 2359300
  237.5 13.7 %copy-start.16 = (bf16[512,768]{1,0:T(8,128)(2,1)}, bf16[512,768]{1,0:T(8,128)(2,1)S(1)}, u32[]{:S(2)}) copy-start(bf16[512,768]{1,0:T(8,128)(2,1)S(1)} %get-tuple-element.270.e1_ref) | copy-start | bytes 2359300
  247.8 4.2 %collective-permute-start.31 = (bf16[2,512,768]{2,1,0:T(8,128)(2,1)}, bf16[2,512,768]{2,1,0:T(8,128)(2,1)S(1)}, u32[]{:S(2)}, u32[]{:S(2)}) collective-permute-start(bf16[2,512,768]{2,1,0:T(8,128)(2,1)} %get-tuple-element.267), channel_id=1, source_target_pairs={{0,1},{1,0},{2,3},{3,2},{4,5},{5,4},{6,7},{7,6},{8,9},{9,8},{10,11... | collective-permute-start | bytes 4718600 | tf_op jit(solution)/shard_map/ppermute | solution.py:34
  247.8 3.6 collective-permute-start.32
  252.0 16.6 %collective-permute-start.33 = (bf16[4,104,768]{2,1,0:T(8,128)(2,1)}, bf16[4,104,768]{2,1,0:T(8,128)(2,1)S(1)}, u32[]{:S(2)}, u32[]{:S(2)}) collective-permute-start(bf16[4,104,768]{2,1,0:T(8,128)(2,1)} %get-tuple-element.279), channel_id=1, source_target_pairs={{0,4},{4,0},{8,12},{12,8},{16,20},{20,16},{24,28},{28,24},{1,5},{5... | collective-permute-start | bytes 1916936 | tf_op jit(solution)/shard_map/ppermute | solution.py:43
  252.7 16.4 %collective-permute-start.34 = (bf16[4,104,768]{2,1,0:T(8,128)(2,1)}, bf16[4,104,768]{2,1,0:T(8,128)(2,1)S(1)}, u32[]{:S(2)}, u32[]{:S(2)}) collective-permute-start(bf16[4,104,768]{2,1,0:T(8,128)(2,1)} %get-tuple-element.280), channel_id=1, source_target_pairs={{0,2},{2,0},{1,3},{3,1},{4,6},{6,4},{5,7},{7,5},{8,10},{10,8},{9,1... | collective-permute-start | bytes 1916936 | tf_op jit(solution)/shard_map/ppermute | solution.py:38
  253.7 16.2 %copy-start.30 = (bf16[2,4,104,768]{3,2,1,0:T(8,128)(2,1)S(1)}, bf16[2,4,104,768]{3,2,1,0:T(8,128)(2,1)}, u32[]{:S(2)}) copy-start(bf16[2,4,104,768]{3,2,1,0:T(8,128)(2,1)} %copy-done.29) | copy-start | bytes 3833860
  269.9 21.2 %collective-permute-start.35 = (bf16[2,2,4,112,960]{4,3,2,1,0:T(8,128)(2,1)}, bf16[2,2,4,112,960]{4,3,2,1,0:T(8,128)(2,1)}, u32[]{:S(2)}, u32[]{:S(2)}) collective-permute-start(bf16[2,2,4,112,960]{4,3,2,1,0:T(8,128)(2,1)} %get-tuple-element.287), channel_id=1, source_target_pairs={{0,1},{1,0},{2,3},{3,2},{4,5},{5,4},{6,7},{7,6},{8,9},{9,8},{10,11... | collective-permute-start | bytes 10321928 | tf_op jit(solution)/shard_map/ppermute | solution.py:34
  273.7 56.3 %all-to-all-start.3 = ((bf16[4,104,1536]{2,1,0:T(8,128)(2,1)}), bf16[4,104,1536]{2,1,0:T(8,128)(2,1)}, u32[]{:S(2)}, u32[]{:S(2)}) async-start(bf16[4,104,1536]{2,1,0:T(8,128)(2,1)} %pad_maximum_fusion), calls=%async_computation.3 | async-start | bytes 2555904 | tf_op jit(solution)/shard_map/all_to_all | solution.py:384
  278.3 19.9 %collective-permute-start.36 = (bf16[512,768]{1,0:T(8,128)(2,1)S(1)}, bf16[512,768]{1,0:T(8,128)(2,1)S(1)}, u32[]{:S(2)}, u32[]{:S(2)}) collective-permute-start(bf16[512,768]{1,0:T(8,128)(2,1)S(1)} %copy-done.14), channel_id=1, source_target_pairs={{0,2},{2,0},{1,3},{3,1},{4,6},{6,4},{5,7},{7,5},{8,10},{10,8},{9,1... | collective-permute-start | bytes 2359304 | tf_op jit(solution)/shard_map/ppermute | solution.py:38
  298.2 23.6 %collective-permute-start.37 = (bf16[4,112,960]{2,1,0:T(8,128)(2,1)}, bf16[4,112,960]{2,1,0:T(8,128)(2,1)}, u32[]{:S(2)}, u32[]{:S(2)}) collective-permute-start(bf16[4,112,960]{2,1,0:T(8,128)(2,1)} %get-tuple-element.300), channel_id=1, source_target_pairs={{0,2},{2,0},{1,3},{3,1},{4,6},{6,4},{5,7},{7,5},{8,10},{10,8},{9,1... | collective-permute-start | bytes 2580488 | tf_op jit(solution)/shard_map/ppermute | solution.py:38
  299.2 43.3 %collective-permute-start.38 = (bf16[4,112,960]{2,1,0:T(8,128)(2,1)}, bf16[4,112,960]{2,1,0:T(8,128)(2,1)}, u32[]{:S(2)}, u32[]{:S(2)}) collective-permute-start(bf16[4,112,960]{2,1,0:T(8,128)(2,1)} %get-tuple-element.301), channel_id=1, source_target_pairs={{0,4},{4,0},{8,12},{12,8},{16,20},{20,16},{24,28},{28,24},{1,5},{5... | collective-permute-start | bytes 2580488 | tf_op jit(solution)/shard_map/ppermute | solution.py:43
  300.5 42.0 %collective-permute-start.39 = (bf16[4,112,960]{2,1,0:T(8,128)(2,1)}, bf16[4,112,960]{2,1,0:T(8,128)(2,1)}, u32[]{:S(2)}, u32[]{:S(2)}) collective-permute-start(bf16[4,112,960]{2,1,0:T(8,128)(2,1)} %get-tuple-element.302), channel_id=1, source_target_pairs={{0,6},{1,7},{2,4},{3,5},{4,2},{5,3},{6,0},{7,1},{8,14},{9,15},{10,... | collective-permute-start | bytes 2580488 | tf_op jit(solution)/shard_map/ppermute | solution.py:379
  315.6 37.1 %collective-permute-start.40 = (bf16[4,104,576]{2,1,0:T(8,128)(2,1)}, bf16[4,104,576]{2,1,0:T(8,128)(2,1)S(1)}, u32[]{:S(2)}, u32[]{:S(2)}) collective-permute-start(bf16[4,104,576]{2,1,0:T(8,128)(2,1)} %get-tuple-element.305), channel_id=1, source_target_pairs={{0,2},{2,0},{1,3},{3,1},{4,6},{6,4},{5,7},{7,5},{8,10},{10,8},{9,1... | collective-permute-start | bytes 1437704 | tf_op jit(solution)/shard_map/ppermute | solution.py:38
  316.6 45.9 %collective-permute-start.41 = (bf16[4,104,576]{2,1,0:T(8,128)(2,1)}, bf16[4,104,576]{2,1,0:T(8,128)(2,1)S(1)}, u32[]{:S(2)}, u32[]{:S(2)}) collective-permute-start(bf16[4,104,576]{2,1,0:T(8,128)(2,1)} %get-tuple-element.306), channel_id=1, source_target_pairs={{0,4},{4,0},{8,12},{12,8},{16,20},{20,16},{24,28},{28,24},{1,5},{5... | collective-permute-start | bytes 1437704 | tf_op jit(solution)/shard_map/ppermute | solution.py:43
  321.7 42.0 %collective-permute-start.42 = (bf16[4,104,576]{2,1,0:T(8,128)(2,1)}, bf16[4,104,576]{2,1,0:T(8,128)(2,1)}, u32[]{:S(2)}, u32[]{:S(2)}) collective-permute-start(bf16[4,104,576]{2,1,0:T(8,128)(2,1)} %get-tuple-element.307), channel_id=1, source_target_pairs={{0,6},{1,7},{2,4},{3,5},{4,2},{5,3},{6,0},{7,1},{8,14},{9,15},{10,... | collective-permute-start | bytes 1437704 | tf_op jit(solution)/shard_map/ppermute | solution.py:379
  346.7 17.1 %copy-start.45 = (bf16[4,104,576]{2,1,0:T(8,128)(2,1)S(1)}, bf16[4,104,576]{2,1,0:T(8,128)(2,1)}, u32[]{:S(2)}) copy-start(bf16[4,104,576]{2,1,0:T(8,128)(2,1)} %get-tuple-element.304) | copy-start | bytes 1437700
  346.7 25.1 %all-to-all-start.4 = ((bf16[4,112,960]{2,1,0:T(8,128)(2,1)}), bf16[4,112,960]{2,1,0:T(8,128)(2,1)}, u32[]{:S(2)}, u32[]{:S(2)}) async-start(bf16[4,112,960]{2,1,0:T(8,128)(2,1)} %fusion), calls=%async_computation.4 | async-start | bytes 1835008 | tf_op jit(solution)/shard_map/all_to_all | solution.py:384
  351.5 24.5 %copy-start.47 = (s32[2,16]{1,0:T(2,128)S(1)}, s32[2,16]{1,0:T(2,128)}, u32[]{:S(2)}) copy-start(s32[2,16]{1,0:T(2,128)} %blocks_ref.1) | copy-start | bytes 388
  365.9 3.4 collective-permute-start.44
  365.9 12.6 %collective-permute-start.43 = (bf16[512,768]{1,0:T(8,128)(2,1)}, bf16[512,768]{1,0:T(8,128)(2,1)}, u32[]{:S(2)}, u32[]{:S(2)}) collective-permute-start(bf16[512,768]{1,0:T(8,128)(2,1)} %get-tuple-element.308), channel_id=1, source_target_pairs={{0,1},{1,0},{2,3},{3,2},{4,5},{5,4},{6,7},{7,6},{8,9},{9,8},{10,11... | collective-permute-start | bytes 2359304 | tf_op jit(solution)/shard_map/ppermute | solution.py:34
  369.2 11.9 %collective-permute-start.45 = (bf16[8,64,768]{2,1,0:T(8,128)(2,1)S(1)}, bf16[8,64,768]{2,1,0:T(8,128)(2,1)S(1)}, u32[]{:S(2)}, u32[]{:S(2)}) collective-permute-start(bf16[8,64,768]{2,1,0:T(8,128)(2,1)S(1)} %bitcast.61), channel_id=1, source_target_pairs={{0,1},{1,0},{2,3},{3,2},{4,5},{5,4},{6,7},{7,6},{8,9},{9,8},{10,11... | collective-permute-start | bytes 2359304 | tf_op jit(solution)/shard_map/ppermute | solution.py:34
  371.8 17.7 %all-to-all-start.5 = ((bf16[4,104,576]{2,1,0:T(8,128)(2,1)}), bf16[4,104,576]{2,1,0:T(8,128)(2,1)}, u32[]{:S(2)}, u32[]{:S(2)}) async-start(bf16[4,104,576]{2,1,0:T(8,128)(2,1)} %add_convert_fusion.6), calls=%async_computation.5 | async-start | bytes 1064960 | tf_op jit(solution)/shard_map/all_to_all | solution.py:384
  (52 other events, 265.2 us)
